TPU v7x, 32 devices: a whole 2x2x4 slice. The times are simulated.
32 devices in a mesh: seq: 4 (over y, x), wt: 8 (over z, core).
Axes of the slice: x: 2, y: 2, z: 4, core: 2. Of those that a mesh axis runs over, the one named last changes fastest.
Arguments:
- inputs: bfloat16 [8, 512, 2048], P('wt', 'seq'), may hold values from -6 to 6
- segment_ids: int32 [8, 512], P('wt'), may hold values from 0 to 2, never falling along the last dimension, each value on 1 to 256 neighbouring positions
- valid_lengths: int32 [8], replicated, may hold values from 256 to 512, as said below
- teacher: bfloat16 [8, 512, 2048], P('wt', 'seq')
- w_qkv: bfloat16 [2048, 2560], P(('seq', 'wt')), may hold values from -0.125 to 0.125
- conv_weight: bfloat16 [3, 2048], P(None, 'seq'), may hold values from -3 to 3
- w_out: bfloat16 [2048, 2048], P(('seq', 'wt')), may hold values from -2 to 2
- norm_gain: bfloat16 [2048], P(('seq', 'wt')), may hold values from 0.5 to 1.5
- w_gate_up: bfloat16 [2, 2048, 5632], P(None, 'seq', 'wt'), may hold values from -0.125 to 0.125
- w_down: bfloat16 [5632, 2048], P('wt', 'seq'), may hold values from -0.078125 to 0.078125
- mlp_gain: bfloat16 [2048], P(('seq', 'wt')), may hold values from 0.5 to 1.5
Outputs:
- outputs: bfloat16 [8, 512, 2048], P('wt', 'seq')
- inputs_grad: float32 [8, 512, 2048], P('wt', 'seq')
- mean_loss: float32 [], replicated
- grad_w_qkv: float32 [2048, 2560], P(('seq', 'wt'))
- grad_conv: float32 [3, 2048], P(None, ('seq', 'wt'))
- grad_w_out: float32 [2048, 2048], P(('seq', 'wt'))
- grad_norm_gain: float32 [2048], P(('seq', 'wt'))
- grad_w_gate_up: float32 [2, 2048, 5632], P(None, 'seq', 'wt')
- grad_w_down: float32 [5632, 2048], P('wt', 'seq')
- grad_mlp_gain: float32 [2048], P(('seq', 'wt'))
Inputs may be any that keep to these rules, and one draw needn't show every extreme that they name: `segment_ids`: in each sequence the document numbers start at 0, never fall and take every value up to 2; a document holds at most 256 tokens, and some document exactly that many. `valid_lengths`: some sequence counts in full, another in its first half.
All inputs are finite; a program needn't handle non-finite values.
Results may differ from a plain program's by a relative error of at most 0.011.
Values may be sent and summed in bfloat16 or wider, within the bound.
A program may use at most 192 MiB of HBM per device.

v0:
```python
import jax
import jax.numpy as jnp
from jax import lax
from jax.sharding import PartitionSpec as P

H = 16
FEAT = 16
KCONV = 3
DV = 128


epsilon = 1e-05
block_limit = 512


def rms_norm(values, gain_vector):
    inverse_root = lax.rsqrt(jnp.mean(values * values, axis=-1, keepdims=True) + epsilon)
    return values * inverse_root * gain_vector


def contract_last(former, latter):
    return lax.dot_general(
        former, latter, (((1,), (1,)), ((), ())), preferred_element_type=jnp.float32
    )


def contract_first(former, latter):
    return lax.dot_general(
        former, latter, (((0,), (0,)), ((), ())), preferred_element_type=jnp.float32
    )


def shift_down(values, amount, filler):
    padding = jnp.full((amount,) + values.shape[1:], filler, values.dtype)
    return jnp.concatenate([padding, values[:-amount]], axis=0)


def shift_up(values, amount):
    padding = jnp.zeros((amount,) + values.shape[1:], values.dtype)
    return jnp.concatenate([values[amount:], padding], axis=0)


def gated_unit(gate_in, up_in):
    return jax.nn.silu(gate_in) * up_in


def block_kernel(query_block, key_block, query_segments, key_segments, query_start, key_start):
    row_width = query_segments.shape[0]
    scaled_dots = (
        jnp.einsum("hfq,hfk->hqk", query_block, key_block, preferred_element_type=jnp.float32)
        * 0.25
    )
    query_places = query_start + jnp.arange(row_width, dtype=jnp.int32)
    key_places = key_start + jnp.arange(row_width, dtype=jnp.int32)
    allowed = (query_segments[:, None] == key_segments[None, :]) & (
        query_places[:, None] >= key_places[None, :]
    )
    kernel = jnp.where(allowed[None], 1.0 + scaled_dots + 0.5 * scaled_dots * scaled_dots, 0.0)
    return (scaled_dots, allowed, kernel)


def attend_forward(queries, key_rows, values, segments, block_rows):
    head_count, length, value_width = values.shape
    block_count = length // block_rows

    def query_step(query_index, running):
        outputs, denominators = running
        query_start = query_index * block_rows
        query_block = lax.dynamic_slice_in_dim(queries, query_start, block_rows, 2)
        query_segments = lax.dynamic_slice_in_dim(segments, query_start, block_rows, 0)

        def key_step(inner_index, inner_running):
            numerator, denominator = inner_running
            key_start = inner_index * block_rows
            key_block = lax.dynamic_slice_in_dim(key_rows, key_start, block_rows, 2)
            value_block = lax.dynamic_slice_in_dim(values, key_start, block_rows, 1)
            key_segments = lax.dynamic_slice_in_dim(segments, key_start, block_rows, 0)
            scaled_dots, allowed, kernel = block_kernel(
                query_block, key_block, query_segments, key_segments, query_start, key_start
            )
            numerator = numerator + jnp.einsum(
                "hqk,hkd->hqd",
                kernel.astype(jnp.bfloat16),
                value_block,
                preferred_element_type=jnp.float32,
            )
            denominator = denominator + jnp.sum(kernel, axis=2)
            return (numerator, denominator)

        starting = (
            jnp.zeros((head_count, block_rows, value_width), jnp.float32),
            jnp.zeros((head_count, block_rows), jnp.float32),
        )
        numerator, denominator = lax.fori_loop(0, query_index + 1, key_step, starting)
        outputs = lax.dynamic_update_slice_in_dim(
            outputs, numerator / denominator[:, :, None], query_start, 1
        )
        denominators = lax.dynamic_update_slice_in_dim(denominators, denominator, query_start, 1)
        return (outputs, denominators)

    initial = (
        jnp.zeros((head_count, length, value_width), jnp.float32),
        jnp.zeros((head_count, length), jnp.float32),
    )
    return lax.fori_loop(0, block_count, query_step, initial)


def attend_backward(
    queries, key_rows, values, segments, outputs, denominators, incoming, block_rows
):
    head_count, length, value_width = values.shape
    feature_width = queries.shape[1]
    block_count = length // block_rows

    def query_step(query_index, running):
        query_grads, key_grads, value_grads = running
        query_start = query_index * block_rows
        query_block = lax.dynamic_slice_in_dim(queries, query_start, block_rows, 2)
        query_segments = lax.dynamic_slice_in_dim(segments, query_start, block_rows, 0)
        incoming_block = lax.dynamic_slice_in_dim(incoming, query_start, block_rows, 1)
        output_block = lax.dynamic_slice_in_dim(outputs, query_start, block_rows, 1)
        denominator = lax.dynamic_slice_in_dim(denominators, query_start, block_rows, 1)
        numerator_grad = (incoming_block / denominator[:, :, None]).astype(jnp.bfloat16)
        denominator_grad = -jnp.sum(incoming_block * output_block, axis=2) / denominator

        def key_step(inner_index, inner_running):
            query_total, key_grads, value_grads = inner_running
            key_start = inner_index * block_rows
            key_block = lax.dynamic_slice_in_dim(key_rows, key_start, block_rows, 2)
            value_block = lax.dynamic_slice_in_dim(values, key_start, block_rows, 1)
            key_segments = lax.dynamic_slice_in_dim(segments, key_start, block_rows, 0)
            scaled_dots, allowed, kernel = block_kernel(
                query_block, key_block, query_segments, key_segments, query_start, key_start
            )
            weights_low = kernel.astype(jnp.bfloat16)
            weight_grad = jnp.einsum(
                "hqd,hkd->hqk", numerator_grad, value_block, preferred_element_type=jnp.float32
            )
            kernel_grad = jnp.where(allowed[None], weight_grad + denominator_grad[:, :, None], 0.0)
            dots_grad = (0.25 * kernel_grad * (1.0 + scaled_dots)).astype(jnp.bfloat16)
            query_total = query_total + jnp.einsum(
                "hqk,hfk->hfq", dots_grad, key_block, preferred_element_type=jnp.float32
            )
            key_part = jnp.einsum(
                "hqk,hfq->hfk", dots_grad, query_block, preferred_element_type=jnp.float32
            )
            value_part = jnp.einsum(
                "hqk,hqd->hkd", weights_low, numerator_grad, preferred_element_type=jnp.float32
            )
            key_grads = lax.dynamic_update_slice_in_dim(
                key_grads,
                lax.dynamic_slice_in_dim(key_grads, key_start, block_rows, 2) + key_part,
                key_start,
                2,
            )
            value_grads = lax.dynamic_update_slice_in_dim(
                value_grads,
                lax.dynamic_slice_in_dim(value_grads, key_start, block_rows, 1) + value_part,
                key_start,
                1,
            )
            return (query_total, key_grads, value_grads)

        starting = jnp.zeros((head_count, feature_width, block_rows), jnp.float32)
        query_total, key_grads, value_grads = lax.fori_loop(
            0, query_index + 1, key_step, (starting, key_grads, value_grads)
        )
        query_grads = lax.dynamic_update_slice_in_dim(query_grads, query_total, query_start, 2)
        return (query_grads, key_grads, value_grads)

    initial = (
        jnp.zeros((head_count, feature_width, length), jnp.float32),
        jnp.zeros((head_count, feature_width, length), jnp.float32),
        jnp.zeros((head_count, length, value_width), jnp.float32),
    )
    return lax.fori_loop(0, block_count, query_step, initial)


def body(
    inputs,
    segment_ids,
    valid_lengths,
    teacher,
    w_qkv,
    conv_weight,
    w_out,
    norm_gain,
    w_gate_up,
    w_down,
    mlp_gain,
):
    seq_parts = lax.axis_size("seq")
    tok_count = inputs.shape[1]
    model_width = inputs.shape[2]
    length = tok_count * seq_parts
    block_rows = min(block_limit, length)
    head_count = H // seq_parts
    head_width = 2 * FEAT + DV
    rows_in = inputs[0].astype(jnp.float32)
    gathered_qkv, gathered_out, gain_one, gain_two = (
        lax.all_gather(w_qkv, ("seq", "wt"), axis=0, tiled=True),
        lax.all_gather(w_out, ("seq", "wt"), axis=0, tiled=True),
        lax.all_gather(norm_gain, ("seq", "wt"), axis=0, tiled=True),
        lax.all_gather(mlp_gain, ("seq", "wt"), axis=0, tiled=True),
    )
    gain_first = gain_one.astype(jnp.float32)
    hidden_value, first_pull = jax.vjp(rms_norm, rows_in, gain_first)
    hidden_low = hidden_value.astype(jnp.bfloat16)
    projected = jnp.dot(hidden_low, gathered_qkv, preferred_element_type=jnp.float32).astype(
        jnp.bfloat16
    )
    arrived = lax.all_to_all(
        projected.reshape(tok_count, seq_parts, head_count * head_width),
        "seq",
        split_axis=1,
        concat_axis=0,
        tiled=True,
    )
    grouped = arrived.reshape(length, head_count, head_width)
    head_queries = grouped[:, :, :FEAT].transpose(1, 2, 0)
    head_keys = grouped[:, :, FEAT : 2 * FEAT].transpose(1, 2, 0)
    raw_values = grouped[:, :, 2 * FEAT :].astype(jnp.float32)
    segments = segment_ids[0]
    conv_taps = conv_weight.astype(jnp.float32).reshape(KCONV, head_count, DV)
    tap_masks = [jnp.ones((length,), jnp.float32)]
    mixed_values = conv_taps[0] * raw_values
    for tap_index in range(1, KCONV):
        earlier = shift_down(segments, tap_index, -1)
        tap_masks.append((earlier == segments).astype(jnp.float32))
        mixed_values = (
            mixed_values
            + conv_taps[tap_index]
            * shift_down(raw_values, tap_index, 0.0)
            * tap_masks[tap_index][:, None, None]
        )
    conv_low = mixed_values.astype(jnp.bfloat16).transpose(1, 0, 2)
    head_outputs, denominators = attend_forward(
        head_queries, head_keys, conv_low, segments, block_rows
    )
    mixer_low = (
        head_outputs.transpose(1, 0, 2)
        .reshape(seq_parts, tok_count, head_count * DV)
        .astype(jnp.bfloat16)
    )
    mixer_tok = lax.all_to_all(mixer_low, "seq", split_axis=0, concat_axis=2, tiled=True).reshape(
        tok_count, model_width
    )
    attended = rows_in + jnp.dot(mixer_tok, gathered_out, preferred_element_type=jnp.float32)
    gate_up_part, down_part = (
        lax.all_gather(w_gate_up, "seq", axis=1, tiled=True),
        lax.all_gather(w_down, "seq", axis=1, tiled=True),
    )
    gain_second = gain_two.astype(jnp.float32)
    normed_value, second_pull = jax.vjp(rms_norm, attended, gain_second)
    normed_low = normed_value.astype(jnp.bfloat16)
    normed_all = lax.all_gather(normed_low, "wt", axis=0, tiled=True)
    gate_all = jnp.dot(normed_all, gate_up_part[0], preferred_element_type=jnp.float32)
    up_all = jnp.dot(normed_all, gate_up_part[1], preferred_element_type=jnp.float32)
    active_value, gate_pull = jax.vjp(gated_unit, gate_all, up_all)
    active_all = active_value.astype(jnp.bfloat16)
    branch_out = lax.psum_scatter(
        jnp.dot(active_all, down_part, preferred_element_type=jnp.float32).astype(jnp.bfloat16),
        "wt",
        scatter_dimension=0,
        tiled=True,
    ).astype(jnp.float32)
    outputs = attended + branch_out
    sequence_length = lax.dynamic_index_in_dim(
        valid_lengths, lax.axis_index("wt"), 0, keepdims=False
    )
    positions = lax.axis_index("seq") * tok_count + jnp.arange(tok_count, dtype=jnp.int32)
    keep_mask = (positions < sequence_length).astype(jnp.float32)
    residual_error = (outputs - teacher[0].astype(jnp.float32)) * keep_mask[:, None]
    total_energy = lax.psum(0.5 * jnp.sum(residual_error * residual_error), ("seq", "wt"))
    valid_total = jnp.sum(valid_lengths).astype(jnp.float32)
    mean_loss = 2.0 * total_energy / (valid_total * model_width)
    branch_grad = residual_error.astype(jnp.bfloat16)
    error_all = lax.all_gather(branch_grad, "wt", axis=0, tiled=True)
    active_grad = contract_last(error_all, down_part)
    down_term = contract_first(active_all, error_all)
    gate_grad, up_grad = gate_pull(active_grad)
    gate_up_grad = jnp.stack([gate_grad, up_grad]).astype(jnp.bfloat16)
    gate_up_term = jnp.einsum(
        "tc,gtf->gcf", normed_all, gate_up_grad, preferred_element_type=jnp.float32
    )
    normed_grad = lax.psum_scatter(
        jnp.einsum(
            "gtf,gcf->tc", gate_up_grad, gate_up_part, preferred_element_type=jnp.float32
        ).astype(jnp.bfloat16),
        "wt",
        scatter_dimension=0,
        tiled=True,
    ).astype(jnp.float32)
    attended_back, gain_two_term = second_pull(normed_grad)
    attended_grad = residual_error + attended_back
    grad_w_gate_up, grad_w_down = (
        lax.psum_scatter(
            gate_up_term.astype(jnp.bfloat16), "seq", scatter_dimension=1, tiled=True
        ).astype(jnp.float32),
        lax.psum_scatter(
            down_term.astype(jnp.bfloat16), "seq", scatter_dimension=1, tiled=True
        ).astype(jnp.float32),
    )
    mixer_branch = attended_grad.astype(jnp.bfloat16)
    out_term = contract_first(mixer_tok, mixer_branch)
    mixer_grad = contract_last(mixer_branch, gathered_out).astype(jnp.bfloat16)
    head_incoming = lax.all_to_all(
        mixer_grad.reshape(tok_count, seq_parts, head_count * DV),
        "seq",
        split_axis=1,
        concat_axis=0,
        tiled=True,
    )
    head_incoming = (
        head_incoming.reshape(length, head_count, DV).transpose(1, 0, 2).astype(jnp.float32)
    )
    query_grads, key_grads, value_grads = attend_backward(
        head_queries,
        head_keys,
        conv_low,
        segments,
        head_outputs,
        denominators,
        head_incoming,
        block_rows,
    )
    mixed_grad = value_grads.transpose(1, 0, 2)
    conv_terms = [jnp.sum(mixed_grad * raw_values, axis=0)]
    raw_grad = conv_taps[0] * mixed_grad
    for tap_index in range(1, KCONV):
        masked = mixed_grad * tap_masks[tap_index][:, None, None]
        conv_terms.append(jnp.sum(masked * shift_down(raw_values, tap_index, 0.0), axis=0))
        raw_grad = raw_grad + conv_taps[tap_index] * shift_up(masked, tap_index)
    conv_block = jnp.stack(conv_terms).reshape(KCONV, head_count * DV)
    conv_full = lax.dynamic_update_slice_in_dim(
        jnp.zeros((KCONV, model_width), jnp.float32),
        conv_block,
        lax.axis_index("seq") * (head_count * DV),
        1,
    )
    projected_grad = jnp.concatenate(
        [query_grads.transpose(2, 0, 1), key_grads.transpose(2, 0, 1), raw_grad], axis=2
    ).astype(jnp.bfloat16)
    returned = lax.all_to_all(
        projected_grad.reshape(seq_parts, tok_count, head_count * head_width),
        "seq",
        split_axis=0,
        concat_axis=2,
        tiled=True,
    )
    returned = returned.reshape(tok_count, seq_parts * head_count * head_width)
    qkv_term = contract_first(hidden_low, returned)
    hidden_grad = contract_last(returned, gathered_qkv)
    inputs_back, gain_one_term = first_pull(hidden_grad)
    inputs_grad = attended_grad + inputs_back
    grad_w_qkv, grad_w_out, grad_norm_gain, grad_mlp_gain, grad_conv = (
        lax.psum_scatter(qkv_term, ("seq", "wt"), scatter_dimension=0, tiled=True),
        lax.psum_scatter(out_term, ("seq", "wt"), scatter_dimension=0, tiled=True),
        lax.psum_scatter(gain_one_term, ("seq", "wt"), scatter_dimension=0, tiled=True),
        lax.psum_scatter(gain_two_term, ("seq", "wt"), scatter_dimension=0, tiled=True),
        lax.psum_scatter(conv_full, ("seq", "wt"), scatter_dimension=1, tiled=True),
    )
    return (
        outputs.astype(jnp.bfloat16)[None],
        inputs_grad[None],
        mean_loss,
        grad_w_qkv,
        grad_conv,
        grad_w_out,
        grad_norm_gain,
        grad_w_gate_up,
        grad_w_down,
        grad_mlp_gain,
    )


def solution(mesh):
    in_specs = (
        P("wt", "seq", None),
        P("wt", None),
        P(),
        P("wt", "seq", None),
        P(("seq", "wt"), None),
        P(None, "seq"),
        P(("seq", "wt"), None),
        P(("seq", "wt")),
        P(None, "seq", "wt"),
        P("wt", "seq"),
        P(("seq", "wt")),
    )
    out_specs = (
        P("wt", "seq", None),
        P("wt", "seq", None),
        P(),
        P(("seq", "wt"), None),
        P(None, ("seq", "wt")),
        P(("seq", "wt"), None),
        P(("seq", "wt")),
        P(None, "seq", "wt"),
        P("wt", "seq"),
        P(("seq", "wt")),
    )
    return jax.shard_map(body, mesh=mesh, in_specs=in_specs, out_specs=out_specs, check_vma=False)
```

profile of v0, /device:TPU:8, one launch (start us, length us, event | category | flops | bytes accessed | tf_op | source)
XLA Modules:
  0.0 1195.3 jit_solution(15472349918996663615)
XLA Ops:
  11.1 41.0 %all-reduce.10 = (bf16[2048]{0:T(1024)(128)(2,1)S(1)}, bf16[2048]{0:T(1024)(128)(2,1)S(1)}) all-reduce(bf16[2048]{0:T(1024)(128)(2,1)S(1)} %dynamic-update-slice, bf16[2048]{0:T(1024)(128)(2,1)S(1)} %dynamic-update-slice.1), channel_id=1, replica_groups=mesh['seq'=4,'wt'=8] {'seq','wt'}, use_global_device_ids=true, to_apply=%add.5 | all-reduce | flops 4096 | bytes 16384
  53.4 45.8 %all-gather.7.cloned.1.call-done = bf16[2048,2560]{1,0:T(8,128)(2,1)} async-done(((bf16[64,2560]{1,0:T(8,128)(2,1)}), bf16[2048,2560]{1,0:T(8,128)(2,1)}) %all-gather.7.cloned.1.call-update) | async-done | bytes 10485776 | tf_op jit(solution)/shard_map/all_gather | solution.py:201
  109.7 11.5 all-to-all-done
  131.7 55.9 %all-gather.9.cloned.1.call-done = bf16[2048,2048]{1,0:T(8,128)(2,1)} async-done(((bf16[64,2048]{1,0:T(8,128)(2,1)}), bf16[2048,2048]{1,0:T(8,128)(2,1)}) %all-gather.9.cloned.1.call-update) | async-done | bytes 8388624 | tf_op jit(solution)/shard_map/all_gather | solution.py:202
  194.2 59.5 %all-gather.13.cloned.1.call-done = bf16[2,2048,704]{1,2,0:T(8,128)(2,1)} async-done(((bf16[2,512,704]{1,2,0:T(8,128)(2,1)}), bf16[2,2048,704]{1,2,0:T(8,128)(2,1)}) %all-gather.13.cloned.1.call-update) | async-done | bytes 5767184 | tf_op jit(solution)/shard_map/all_gather | solution.py:250
  253.7 47.7 %all-gather.11.cloned.1.call-done = bf16[1024,2048]{1,0:T(8,128)(2,1)} async-done(((bf16[128,2048]{1,0:T(8,128)(2,1)}), bf16[1024,2048]{1,0:T(8,128)(2,1)}) %all-gather.11.cloned.1.call-update) | async-done | bytes 4194320 | tf_op jit(solution)/shard_map/all_gather | solution.py:256
  314.2 30.7 %all-gather.15.cloned.1.call-done = bf16[704,2048]{1,0:T(8,128)(2,1)} async-done(((bf16[704,512]{1,0:T(8,128)(2,1)}), bf16[704,2048]{1,0:T(8,128)(2,1)}) %all-gather.15.cloned.1.call-update) | async-done | bytes 2883600 | tf_op jit(solution)/shard_map/all_gather | solution.py:251
  345.0 7.7 convolution_convert_fusion
  354.6 44.5 %reduce-scatter.10.cloned.1.call-done = bf16[128,2048]{1,0:T(8,128)(2,1)} async-done(((bf16[1024,2048]{1,0:T(8,128)(2,1)}), bf16[128,2048]{1,0:T(8,128)(2,1)}) %reduce-scatter.10.cloned.1.call-update) | async-done | bytes 524304 | tf_op jit(solution)/shard_map/reduce_scatter | solution.py:261
  401.2 47.7 %all-gather.17.cloned.1.call-done = bf16[1024,2048]{1,0:T(8,128)(2,1)} async-done(((bf16[128,2048]{1,0:T(8,128)(2,1)}), bf16[1024,2048]{1,0:T(8,128)(2,1)}) %all-gather.17.cloned.1.call-update) | async-done | bytes 4194320 | tf_op jit(solution)/shard_map/all_gather | solution.py:278
  448.9 8.7 fusion.10
  459.2 11.1 bitcast_convert_fusion
  478.2 38.8 %reduce-scatter.12.cloned.1.call-done = bf16[128,2048]{1,0:T(8,128)(2,1)} async-done(((bf16[1024,2048]{1,0:T(8,128)(2,1)}), bf16[128,2048]{1,0:T(8,128)(2,1)}) %reduce-scatter.12.cloned.1.call-update) | async-done | bytes 524304 | tf_op jit(solution)/shard_map/reduce_scatter | solution.py:286
  535.4 14.6 %all-to-all-done.2 = bf16[128,4,512]{0,2,1:T(8,128)(2,1)} async-done(((bf16[128,4,512]{0,2,1:T(8,128)(2,1)}), bf16[128,4,512]{0,2,1:T(8,128)(2,1)}, u32[]{:S(2)}, u32[]{:S(2)}) %all-to-all-start.2) | async-done | bytes 524320 | tf_op jit(solution)/shard_map/all_to_all | solution.py:307
  562.7 10.6 convert_bitcast_fusion
  573.6 8.2 fusion.50
  591.0 13.5 %all_to_all.54 = bf16[4,128,640]{1,2,0:T(8,128)(2,1)S(1)} all-to-all(bf16[4,128,640]{1,2,0:T(8,128)(2,1)S(1)} %copy.53), channel_id=1, replica_groups=mesh['seq'=4,'wt'=8] {'seq'}, dimensions={0} | all-to-all | bytes 1310720 | tf_op jit(solution)/shard_map/all_to_all | solution.py:344
  604.5 8.8 fusion.40
  617.7 84.0 %reduce-scatter.22.cloned.1.call-done = f32[64,3]{1,0:T(8,128)} async-done(((f32[2048,3]{1,0:T(8,128)}), f32[64,3]{1,0:T(8,128)}) %reduce-scatter.22.cloned.1.call-update) | async-done | bytes 784
  703.1 8.5 fusion.22
  711.7 44.3 %all-reduce.9 = (f32[]{:T(128)}, f32[2048]{0:T(1024)S(1)}, f32[2048]{0:T(1024)S(1)}) all-reduce(f32[]{:T(128)S(6)} %mul.382, f32[2048]{0:T(1024)S(1)} %get-tuple-element.252, f32[2048]{0:T(1024)S(1)} %get-tuple-element.250), channel_id=1, replica_groups=mesh['seq'=4,'wt'=8] {'seq','wt'}, use_global_device_ids=true, to_apply=%region_9.10 | all-reduce | flops 4097 | bytes 32776 | tf_op jit(solution)/shard_map/psum | solution.py:274
  760.3 13.0 %reduce-scatter.18.cloned.1.call-done = bf16[2,512,704]{1,2,0:T(8,128)(2,1)} async-done(((bf16[2,2048,704]{1,2,0:T(8,128)(2,1)}), bf16[2,512,704]{1,2,0:T(8,128)(2,1)}) %reduce-scatter.18.cloned.1.call-update) | async-done | bytes 1441808 | tf_op jit(solution)/shard_map/reduce_scatter | solution.py:297
  776.6 179.9 %reduce-scatter.16.cloned.1.call-done = f32[64,2048]{1,0:T(8,128)} async-done(((f32[2048,2048]{1,0:T(8,128)}), f32[64,2048]{1,0:T(8,128)}) %reduce-scatter.16.cloned.1.call-update) | async-done | bytes 524304 | tf_op jit(solution)/shard_map/reduce_scatter | solution.py:358
  956.5 231.0 %reduce-scatter.14.cloned.1.call-done = f32[64,2560]{1,0:T(8,128)} async-done(((f32[2048,2560]{1,0:T(8,128)}), f32[64,2560]{1,0:T(8,128)}) %reduce-scatter.14.cloned.1.call-update) | async-done | bytes 655376 | tf_op jit(solution)/shard_map/reduce_scatter | solution.py:357
  (134 shorter events, 110.6 us)
Async XLA Ops:
  7.2 92.1 %all-gather.7.cloned.1.call-start = ((), (), s32[]{:S(2)}) async-start(), calls=%async_computation.11 | async-start | bytes 10813440 | tf_op jit(solution)/shard_map/all_gather | solution.py:201
  7.9 179.7 %all-gather.9.cloned.1.call-start = ((), (), s32[]{:S(2)}) async-start(), calls=%async_computation.12 | async-start | bytes 8650752 | tf_op jit(solution)/shard_map/all_gather | solution.py:202
  8.7 245.0 %all-gather.13.cloned.1.call-start = ((), (), s32[]{:S(2)}) async-start(), calls=%async_computation.14 | async-start | bytes 7208960 | tf_op jit(solution)/shard_map/all_gather | solution.py:250
  53.4 56.0 %copy-start.11 = (s32[1,512]{1,0:T(1,128)S(1)}, s32[1,512]{1,0:T(1,128)}, u32[]{:S(2)}) copy-start(s32[1,512]{1,0:T(1,128)} %param.12) | copy-start | bytes 6148
  53.4 56.1 %copy-start.12 = (bf16[3,512]{1,0:T(4,128)(2,1)S(1)}, bf16[3,512]{1,0:T(4,128)(2,1)}, u32[]{:S(2)}) copy-start(bf16[3,512]{1,0:T(4,128)(2,1)} %param.16) | copy-start | bytes 9220
  105.9 15.3 %all-to-all-start = ((bf16[128,4,640]{2,0,1:T(8,128)(2,1)}), bf16[128,4,640]{2,0,1:T(8,128)(2,1)S(1)}, u32[]{:S(2)}, u32[]{:S(2)}) async-start(bf16[128,4,640]{2,0,1:T(8,128)(2,1)} %bitcast.168), calls=%async_computation | async-start | bytes 1310720 | tf_op jit(solution)/shard_map/all_to_all | solution.py:212
  124.8 62.8 %copy-start = (bf16[1,128,2048]{2,1,0:T(8,128)(2,1)S(1)}, bf16[1,128,2048]{2,1,0:T(8,128)(2,1)}, u32[]{:S(2)}) copy-start(bf16[1,128,2048]{2,1,0:T(8,128)(2,1)} %param.11) | copy-start | bytes 1572868
  128.2 59.4 %all-to-all-start.1 = ((bf16[4,128,512]{1,2,0:T(8,128)(2,1)}), bf16[4,128,512]{1,2,0:T(8,128)(2,1)S(1)}, u32[]{:S(2)}, u32[]{:S(2)}) async-start(bf16[4,128,512]{1,2,0:T(8,128)(2,1)} %copy.44), calls=%async_computation.1 | async-start | bytes 1048576 | tf_op jit(solution)/shard_map/all_to_all | solution.py:245
  131.6 169.7 %all-gather.11.cloned.1.call-start = ((), (), s32[]{:S(2)}) async-start(), calls=%async_computation.13 | async-start | bytes 4718592 | tf_op jit(solution)/shard_map/all_gather | solution.py:256
  193.3 151.6 %all-gather.15.cloned.1.call-start = ((), (), s32[]{:S(2)}) async-start(), calls=%async_computation.15 | async-start | bytes 3604480 | tf_op jit(solution)/shard_map/all_gather | solution.py:251
  193.9 205.2 %reduce-scatter.10.cloned.1.call-start = ((), (), s32[]{:S(2)}) async-start(), calls=%async_computation.16 | async-start | bytes 4718592 | tf_op jit(solution)/shard_map/reduce_scatter | solution.py:261
  301.4 7.9 copy-start.13
  301.4 7.9 copy-start.14
  352.7 46.4 %copy-start.4 = (bf16[1,128,2048]{2,1,0:T(8,128)(2,1)S(1)}, bf16[1,128,2048]{2,1,0:T(8,128)(2,1)}, u32[]{:S(2)}) copy-start(bf16[1,128,2048]{2,1,0:T(8,128)(2,1)} %param.14) | copy-start | bytes 1572868
  352.7 96.1 %all-gather.17.cloned.1.call-start = ((), (), s32[]{:S(2)}) async-start(), calls=%async_computation.17 | async-start | bytes 4718592 | tf_op jit(solution)/shard_map/all_gather | solution.py:278
  401.2 115.8 %reduce-scatter.12.cloned.1.call-start = ((), (), s32[]{:S(2)}) async-start(), calls=%async_computation.18 | async-start | bytes 4718592 | tf_op jit(solution)/shard_map/reduce_scatter | solution.py:286
  470.3 46.6 %copy-start.5 = (bf16[128,2048]{1,0:T(8,128)(2,1)S(1)}, bf16[128,2048]{1,0:T(8,128)(2,1)}, u32[]{:S(2)}) copy-start(bf16[128,2048]{1,0:T(8,128)(2,1)} %reduce-scatter.10.cloned.1.call-done) | copy-start | bytes 1572868
  470.3 144.3 %reduce-scatter.20.cloned.1.call-start = ((), (), s32[]{:S(2)}) async-start(), calls=%async_computation.22 | async-start | bytes 3604480 | tf_op jit(solution)/shard_map/reduce_scatter | solution.py:300
  529.0 26.5 %copy-start.2 = (f32[512,4,128]{0,2,1:T(8,128)S(1)}, f32[512,4,128]{0,2,1:T(8,128)}, u32[]{:S(2)}) copy-start(f32[512,4,128]{0,2,1:T(8,128)} %copy-done.1) | copy-start | bytes 3145732
  531.2 18.8 %all-to-all-start.2 = ((bf16[128,4,512]{0,2,1:T(8,128)(2,1)}), bf16[128,4,512]{0,2,1:T(8,128)(2,1)}, u32[]{:S(2)}, u32[]{:S(2)}) async-start(bf16[128,4,512]{0,2,1:T(8,128)(2,1)} %bitcast.184), calls=%async_computation.4 | async-start | bytes 1048576 | tf_op jit(solution)/shard_map/all_to_all | solution.py:307
  535.4 166.3 %reduce-scatter.22.cloned.1.call-start = ((), (), s32[]{:S(2)}) async-start(), calls=%async_computation.23 | async-start | bytes 1081344
  562.7 210.6 %reduce-scatter.18.cloned.1.call-start = ((), (), s32[]{:S(2)}) async-start(), calls=%async_computation.21 | async-start | bytes 7208960 | tf_op jit(solution)/shard_map/reduce_scatter | solution.py:297
  573.3 383.2 %reduce-scatter.16.cloned.1.call-start = ((), (), s32[]{:S(2)}) async-start(), calls=%async_computation.20 | async-start | bytes 17301504 | tf_op jit(solution)/shard_map/reduce_scatter | solution.py:358
  581.8 605.7 %reduce-scatter.14.cloned.1.call-start = ((), (), s32[]{:S(2)}) async-start(), calls=%async_computation.19 | async-start | bytes 21626880 | tf_op jit(solution)/shard_map/reduce_scatter | solution.py:357
  (13 other events, 29.6 us)
Sparse Core Ops, SparseCore 0:
  10.9 88.3 all-gather.6
  102.2 85.3 all-gather.8
  189.4 64.2 all-gather.12
  255.7 45.6 all-gather.10
  303.0 41.9 all-gather.14
  352.9 46.1 reduce-scatter.9
  401.3 47.5 all-gather.16
  470.5 46.4 reduce-scatter.11
  520.6 49.3 reduce-scatter.19
  572.0 129.6 reduce-scatter.21
  705.0 68.2 reduce-scatter.17
  776.1 180.3 reduce-scatter.15
  959.5 227.9 reduce-scatter.13
where the time goes:
time: 1210 us; the launch traced here: 1200 us
  waiting for transfers between devices  907 us (75%)
  matrix products  114 us (9%)
  blocking collectives  98.9 us (8%)
  local copies, waits for them, and re-layouts  23.6 us (2%)
  other arithmetic  21.9 us (2%)
  between operations  17.7 us (1%)
  starting transfers between devices  12.4 us (1%)
    reduce_scatter x1, waiting for transfers between devices, body(): lax.psum_scatter(qkv_term, ('seq', 'wt'), scatter_dimension=0, tiled=True)  231 us
    reduce_scatter x1, waiting for transfers between devices, body(): lax.psum_scatter(out_term, ('seq', 'wt'), scatter_dimension=0, tiled=True)  180 us
    unnamed x14, waiting for transfers between devices  86.8 us
    all_gather x1, waiting for transfers between devices, body(): lax.all_gather(w_gate_up, 'seq', axis=1, tiled=True)  59.5 us
    all_gather x1, waiting for transfers between devices, body(): lax.all_gather(w_out, ('seq', 'wt'), axis=0, tiled=True)  55.9 us
    all_gather x1, waiting for transfers between devices, body(): normed_all = lax.all_gather(normed_low, 'wt', axis=0, tiled=True)  47.7 us
    all_gather x1, waiting for transfers between devices, body(): error_all = lax.all_gather(branch_grad, 'wt', axis=0, tiled=True)  47.7 us
    all_gather x1, waiting for transfers between devices, body(): lax.all_gather(w_qkv, ('seq', 'wt'), axis=0, tiled=True)  45.8 us
  transfers between devices with their start and end apart: 16, of which 14 were waited for; matrix products, arithmetic and copies ran while one was open for 10% of the time, Pallas kernels for 0%

commit v1 on v0

--- a/solution.py
+++ b/solution.py
@@ -1,6 +1,8 @@
 import jax
 import jax.numpy as jnp
 from jax import lax
+from jax.experimental import pallas as pl
+from jax.experimental.pallas import tpu as pltpu
 from jax.sharding import PartitionSpec as P
 
 H = 16
@@ -175,6 +177,758 @@
     )
     return lax.fori_loop(0, block_count, query_step, initial)
 
+
+MESH = pl.DeviceIdType.MESH
+VMEM = pl.BlockSpec(memory_space=pltpu.VMEM)
+
+
+class Place:
+    def __init__(self, seq, wt):
+        self.seq, self.wt = seq, wt
+        self.ys, self.zs = seq // 2, wt // 2
+        self.s, self.w = lax.axis_index("seq"), lax.axis_index("wt")
+        self.y, self.x = lax.div(self.s, 2), lax.rem(self.s, 2)
+        self.z, self.c = lax.div(self.w, 2), lax.rem(self.w, 2)
+
+    def across(self):
+        return (self.y * 2 + 1 - self.x, self.w)
+
+    def beside(self, step):
+        return lax.rem(self.y + step, self.ys)
+
+    def column(self, y):
+        return (y * 2 + self.x, self.w)
+
+    def partner(self):
+        return (self.s, self.z * 2 + 1 - self.c)
+
+    def level(self, z):
+        return (self.s, z * 2 + self.c)
+
+    def meet(self, square, line):
+        barrier = pltpu.get_barrier_semaphore()
+        count = 0
+        if square:
+            for step in range(1, self.seq):
+                device = (lax.rem(self.s + step, self.seq), self.w)
+                pl.semaphore_signal(barrier, inc=1, device_id=device, device_id_type=MESH)
+                count += 1
+        if line:
+            for step in range(1, self.wt):
+                device = (self.s, lax.rem(self.w + step, self.wt))
+                pl.semaphore_signal(barrier, inc=1, device_id=device, device_id_type=MESH)
+                count += 1
+        pl.semaphore_wait(barrier, count)
+
+
+def send(source, target, leaving, arriving, device):
+    return pltpu.make_async_remote_copy(
+        src_ref=source,
+        dst_ref=target,
+        send_sem=leaving,
+        recv_sem=arriving,
+        device_id=device,
+        device_id_type=MESH,
+    )
+
+
+def add_into(target, sources):
+    if len(target.shape) == 3:
+        for index in range(target.shape[0]):
+            add_into(target.at[index], [source.at[index] for source in sources])
+        return
+    rows = target.shape[0]
+    tile = next(t for t in (64, 32, 16, 8, rows) if rows % t == 0)
+
+    def step(index, carry):
+        window = pl.ds(pl.multiple_of(index * tile, tile), tile)
+        total = sources[0][window, :].astype(jnp.float32)
+        for source in sources[1:]:
+            total = total + source[window, :].astype(jnp.float32)
+        target[window, :] = total.astype(target.dtype)
+        return carry
+
+    lax.fori_loop(0, rows // tile, step, 0)
+
+
+class SquareGather:
+    @staticmethod
+    def semaphores(seq):
+        return [
+            pltpu.SemaphoreType.DMA((2 + seq // 2,)),
+            pltpu.SemaphoreType.DMA((seq // 2, 3)),
+            pltpu.SemaphoreType.DMA((seq, 2)),
+        ]
+
+    def __init__(self, at, view, own, sems):
+        self.at, self.view, self.own = at, view, own
+        self.over_x, self.over_y, self.got = sems
+        self.sent = []
+
+    def go(self, source, s, half, leaving, device):
+        copy = send(source, self.view(s, half), leaving, self.got.at[s, half], device)
+        copy.start()
+        self.sent.append(copy)
+
+    def wait(self, s, half):
+        slot = self.view(s, half)
+        send(slot, slot, self.over_x.at[0], self.got.at[s, half], self.at.across()).wait_recv()
+
+    def start(self):
+        at = self.at
+        for half in range(2):
+            self.go(self.own(half), at.s, half, self.over_x.at[half], at.across())
+            for step in range(1, at.ys):
+                target = at.column(at.beside(step))
+                self.go(self.own(1 - half), at.s, 1 - half, self.over_y.at[step, half], target)
+
+    def relay(self):
+        at = self.at
+        other = at.y * 2 + 1 - at.x
+        self.wait(other, 0)
+        for step in range(1, at.ys):
+            self.go(self.view(other, 0), other, 0, self.over_y.at[step, 2], at.column(at.beside(step)))
+        for step in range(1, at.ys):
+            s = at.beside(step) * 2 + at.x
+            self.wait(s, 1)
+            self.go(self.view(s, 1), s, 1, self.over_x.at[1 + step], at.across())
+
+    def finish(self):
+        at = self.at
+        self.wait(at.y * 2 + 1 - at.x, 1)
+        for step in range(1, at.ys):
+            y = at.beside(step)
+            self.wait(y * 2 + at.x, 0)
+            self.wait(y * 2 + 1 - at.x, 0)
+            self.wait(y * 2 + 1 - at.x, 1)
+        for copy in self.sent:
+            copy.wait_send()
+
+
+class SquareSum:
+    @staticmethod
+    def scratch(seq, half_shape):
+        ys = seq // 2
+        return [
+            pltpu.VMEM((ys,) + half_shape, jnp.bfloat16),
+            pltpu.VMEM((ys, 2) + half_shape, jnp.bfloat16),
+            pltpu.VMEM((ys,) + half_shape, jnp.bfloat16),
+            pltpu.VMEM(half_shape, jnp.bfloat16),
+            pltpu.VMEM((ys,) + half_shape, jnp.bfloat16),
+            pltpu.VMEM(half_shape, jnp.bfloat16),
+            pltpu.SemaphoreType.DMA((ys, 2, 2)),
+            pltpu.SemaphoreType.DMA((ys, 3, 2)),
+        ]
+
+    def __init__(self, at, part, scratch):
+        self.at, self.part = at, part
+        self.from_x, self.from_y, self.last_y, self.last_x, self.sum_y, self.sum_x, self.xs, self.yss = scratch
+        self.sent = []
+
+    def go(self, source, target, leaving, arriving, device):
+        copy = send(source, target, leaving, arriving, device)
+        copy.start()
+        self.sent.append(copy)
+
+    def wait(self, slot, leaving, arriving):
+        send(slot, slot, leaving, arriving, self.at.across()).wait_recv()
+
+    def start(self):
+        at = self.at
+        for y in range(at.ys):
+            self.go(
+                self.part(y * 2 + 1 - at.x, 0),
+                self.from_x.at[y],
+                self.xs.at[y, 0, 0],
+                self.xs.at[y, 0, 1],
+                at.across(),
+            )
+        for step in range(1, at.ys):
+            y = at.beside(step)
+            for x in range(2):
+                self.go(
+                    self.part(y * 2 + x, 1),
+                    self.from_y.at[at.y, x],
+                    self.yss.at[step, x, 0],
+                    self.yss.at[at.y, x, 1],
+                    at.column(y),
+                )
+
+    def relay(self):
+        at = self.at
+        for step in range(1, at.ys):
+            y = at.beside(step)
+            self.wait(self.from_x.at[y], self.xs.at[y, 0, 0], self.xs.at[y, 0, 1])
+            add_into(self.sum_y.at[y], [self.part(y * 2 + at.x, 0), self.from_x.at[y]])
+            self.go(
+                self.sum_y.at[y],
+                self.last_y.at[at.y],
+                self.yss.at[step, 2, 0],
+                self.yss.at[at.y, 2, 1],
+                at.column(y),
+            )
+        terms = []
+        for step in range(1, at.ys):
+            y = at.beside(step)
+            for x in range(2):
+                self.wait(self.from_y.at[y, x], self.yss.at[step, x, 0], self.yss.at[y, x, 1])
+            terms.append(self.from_y.at[y, 1 - at.x])
+        add_into(self.sum_x, [self.part(at.y * 2 + 1 - at.x, 1)] + terms)
+        self.go(self.sum_x, self.last_x, self.xs.at[0, 1, 0], self.xs.at[0, 1, 1], at.across())
+
+    def finish(self, total):
+        at = self.at
+        self.wait(self.from_x.at[at.y], self.xs.at[0, 0, 0], self.xs.at[at.y, 0, 1])
+        terms = [self.part(at.s, 0), self.from_x.at[at.y]]
+        for step in range(1, at.ys):
+            y = at.beside(step)
+            self.wait(self.last_y.at[y], self.yss.at[step, 2, 0], self.yss.at[y, 2, 1])
+            terms.append(self.last_y.at[y])
+        add_into(total(0), terms)
+        self.wait(self.last_x, self.xs.at[0, 1, 0], self.xs.at[0, 1, 1])
+        terms = [self.part(at.s, 1), self.last_x]
+        for step in range(1, at.ys):
+            terms.append(self.from_y.at[at.beside(step), at.x])
+        add_into(total(1), terms)
+        for copy in self.sent:
+            copy.wait_send()
+
+
+class LineGather:
+    @staticmethod
+    def semaphores(wt):
+        return [pltpu.SemaphoreType.DMA((5, wt // 2))]
+
+    def __init__(self, at, view, sems):
+        self.at, self.view, self.sems = at, view, sems[0]
+
+    def up(self, z, source=None):
+        slot = self.view(z * 2 + self.at.c)
+        source = slot if source is None else source
+        return send(source, slot, self.sems.at[0, z], self.sems.at[3, z], self.at.level(self.at.z + 1))
+
+    def down(self, z, source=None):
+        slot = self.view(z * 2 + self.at.c)
+        source = slot if source is None else source
+        return send(source, slot, self.sems.at[1, z], self.sems.at[3, z], self.at.level(self.at.z - 1))
+
+    def over(self, z, source=None):
+        slot = self.view(z * 2 + self.at.c)
+        source = slot if source is None else source
+        return send(source, slot, self.sems.at[2, z], self.sems.at[4, z], self.at.partner())
+
+    def start(self, source=None):
+        at = self.at
+
+        @pl.when(at.z + 1 < at.zs)
+        def _():
+            self.up(at.z, source).start()
+
+        @pl.when(at.z > 0)
+        def _():
+            self.down(at.z, source).start()
+
+        self.over(at.z, source).start()
+
+    def step(self, index):
+        at = self.at
+        below, above = at.z - 1 - index, at.z + 1 + index
+
+        @pl.when(below >= 0)
+        def _():
+            self.up(below).wait_recv()
+
+            @pl.when(at.z + 1 < at.zs)
+            def _():
+                self.up(below).start()
+
+            self.over(below).start()
+
+        @pl.when(above < at.zs)
+        def _():
+            self.down(above).wait_recv()
+
+            @pl.when(at.z > 0)
+            def _():
+                self.down(above).start()
+
+            self.over(above).start()
+
+    def finish(self):
+        at = self.at
+        for z in range(at.zs):
+            slot = self.view(z * 2 + 1 - at.c)
+            send(slot, slot, self.sems.at[2, z], self.sems.at[4, z], at.partner()).wait_recv()
+        for z in range(at.zs):
+
+            @pl.when((at.z >= z) & (at.z + 1 < at.zs))
+            def _():
+                self.up(z).wait_send()
+
+            @pl.when((at.z <= z) & (at.z > 0))
+            def _():
+                self.down(z).wait_send()
+
+            self.over(z).wait_send()
+
+
+class LineSum:
+    @staticmethod
+    def scratch(wt, shape):
+        zs = wt // 2
+        return [
+            pltpu.VMEM((zs,) + shape, jnp.bfloat16),
+            pltpu.VMEM((zs,) + shape, jnp.bfloat16),
+            pltpu.VMEM((zs,) + shape, jnp.bfloat16),
+            pltpu.VMEM((zs,) + shape, jnp.bfloat16),
+            pltpu.SemaphoreType.DMA((6, zs)),
+        ]
+
+    def __init__(self, at, part, scratch):
+        self.at, self.part = at, part
+        self.pair, self.held, self.below, self.above, self.sems = scratch
+
+    def over(self, z):
+        return send(
+            self.part(z * 2 + 1 - self.at.c),
+            self.pair.at[z],
+            self.sems.at[0, z],
+            self.sems.at[1, z],
+            self.at.partner(),
+        )
+
+    def up(self, z):
+        return send(
+            self.held.at[z], self.below.at[z], self.sems.at[2, z], self.sems.at[3, z], self.at.level(self.at.z + 1)
+        )
+
+    def down(self, z):
+        return send(
+            self.held.at[z], self.above.at[z], self.sems.at[4, z], self.sems.at[5, z], self.at.level(self.at.z - 1)
+        )
+
+    def start(self):
+        zs = self.at.zs
+        for index in range(zs // 2):
+            self.over(zs - 1 - index).start()
+            self.over(index).start()
+
+    def paired(self, z):
+        self.over(z).wait_recv()
+        return [self.part(z * 2 + self.at.c), self.pair.at[z]]
+
+    def step(self, index):
+        at = self.at
+        high, low = at.zs - 1 - index, index
+
+        @pl.when(at.z < high)
+        def _():
+            terms = self.paired(high)
+
+            @pl.when(at.z == 0)
+            def _():
+                add_into(self.held.at[high], terms)
+
+            @pl.when(at.z > 0)
+            def _():
+                self.up(high).wait_recv()
+                add_into(self.held.at[high], terms + [self.below.at[high]])
+
+            self.up(high).start()
+
+        @pl.when(at.z > low)
+        def _():
+            terms = self.paired(low)
+
+            @pl.when(at.z == at.zs - 1)
+            def _():
+                add_into(self.held.at[low], terms)
+
+            @pl.when(at.z < at.zs - 1)
+            def _():
+                self.down(low).wait_recv()
+                add_into(self.held.at[low], terms + [self.above.at[low]])
+
+            self.down(low).start()
+
+    def finish(self, total):
+        at = self.at
+        terms = self.paired(at.z)
+
+        @pl.when(at.z == 0)
+        def _():
+            self.down(0).wait_recv()
+            add_into(total, terms + [self.above.at[0]])
+
+        @pl.when(at.z == at.zs - 1)
+        def _():
+            self.up(at.zs - 1).wait_recv()
+            add_into(total, terms + [self.below.at[at.zs - 1]])
+
+        @pl.when((at.z > 0) & (at.z < at.zs - 1))
+        def _():
+            self.up(at.z).wait_recv()
+            self.down(at.z).wait_recv()
+            add_into(total, terms + [self.below.at[at.z], self.above.at[at.z]])
+
+        for z in range(at.zs):
+
+            @pl.when(at.z < z)
+            def _():
+                self.up(z).wait_send()
+
+            @pl.when(at.z > z)
+            def _():
+                self.down(z).wait_send()
+
+            self.over(z).wait_send()
+
+
+def remote_call(kernel, name, number, outs, scratch, *operands):
+    return pl.pallas_call(
+        kernel,
+        name=name,
+        out_shape=outs,
+        in_specs=[VMEM] * len(operands),
+        out_specs=jax.tree.map(lambda _: VMEM, outs),
+        scratch_shapes=scratch,
+        compiler_params=pltpu.CompilerParams(
+            collective_id=number, has_side_effects=True, vmem_limit_bytes=60 * 1024 * 1024
+        ),
+    )(*operands)
+
+
+def gather_start(tokens, qkv_rows, out_rows, gains):
+    seq, wt = lax.axis_size("seq"), lax.axis_size("wt")
+    count, width = tokens.shape
+    parts, rows, columns = qkv_rows.shape
+
+    def kernel(x_ref, qkv_ref, out_ref, gain_ref, xs, qkvs, outs, gains_out, *scratch):
+        at = Place(seq, wt)
+        x_sems, scratch = scratch[:3], scratch[3:]
+        line_sems, scratch = [scratch[index : index + 1] for index in range(3)], scratch[3:]
+        swap_q, swap_g, local = scratch
+        at.meet(True, True)
+        half = count // 2
+        gather_x = SquareGather(
+            at,
+            lambda s, h: xs.at[pl.ds(pl.multiple_of(s * count + h * half, half), half)],
+            lambda h: x_ref.at[pl.ds(h * half, half)],
+            x_sems,
+        )
+        gather_q = LineGather(at, lambda w: qkvs.at[:, w], line_sems[0])
+        gather_g = LineGather(at, lambda w: gains_out.at[:, w], line_sems[1])
+        gather_o = LineGather(at, lambda w: outs.at[w], line_sems[2])
+        swaps = []
+        for step in range(1, seq):
+            to = lax.rem(at.s + step, seq)
+            swaps.append(
+                send(gain_ref, gains_out.at[at.s, at.w], swap_g.at[step, 0], swap_g.at[at.s, 1], (to, at.w))
+            )
+            swaps.append(
+                send(qkv_ref.at[to], qkvs.at[at.s, at.w], swap_q.at[step, 0], swap_q.at[at.s, 1], (to, at.w))
+            )
+        for copy in swaps:
+            copy.start()
+        gather_x.start()
+        own = [
+            pltpu.make_async_copy(qkv_ref.at[at.s], qkvs.at[at.s, at.w], local.at[0]),
+            pltpu.make_async_copy(gain_ref, gains_out.at[at.s, at.w], local.at[1]),
+            pltpu.make_async_copy(out_ref, outs.at[at.w], local.at[2]),
+            pltpu.make_async_copy(x_ref, xs.at[pl.ds(pl.multiple_of(at.s * count, count), count)], local.at[3]),
+        ]
+        for copy in own:
+            copy.start()
+        for copy in own:
+            copy.wait()
+        for step in range(1, seq):
+            s = lax.rem(at.s + step, seq)
+            slot = gains_out.at[s, at.w]
+            send(slot, slot, swap_g.at[step, 0], swap_g.at[s, 1], at.across()).wait_recv()
+            slot = qkvs.at[s, at.w]
+            send(slot, slot, swap_q.at[step, 0], swap_q.at[s, 1], at.across()).wait_recv()
+        gather_g.start()
+        gather_q.start()
+        gather_o.start()
+        gather_x.relay()
+        for index in range(at.zs - 1):
+            gather_g.step(index)
+            gather_q.step(index)
+            gather_o.step(index)
+        gather_x.finish()
+        gather_g.finish()
+        gather_q.finish()
+        gather_o.finish()
+        for copy in swaps:
+            copy.wait_send()
+
+    return remote_call(
+        kernel,
+        "gather_start",
+        0,
+        [
+            jax.ShapeDtypeStruct((seq * count, width), tokens.dtype),
+            jax.ShapeDtypeStruct((seq, wt, rows, columns), qkv_rows.dtype),
+            jax.ShapeDtypeStruct((wt,) + out_rows.shape, out_rows.dtype),
+            jax.ShapeDtypeStruct((seq, wt) + gains.shape, gains.dtype),
+        ],
+        SquareGather.semaphores(seq)
+        + LineGather.semaphores(wt) * 3
+        + [
+            pltpu.SemaphoreType.DMA((seq, 2)),
+            pltpu.SemaphoreType.DMA((seq, 2)),
+            pltpu.SemaphoreType.DMA((4,)),
+        ],
+        tokens,
+        qkv_rows,
+        out_rows,
+        gains,
+    )
+
+
+def square_sum(parts, name, number):
+    seq, wt = lax.axis_size("seq"), lax.axis_size("wt")
+    half_shape = parts.shape[2:]
+
+    def kernel(parts_ref, total_ref, *scratch):
+        at = Place(seq, wt)
+        at.meet(True, False)
+        work = SquareSum(at, lambda s, h: parts_ref.at[s, h], scratch)
+        work.start()
+        work.relay()
+        work.finish(lambda h: total_ref.at[h])
+
+    return remote_call(
+        kernel,
+        name,
+        number,
+        jax.ShapeDtypeStruct((2,) + half_shape, jnp.float32),
+        SquareSum.scratch(seq, half_shape),
+        parts,
+    )
+
+
+def square_gather(shard, name, number):
+    seq, wt = lax.axis_size("seq"), lax.axis_size("wt")
+    count, width = shard.shape
+    half = count // 2
+
+    def kernel(shard_ref, all_ref, *scratch):
+        at = Place(seq, wt)
+        at.meet(True, False)
+        work = SquareGather(
+            at,
+            lambda s, h: all_ref.at[pl.ds(pl.multiple_of(s * count + h * half, half), half)],
+            lambda h: shard_ref.at[pl.ds(h * half, half)],
+            scratch[:3],
+        )
+        work.start()
+        own = pltpu.make_async_copy(
+            shard_ref, all_ref.at[pl.ds(pl.multiple_of(at.s * count, count), count)], scratch[3].at[0]
+        )
+        own.start()
+        own.wait()
+        work.relay()
+        work.finish()
+
+    return remote_call(
+        kernel,
+        name,
+        number,
+        jax.ShapeDtypeStruct((seq * count, width), shard.dtype),
+        SquareGather.semaphores(seq) + [pltpu.SemaphoreType.DMA((1,))],
+        shard,
+    )
+
+
+def line_gather(shard, name, number):
+    seq, wt = lax.axis_size("seq"), lax.axis_size("wt")
+    count, width = shard.shape
+
+    def kernel(shard_ref, all_ref, *scratch):
+        at = Place(seq, wt)
+        at.meet(False, True)
+        work = LineGather(
+            at, lambda w: all_ref.at[pl.ds(pl.multiple_of(w * count, count), count)], scratch[:1]
+        )
+        work.start(shard_ref)
+        own = pltpu.make_async_copy(
+            shard_ref, all_ref.at[pl.ds(pl.multiple_of(at.w * count, count), count)], scratch[1].at[0]
+        )
+        own.start()
+        own.wait()
+        for index in range(at.zs - 1):
+            work.step(index)
+        work.finish()
+
+    return remote_call(
+        kernel,
+        name,
+        number,
+        jax.ShapeDtypeStruct((wt * count, width), shard.dtype),
+        LineGather.semaphores(wt) + [pltpu.SemaphoreType.DMA((1,))],
+        shard,
+    )
+
+
+def line_sum(parts, name, number):
+    seq, wt = lax.axis_size("seq"), lax.axis_size("wt")
+    rows, width = parts.shape
+    count = rows // wt
+
+    def kernel(parts_ref, total_ref, *scratch):
+        at = Place(seq, wt)
+        at.meet(False, True)
+        work = LineSum(at, lambda w: parts_ref.at[pl.ds(pl.multiple_of(w * count, count), count)], scratch)
+        work.start()
+        for index in range(at.zs - 1):
+            work.step(index)
+        work.finish(total_ref)
+
+    return remote_call(
+        kernel,
+        name,
+        number,
+        jax.ShapeDtypeStruct((count, width), jnp.float32),
+        LineSum.scratch(wt, (count, width)),
+        parts,
+    )
+
+
+def final_sums(hidden_parts, gate_up_parts, down_parts, qkv_parts, out_parts):
+    seq, wt = lax.axis_size("seq"), lax.axis_size("wt")
+    hidden_half = hidden_parts.shape[2:]
+    gate_up_half = gate_up_parts.shape[2:]
+    down_rows, down_all = down_parts.shape[1:]
+    down_columns = down_all // seq
+    down_half = (down_rows, down_columns)
+    qkv_shape = (seq,) + qkv_parts.shape[2:]
+
+    def kernel(hidden_ref, gate_up_ref, down_ref, qkv_ref, out_ref, h_total, gu_total, d_total, q_total, o_total, *scratch):
+        at = Place(seq, wt)
+        at.meet(True, True)
+        square, scratch = [scratch[8 * index : 8 * index + 8] for index in range(3)], scratch[24:]
+        line, scratch = [scratch[5 * index : 5 * index + 5] for index in range(2)], scratch[10:]
+        q_sum, swap = scratch
+        hidden = SquareSum(at, lambda s, h: hidden_ref.at[s, h], square[0])
+        gate_up = SquareSum(at, lambda s, h: gate_up_ref.at[h, s], square[1])
+        down = SquareSum(
+            at,
+            lambda s, h: down_ref.at[h, :, pl.ds(pl.multiple_of(s * down_columns, down_columns), down_columns)],
+            square[2],
+        )
+        qkv = LineSum(at, lambda w: qkv_ref.at[:, w], line[0])
+        out = LineSum(at, lambda w: out_ref.at[w], line[1])
+        qkv.start()
+        out.start()
+        hidden.start()
+        gate_up.start()
+        down.start()
+        hidden.relay()
+        for index in range(at.zs - 1):
+            qkv.step(index)
+            out.step(index)
+        qkv.finish(q_sum)
+        out.finish(o_total)
+        swaps = []
+        for step in range(1, seq):
+            to = lax.rem(at.s + step, seq)
+            copy = send(q_sum.at[to], q_total.at[at.s], swap.at[step, 0], swap.at[at.s, 1], (to, at.w))
+            copy.start()
+            swaps.append(copy)
+        add_into(q_total.at[at.s], [q_sum.at[at.s]])
+        gate_up.relay()
+        down.relay()
+        hidden.finish(lambda h: h_total.at[h])
+        gate_up.finish(lambda h: gu_total.at[h])
+        down.finish(lambda h: d_total.at[h])
+        for step in range(1, seq):
+            s = lax.rem(at.s + step, seq)
+            slot = q_total.at[s]
+            send(slot, slot, swap.at[step, 0], swap.at[s, 1], at.across()).wait_recv()
+        for copy in swaps:
+            copy.wait_send()
+
+    return remote_call(
+        kernel,
+        "final_sums",
+        7,
+        [
+            jax.ShapeDtypeStruct((2,) + hidden_half, jnp.float32),
+            jax.ShapeDtypeStruct((2,) + gate_up_half, jnp.float32),
+            jax.ShapeDtypeStruct((2,) + down_half, jnp.float32),
+            jax.ShapeDtypeStruct(qkv_shape, jnp.float32),
+            jax.ShapeDtypeStruct(out_parts.shape[1:], jnp.float32),
+        ],
+        SquareSum.scratch(seq, hidden_half)
+        + SquareSum.scratch(seq, gate_up_half)
+        + SquareSum.scratch(seq, down_half)
+        + LineSum.scratch(wt, qkv_shape)
+        + LineSum.scratch(wt, out_parts.shape[1:])
+        + [pltpu.VMEM(qkv_shape, jnp.float32), pltpu.SemaphoreType.DMA((seq, 2))],
+        hidden_parts,
+        gate_up_parts,
+        down_parts,
+        qkv_parts,
+        out_parts,
+    )
+
+
+def small_sums(spread, lined):
+    seq, wt = lax.axis_size("seq"), lax.axis_size("wt")
+    tile = spread.shape[2:]
+
+    def kernel(spread_ref, lined_ref, total_ref, first, middle, last, first_sems, last_sems):
+        at = Place(seq, wt)
+        at.meet(True, True)
+        copies = []
+        for step in range(1, seq):
+            to = lax.rem(at.s + step, seq)
+            copy = send(spread_ref.at[to], first.at[at.s], first_sems.at[step, 0], first_sems.at[at.s, 1], (to, at.w))
+            copy.start()
+            copies.append(copy)
+        terms = [spread_ref.at[at.s]]
+        for step in range(1, seq):
+            s = lax.rem(at.s + step, seq)
+            slot = first.at[s]
+            send(slot, slot, first_sems.at[step, 0], first_sems.at[s, 1], at.across()).wait_recv()
+            terms.append(slot)
+        add_into(middle, terms + [lined_ref])
+        for step in range(1, wt):
+            to = lax.rem(at.w + step, wt)
+            copy = send(middle.at[to], last.at[at.w], last_sems.at[step, 0], last_sems.at[at.w, 1], (at.s, to))
+            copy.start()
+            copies.append(copy)
+        terms = [middle.at[at.w]]
+        for step in range(1, wt):
+            w = lax.rem(at.w + step, wt)
+            slot = last.at[w]
+            send(slot, slot, last_sems.at[step, 0], last_sems.at[w, 1], at.partner()).wait_recv()
+            terms.append(slot)
+        add_into(total_ref, terms)
+        for copy in copies:
+            copy.wait_send()
+
+    return remote_call(
+        kernel,
+        "small_sums",
+        8,
+        jax.ShapeDtypeStruct(tile, jnp.float32),
+        [
+            pltpu.VMEM((seq, wt) + tile, jnp.float32),
+            pltpu.VMEM((wt,) + tile, jnp.float32),
+            pltpu.VMEM((wt,) + tile, jnp.float32),
+            pltpu.SemaphoreType.DMA((seq, 2)),
+            pltpu.SemaphoreType.DMA((wt, 2)),
+        ],
+        spread,
+        lined,
+    )
+
+
+def rows_of_tile(values, row):
+    pad = [(0, 0)] * (values.ndim - 1)
+    return jnp.pad(values[..., None, :], pad + [(row, 7 - row), (0, 128 - values.shape[-1])])
 
 def body(
     inputs,
@@ -189,34 +943,33 @@
     w_down,
     mlp_gain,
 ):
-    seq_parts = lax.axis_size("seq")
+    seq_parts, wt_parts = lax.axis_size("seq"), lax.axis_size("wt")
     tok_count = inputs.shape[1]
     model_width = inputs.shape[2]
     length = tok_count * seq_parts
     block_rows = min(block_limit, length)
     head_count = H // seq_parts
     head_width = 2 * FEAT + DV
-    rows_in = inputs[0].astype(jnp.float32)
-    gathered_qkv, gathered_out, gain_one, gain_two = (
-        lax.all_gather(w_qkv, ("seq", "wt"), axis=0, tiled=True),
-        lax.all_gather(w_out, ("seq", "wt"), axis=0, tiled=True),
-        lax.all_gather(norm_gain, ("seq", "wt"), axis=0, tiled=True),
-        lax.all_gather(mlp_gain, ("seq", "wt"), axis=0, tiled=True),
-    )
-    gain_first = gain_one.astype(jnp.float32)
-    hidden_value, first_pull = jax.vjp(rms_norm, rows_in, gain_first)
-    hidden_low = hidden_value.astype(jnp.bfloat16)
-    projected = jnp.dot(hidden_low, gathered_qkv, preferred_element_type=jnp.float32).astype(
+    qkv_width = head_count * head_width
+    rows_low = inputs[0]
+    rows_in = rows_low.astype(jnp.float32)
+    gain_lanes = norm_gain.shape[0]
+    gains = rows_of_tile(norm_gain.astype(jnp.float32), 0) + rows_of_tile(mlp_gain.astype(jnp.float32), 1)
+    qkv_rows = w_qkv.reshape(w_qkv.shape[0], seq_parts, qkv_width).transpose(1, 0, 2)
+    tokens_all, qkv_columns, out_rows, gains_all = gather_start(rows_low, qkv_rows, w_out, gains)
+    qkv_columns = qkv_columns.reshape(model_width, qkv_width)
+    out_rows = out_rows.reshape(head_count * DV, model_width)
+    gain_first = gains_all[:, :, 0, :gain_lanes].reshape(model_width)
+    gain_second = gains_all[:, :, 1, :gain_lanes].reshape(model_width)
+    gate_up_part, down_part = (
+        lax.all_gather(w_gate_up, "seq", axis=1, tiled=True),
+        lax.all_gather(w_down, "seq", axis=1, tiled=True),
+    )
+    hidden_low = rms_norm(tokens_all.astype(jnp.float32), gain_first).astype(jnp.bfloat16)
+    projected = jnp.dot(hidden_low, qkv_columns, preferred_element_type=jnp.float32).astype(
         jnp.bfloat16
     )
-    arrived = lax.all_to_all(
-        projected.reshape(tok_count, seq_parts, head_count * head_width),
-        "seq",
-        split_axis=1,
-        concat_axis=0,
-        tiled=True,
-    )
-    grouped = arrived.reshape(length, head_count, head_width)
+    grouped = projected.reshape(length, head_count, head_width)
     head_queries = grouped[:, :, :FEAT].transpose(1, 2, 0)
     head_keys = grouped[:, :, FEAT : 2 * FEAT].transpose(1, 2, 0)
     raw_values = grouped[:, :, 2 * FEAT :].astype(jnp.float32)
@@ -237,33 +990,23 @@
     head_outputs, denominators = attend_forward(
         head_queries, head_keys, conv_low, segments, block_rows
     )
-    mixer_low = (
-        head_outputs.transpose(1, 0, 2)
-        .reshape(seq_parts, tok_count, head_count * DV)
-        .astype(jnp.bfloat16)
-    )
-    mixer_tok = lax.all_to_all(mixer_low, "seq", split_axis=0, concat_axis=2, tiled=True).reshape(
-        tok_count, model_width
-    )
-    attended = rows_in + jnp.dot(mixer_tok, gathered_out, preferred_element_type=jnp.float32)
-    gate_up_part, down_part = (
-        lax.all_gather(w_gate_up, "seq", axis=1, tiled=True),
-        lax.all_gather(w_down, "seq", axis=1, tiled=True),
-    )
-    gain_second = gain_two.astype(jnp.float32)
+    mixer_low = head_outputs.transpose(1, 0, 2).reshape(length, head_count * DV).astype(jnp.bfloat16)
+    mixed_parts = jnp.dot(mixer_low, out_rows, preferred_element_type=jnp.float32).astype(jnp.bfloat16)
+    attended = rows_in + square_sum(
+        mixed_parts.reshape(seq_parts, 2, tok_count // 2, model_width), "mixed_sum", 1
+    ).reshape(tok_count, model_width)
     normed_value, second_pull = jax.vjp(rms_norm, attended, gain_second)
     normed_low = normed_value.astype(jnp.bfloat16)
-    normed_all = lax.all_gather(normed_low, "wt", axis=0, tiled=True)
+    normed_all = line_gather(normed_low, "normed_gather", 2)
     gate_all = jnp.dot(normed_all, gate_up_part[0], preferred_element_type=jnp.float32)
     up_all = jnp.dot(normed_all, gate_up_part[1], preferred_element_type=jnp.float32)
     active_value, gate_pull = jax.vjp(gated_unit, gate_all, up_all)
     active_all = active_value.astype(jnp.bfloat16)
-    branch_out = lax.psum_scatter(
+    branch_out = line_sum(
         jnp.dot(active_all, down_part, preferred_element_type=jnp.float32).astype(jnp.bfloat16),
-        "wt",
-        scatter_dimension=0,
-        tiled=True,
-    ).astype(jnp.float32)
+        "branch_sum",
+        3,
+    )
     outputs = attended + branch_out
     sequence_length = lax.dynamic_index_in_dim(
         valid_lengths, lax.axis_index("wt"), 0, keepdims=False
@@ -271,11 +1014,9 @@
     positions = lax.axis_index("seq") * tok_count + jnp.arange(tok_count, dtype=jnp.int32)
     keep_mask = (positions < sequence_length).astype(jnp.float32)
     residual_error = (outputs - teacher[0].astype(jnp.float32)) * keep_mask[:, None]
-    total_energy = lax.psum(0.5 * jnp.sum(residual_error * residual_error), ("seq", "wt"))
-    valid_total = jnp.sum(valid_lengths).astype(jnp.float32)
-    mean_loss = 2.0 * total_energy / (valid_total * model_width)
+    energy = 0.5 * jnp.sum(residual_error * residual_error)
     branch_grad = residual_error.astype(jnp.bfloat16)
-    error_all = lax.all_gather(branch_grad, "wt", axis=0, tiled=True)
+    error_all = line_gather(branch_grad, "error_gather", 4)
     active_grad = contract_last(error_all, down_part)
     down_term = contract_first(active_all, error_all)
     gate_grad, up_grad = gate_pull(active_grad)
@@ -283,36 +1024,20 @@
     gate_up_term = jnp.einsum(
         "tc,gtf->gcf", normed_all, gate_up_grad, preferred_element_type=jnp.float32
     )
-    normed_grad = lax.psum_scatter(
+    normed_grad = line_sum(
         jnp.einsum(
             "gtf,gcf->tc", gate_up_grad, gate_up_part, preferred_element_type=jnp.float32
         ).astype(jnp.bfloat16),
-        "wt",
-        scatter_dimension=0,
-        tiled=True,
-    ).astype(jnp.float32)
+        "normed_back_sum",
+        5,
+    )
     attended_back, gain_two_term = second_pull(normed_grad)
     attended_grad = residual_error + attended_back
-    grad_w_gate_up, grad_w_down = (
-        lax.psum_scatter(
-            gate_up_term.astype(jnp.bfloat16), "seq", scatter_dimension=1, tiled=True
-        ).astype(jnp.float32),
-        lax.psum_scatter(
-            down_term.astype(jnp.bfloat16), "seq", scatter_dimension=1, tiled=True
-        ).astype(jnp.float32),
-    )
-    mixer_branch = attended_grad.astype(jnp.bfloat16)
-    out_term = contract_first(mixer_tok, mixer_branch)
-    mixer_grad = contract_last(mixer_branch, gathered_out).astype(jnp.bfloat16)
-    head_incoming = lax.all_to_all(
-        mixer_grad.reshape(tok_count, seq_parts, head_count * DV),
-        "seq",
-        split_axis=1,
-        concat_axis=0,
-        tiled=True,
-    )
+    mixer_branch = square_gather(attended_grad.astype(jnp.bfloat16), "mix_back_gather", 6)
+    out_term = contract_first(mixer_low, mixer_branch)
+    mixer_grad = contract_last(mixer_branch, out_rows).astype(jnp.bfloat16)
     head_incoming = (
-        head_incoming.reshape(length, head_count, DV).transpose(1, 0, 2).astype(jnp.float32)
+        mixer_grad.reshape(length, head_count, DV).transpose(1, 0, 2).astype(jnp.float32)
     )
     query_grads, key_grads, value_grads = attend_backward(
         head_queries,
@@ -331,35 +1056,39 @@
         masked = mixed_grad * tap_masks[tap_index][:, None, None]
         conv_terms.append(jnp.sum(masked * shift_down(raw_values, tap_index, 0.0), axis=0))
         raw_grad = raw_grad + conv_taps[tap_index] * shift_up(masked, tap_index)
-    conv_block = jnp.stack(conv_terms).reshape(KCONV, head_count * DV)
-    conv_full = lax.dynamic_update_slice_in_dim(
-        jnp.zeros((KCONV, model_width), jnp.float32),
-        conv_block,
-        lax.axis_index("seq") * (head_count * DV),
-        1,
-    )
     projected_grad = jnp.concatenate(
         [query_grads.transpose(2, 0, 1), key_grads.transpose(2, 0, 1), raw_grad], axis=2
     ).astype(jnp.bfloat16)
-    returned = lax.all_to_all(
-        projected_grad.reshape(seq_parts, tok_count, head_count * head_width),
-        "seq",
-        split_axis=0,
-        concat_axis=2,
-        tiled=True,
-    )
-    returned = returned.reshape(tok_count, seq_parts * head_count * head_width)
-    qkv_term = contract_first(hidden_low, returned)
-    hidden_grad = contract_last(returned, gathered_qkv)
-    inputs_back, gain_one_term = first_pull(hidden_grad)
+    returned = projected_grad.reshape(length, qkv_width)
+    qkv_term = contract_first(hidden_low, returned).astype(jnp.bfloat16)
+    hidden_parts = contract_last(returned, qkv_columns).astype(jnp.bfloat16)
+    hidden_units = gate_up_part.shape[2]
+    hidden_grad, gate_up_total, down_total, qkv_total, out_total = final_sums(
+        hidden_parts.reshape(seq_parts, 2, tok_count // 2, model_width),
+        gate_up_term.astype(jnp.bfloat16).reshape(2, seq_parts, model_width // seq_parts, hidden_units),
+        down_term.astype(jnp.bfloat16).reshape(2, hidden_units // 2, model_width),
+        qkv_term.reshape(seq_parts, wt_parts, w_qkv.shape[0], qkv_width),
+        out_term.astype(jnp.bfloat16).reshape(wt_parts, w_out.shape[0], model_width),
+    )
+    _, first_pull = jax.vjp(rms_norm, rows_in, gain_first)
+    inputs_back, gain_one_term = first_pull(hidden_grad.reshape(tok_count, model_width))
     inputs_grad = attended_grad + inputs_back
-    grad_w_qkv, grad_w_out, grad_norm_gain, grad_mlp_gain, grad_conv = (
-        lax.psum_scatter(qkv_term, ("seq", "wt"), scatter_dimension=0, tiled=True),
-        lax.psum_scatter(out_term, ("seq", "wt"), scatter_dimension=0, tiled=True),
-        lax.psum_scatter(gain_one_term, ("seq", "wt"), scatter_dimension=0, tiled=True),
-        lax.psum_scatter(gain_two_term, ("seq", "wt"), scatter_dimension=0, tiled=True),
-        lax.psum_scatter(conv_full, ("seq", "wt"), scatter_dimension=1, tiled=True),
-    )
+    grad_w_qkv = qkv_total.transpose(1, 0, 2).reshape(w_qkv.shape)
+    grad_w_gate_up = gate_up_total
+    grad_w_down = down_total.reshape(w_down.shape)
+    grad_w_out = out_total
+    spread = (
+        rows_of_tile(gain_one_term.reshape(seq_parts, wt_parts, gain_lanes), 0)
+        + rows_of_tile(gain_two_term.reshape(seq_parts, wt_parts, gain_lanes), 1)
+        + rows_of_tile(jnp.broadcast_to(energy, (seq_parts, wt_parts, 1)), 2)
+    )
+    conv_block = jnp.stack(conv_terms).reshape(KCONV, wt_parts, gain_lanes)
+    lined = sum(rows_of_tile(conv_block[tap], 3 + tap) for tap in range(KCONV))
+    totals = small_sums(spread, lined)
+    grad_norm_gain, grad_mlp_gain = totals[0, :gain_lanes], totals[1, :gain_lanes]
+    grad_conv = totals[3 : 3 + KCONV, :gain_lanes]
+    valid_total = jnp.sum(valid_lengths).astype(jnp.float32)
+    mean_loss = 2.0 * totals[2, 0] / (valid_total * model_width)
     return (
         outputs.astype(jnp.bfloat16)[None],
         inputs_grad[None],

time: 1210 us -> 596 us (0.49)
  waiting for transfers between devices: 907 us -> 1.38 us
  Pallas kernels: 0 us -> 431 us
  blocking collectives: 98.9 us -> 0 us
  matrix products: 114 us -> 79.2 us
  starting transfers between devices: 12.4 us -> 0.08 us
    reduce_scatter x6 -> x0, waiting for transfers between devices: 507 us -> none  [the longest x1 231 us: body(): lax.psum_scatter(qkv_term, ('seq', 'wt'), scatter_dimension=0, tiled=True)]
    pallas_call x0 -> x9, Pallas kernels: none -> 431 us  [remote_call(): pl.pallas_call(kernel, name=name, out_shape=outs, in_specs=[VMEM] * len(o...]
    all_gather x4 -> x0, waiting for transfers between devices: 197 us -> none  [the longest x1 55.9 us: body(): lax.all_gather(w_out, ('seq', 'wt'), axis=0, tiled=True)]
    unnamed x14 -> x2, waiting for transfers between devices: 86.8 us -> 1.38 us
    all_gather x1, waiting for transfers between devices: 59.5 us -> 0.01 us  [body(): lax.all_gather(w_gate_up, 'seq', axis=1, tiled=True)]
    psum x1 -> x0, blocking collectives: 44.3 us -> none  [body(): lax.psum(0.5 * jnp.sum(residual_error * residual_error), ('seq', 'wt'))]
    unnamed x1 -> x0, blocking collectives: 41 us -> none
    all_gather x1, waiting for transfers between devices: 30.7 us -> 0.01 us  [body(): lax.all_gather(w_down, 'seq', axis=1, tiled=True)]
  transfers between devices with their start and end apart: 16 -> 2, of which waited for: 14 -> 0; matrix products, arithmetic and copies ran while one was open for 10% -> 6% of each run, Pallas kernels for 0% -> 22%
where the time goes in v1:
time: 596 us; the launch traced here: 586 us
  Pallas kernels  431 us (72%)
  matrix products  79.2 us (13%)
  local copies, waits for them, and re-layouts  30.8 us (5%)
  other arithmetic  24.8 us (4%)
  between operations  18.1 us (3%)
    pallas_call x9, Pallas kernels, remote_call(): pl.pallas_call(kernel, name=name, out_shape=outs, in_specs=[VMEM] * len(o...  431 us
    dot_general x3, matrix products, contract_last(): lax.dot_general(former, latter, (((1,), (1,)), ((), ())), preferred_eleme...  15.6 us
    unnamed x109, local copies, waits for them, and re-layouts  12.7 us
  transfers between devices with their start and end apart: 2, of which 0 were waited for; matrix products, arithmetic and copies ran while one was open for 6% of the time, Pallas kernels for 22%

profile of v1, /device:TPU:8, one launch (start us, length us, event | category | flops | bytes accessed | tf_op | source)
XLA Modules:
  0.0 585.5 jit_solution(5982369352935675412)
XLA Ops:
  11.7 52.8 %gather_start.1 = (bf16[512,2048]{1,0:T(8,128)(2,1)}, bf16[4,8,64,640]{3,2,1,0:T(8,128)(2,1)}, bf16[8,64,2048]{2,1,0:T(8,128)(2,1)}, f32[4,8,8,128]{3,2,1,0:T(8,128)}) custom-call(bf16[128,2048]{1,0:T(8,128)(2,1)} %bitcast.158, bf16[4,64,640]{2,1,0:T(8,128)(2,1)} %bitcast.177, bf16[64,2048]{1,0:T(8,128)(2,1)} %out_ref.1, f32[8,128]{1,0:T(8,128)} %convert_add_fusion.2.gain_ref), custom_call_target="tpu_custom_call" | custom-call | tf_op jit(solution)/shard_map/gather_start/pallas_call | solution.py:588
  67.7 4.2 convolution_convert_fusion.6
  81.2 29.5 %mixed_sum.1 = f32[2,64,2048]{2,1,0:T(8,128)} custom-call(bf16[4,2,64,2048]{3,2,1,0:T(8,128)(2,1)} %bitcast.175), custom_call_target="tpu_custom_call" | custom-call | tf_op jit(solution)/shard_map/mixed_sum/pallas_call | solution.py:588
  115.1 44.1 %normed_gather.1 = bf16[1024,2048]{1,0:T(8,128)(2,1)} custom-call(bf16[128,2048]{1,0:T(8,128)(2,1)} %get-tuple-element.302.shard_ref), custom_call_target="tpu_custom_call" | custom-call | tf_op jit(solution)/shard_map/normed_gather/pallas_call | solution.py:588
  162.3 6.0 %fusion.8 = f32[1024,704]{0,1:T(8,128)S(1)} fusion(bf16[1024,2048]{1,0:T(8,128)(2,1)} %normed_gather.1, bf16[2,2048,704]{1,2,0:T(8,128)(2,1)} %all-gather.3.cloned.1.call-done), kind=kOutput, calls=%fused_computation.23 | convolution fusion | flops 2952790016 | bytes 9961472 | tf_op jit(solution)/shard_map/dot_general | solution.py:1001
  169.8 5.0 multiply_convert_fusion.2
  174.8 7.8 %convolution_convert_fusion.parts_ref = bf16[1024,2048]{1,0:T(8,128)(2,1)} fusion(bf16[1024,704]{0,1:T(8,128)(2,1)} %get-tuple-element.324, bf16[704,2048]{1,0:T(8,128)(2,1)} %all-gather.5.cloned.1.call-done), kind=kOutput, calls=%fused_computation.11 | convolution fusion | flops 2954887168 | bytes 8519680 | tf_op jit(solution)/shard_map/dot_general | solution.py:1006
  182.6 61.0 %branch_sum.1 = f32[128,2048]{1,0:T(8,128)} custom-call(bf16[1024,2048]{1,0:T(8,128)(2,1)} %convolution_convert_fusion.parts_ref), custom_call_target="tpu_custom_call" | custom-call | tf_op jit(solution)/shard_map/branch_sum/pallas_call | solution.py:588
  243.7 3.0 multiply_reduce_fusion.3
  247.5 42.1 %error_gather.1 = bf16[1024,2048]{1,0:T(8,128)(2,1)} custom-call(bf16[128,2048]{1,0:T(8,128)(2,1)} %convert_element_type.193.shard_ref), custom_call_target="tpu_custom_call" | custom-call | tf_op jit(solution)/shard_map/error_gather/pallas_call | solution.py:588
  289.6 8.7 %fusion.13 = (bf16[1,1024,704]{1,2,0:T(8,128)(2,1)S(1)}, bf16[1,1024,704]{1,2,0:T(8,128)(2,1)S(1)}) fusion(f32[1024,704]{0,1:T(8,128)} %copy-done.47, f32[1024,704]{0,1:T(8,128)} %get-tuple-element.325, bf16[1024,2048]{1,0:T(8,128)(2,1)} %error_gather.1, bf16[704,2048]{1,0:T(8,128)(2,1)} %all-gather.5.cloned.1.call-done), kind=kOutput, calls=%fused_computation.38 | convolution fusion | flops 2962882560 | bytes 15728640 | tf_op jit(solution)/shard_map/dot_general | solution.py:24
  300.0 11.0 %bitcast_convert_fusion.parts_ref = bf16[1024,2048]{1,0:T(8,128)(2,1)} fusion(bf16[2,2048,704]{1,2,0:T(8,128)(2,1)} %all-gather.3.cloned.1.call-done, bf16[1,1024,704]{1,2,0:T(8,128)(2,1)S(1)} %get-tuple-element.305, bf16[1,1024,704]{1,2,0:T(8,128)(2,1)S(1)} %get-tuple-element.304), kind=kOutput, calls=%fused_computation | convolution fusion | flops 5909118976 | bytes 12845056 | tf_op jit(solution)/shard_map/gtf,gcf->tc/dot_general | solution.py:1028
  311.0 60.3 %normed_back_sum.1 = f32[128,2048]{1,0:T(8,128)} custom-call(bf16[1024,2048]{1,0:T(8,128)(2,1)} %bitcast_convert_fusion.parts_ref), custom_call_target="tpu_custom_call" | custom-call | tf_op jit(solution)/shard_map/normed_back_sum/pallas_call | solution.py:588
  373.4 2.7 fusion.46
  376.1 20.4 %mix_back_gather.1 = bf16[512,2048]{1,0:T(8,128)(2,1)} custom-call(bf16[128,2048]{1,0:T(8,128)(2,1)} %get-tuple-element.300.shard_ref), custom_call_target="tpu_custom_call" | custom-call | tf_op jit(solution)/shard_map/mix_back_gather/pallas_call | solution.py:588
  396.6 3.6 convolution_convert_fusion.7
  406.0 4.5 convolution_convert_fusion.1
  410.5 8.1 %convert_bitcast_fusion = bf16[2,2048,704]{1,2,0:T(8,128)(2,1)} fusion(bf16[1024,2048]{1,0:T(8,128)(2,1)S(1)} %copy-done.5, bf16[1,1024,704]{1,2,0:T(8,128)(2,1)S(1)} %copy-done.51, bf16[1,1024,704]{1,2,0:T(8,128)(2,1)S(1)} %copy-done.49), kind=kOutput, calls=%fused_computation.1 | convolution fusion | flops 5909905408 | bytes 12845056 | tf_op jit(solution)/shard_map/tc,gtf->gcf/dot_general | solution.py:1024
  423.5 3.6 convolution_convert_fusion.2
  427.0 3.3 convolution_convert_fusion.5
  430.3 8.5 %copy.42 = bf16[2,2048,704]{2,1,0:T(8,128)(2,1)} copy(bf16[2,2048,704]{1,2,0:T(8,128)(2,1)} %convert_bitcast_fusion) | data formatting | bytes 11534336 | tf_op jit(solution)/shard_map/convert_element_type | solution.py:1068
  439.0 110.0 %final_sums.1 = (f32[2,64,2048]{2,1,0:T(8,128)}, f32[2,512,704]{2,1,0:T(8,128)}, f32[2,352,512]{2,1,0:T(8,128)}, f32[4,64,640]{2,1,0:T(8,128)}, f32[64,2048]{1,0:T(8,128)}) custom-call(bf16[4,2,64,2048]{3,2,1,0:T(8,128)(2,1)} %bitcast.174, bf16[2,4,512,704]{3,2,1,0:T(8,128)(2,1)} %bitcast.157, bf16[2,352,2048]{2,1,0:T(8,128)(2,1)} %bitcast.171, ...), custom_call_target="tpu_custom_call" | custom-call | tf_op jit(solution)/shard_map/final_sums/pallas_call | solution.py:588
  554.2 11.0 %small_sums.1 = f32[8,128]{1,0:T(8,128)} custom-call(f32[4,8,8,128]{3,2,1,0:T(8,128)} %add_add_fusion.2.spread_ref, f32[8,8,128]{2,1,0:T(8,128)} %pad_add_fusion.lined_ref), custom_call_target="tpu_custom_call" | custom-call | tf_op jit(solution)/shard_map/small_sums/pallas_call | solution.py:588
  568.9 3.6 copy.44
  (169 shorter events, 52.8 us)
Async XLA Ops:
  7.2 155.1 %all-gather.3.cloned.1.call-start = ((), (), s32[]{:S(2)}) async-start(), calls=%async_computation | async-start | bytes 7208960 | tf_op jit(solution)/shard_map/all_gather | solution.py:965
  7.9 166.9 %all-gather.5.cloned.1.call-start = ((), (), s32[]{:S(2)}) async-start(), calls=%async_computation.1 | async-start | bytes 3604480 | tf_op jit(solution)/shard_map/all_gather | solution.py:966
  67.7 4.2 copy-start.34
  81.2 29.5 %copy-start = (bf16[1,128,2048]{2,1,0:T(8,128)(2,1)S(1)}, bf16[1,128,2048]{2,1,0:T(8,128)(2,1)}, u32[]{:S(2)}) copy-start(bf16[1,128,2048]{2,1,0:T(8,128)(2,1)} %param.11) | copy-start | bytes 1572868
  112.9 46.3 %copy-start.32 = (f32[128]{0:T(128)}, f32[128]{0:T(128)S(1)}, u32[]{:S(2)}) copy-start(f32[128]{0:T(128)S(1)} %rsqrt.33) | copy-start | bytes 1540
  115.1 44.1 %copy-start.40 = (s32[8]{0:T(128)S(1)}, s32[8]{0:T(128)}, u32[]{:S(2)}) copy-start(s32[8]{0:T(128)} %param.13) | copy-start | bytes 100
  162.2 7.6 %copy-start.4 = (bf16[1024,2048]{1,0:T(8,128)(2,1)S(1)}, bf16[1024,2048]{1,0:T(8,128)(2,1)}, u32[]{:S(2)}) copy-start(bf16[1024,2048]{1,0:T(8,128)(2,1)} %normed_gather.1) | copy-start | bytes 12582916
  162.3 7.6 %copy-start.37 = (bf16[2,2048,704]{1,2,0:T(8,128)(2,1)S(1)}, bf16[2,2048,704]{1,2,0:T(8,128)(2,1)}, u32[]{:S(2)}) copy-start(bf16[2,2048,704]{1,2,0:T(8,128)(2,1)} %all-gather.3.cloned.1.call-done) | copy-start | bytes 17301508
  182.6 61.0 %copy-start.13 = (bf16[1,128,2048]{2,1,0:T(8,128)(2,1)S(1)}, bf16[1,128,2048]{2,1,0:T(8,128)(2,1)}, u32[]{:S(2)}) copy-start(bf16[1,128,2048]{2,1,0:T(8,128)(2,1)} %param.14) | copy-start | bytes 1572868
  182.6 61.0 %copy-start.36 = (f32[128]{0:T(128)S(1)}, f32[128]{0:T(128)}, u32[]{:S(2)}) copy-start(f32[128]{0:T(128)} %compare_convert_fusion) | copy-start | bytes 1540
  311.0 60.3 %copy-start.33 = (f32[128]{0:T(128)S(1)}, f32[128]{0:T(128)}, u32[]{:S(2)}) copy-start(f32[128]{0:T(128)} %copy-done.32) | copy-start | bytes 1540
  311.0 62.4 %copy-start.44 = (f32[128]{0:T(128)S(1)}, f32[128]{0:T(128)}, u32[]{:S(2)}) copy-start(f32[128]{0:T(128)} %copy-done.43) | copy-start | bytes 1540
  396.6 3.7 copy-start.11
  396.6 3.7 copy-start.19
  396.6 3.9 copy-start.16
  396.6 3.9 copy-start.46
  406.0 4.5 copy-start.5
  406.0 4.5 copy-start.49
  406.0 4.5 copy-start.51
  410.5 8.1 %copy-start.8 = (bf16[512,2048]{1,0:T(8,128)(2,1)S(1)}, bf16[512,2048]{1,0:T(8,128)(2,1)}, u32[]{:S(2)}) copy-start(bf16[512,2048]{1,0:T(8,128)(2,1)} %mix_back_gather.1) | copy-start | bytes 6291460
  410.5 8.1 %copy-start.42 = (bf16[512,4,128]{0,2,1:T(8,128)(2,1)S(1)}, bf16[512,4,128]{0,2,1:T(8,128)(2,1)}, u32[]{:S(2)}) copy-start(bf16[512,4,128]{0,2,1:T(8,128)(2,1)} %copy-done.41) | copy-start | bytes 1572868
  568.9 3.6 copy-start.12
  568.9 5.3 copy-start.1
  568.9 5.3 copy-start.7
  (31 other events, 58.5 us)
Sparse Core Ops, SparseCore 0:
  9.8 86.6 all-gather.2
  98.3 42.4 all-gather.4

commit v2 on v1

--- a/solution.py
+++ b/solution.py
@@ -454,11 +454,17 @@
 
             self.over(above).start()
 
+    def wait_over(self, z):
+        slot = self.view(z * 2 + 1 - self.at.c)
+        send(slot, slot, self.sems.at[2, z], self.sems.at[4, z], self.at.partner()).wait_recv()
+
     def finish(self):
+        for z in range(self.at.zs):
+            self.wait_over(z)
+        self.sent()
+
+    def sent(self):
         at = self.at
-        for z in range(at.zs):
-            slot = self.view(z * 2 + 1 - at.c)
-            send(slot, slot, self.sems.at[2, z], self.sems.at[4, z], at.partner()).wait_recv()
         for z in range(at.zs):
 
             @pl.when((at.z >= z) & (at.z + 1 < at.zs))
@@ -584,13 +590,13 @@
             self.over(z).wait_send()
 
 
-def remote_call(kernel, name, number, outs, scratch, *operands):
+def remote_call(kernel, name, number, outs, scratch, *operands, in_specs=None, out_specs=None):
     return pl.pallas_call(
         kernel,
         name=name,
         out_shape=outs,
-        in_specs=[VMEM] * len(operands),
-        out_specs=jax.tree.map(lambda _: VMEM, outs),
+        in_specs=[VMEM] * len(operands) if in_specs is None else in_specs,
+        out_specs=jax.tree.map(lambda _: VMEM, outs) if out_specs is None else out_specs,
         scratch_shapes=scratch,
         compiler_params=pltpu.CompilerParams(
             collective_id=number, has_side_effects=True, vmem_limit_bytes=60 * 1024 * 1024
@@ -741,57 +747,423 @@
     )
 
 
-def line_gather(shard, name, number):
+class LinePieces:
+    @staticmethod
+    def scratch(wt, shape, pieces):
+        zs = wt // 2
+        return [pltpu.VMEM((zs,) + shape, jnp.bfloat16)] * 4 + [pltpu.SemaphoreType.DMA((6, zs, pieces))]
+
+    def __init__(self, at, part, scratch):
+        self.at, self.part = at, part
+        self.pair, self.held, self.below, self.above, self.sems = scratch
+        self.pieces = self.sems.shape[2]
+        self.width = self.pair.shape[2] // self.pieces
+
+    def cut(self, ref, piece):
+        return ref.at[:, pl.ds(pl.multiple_of(piece * self.width, self.width), self.width)]
+
+    def over(self, z, piece):
+        return send(
+            self.cut(self.part(z * 2 + 1 - self.at.c), piece),
+            self.cut(self.pair.at[z], piece),
+            self.sems.at[0, z, piece],
+            self.sems.at[1, z, piece],
+            self.at.partner(),
+        )
+
+    def up(self, z, piece):
+        return send(
+            self.cut(self.held.at[z], piece),
+            self.cut(self.below.at[z], piece),
+            self.sems.at[2, z, piece],
+            self.sems.at[3, z, piece],
+            self.at.level(self.at.z + 1),
+        )
+
+    def down(self, z, piece):
+        return send(
+            self.cut(self.held.at[z], piece),
+            self.cut(self.above.at[z], piece),
+            self.sems.at[4, z, piece],
+            self.sems.at[5, z, piece],
+            self.at.level(self.at.z - 1),
+        )
+
+    def terms(self, z, piece):
+        self.over(z, piece).wait_recv()
+        return [self.cut(self.part(z * 2 + self.at.c), piece), self.cut(self.pair.at[z], piece)]
+
+    def ends(self, z, piece):
+        at = self.at
+
+        @pl.when((at.z == 0) & (z > 0))
+        def _():
+            add_into(self.cut(self.held.at[z], piece), self.terms(z, piece))
+            self.up(z, piece).start()
+
+        @pl.when((at.z == at.zs - 1) & (z < at.zs - 1))
+        def _():
+            add_into(self.cut(self.held.at[z], piece), self.terms(z, piece))
+            self.down(z, piece).start()
+
+    def pass_on(self):
+        at = self.at
+        for index in range(1, at.zs):
+            high, low = index, at.zs - 1 - index
+
+            def step(piece, carry):
+                @pl.when((at.z < high) & (at.z > 0))
+                def _():
+                    terms = self.terms(high, piece)
+                    self.up(high, piece).wait_recv()
+                    add_into(
+                        self.cut(self.held.at[high], piece), terms + [self.cut(self.below.at[high], piece)]
+                    )
+                    self.up(high, piece).start()
+
+                @pl.when((at.z > low) & (at.z < at.zs - 1))
+                def _():
+                    terms = self.terms(low, piece)
+                    self.down(low, piece).wait_recv()
+                    add_into(
+                        self.cut(self.held.at[low], piece), terms + [self.cut(self.above.at[low], piece)]
+                    )
+                    self.down(low, piece).start()
+
+                return carry
+
+            lax.fori_loop(0, self.pieces, step, 0)
+
+    def finish(self, total):
+        at = self.at
+
+        def step(piece, carry):
+            terms = self.terms(at.z, piece)
+            below, above = self.cut(self.below.at[at.z], piece), self.cut(self.above.at[at.z], piece)
+
+            @pl.when(at.z == 0)
+            def _():
+                self.down(at.z, piece).wait_recv()
+                add_into(self.cut(total, piece), terms + [above])
+
+            @pl.when(at.z == at.zs - 1)
+            def _():
+                self.up(at.z, piece).wait_recv()
+                add_into(self.cut(total, piece), terms + [below])
+
+            @pl.when((at.z > 0) & (at.z < at.zs - 1))
+            def _():
+                self.up(at.z, piece).wait_recv()
+                self.down(at.z, piece).wait_recv()
+                add_into(self.cut(total, piece), terms + [below, above])
+
+            for z in range(at.zs):
+
+                @pl.when(at.z < z)
+                def _():
+                    self.up(z, piece).wait_send()
+
+                @pl.when(at.z > z)
+                def _():
+                    self.down(z, piece).wait_send()
+
+                self.over(z, piece).wait_send()
+            return carry
+
+        lax.fori_loop(0, self.pieces, step, 0)
+
+
+def exchange(at, shard, everyone, gather_sems, local, sums, first, second, total, ready, wait_for_ready):
+    count = shard.shape[0]
+    gather = LineGather(
+        at, lambda w: everyone.at[pl.ds(pl.multiple_of(w * count, count), count)], gather_sems
+    )
+    gather.start(shard)
+    own = pltpu.make_async_copy(
+        shard, everyone.at[pl.ds(pl.multiple_of(at.w * count, count), count)], local
+    )
+    own.start()
+    own.wait()
+    ready[0]()
+    last = 2 * (at.zs - 1)
+    late = 3 if wait_for_ready else 0
+
+    def turn(index, carry):
+        fresh = index <= last
+        place = jnp.where(fresh, index, jnp.where(index == last + 3, 0, index - last))
+        far, side = lax.div(place + 1, 2), lax.rem(place, 2)
+        z = at.z + jnp.where(side == 1, -far, far)
+        valid = (z >= 0) & (z < at.zs)
+
+        @pl.when(fresh & (side == 1))
+        def _():
+            gather.step(far - 1)
+
+        @pl.when(fresh & valid)
+        def _():
+            gather.wait_over(z)
+            first(z)
+
+        if wait_for_ready:
+
+            @pl.when(index == late)
+            def _():
+                ready[1]()
+
+        @pl.when(valid & (index >= late))
+        def _():
+            def step(piece, inner):
+                second(z, piece)
+                sums.over(z, piece).start()
+
+                @pl.when(piece > 0)
+                def _():
+                    sums.ends(z, piece - 1)
+
+                return inner
+
+            lax.fori_loop(0, sums.pieces, step, 0)
+            sums.ends(z, sums.pieces - 1)
+
+        return carry
+
+    lax.fori_loop(0, last + 1 + late, turn, 0)
+    sums.pass_on()
+    sums.finish(total)
+    gather.sent()
+
+
+PIECES = 4
+ANY = pl.BlockSpec(memory_space=pl.ANY)
+
+
+def feed_forward(normed, gate_up, down_shard):
     seq, wt = lax.axis_size("seq"), lax.axis_size("wt")
-    count, width = shard.shape
-
-    def kernel(shard_ref, all_ref, *scratch):
+    count, width = normed.shape
+    units = gate_up.shape[2]
+    columns = down_shard.shape[1]
+    tokens = wt * count
+    zs = wt // 2
+    half = units // 2
+
+    def kernel(normed_ref, gate_up_ref, shard_ref, total_ref, normed_out, gate_out, up_out, active_out, down_out, *scratch):
         at = Place(seq, wt)
-        at.meet(False, True)
-        work = LineGather(
-            at, lambda w: all_ref.at[pl.ds(pl.multiple_of(w * count, count), count)], scratch[:1]
-        )
-        work.start(shard_ref)
-        own = pltpu.make_async_copy(
-            shard_ref, all_ref.at[pl.ds(pl.multiple_of(at.w * count, count), count)], scratch[1].at[0]
-        )
-        own.start()
-        own.wait()
-        for index in range(at.zs - 1):
-            work.step(index)
-        work.finish()
+        everyone, gates, downs, gate_all, up_all, active_all, parts = scratch[:7]
+        gather_sems, sum_scratch, square_sems, local, outgoing = (
+            scratch[7:8],
+            scratch[8:13],
+            scratch[13:16],
+            scratch[16],
+            scratch[17],
+        )
+        load = pltpu.make_async_copy(gate_up_ref, gates, local.at[0])
+        load.start()
+        at.meet(True, True)
+        weights = SquareGather(
+            at,
+            lambda s, h: downs.at[
+                pl.ds(h * half, half), pl.ds(pl.multiple_of(s * columns, columns), columns)
+            ],
+            lambda h: shard_ref.at[pl.ds(h * half, half)],
+            square_sems,
+        )
+        sums = LinePieces(
+            at, lambda w: parts.at[pl.ds(pl.multiple_of(w * count, count), count)], sum_scratch
+        )
+        down_store = pltpu.make_async_copy(downs, down_out, local.at[2])
+
+        def ready_first():
+            weights.start()
+            own = pltpu.make_async_copy(
+                shard_ref, downs.at[:, pl.ds(pl.multiple_of(at.s * columns, columns), columns)], local.at[3]
+            )
+            own.start()
+            own.wait()
+            load.wait()
+
+        def ready_later():
+            weights.relay()
+            weights.finish()
+            down_store.start()
+
+        def rows(z):
+            return pl.ds(pl.multiple_of(z * 2 * count, 2 * count), 2 * count)
+
+        def stores(z):
+            return [
+                pltpu.make_async_copy(source.at[rows(z)], target.at[rows(z)], outgoing.at[index, z])
+                for index, (source, target) in enumerate(
+                    ((everyone, normed_out), (gate_all, gate_out), (up_all, up_out), (active_all, active_out))
+                )
+            ]
+
+        def first(z):
+            here = everyone[rows(z), :]
+            gate = jnp.dot(here, gates[0], preferred_element_type=jnp.float32)
+            up = jnp.dot(here, gates[1], preferred_element_type=jnp.float32)
+            gate_all[rows(z), :] = gate
+            up_all[rows(z), :] = up
+            active_all[rows(z), :] = gated_unit(gate, up).astype(jnp.bfloat16)
+            for copy in stores(z):
+                copy.start()
+
+        def second(z, piece):
+            window = pl.ds(pl.multiple_of(piece * sums.width, sums.width), sums.width)
+            parts[rows(z), window] = jnp.dot(
+                active_all[rows(z), :], downs[:, window], preferred_element_type=jnp.float32
+            ).astype(jnp.bfloat16)
+
+        exchange(
+            at,
+            normed_ref,
+            everyone,
+            gather_sems,
+            local.at[1],
+            sums,
+            first,
+            second,
+            total_ref,
+            (ready_first, ready_later),
+            True,
+        )
+        down_store.wait()
+        for z in range(zs):
+            for copy in stores(z):
+                copy.wait()
 
     return remote_call(
         kernel,
-        name,
-        number,
-        jax.ShapeDtypeStruct((wt * count, width), shard.dtype),
-        LineGather.semaphores(wt) + [pltpu.SemaphoreType.DMA((1,))],
-        shard,
-    )
-
-
-def line_sum(parts, name, number):
+        "feed_forward",
+        2,
+        [
+            jax.ShapeDtypeStruct((count, width), jnp.float32),
+            jax.ShapeDtypeStruct((tokens, width), jnp.bfloat16),
+            jax.ShapeDtypeStruct((tokens, units), jnp.float32),
+            jax.ShapeDtypeStruct((tokens, units), jnp.float32),
+            jax.ShapeDtypeStruct((tokens, units), jnp.bfloat16),
+            jax.ShapeDtypeStruct((units, width), jnp.bfloat16),
+        ],
+        [
+            pltpu.VMEM((tokens, width), jnp.bfloat16),
+            pltpu.VMEM(gate_up.shape, jnp.bfloat16),
+            pltpu.VMEM((units, width), jnp.bfloat16),
+            pltpu.VMEM((tokens, units), jnp.float32),
+            pltpu.VMEM((tokens, units), jnp.float32),
+            pltpu.VMEM((tokens, units), jnp.bfloat16),
+            pltpu.VMEM((tokens, width), jnp.bfloat16),
+        ]
+        + LineGather.semaphores(wt)
+        + LinePieces.scratch(wt, (count, width), PIECES)
+        + SquareGather.semaphores(seq)
+        + [pltpu.SemaphoreType.DMA((4,)), pltpu.SemaphoreType.DMA((4, zs))],
+        normed,
+        gate_up,
+        down_shard,
+        in_specs=[VMEM, ANY, VMEM],
+        out_specs=[VMEM] + [ANY] * 5,
+    )
+
+
+def feed_back(error, gate_up, down, gate, up):
     seq, wt = lax.axis_size("seq"), lax.axis_size("wt")
-    rows, width = parts.shape
-    count = rows // wt
-
-    def kernel(parts_ref, total_ref, *scratch):
+    count, width = error.shape
+    units = gate_up.shape[2]
+    tokens = wt * count
+    zs = wt // 2
+
+    def kernel(error_ref, gate_up_ref, down_ref, gate_ref, up_ref, total_ref, error_out, back_out, *scratch):
         at = Place(seq, wt)
+        everyone, gates, downs, gate_all, up_all, back_all, parts = scratch[:7]
+        gather_sems, sum_scratch, local, outgoing = scratch[7:8], scratch[8:13], scratch[13], scratch[14]
+        loads = [
+            pltpu.make_async_copy(source, target, local.at[index])
+            for index, (source, target) in enumerate(
+                ((down_ref, downs), (gate_ref, gate_all), (up_ref, up_all), (gate_up_ref, gates))
+            )
+        ]
+        for load in loads:
+            load.start()
         at.meet(False, True)
-        work = LineSum(at, lambda w: parts_ref.at[pl.ds(pl.multiple_of(w * count, count), count)], scratch)
-        work.start()
-        for index in range(at.zs - 1):
-            work.step(index)
-        work.finish(total_ref)
+        sums = LinePieces(
+            at, lambda w: parts.at[pl.ds(pl.multiple_of(w * count, count), count)], sum_scratch
+        )
+
+        def ready_first():
+            for load in loads:
+                load.wait()
+
+        def rows(z):
+            return pl.ds(pl.multiple_of(z * 2 * count, 2 * count), 2 * count)
+
+        def stores(z):
+            return [
+                pltpu.make_async_copy(everyone.at[rows(z)], error_out.at[rows(z)], outgoing.at[0, z]),
+                pltpu.make_async_copy(back_all.at[:, rows(z)], back_out.at[:, rows(z)], outgoing.at[1, z]),
+            ]
+
+        def first(z):
+            active_back = contract_last(everyone[rows(z), :], downs[...])
+            gate_here, up_here = gate_all[rows(z), :], up_all[rows(z), :]
+            share = jax.nn.sigmoid(gate_here)
+            back_all[0, rows(z), :] = (
+                active_back * up_here * share * (1.0 + gate_here * (1.0 - share))
+            ).astype(jnp.bfloat16)
+            back_all[1, rows(z), :] = (active_back * gate_here * share).astype(jnp.bfloat16)
+            for copy in stores(z):
+                copy.start()
+
+        def second(z, piece):
+            window = pl.ds(pl.multiple_of(piece * sums.width, sums.width), sums.width)
+            parts[rows(z), window] = (
+                contract_last(back_all[0, rows(z), :], gates[0, window, :])
+                + contract_last(back_all[1, rows(z), :], gates[1, window, :])
+            ).astype(jnp.bfloat16)
+
+        exchange(
+            at,
+            error_ref,
+            everyone,
+            gather_sems,
+            local.at[4],
+            sums,
+            first,
+            second,
+            total_ref,
+            (ready_first,),
+            False,
+        )
+        for z in range(zs):
+            for copy in stores(z):
+                copy.wait()
 
     return remote_call(
         kernel,
-        name,
-        number,
-        jax.ShapeDtypeStruct((count, width), jnp.float32),
-        LineSum.scratch(wt, (count, width)),
-        parts,
+        "feed_back",
+        3,
+        [
+            jax.ShapeDtypeStruct((count, width), jnp.float32),
+            jax.ShapeDtypeStruct((tokens, width), jnp.bfloat16),
+            jax.ShapeDtypeStruct((2, tokens, units), jnp.bfloat16),
+        ],
+        [
+            pltpu.VMEM((tokens, width), jnp.bfloat16),
+            pltpu.VMEM(gate_up.shape, jnp.bfloat16),
+            pltpu.VMEM((units, width), jnp.bfloat16),
+            pltpu.VMEM((tokens, units), jnp.float32),
+            pltpu.VMEM((tokens, units), jnp.float32),
+            pltpu.VMEM((2, tokens, units), jnp.bfloat16),
+            pltpu.VMEM((tokens, width), jnp.bfloat16),
+        ]
+        + LineGather.semaphores(wt)
+        + LinePieces.scratch(wt, (count, width), PIECES)
+        + [pltpu.SemaphoreType.DMA((5,)), pltpu.SemaphoreType.DMA((2, zs))],
+        error,
+        gate_up,
+        down,
+        gate,
+        up,
+        in_specs=[VMEM, ANY, ANY, ANY, ANY],
+        out_specs=[VMEM, ANY, ANY],
     )
 
 
@@ -961,10 +1333,7 @@
     out_rows = out_rows.reshape(head_count * DV, model_width)
     gain_first = gains_all[:, :, 0, :gain_lanes].reshape(model_width)
     gain_second = gains_all[:, :, 1, :gain_lanes].reshape(model_width)
-    gate_up_part, down_part = (
-        lax.all_gather(w_gate_up, "seq", axis=1, tiled=True),
-        lax.all_gather(w_down, "seq", axis=1, tiled=True),
-    )
+    gate_up_part = lax.all_gather(w_gate_up, "seq", axis=1, tiled=True)
     hidden_low = rms_norm(tokens_all.astype(jnp.float32), gain_first).astype(jnp.bfloat16)
     projected = jnp.dot(hidden_low, qkv_columns, preferred_element_type=jnp.float32).astype(
         jnp.bfloat16
@@ -997,15 +1366,8 @@
     ).reshape(tok_count, model_width)
     normed_value, second_pull = jax.vjp(rms_norm, attended, gain_second)
     normed_low = normed_value.astype(jnp.bfloat16)
-    normed_all = line_gather(normed_low, "normed_gather", 2)
-    gate_all = jnp.dot(normed_all, gate_up_part[0], preferred_element_type=jnp.float32)
-    up_all = jnp.dot(normed_all, gate_up_part[1], preferred_element_type=jnp.float32)
-    active_value, gate_pull = jax.vjp(gated_unit, gate_all, up_all)
-    active_all = active_value.astype(jnp.bfloat16)
-    branch_out = line_sum(
-        jnp.dot(active_all, down_part, preferred_element_type=jnp.float32).astype(jnp.bfloat16),
-        "branch_sum",
-        3,
+    branch_out, normed_all, gate_all, up_all, active_all, down_part = feed_forward(
+        normed_low, gate_up_part, w_down
     )
     outputs = attended + branch_out
     sequence_length = lax.dynamic_index_in_dim(
@@ -1016,20 +1378,10 @@
     residual_error = (outputs - teacher[0].astype(jnp.float32)) * keep_mask[:, None]
     energy = 0.5 * jnp.sum(residual_error * residual_error)
     branch_grad = residual_error.astype(jnp.bfloat16)
-    error_all = line_gather(branch_grad, "error_gather", 4)
-    active_grad = contract_last(error_all, down_part)
+    normed_grad, error_all, gate_up_grad = feed_back(branch_grad, gate_up_part, down_part, gate_all, up_all)
     down_term = contract_first(active_all, error_all)
-    gate_grad, up_grad = gate_pull(active_grad)
-    gate_up_grad = jnp.stack([gate_grad, up_grad]).astype(jnp.bfloat16)
     gate_up_term = jnp.einsum(
         "tc,gtf->gcf", normed_all, gate_up_grad, preferred_element_type=jnp.float32
-    )
-    normed_grad = line_sum(
-        jnp.einsum(
-            "gtf,gcf->tc", gate_up_grad, gate_up_part, preferred_element_type=jnp.float32
-        ).astype(jnp.bfloat16),
-        "normed_back_sum",
-        5,
     )
     attended_back, gain_two_term = second_pull(normed_grad)
     attended_grad = residual_error + attended_back

time: 596 us -> 539 us (0.904)
  matrix products: 79.2 us -> 43.4 us
  Pallas kernels: 431 us -> 414 us
    dot_general x4 -> x0, matrix products: 29.8 us -> none  [the longest x1 11 us: body(): jnp.einsum('gtf,gcf->tc', gate_up_grad, gate_up_part, preferred_element_t...]
    pallas_call x9 -> x7, Pallas kernels: 431 us -> 414 us  [remote_call(): pl.pallas_call(kernel, name=name, out_shape=outs, in_specs=[VMEM] * len(o...]
    dot_general x3 -> x2, matrix products: 15.6 us -> 6.84 us  [contract_last(): lax.dot_general(former, latter, (((1,), (1,)), ((), ())), preferred_eleme...]
    unnamed x109 -> x100, local copies, waits for them, and re-layouts: 12.7 us -> 12.2 us
  transfers between devices with their start and end apart: 2 -> 1, of which waited for: 0 -> 0; matrix products, arithmetic and copies ran while one was open for 6% -> 4% of each run, Pallas kernels for 22% -> 16%
where the time goes in v2:
time: 539 us; the launch traced here: 529 us
  Pallas kernels  414 us (77%)
  matrix products  43.4 us (8%)
  local copies, waits for them, and re-layouts  29.5 us (5%)
  other arithmetic  24.2 us (4%)
  between operations  18.2 us (3%)
    pallas_call x7, Pallas kernels, remote_call(): pl.pallas_call(kernel, name=name, out_shape=outs, in_specs=[VMEM] * len(o...  414 us
    dot_general x3, matrix products, contract_first(): lax.dot_general(former, latter, (((0,), (0,)), ((), ())), preferred_eleme...  13.3 us
    unnamed x100, local copies, waits for them, and re-layouts  12.2 us
  transfers between devices with their start and end apart: 1, of which 0 were waited for; matrix products, arithmetic and copies ran while one was open for 4% of the time, Pallas kernels for 16%

profile of v2, /device:TPU:8, one launch (start us, length us, event | category | flops | bytes accessed | tf_op | source)
XLA Modules:
  0.0 529.2 jit_solution(16445338429595773736)
XLA Ops:
  7.3 2.6 copy.38
  11.3 52.8 %gather_start.1 = (bf16[512,2048]{1,0:T(8,128)(2,1)}, bf16[4,8,64,640]{3,2,1,0:T(8,128)(2,1)}, bf16[8,64,2048]{2,1,0:T(8,128)(2,1)}, f32[4,8,8,128]{3,2,1,0:T(8,128)}) custom-call(bf16[128,2048]{1,0:T(8,128)(2,1)} %bitcast.138, bf16[4,64,640]{2,1,0:T(8,128)(2,1)} %bitcast.157, bf16[64,2048]{1,0:T(8,128)(2,1)} %out_ref.1, f32[8,128]{1,0:T(8,128)} %convert_add_fusion.2.gain_ref), custom_call_target="tpu_custom_call" | custom-call | tf_op jit(solution)/shard_map/gather_start/pallas_call | solution.py:594
  65.2 2.1 fusion
  67.3 4.2 convolution_convert_fusion.5
  75.0 2.2 fusion.20
  78.1 2.6 convolution_convert_fusion.3
  80.8 34.2 %mixed_sum.1 = f32[2,64,2048]{2,1,0:T(8,128)} custom-call(bf16[4,2,64,2048]{3,2,1,0:T(8,128)(2,1)} %bitcast.155), custom_call_target="tpu_custom_call" | custom-call | tf_op jit(solution)/shard_map/mixed_sum/pallas_call | solution.py:594
  120.1 2.2 multiply_convert_fusion.1
  122.3 97.7 %feed_forward.1 = (f32[128,2048]{1,0:T(8,128)}, bf16[1024,2048]{1,0:T(8,128)(2,1)}, f32[1024,704]{1,0:T(8,128)}, f32[1024,704]{1,0:T(8,128)}, bf16[1024,704]{1,0:T(8,128)(2,1)}, /*index=5*/bf16[704,2048]{1,0:T(8,128)(2,1)}) custom-call(bf16[128,2048]{1,0:T(8,128)(2,1)} %get-tuple-element.320.normed_ref, ...), custom_call_target="tpu_custom_call" | custom-call | tf_op jit(solution)/shard_map/feed_forward/pallas_call | solution.py:594
  220.0 3.0 multiply_reduce_fusion.3
  223.8 91.1 %feed_back.1 = (f32[128,2048]{1,0:T(8,128)}, bf16[1024,2048]{1,0:T(8,128)(2,1)}, bf16[2,1024,704]{2,1,0:T(8,128)(2,1)}) custom-call(bf16[128,2048]{1,0:T(8,128)(2,1)} %convert_element_type.181.error_ref, bf16[2,2048,704]{2,1,0:T(8,128)(2,1)} %all-gather.2.cloned.1.call-done.gate_up_ref, bf16[704,2048]{1,0:T(8,128)(2,1)} %get-tuple-element.273.down_ref, ...), custom_call_target="tpu_custom_call" | custom-call | tf_op jit(solution)/shard_map/feed_back/pallas_call | solution.py:594
  315.0 2.1 multiply_reduce_fusion.4
  317.1 2.7 fusion.36
  319.7 15.4 %mix_back_gather.1 = bf16[512,2048]{1,0:T(8,128)(2,1)} custom-call(bf16[128,2048]{1,0:T(8,128)(2,1)} %get-tuple-element.318.shard_ref), custom_call_target="tpu_custom_call" | custom-call | tf_op jit(solution)/shard_map/mix_back_gather/pallas_call | solution.py:594
  335.2 3.7 convolution_convert_fusion.6
  343.9 2.7 convolution_convert_fusion.2
  348.2 3.6 convolution_convert_fusion.1
  351.8 3.2 convolution_convert_fusion.4
  355.7 8.3 %convert_bitcast_fusion = bf16[2,2048,704]{1,2,0:T(8,128)(2,1)} fusion(bf16[2,1024,704]{2,1,0:T(8,128)(2,1)S(1)} %copy-done.37, bf16[1024,2048]{1,0:T(8,128)(2,1)S(1)} %copy-done.36), kind=kOutput, calls=%fused_computation | convolution fusion | flops 5908463616 | bytes 12845056 | tf_op jit(solution)/shard_map/tc,gtf->gcf/dot_general | solution.py:1383
  364.0 8.6 %copy.46 = bf16[2,2048,704]{2,1,0:T(8,128)(2,1)} copy(bf16[2,2048,704]{1,2,0:T(8,128)(2,1)} %convert_bitcast_fusion) | data formatting | bytes 11534336 | tf_op jit(solution)/shard_map/convert_element_type | solution.py:1420
  372.9 7.0 %convolution_convert_fusion = bf16[704,2048]{1,0:T(8,128)(2,1)} fusion(bf16[1024,704]{1,0:T(8,128)(2,1)S(1)} %copy-done.40, bf16[1024,2048]{1,0:T(8,128)(2,1)} %get-tuple-element.280), kind=kOutput, calls=%fused_computation.9 | convolution fusion | flops 2954231808 | bytes 8519680 | tf_op jit(solution)/shard_map/dot_general | solution.py:30
  379.8 111.8 %final_sums.1 = (f32[2,64,2048]{2,1,0:T(8,128)}, f32[2,512,704]{2,1,0:T(8,128)}, f32[2,352,512]{2,1,0:T(8,128)}, f32[4,64,640]{2,1,0:T(8,128)}, f32[64,2048]{1,0:T(8,128)}) custom-call(bf16[4,2,64,2048]{3,2,1,0:T(8,128)(2,1)} %bitcast.154, bf16[2,4,512,704]{3,2,1,0:T(8,128)(2,1)} %bitcast.137, bf16[2,352,2048]{2,1,0:T(8,128)(2,1)} %bitcast.151, ...), custom_call_target="tpu_custom_call" | custom-call | tf_op jit(solution)/shard_map/final_sums/pallas_call | solution.py:594
  497.1 10.8 %small_sums.1 = f32[8,128]{1,0:T(8,128)} custom-call(f32[4,8,8,128]{3,2,1,0:T(8,128)} %add_add_fusion.2.spread_ref, f32[8,8,128]{2,1,0:T(8,128)} %pad_add_fusion.lined_ref), custom_call_target="tpu_custom_call" | custom-call | tf_op jit(solution)/shard_map/small_sums/pallas_call | solution.py:594
  511.7 3.4 copy.48
  (150 shorter events, 33.1 us)
Async XLA Ops:
  7.2 3.5 copy-start.35
  7.2 115.1 %all-gather.2.cloned.1.call-start = ((), (), s32[]{:S(2)}) async-start(), calls=%async_computation | async-start | bytes 7864320 | tf_op jit(solution)/shard_map/all_gather | solution.py:1336
  67.3 4.3 copy-start.31
  67.3 4.5 copy-start.14
  67.3 4.6 copy-start.24
  77.5 37.5 %copy-start.42 = (bf16[512,4,128]{0,2,1:T(8,128)(2,1)}, bf16[512,4,128]{0,2,1:T(8,128)(2,1)S(1)}, u32[]{:S(2)}) copy-start(bf16[512,4,128]{0,2,1:T(8,128)(2,1)S(1)} %get-tuple-element.338) | copy-start | bytes 1572868
  78.1 36.8 %copy-start = (bf16[1,128,2048]{2,1,0:T(8,128)(2,1)S(1)}, bf16[1,128,2048]{2,1,0:T(8,128)(2,1)}, u32[]{:S(2)}) copy-start(bf16[1,128,2048]{2,1,0:T(8,128)(2,1)} %param.11) | copy-start | bytes 1572868
  78.1 38.9 %copy-start.41 = (s32[8]{0:T(128)S(1)}, s32[8]{0:T(128)}, u32[]{:S(2)}) copy-start(s32[8]{0:T(128)} %param.13) | copy-start | bytes 100
  117.0 103.0 %copy-start.29 = (f32[128]{0:T(128)}, f32[128]{0:T(128)S(1)}, u32[]{:S(2)}) copy-start(f32[128]{0:T(128)S(1)} %rsqrt.33) | copy-start | bytes 1540
  122.3 97.7 %copy-start.10 = (bf16[1,128,2048]{2,1,0:T(8,128)(2,1)S(1)}, bf16[1,128,2048]{2,1,0:T(8,128)(2,1)}, u32[]{:S(2)}) copy-start(bf16[1,128,2048]{2,1,0:T(8,128)(2,1)} %param.14) | copy-start | bytes 1572868
  122.3 97.7 %copy-start.33 = (f32[128]{0:T(128)S(1)}, f32[128]{0:T(128)}, u32[]{:S(2)}) copy-start(f32[128]{0:T(128)} %compare_convert_fusion) | copy-start | bytes 1540
  223.8 91.2 %copy-start.30 = (f32[128]{0:T(128)S(1)}, f32[128]{0:T(128)}, u32[]{:S(2)}) copy-start(f32[128]{0:T(128)} %copy-done.29) | copy-start | bytes 1540
  223.8 93.2 %copy-start.45 = (f32[128]{0:T(128)S(1)}, f32[128]{0:T(128)}, u32[]{:S(2)}) copy-start(f32[128]{0:T(128)} %copy-done.44) | copy-start | bytes 1540
  335.1 3.7 copy-start.8
  335.2 3.7 copy-start.16
  335.2 3.9 copy-start.12
  335.2 3.9 copy-start.47
  348.2 3.6 copy-start.38
  351.8 3.8 copy-start.37
  364.0 8.9 %copy-start.40 = (bf16[1024,704]{1,0:T(8,128)(2,1)S(1)}, bf16[1024,704]{1,0:T(8,128)(2,1)}, u32[]{:S(2)}) copy-start(bf16[1024,704]{1,0:T(8,128)(2,1)} %get-tuple-element.279) | copy-start | bytes 4325380
  379.8 115.1 %copy-start.17 = (f32[2048]{0:T(1024)S(1)}, f32[2048]{0:T(1024)}, u32[]{:S(2)}) copy-start(f32[2048]{0:T(1024)} %get-tuple-element.306) | copy-start | bytes 24580
  493.2 21.9 %copy-start.9 = (f32[4,64,640]{2,1,0:T(8,128)S(1)}, f32[4,64,640]{2,1,0:T(8,128)}, u32[]{:S(2)}) copy-start(f32[4,64,640]{2,1,0:T(8,128)} %get-tuple-element.282) | copy-start | bytes 1966084
  494.8 21.9 %copy-start.1 = (f32[2,64,2048]{2,1,0:T(8,128)S(1)}, f32[2,64,2048]{2,1,0:T(8,128)}, u32[]{:S(2)}) copy-start(f32[2,64,2048]{2,1,0:T(8,128)} %get-tuple-element.281) | copy-start | bytes 3145732
  494.8 21.9 %copy-start.4 = (f32[128,2048]{1,0:T(8,128)S(1)}, f32[128,2048]{1,0:T(8,128)}, u32[]{:S(2)}) copy-start(f32[128,2048]{1,0:T(8,128)} %get-tuple-element.319) | copy-start | bytes 3145732
  (25 other events, 50.5 us)
Sparse Core Ops, SparseCore 0:
  10.0 94.7 all-gather.1

commit v3 on v2

--- a/solution.py
+++ b/solution.py
@@ -35,11 +35,6 @@
 def shift_down(values, amount, filler):
     padding = jnp.full((amount,) + values.shape[1:], filler, values.dtype)
     return jnp.concatenate([padding, values[:-amount]], axis=0)
-
-
-def shift_up(values, amount):
-    padding = jnp.zeros((amount,) + values.shape[1:], values.dtype)
-    return jnp.concatenate([values[amount:], padding], axis=0)
 
 
 def gated_unit(gate_in, up_in):
@@ -107,79 +102,10 @@
     return lax.fori_loop(0, block_count, query_step, initial)
 
 
-def attend_backward(
-    queries, key_rows, values, segments, outputs, denominators, incoming, block_rows
-):
-    head_count, length, value_width = values.shape
-    feature_width = queries.shape[1]
-    block_count = length // block_rows
-
-    def query_step(query_index, running):
-        query_grads, key_grads, value_grads = running
-        query_start = query_index * block_rows
-        query_block = lax.dynamic_slice_in_dim(queries, query_start, block_rows, 2)
-        query_segments = lax.dynamic_slice_in_dim(segments, query_start, block_rows, 0)
-        incoming_block = lax.dynamic_slice_in_dim(incoming, query_start, block_rows, 1)
-        output_block = lax.dynamic_slice_in_dim(outputs, query_start, block_rows, 1)
-        denominator = lax.dynamic_slice_in_dim(denominators, query_start, block_rows, 1)
-        numerator_grad = (incoming_block / denominator[:, :, None]).astype(jnp.bfloat16)
-        denominator_grad = -jnp.sum(incoming_block * output_block, axis=2) / denominator
-
-        def key_step(inner_index, inner_running):
-            query_total, key_grads, value_grads = inner_running
-            key_start = inner_index * block_rows
-            key_block = lax.dynamic_slice_in_dim(key_rows, key_start, block_rows, 2)
-            value_block = lax.dynamic_slice_in_dim(values, key_start, block_rows, 1)
-            key_segments = lax.dynamic_slice_in_dim(segments, key_start, block_rows, 0)
-            scaled_dots, allowed, kernel = block_kernel(
-                query_block, key_block, query_segments, key_segments, query_start, key_start
-            )
-            weights_low = kernel.astype(jnp.bfloat16)
-            weight_grad = jnp.einsum(
-                "hqd,hkd->hqk", numerator_grad, value_block, preferred_element_type=jnp.float32
-            )
-            kernel_grad = jnp.where(allowed[None], weight_grad + denominator_grad[:, :, None], 0.0)
-            dots_grad = (0.25 * kernel_grad * (1.0 + scaled_dots)).astype(jnp.bfloat16)
-            query_total = query_total + jnp.einsum(
-                "hqk,hfk->hfq", dots_grad, key_block, preferred_element_type=jnp.float32
-            )
-            key_part = jnp.einsum(
-                "hqk,hfq->hfk", dots_grad, query_block, preferred_element_type=jnp.float32
-            )
-            value_part = jnp.einsum(
-                "hqk,hqd->hkd", weights_low, numerator_grad, preferred_element_type=jnp.float32
-            )
-            key_grads = lax.dynamic_update_slice_in_dim(
-                key_grads,
-                lax.dynamic_slice_in_dim(key_grads, key_start, block_rows, 2) + key_part,
-                key_start,
-                2,
-            )
-            value_grads = lax.dynamic_update_slice_in_dim(
-                value_grads,
-                lax.dynamic_slice_in_dim(value_grads, key_start, block_rows, 1) + value_part,
-                key_start,
-                1,
-            )
-            return (query_total, key_grads, value_grads)
-
-        starting = jnp.zeros((head_count, feature_width, block_rows), jnp.float32)
-        query_total, key_grads, value_grads = lax.fori_loop(
-            0, query_index + 1, key_step, (starting, key_grads, value_grads)
-        )
-        query_grads = lax.dynamic_update_slice_in_dim(query_grads, query_total, query_start, 2)
-        return (query_grads, key_grads, value_grads)
-
-    initial = (
-        jnp.zeros((head_count, feature_width, length), jnp.float32),
-        jnp.zeros((head_count, feature_width, length), jnp.float32),
-        jnp.zeros((head_count, length, value_width), jnp.float32),
-    )
-    return lax.fori_loop(0, block_count, query_step, initial)
-
-
 MESH = pl.DeviceIdType.MESH
 VMEM = pl.BlockSpec(memory_space=pltpu.VMEM)
+ANY = pl.BlockSpec(memory_space=pl.ANY)
+VMEM_LIMIT = 63 * 1024 * 1024
 
 
 class Place:
@@ -599,7 +525,7 @@
         out_specs=jax.tree.map(lambda _: VMEM, outs) if out_specs is None else out_specs,
         scratch_shapes=scratch,
         compiler_params=pltpu.CompilerParams(
-            collective_id=number, has_side_effects=True, vmem_limit_bytes=60 * 1024 * 1024
+            collective_id=number, has_side_effects=True, vmem_limit_bytes=VMEM_LIMIT
         ),
     )(*operands)
 
@@ -714,53 +640,23 @@
     )
 
 
-def square_gather(shard, name, number):
-    seq, wt = lax.axis_size("seq"), lax.axis_size("wt")
-    count, width = shard.shape
-    half = count // 2
-
-    def kernel(shard_ref, all_ref, *scratch):
-        at = Place(seq, wt)
-        at.meet(True, False)
-        work = SquareGather(
-            at,
-            lambda s, h: all_ref.at[pl.ds(pl.multiple_of(s * count + h * half, half), half)],
-            lambda h: shard_ref.at[pl.ds(h * half, half)],
-            scratch[:3],
-        )
-        work.start()
-        own = pltpu.make_async_copy(
-            shard_ref, all_ref.at[pl.ds(pl.multiple_of(at.s * count, count), count)], scratch[3].at[0]
-        )
-        own.start()
-        own.wait()
-        work.relay()
-        work.finish()
-
-    return remote_call(
-        kernel,
-        name,
-        number,
-        jax.ShapeDtypeStruct((seq * count, width), shard.dtype),
-        SquareGather.semaphores(seq) + [pltpu.SemaphoreType.DMA((1,))],
-        shard,
-    )
-
-
 class LinePieces:
     @staticmethod
     def scratch(wt, shape, pieces):
         zs = wt // 2
-        return [pltpu.VMEM((zs,) + shape, jnp.bfloat16)] * 4 + [pltpu.SemaphoreType.DMA((6, zs, pieces))]
+        return [pltpu.VMEM((zs,) + shape, jnp.bfloat16)] * 3 + [pltpu.SemaphoreType.DMA((6, zs, pieces))]
 
     def __init__(self, at, part, scratch):
         self.at, self.part = at, part
-        self.pair, self.held, self.below, self.above, self.sems = scratch
+        self.pair, self.below, self.above, self.sems = scratch
         self.pieces = self.sems.shape[2]
         self.width = self.pair.shape[2] // self.pieces
 
     def cut(self, ref, piece):
         return ref.at[:, pl.ds(pl.multiple_of(piece * self.width, self.width), self.width)]
+
+    def own(self, z, piece):
+        return self.cut(self.part(z * 2 + self.at.c), piece)
 
     def over(self, z, piece):
         return send(
@@ -773,7 +669,7 @@
 
     def up(self, z, piece):
         return send(
-            self.cut(self.held.at[z], piece),
+            self.own(z, piece),
             self.cut(self.below.at[z], piece),
             self.sems.at[2, z, piece],
             self.sems.at[3, z, piece],
@@ -782,7 +678,7 @@
 
     def down(self, z, piece):
         return send(
-            self.cut(self.held.at[z], piece),
+            self.own(z, piece),
             self.cut(self.above.at[z], piece),
             self.sems.at[4, z, piece],
             self.sems.at[5, z, piece],
@@ -791,53 +687,58 @@
 
     def terms(self, z, piece):
         self.over(z, piece).wait_recv()
-        return [self.cut(self.part(z * 2 + self.at.c), piece), self.cut(self.pair.at[z], piece)]
+        return [self.own(z, piece), self.cut(self.pair.at[z], piece)]
 
     def ends(self, z, piece):
         at = self.at
 
         @pl.when((at.z == 0) & (z > 0))
         def _():
-            add_into(self.cut(self.held.at[z], piece), self.terms(z, piece))
+            add_into(self.own(z, piece), self.terms(z, piece))
             self.up(z, piece).start()
 
         @pl.when((at.z == at.zs - 1) & (z < at.zs - 1))
         def _():
-            add_into(self.cut(self.held.at[z], piece), self.terms(z, piece))
+            add_into(self.own(z, piece), self.terms(z, piece))
             self.down(z, piece).start()
 
-    def pass_on(self):
-        at = self.at
+    def pass_on(self, fill=None):
+        at = self.at
+        upper = at.z * 2 >= at.zs
         for index in range(1, at.zs):
             high, low = index, at.zs - 1 - index
 
+            def lower(piece, when):
+                @pl.when((at.z > low) & (at.z < at.zs - 1) & when)
+                def _():
+                    terms = self.terms(low, piece)
+                    self.down(low, piece).wait_recv()
+                    add_into(self.own(low, piece), terms + [self.cut(self.above.at[low], piece)])
+                    self.down(low, piece).start()
+
             def step(piece, carry):
+                lower(piece, upper)
+
                 @pl.when((at.z < high) & (at.z > 0))
                 def _():
                     terms = self.terms(high, piece)
                     self.up(high, piece).wait_recv()
-                    add_into(
-                        self.cut(self.held.at[high], piece), terms + [self.cut(self.below.at[high], piece)]
-                    )
+                    add_into(self.own(high, piece), terms + [self.cut(self.below.at[high], piece)])
                     self.up(high, piece).start()
 
-                @pl.when((at.z > low) & (at.z < at.zs - 1))
-                def _():
-                    terms = self.terms(low, piece)
-                    self.down(low, piece).wait_recv()
-                    add_into(
-                        self.cut(self.held.at[low], piece), terms + [self.cut(self.above.at[low], piece)]
-                    )
-                    self.down(low, piece).start()
-
+                lower(piece, jnp.logical_not(upper))
+                if fill is not None and index == at.zs - 1:
+                    fill(piece)
                 return carry
 
             lax.fori_loop(0, self.pieces, step, 0)
 
-    def finish(self, total):
+    def finish(self, total, fill=None):
         at = self.at
 
         def step(piece, carry):
+            if fill is not None:
+                fill(self.pieces + piece)
             terms = self.terms(at.z, piece)
             below, above = self.cut(self.below.at[at.z], piece), self.cut(self.above.at[at.z], piece)
 
@@ -873,7 +774,131 @@
         lax.fori_loop(0, self.pieces, step, 0)
 
 
-def exchange(at, shard, everyone, gather_sems, local, sums, first, second, total, ready, wait_for_ready):
+class SquareTerms:
+    @staticmethod
+    def semaphores(seq):
+        return [pltpu.SemaphoreType.DMA((seq // 2, 2)), pltpu.SemaphoreType.DMA((seq // 2, 2, 2))]
+
+    @staticmethod
+    def scratch(seq, half_shape):
+        ys = seq // 2
+        return [
+            pltpu.VMEM((ys,) + half_shape, jnp.bfloat16),
+            pltpu.VMEM((ys,) + half_shape, jnp.bfloat16),
+            pltpu.VMEM(half_shape, jnp.bfloat16),
+            pltpu.VMEM(half_shape, jnp.bfloat16),
+            pltpu.SemaphoreType.DMA((ys + 1, 2)),
+        ]
+
+    def __init__(self, at, terms, from_x, from_y, sems=None, scratch=None):
+        self.at, self.terms, self.from_x, self.from_y = at, terms, from_x, from_y
+        if sems is not None:
+            self.xs, self.ys = sems
+        if scratch is not None:
+            self.sum_y, self.last_y, self.sum_x, self.last_x, self.last = scratch
+
+    def first_x(self, y):
+        at = self.at
+        return send(
+            self.terms(y * 2 + 1 - at.x, 0), self.from_x.at[y], self.xs.at[y, 0], self.xs.at[y, 1], at.across()
+        )
+
+    def first_y(self, step, x):
+        at = self.at
+        y = at.beside(step)
+        return send(
+            self.terms(y * 2 + x, 1),
+            self.from_y.at[at.y, x],
+            self.ys.at[step, x, 0],
+            self.ys.at[at.y, x, 1],
+            at.column(y),
+        )
+
+    def first_start(self):
+        for y in range(self.at.ys):
+            self.first_x(y).start()
+        for step in range(1, self.at.ys):
+            for x in range(2):
+                self.first_y(step, x).start()
+
+    def first_wait(self):
+        at = self.at
+        for y in range(at.ys):
+            self.first_x(y).wait()
+        for step in range(1, at.ys):
+            y = at.beside(step)
+            for x in range(2):
+                self.first_y(step, x).wait_send()
+                slot = self.from_y.at[y, x]
+                send(slot, slot, self.ys.at[step, x, 0], self.ys.at[y, x, 1], at.across()).wait_recv()
+
+    def second_sends(self):
+        at = self.at
+        copies = []
+        for step in range(1, at.ys):
+            y = at.beside(step)
+            copies.append(
+                send(self.sum_y.at[y], self.last_y.at[at.y], self.last.at[step, 0], self.last.at[at.y, 1], at.column(y))
+            )
+        copies.append(
+            send(self.sum_x, self.last_x, self.last.at[at.ys, 0], self.last.at[at.ys, 1], at.across())
+        )
+        return copies
+
+    def second_start(self, fetch, rooms):
+        at = self.at
+        for step in range(1, at.ys):
+            y = at.beside(step)
+            fetch([(self.terms(y * 2 + at.x, 0), rooms[0]), (self.from_x.at[y], rooms[1])])
+            add_into(self.sum_y.at[y], [rooms[0], rooms[1]])
+        fetch([(self.terms(at.y * 2 + 1 - at.x, 1), self.sum_x)])
+        for step in range(1, at.ys):
+            y = at.beside(step)
+            fetch([(self.from_y.at[y, 1 - at.x], rooms[0])])
+            add_into(self.sum_x, [self.sum_x, rooms[0]])
+
+    def second_go(self):
+        for copy in self.second_sends():
+            copy.start()
+
+    def finish(self, fetch, rooms, total):
+        at = self.at
+        fetch([(self.terms(at.s, 0), rooms[0]), (self.from_x.at[at.y], rooms[1])])
+        terms = [rooms[0], rooms[1]]
+        for step in range(1, at.ys):
+            y = at.beside(step)
+            slot = self.last_y.at[y]
+            send(slot, slot, self.last.at[step, 0], self.last.at[y, 1], at.across()).wait_recv()
+            terms.append(slot)
+        add_into(total(0), terms)
+        fetch([(self.terms(at.s, 1), rooms[0])])
+        self.second_sends()[-1].wait_recv()
+        add_into(total(1), [rooms[0], self.last_x])
+        for step in range(1, at.ys):
+            fetch([(self.from_y.at[at.beside(step), at.x], rooms[0])])
+            add_into(total(1), [total(1), rooms[0]])
+        for copy in self.second_sends():
+            copy.wait_send()
+
+
+def norm_back(rows, load, store, gain, terms):
+    def step(index, carry):
+        window = pl.ds(pl.multiple_of(index * 16, 16), 16)
+        values, incoming, base = load(window)
+        root = lax.rsqrt(jnp.mean(values * values, axis=-1, keepdims=True) + epsilon)
+        scaled = incoming * gain
+        share = jnp.mean(values * scaled, axis=-1, keepdims=True)
+        store(window, base + root * scaled - values * (root * root * root * share))
+        term = incoming * values * root
+        terms[...] += term[:8] + term[8:]
+        return carry
+
+    lax.fori_loop(0, rows // 16, step, 0)
+
+
+def exchange(
+    at, shard, everyone, gather_sems, local, sums, first, second, total, ready, wait_for_ready, fill=None
+):
     count = shard.shape[0]
     gather = LineGather(
         at, lambda w: everyone.at[pl.ds(pl.multiple_of(w * count, count), count)], gather_sems
@@ -928,13 +953,12 @@
         return carry
 
     lax.fori_loop(0, last + 1 + late, turn, 0)
-    sums.pass_on()
-    sums.finish(total)
+    sums.pass_on(fill)
+    sums.finish(total, fill)
     gather.sent()
 
 
 PIECES = 4
-ANY = pl.BlockSpec(memory_space=pl.ANY)
 
 
 def feed_forward(normed, gate_up, down_shard):
@@ -951,10 +975,10 @@
         everyone, gates, downs, gate_all, up_all, active_all, parts = scratch[:7]
         gather_sems, sum_scratch, square_sems, local, outgoing = (
             scratch[7:8],
-            scratch[8:13],
-            scratch[13:16],
+            scratch[8:12],
+            scratch[12:15],
+            scratch[15],
             scratch[16],
-            scratch[17],
         )
         load = pltpu.make_async_copy(gate_up_ref, gates, local.at[0])
         load.start()
@@ -1064,42 +1088,126 @@
     )
 
 
-def feed_back(error, gate_up, down, gate, up):
+def feed_back(error, attended, gain, gate_up, down, gate, up, active, normed):
     seq, wt = lax.axis_size("seq"), lax.axis_size("wt")
     count, width = error.shape
     units = gate_up.shape[2]
     tokens = wt * count
-    zs = wt // 2
-
-    def kernel(error_ref, gate_up_ref, down_ref, gate_ref, up_ref, total_ref, error_out, back_out, *scratch):
+    zs, ys = wt // 2, seq // 2
+    block = width // seq
+    gate_half, down_half = (block // 2, units), (units // 2, block)
+
+    def kernel(*refs):
+        (error_ref, attended_ref, gain_ref, gate_up_ref, down_ref, gate_ref, up_ref, active_ref, normed_ref), refs = (
+            refs[:9],
+            refs[9:],
+        )
+        (grad_ref, mix_ref, gain_terms), refs = refs[:3], refs[3:]
+        (gate_out, up_out, down_out, gate_x, gate_y, down_x, down_y), refs = refs[:7], refs[7:]
+        (low, everyone, gates, downs, gate_all, up_all, back_all, parts, actives, columns), refs = refs[:10], refs[10:]
+        (gate_terms, up_terms, down_terms, total), refs = refs[:4], refs[4:]
+        gather_sems, sum_scratch, gate_sems, down_sems, (local, outgoing) = (
+            refs[:1],
+            refs[1:5],
+            refs[5:7],
+            refs[7:9],
+            refs[9:],
+        )
         at = Place(seq, wt)
-        everyone, gates, downs, gate_all, up_all, back_all, parts = scratch[:7]
-        gather_sems, sum_scratch, local, outgoing = scratch[7:8], scratch[8:13], scratch[13], scratch[14]
         loads = [
             pltpu.make_async_copy(source, target, local.at[index])
             for index, (source, target) in enumerate(
-                ((down_ref, downs), (gate_ref, gate_all), (up_ref, up_all), (gate_up_ref, gates))
+                (
+                    (down_ref, downs),
+                    (gate_ref, gate_all),
+                    (up_ref, up_all),
+                    (gate_up_ref, gates),
+                    (active_ref, actives),
+                )
             )
         ]
         for load in loads:
             load.start()
-        at.meet(False, True)
+        at.meet(True, True)
+        low[...] = error_ref[...].astype(jnp.bfloat16)
         sums = LinePieces(
             at, lambda w: parts.at[pl.ds(pl.multiple_of(w * count, count), count)], sum_scratch
         )
+        gate_sum = SquareTerms(at, lambda s, h: gate_terms.at[s, h], gate_x, gate_y, gate_sems)
+        down_sum = SquareTerms(at, lambda s, h: down_terms.at[s, h], down_x, down_y, down_sems)
+
+        def place(index):
+            step = lax.div(index, 2) + 1
+            x = lax.rem(at.x + 1 + lax.rem(index, 2), 2)
+            return step, x, at.beside(step) * 2 + x
+
+        def column_load(index):
+            s = place(index)[2]
+            return pltpu.make_async_copy(
+                normed_ref.at[:, pl.ds(pl.multiple_of(s * block, block), block)],
+                columns.at[lax.rem(index, 2)],
+                local.at[6 + lax.rem(index, 2)],
+            )
+
+        def leave(sum_, index):
+            step, x, s = place(index)
+
+            @pl.when(x != at.x)
+            def _():
+                sum_.first_x(lax.div(s, 2)).start()
+
+            @pl.when(step < ys)
+            def _():
+                sum_.first_y(step, x).start()
+
+        def down_job(index):
+            s = place(index)[2]
+            term = contract_first(
+                actives[...], everyone[:, pl.ds(pl.multiple_of(s * block, block), block)]
+            ).astype(jnp.bfloat16)
+            down_terms[s, 0] = term[: units // 2]
+            down_terms[s, 1] = term[units // 2 :]
+            leave(down_sum, index)
+
+        def gate_job(index):
+            s = place(index)[2]
+            column_load(index).wait()
+            here = columns.at[lax.rem(index, 2)]
+            for number, terms in enumerate((gate_terms, up_terms)):
+                term = contract_first(here[...], back_all[number]).astype(jnp.bfloat16)
+                terms[s, 0] = term[: block // 2]
+                terms[s, 1] = term[block // 2 :]
+
+            @pl.when(index + 2 < seq)
+            def _():
+                column_load(index + 2).start()
+
+            leave(gate_sum, index)
+
+        def fill(slot):
+            def step(index, carry):
+                job = slot * (seq // 4) + index
+
+                @pl.when(job < seq)
+                def _():
+                    down_job(job)
+
+                @pl.when(job >= seq)
+                def _():
+                    gate_job(job - seq)
+
+                return carry
+
+            lax.fori_loop(0, seq // 4, step, 0)
 
         def ready_first():
+            column_load(0).start()
+            column_load(1).start()
             for load in loads:
                 load.wait()
 
         def rows(z):
             return pl.ds(pl.multiple_of(z * 2 * count, 2 * count), 2 * count)
-
-        def stores(z):
-            return [
-                pltpu.make_async_copy(everyone.at[rows(z)], error_out.at[rows(z)], outgoing.at[0, z]),
-                pltpu.make_async_copy(back_all.at[:, rows(z)], back_out.at[:, rows(z)], outgoing.at[1, z]),
-            ]
 
         def first(z):
             active_back = contract_last(everyone[rows(z), :], downs[...])
@@ -1109,8 +1217,6 @@
                 active_back * up_here * share * (1.0 + gate_here * (1.0 - share))
             ).astype(jnp.bfloat16)
             back_all[1, rows(z), :] = (active_back * gate_here * share).astype(jnp.bfloat16)
-            for copy in stores(z):
-                copy.start()
 
         def second(z, piece):
             window = pl.ds(pl.multiple_of(piece * sums.width, sums.width), sums.width)
@@ -1121,20 +1227,49 @@
 
         exchange(
             at,
-            error_ref,
+            low,
             everyone,
             gather_sems,
-            local.at[4],
+            local.at[5],
             sums,
             first,
             second,
-            total_ref,
+            total,
             (ready_first,),
             False,
-        )
-        for z in range(zs):
-            for copy in stores(z):
-                copy.wait()
+            fill,
+        )
+        stores = [
+            pltpu.make_async_copy(source, target, outgoing.at[index])
+            for index, (source, target) in enumerate(
+                ((gate_terms, gate_out), (up_terms, up_out), (down_terms, down_out))
+            )
+        ]
+        for copy in stores:
+            copy.start()
+        gain_terms[...] = jnp.zeros_like(gain_terms)
+
+        def load_rows(window):
+            return attended_ref[window, :], total[window, :], error_ref[window, :]
+
+        def store_rows(window, value):
+            grad_ref[window, :] = value
+            mix_ref[window, :] = value.astype(jnp.bfloat16)
+
+        norm_back(count, load_rows, store_rows, gain_ref[...], gain_terms)
+        for copy in stores:
+            copy.wait()
+        gate_sum.first_wait()
+        down_sum.first_wait()
+
+    def terms_of(half):
+        return jax.ShapeDtypeStruct((seq, 2) + half, jnp.bfloat16)
+
+    def first_of(half):
+        return [
+            jax.ShapeDtypeStruct((ys,) + half, jnp.bfloat16),
+            jax.ShapeDtypeStruct((ys, 2) + half, jnp.bfloat16),
+        ]
 
     return remote_call(
         kernel,
@@ -1142,10 +1277,16 @@
         3,
         [
             jax.ShapeDtypeStruct((count, width), jnp.float32),
-            jax.ShapeDtypeStruct((tokens, width), jnp.bfloat16),
-            jax.ShapeDtypeStruct((2, tokens, units), jnp.bfloat16),
-        ],
+            jax.ShapeDtypeStruct((count, width), jnp.bfloat16),
+            jax.ShapeDtypeStruct((8, width), jnp.float32),
+            terms_of(gate_half),
+            terms_of(gate_half),
+            terms_of(down_half),
+        ]
+        + first_of(gate_half)
+        + first_of(down_half),
         [
+            pltpu.VMEM((count, width), jnp.bfloat16),
             pltpu.VMEM((tokens, width), jnp.bfloat16),
             pltpu.VMEM(gate_up.shape, jnp.bfloat16),
             pltpu.VMEM((units, width), jnp.bfloat16),
@@ -1153,149 +1294,393 @@
             pltpu.VMEM((tokens, units), jnp.float32),
             pltpu.VMEM((2, tokens, units), jnp.bfloat16),
             pltpu.VMEM((tokens, width), jnp.bfloat16),
+            pltpu.VMEM((tokens, units), jnp.bfloat16),
+            pltpu.VMEM((2, tokens, block), jnp.bfloat16),
+            pltpu.VMEM((seq, 2) + gate_half, jnp.bfloat16),
+            pltpu.VMEM((seq, 2) + gate_half, jnp.bfloat16),
+            pltpu.VMEM((seq, 2) + down_half, jnp.bfloat16),
+            pltpu.VMEM((count, width), jnp.float32),
         ]
         + LineGather.semaphores(wt)
         + LinePieces.scratch(wt, (count, width), PIECES)
-        + [pltpu.SemaphoreType.DMA((5,)), pltpu.SemaphoreType.DMA((2, zs))],
+        + SquareTerms.semaphores(seq)
+        + SquareTerms.semaphores(seq)
+        + [pltpu.SemaphoreType.DMA((8,)), pltpu.SemaphoreType.DMA((3,))],
         error,
+        attended,
+        gain,
         gate_up,
         down,
         gate,
         up,
-        in_specs=[VMEM, ANY, ANY, ANY, ANY],
-        out_specs=[VMEM, ANY, ANY],
-    )
-
-
-def final_sums(hidden_parts, gate_up_parts, down_parts, qkv_parts, out_parts):
+        active,
+        normed,
+        in_specs=[VMEM] * 3 + [ANY] * 6,
+        out_specs=[VMEM] * 3 + [ANY] * 7,
+    )
+
+
+def mixer_back(
+    mix_back,
+    attended_grad,
+    tokens,
+    gain,
+    out_rows,
+    qkv_columns,
+    hidden,
+    projected,
+    mixer,
+    mixed_values,
+    head_outputs,
+    segments,
+    marks,
+    taps,
+    order,
+    gain_terms,
+    energy,
+    gate_parts,
+    up_parts,
+    down_parts,
+):
     seq, wt = lax.axis_size("seq"), lax.axis_size("wt")
-    hidden_half = hidden_parts.shape[2:]
-    gate_up_half = gate_up_parts.shape[2:]
-    down_rows, down_all = down_parts.shape[1:]
-    down_columns = down_all // seq
-    down_half = (down_rows, down_columns)
-    qkv_shape = (seq,) + qkv_parts.shape[2:]
-
-    def kernel(hidden_ref, gate_up_ref, down_ref, qkv_ref, out_ref, h_total, gu_total, d_total, q_total, o_total, *scratch):
+    zs, ys = wt // 2, seq // 2
+    count, width = mix_back.shape
+    length = count * seq
+    heads = mixed_values.shape[0]
+    qkv_width = qkv_columns.shape[1]
+    value_width = heads * DV
+    rank = width // (seq * wt)
+    gate_half, down_half = gate_parts[0].shape[2:], down_parts[0].shape[2:]
+    rows_at_once = 256
+    segment_rows = segments.reshape(1, length)
+    segment_columns = segments.reshape(length, 1)
+    big = [out_rows, qkv_columns, hidden, projected, mixer, mixed_values, head_outputs]
+    small = [mix_back, attended_grad, tokens, gain, segment_rows, segment_columns, marks, taps, order, gain_terms, energy]
+    far = list(gate_parts) + list(down_parts) + list(up_parts)
+
+    def kernel(*refs):
+        big_refs, refs = refs[: len(big)], refs[len(big) :]
+        small_refs, refs = refs[: len(small)], refs[len(small) :]
+        (gate_t, gate_x, gate_y, down_t, down_x, down_y, up_t), refs = refs[: len(far)], refs[len(far) :]
+        (grad_out, sums_out, gate_out, up_out, down_out, qkv_out, w_out_out, up_x, up_y), refs = refs[:9], refs[9:]
+        (w_out_v, w_qkv_v, hidden_v, projected_v, mixer_v, values_v, outputs_v), refs = refs[:7], refs[7:]
+        (mix_all, mixer_grad, sorted_v, query_acc, key_acc, value_acc, back_sorted, back_v), refs = refs[:8], refs[8:]
+        (hidden_parts, qkv_parts, out_parts, hidden_total, gain_acc, spread, taps_acc), refs = refs[:7], refs[7:]
+        (room_gate0, room_gate1, room_down0, room_down1, qkv_sum, first, middle, last), refs = refs[:8], refs[8:]
+        hidden_scratch, refs = refs[:8], refs[8:]
+        qkv_scratch, out_scratch, refs = refs[:5], refs[5:10], refs[10:]
+        gate_scratch, down_scratch, up_scratch, refs = refs[:5], refs[5:10], refs[10:15], refs[15:]
+        gather_sems, up_sems, refs = refs[:3], refs[3:5], refs[5:]
+        local, swap, first_sems, last_sems = refs
+        (
+            mix_ref,
+            grad_ref,
+            token_ref,
+            gain_ref,
+            segment_row,
+            segment_column,
+            mark_ref,
+            tap_ref,
+            order_ref,
+            gain_two,
+            energy_ref,
+        ) = small_refs
         at = Place(seq, wt)
+        loads = [
+            pltpu.make_async_copy(source, target, local.at[4 + index])
+            for index, (source, target) in enumerate(
+                zip(big_refs, (w_out_v, w_qkv_v, hidden_v, projected_v, mixer_v, values_v, outputs_v))
+            )
+        ]
+        for load in loads:
+            load.start()
         at.meet(True, True)
-        square, scratch = [scratch[8 * index : 8 * index + 8] for index in range(3)], scratch[24:]
-        line, scratch = [scratch[5 * index : 5 * index + 5] for index in range(2)], scratch[10:]
-        q_sum, swap = scratch
-        hidden = SquareSum(at, lambda s, h: hidden_ref.at[s, h], square[0])
-        gate_up = SquareSum(at, lambda s, h: gate_up_ref.at[h, s], square[1])
-        down = SquareSum(
+        half = count // 2
+        gather = SquareGather(
             at,
-            lambda s, h: down_ref.at[h, :, pl.ds(pl.multiple_of(s * down_columns, down_columns), down_columns)],
-            square[2],
-        )
-        qkv = LineSum(at, lambda w: qkv_ref.at[:, w], line[0])
-        out = LineSum(at, lambda w: out_ref.at[w], line[1])
-        qkv.start()
-        out.start()
-        hidden.start()
-        gate_up.start()
-        down.start()
-        hidden.relay()
-        for index in range(at.zs - 1):
-            qkv.step(index)
-            out.step(index)
-        qkv.finish(q_sum)
-        out.finish(o_total)
-        swaps = []
-        for step in range(1, seq):
-            to = lax.rem(at.s + step, seq)
-            copy = send(q_sum.at[to], q_total.at[at.s], swap.at[step, 0], swap.at[at.s, 1], (to, at.w))
-            copy.start()
-            swaps.append(copy)
-        add_into(q_total.at[at.s], [q_sum.at[at.s]])
-        gate_up.relay()
-        down.relay()
-        hidden.finish(lambda h: h_total.at[h])
-        gate_up.finish(lambda h: gu_total.at[h])
-        down.finish(lambda h: d_total.at[h])
-        for step in range(1, seq):
-            s = lax.rem(at.s + step, seq)
-            slot = q_total.at[s]
-            send(slot, slot, swap.at[step, 0], swap.at[s, 1], at.across()).wait_recv()
-        for copy in swaps:
-            copy.wait_send()
-
-    return remote_call(
-        kernel,
-        "final_sums",
-        7,
-        [
-            jax.ShapeDtypeStruct((2,) + hidden_half, jnp.float32),
-            jax.ShapeDtypeStruct((2,) + gate_up_half, jnp.float32),
-            jax.ShapeDtypeStruct((2,) + down_half, jnp.float32),
-            jax.ShapeDtypeStruct(qkv_shape, jnp.float32),
-            jax.ShapeDtypeStruct(out_parts.shape[1:], jnp.float32),
-        ],
-        SquareSum.scratch(seq, hidden_half)
-        + SquareSum.scratch(seq, gate_up_half)
-        + SquareSum.scratch(seq, down_half)
-        + LineSum.scratch(wt, qkv_shape)
-        + LineSum.scratch(wt, out_parts.shape[1:])
-        + [pltpu.VMEM(qkv_shape, jnp.float32), pltpu.SemaphoreType.DMA((seq, 2))],
-        hidden_parts,
-        gate_up_parts,
-        down_parts,
-        qkv_parts,
-        out_parts,
-    )
-
-
-def small_sums(spread, lined):
-    seq, wt = lax.axis_size("seq"), lax.axis_size("wt")
-    tile = spread.shape[2:]
-
-    def kernel(spread_ref, lined_ref, total_ref, first, middle, last, first_sems, last_sems):
-        at = Place(seq, wt)
-        at.meet(True, True)
+            lambda s, h: mix_all.at[pl.ds(pl.multiple_of(s * count + h * half, half), half)],
+            lambda h: mix_ref.at[pl.ds(h * half, half)],
+            gather_sems,
+        )
+        gather.start()
+        own = pltpu.make_async_copy(
+            mix_ref, mix_all.at[pl.ds(pl.multiple_of(at.s * count, count), count)], local.at[3]
+        )
+        own.start()
+
+        def fetch(pairs):
+            copies = [
+                pltpu.make_async_copy(source, target, local.at[index])
+                for index, (source, target) in enumerate(pairs)
+            ]
+            for copy in copies:
+                copy.start()
+            for copy in copies:
+                copy.wait()
+
+        gate_sum = SquareTerms(at, lambda s, h: gate_t.at[s, h], gate_x, gate_y, None, gate_scratch)
+        down_sum = SquareTerms(at, lambda s, h: down_t.at[s, h], down_x, down_y, None, down_scratch)
+        up_sum = SquareTerms(at, lambda s, h: up_t.at[s, h], up_x, up_y, up_sems, up_scratch)
+        gate_rooms, down_rooms = (room_gate0, room_gate1), (room_down0, room_down1)
+        gate_sum.second_start(fetch, gate_rooms)
+        down_sum.second_start(fetch, down_rooms)
+        own.wait()
+        for load in loads:
+            load.wait()
+        sorted_v[...] = jnp.dot(
+            projected_v[...], order_ref[...], preferred_element_type=jnp.float32
+        ).astype(jnp.bfloat16)
+        query_acc[...] = jnp.zeros_like(query_acc)
+        key_acc[...] = jnp.zeros_like(key_acc)
+        value_acc[...] = jnp.zeros_like(value_acc)
+        gather.relay()
+        gather.finish()
+        gate_sum.second_go()
+        down_sum.second_go()
+        up_sum.first_start()
+        mixer_grad[...] = contract_last(mix_all[...], w_out_v[...]).astype(jnp.bfloat16)
+        out_sum = LineSum(at, lambda w: out_parts.at[w], out_scratch)
+        out_rank = out_parts.shape[1]
+        out_block = 512 if value_width % 512 == 0 else value_width
+
+        def out_job(index, carry):
+            window = pl.ds(pl.multiple_of(index * 512, 512), 512)
+            term = contract_first(mixer_v[...], mix_all[:, window]).astype(jnp.bfloat16)
+            for w in range(wt):
+                out_parts[w, :, window] = term[w * out_rank : (w + 1) * out_rank]
+            return carry
+
+        lax.fori_loop(0, width // 512, out_job, 0)
+        out_sum.start()
+
+        steps = length // rows_at_once
+        lanes = lax.broadcasted_iota(jnp.int32, (1, 128), 1)
+
+        def attend(index, carry):
+            head, start = lax.div(index, steps), lax.rem(index, steps) * rows_at_once
+            rows = pl.ds(pl.multiple_of(start, rows_at_once), rows_at_once)
+            columns = pl.ds(pl.multiple_of(head * DV, DV), DV)
+            mine = ((lanes >= head * FEAT) & (lanes < head * FEAT + FEAT)).astype(jnp.float32)
+            queries = sorted_v[rows, value_width : value_width + 128] * mine.astype(jnp.bfloat16)
+            keys = sorted_v[:, value_width + 128 :]
+            scores = contract_last(queries, keys) * 0.25
+            places = start + lax.broadcasted_iota(jnp.int32, scores.shape, 0)
+            allowed = (segment_column[rows, :] == segment_row[...]) & (
+                places >= lax.broadcasted_iota(jnp.int32, scores.shape, 1)
+            )
+            kernel_values = jnp.where(allowed, 1.0 + scores + 0.5 * scores * scores, 0.0)
+            denominator = jnp.sum(kernel_values, axis=1, keepdims=True)
+            incoming = mixer_grad[rows, columns].astype(jnp.float32)
+            numerator_back = (incoming / denominator).astype(jnp.bfloat16)
+            denominator_back = (
+                -jnp.sum(incoming * outputs_v[head, rows, :], axis=1, keepdims=True) / denominator
+            )
+            weight_back = contract_last(numerator_back, values_v[head])
+            kernel_back = jnp.where(allowed, weight_back + denominator_back, 0.0)
+            dots_back = (0.25 * kernel_back * (1.0 + scores)).astype(jnp.bfloat16)
+            query_acc[rows, :] += jnp.dot(dots_back, keys, preferred_element_type=jnp.float32) * mine
+            key_acc[...] += contract_first(dots_back, queries)
+            value_acc[:, columns] += contract_first(kernel_values.astype(jnp.bfloat16), numerator_back)
+            return carry
+
+        lax.fori_loop(0, heads * steps, attend, 0)
+        taps_acc[...] = jnp.zeros_like(taps_acc)
+
+        def convolve(head, carry):
+            columns = pl.ds(pl.multiple_of(head * DV, DV), DV)
+            mixed_back = value_acc[:, columns]
+            raw = sorted_v[:, columns].astype(jnp.float32)
+            raw_back = tap_ref[0:1, columns] * mixed_back
+            taps_acc[3:4, columns] = jnp.sum(mixed_back * raw, axis=0, keepdims=True)
+            for tap in range(1, KCONV):
+                masked = mixed_back * mark_ref[:, tap : tap + 1]
+                taps_acc[3 + tap : 4 + tap, columns] = jnp.sum(
+                    masked * pltpu.roll(raw, tap, 0), axis=0, keepdims=True
+                )
+                raw_back = raw_back + tap_ref[tap : tap + 1, columns] * pltpu.roll(masked, length - tap, 0)
+            back_sorted[:, columns] = raw_back.astype(jnp.bfloat16)
+            return carry
+
+        lax.fori_loop(0, heads, convolve, 0)
+        back_sorted[:, value_width : value_width + 128] = query_acc[...].astype(jnp.bfloat16)
+        back_sorted[:, value_width + 128 :] = key_acc[...].astype(jnp.bfloat16)
+        back_v[...] = contract_last(back_sorted[...], order_ref[...]).astype(jnp.bfloat16)
+        hidden_sum = SquareSum(at, lambda s, h: hidden_parts.at[s, h], hidden_scratch)
+
+        def hidden_job(index, carry):
+            window = pl.ds(pl.multiple_of(index * 512, 512), 512)
+            term = contract_last(back_v[...], w_qkv_v[window, :]).astype(jnp.bfloat16)
+            for s in range(seq):
+                for h in range(2):
+                    begin = s * count + h * half
+                    hidden_parts[s, h, :, window] = term[begin : begin + half]
+            return carry
+
+        lax.fori_loop(0, width // 512, hidden_job, 0)
+        hidden_sum.start()
+        qkv_sums = LineSum(at, lambda w: qkv_parts.at[:, w], qkv_scratch)
+        qkv_rank = qkv_parts.shape[2]
+
+        def qkv_job(s, carry):
+            block = wt * qkv_rank
+            window = pl.ds(pl.multiple_of(s * block, block), block)
+            term = contract_first(hidden_v[:, window], back_v[...]).astype(jnp.bfloat16)
+            for w in range(wt):
+                qkv_parts[s, w] = term[w * qkv_rank : (w + 1) * qkv_rank]
+            return carry
+
+        lax.fori_loop(0, seq, qkv_job, 0)
+        qkv_sums.start()
+        hidden_sum.relay()
+        for index in range(zs - 1):
+            out_sum.step(index)
+            qkv_sums.step(index)
+        up_sum.first_wait()
+        up_sum.second_start(fetch, gate_rooms)
+        up_sum.second_go()
+        hidden_sum.finish(lambda h: hidden_total.at[h])
+        gain_acc[...] = jnp.zeros_like(gain_acc)
+        for h in range(2):
+
+            def shift(window):
+                return pl.ds(pl.multiple_of(h * half + window.start, 16), 16)
+
+            def load_rows(window):
+                rows = shift(window)
+                return token_ref[rows, :].astype(jnp.float32), hidden_total[h, window, :], grad_ref[rows, :]
+
+            def store_rows(window, value):
+                grad_out[shift(window), :] = value
+
+            norm_back(half, load_rows, store_rows, gain_ref[...], gain_acc)
+        spread[...] = jnp.zeros_like(spread)
+        spread[0:1, :] = jnp.sum(gain_acc[...], axis=0, keepdims=True)
+        spread[1:2, :] = jnp.sum(gain_two[...], axis=0, keepdims=True)
+        spread[2:3, :] = jnp.broadcast_to(energy_ref[...], (1, width))
         copies = []
         for step in range(1, seq):
             to = lax.rem(at.s + step, seq)
-            copy = send(spread_ref.at[to], first.at[at.s], first_sems.at[step, 0], first_sems.at[at.s, 1], (to, at.w))
+            window = pl.ds(pl.multiple_of(to * value_width, value_width), value_width)
+            copies.append(
+                send(spread.at[:, window], first.at[at.s], first_sems.at[step, 0], first_sems.at[at.s, 1], (to, at.w))
+            )
+        for copy in copies:
+            copy.start()
+        qkv_sums.finish(qkv_sum)
+        for step in range(1, seq):
+            to = lax.rem(at.s + step, seq)
+            copy = send(qkv_sum.at[to], qkv_out.at[at.s], swap.at[step, 0], swap.at[at.s, 1], (to, at.w))
             copy.start()
             copies.append(copy)
-        terms = [spread_ref.at[at.s]]
+        add_into(qkv_out.at[at.s], [qkv_sum.at[at.s]])
+        out_sum.finish(w_out_out)
+        terms = [spread.at[:, pl.ds(pl.multiple_of(at.s * value_width, value_width), value_width)], taps_acc]
         for step in range(1, seq):
             s = lax.rem(at.s + step, seq)
             slot = first.at[s]
             send(slot, slot, first_sems.at[step, 0], first_sems.at[s, 1], at.across()).wait_recv()
             terms.append(slot)
-        add_into(middle, terms + [lined_ref])
+        add_into(middle, terms)
         for step in range(1, wt):
             to = lax.rem(at.w + step, wt)
-            copy = send(middle.at[to], last.at[at.w], last_sems.at[step, 0], last_sems.at[at.w, 1], (at.s, to))
+            copy = send(middle, last.at[at.w], last_sems.at[step, 0], last_sems.at[at.w, 1], (at.s, to))
             copy.start()
             copies.append(copy)
-        terms = [middle.at[at.w]]
+        gate_sum.finish(fetch, gate_rooms, lambda h: gate_out.at[h])
+        down_sum.finish(fetch, down_rooms, lambda h: down_out.at[h])
+        terms = [middle]
         for step in range(1, wt):
             w = lax.rem(at.w + step, wt)
             slot = last.at[w]
             send(slot, slot, last_sems.at[step, 0], last_sems.at[w, 1], at.partner()).wait_recv()
             terms.append(slot)
-        add_into(total_ref, terms)
+        add_into(sums_out, terms)
+        for step in range(1, seq):
+            s = lax.rem(at.s + step, seq)
+            slot = qkv_out.at[s]
+            send(slot, slot, swap.at[step, 0], swap.at[s, 1], at.across()).wait_recv()
+        up_sum.finish(fetch, gate_rooms, lambda h: up_out.at[h])
         for copy in copies:
             copy.wait_send()
 
-    return remote_call(
+    out_rank, qkv_rank = value_width // wt, width // (seq * wt)
+    f32, low = jnp.float32, jnp.bfloat16
+    tile = (8, value_width)
+    results = remote_call(
         kernel,
-        "small_sums",
-        8,
-        jax.ShapeDtypeStruct(tile, jnp.float32),
+        "mixer_back",
+        4,
         [
-            pltpu.VMEM((seq, wt) + tile, jnp.float32),
-            pltpu.VMEM((wt,) + tile, jnp.float32),
-            pltpu.VMEM((wt,) + tile, jnp.float32),
+            jax.ShapeDtypeStruct((count, width), f32),
+            jax.ShapeDtypeStruct(tile, f32),
+            jax.ShapeDtypeStruct((2,) + gate_half, f32),
+            jax.ShapeDtypeStruct((2,) + gate_half, f32),
+            jax.ShapeDtypeStruct((2,) + down_half, f32),
+            jax.ShapeDtypeStruct((seq, qkv_rank, qkv_width), f32),
+            jax.ShapeDtypeStruct((out_rank, width), f32),
+            jax.ShapeDtypeStruct((ys,) + gate_half, low),
+            jax.ShapeDtypeStruct((ys, 2) + gate_half, low),
+        ],
+        [pltpu.VMEM(array.shape, array.dtype) for array in big]
+        + [
+            pltpu.VMEM((length, width), low),
+            pltpu.VMEM((length, value_width), low),
+            pltpu.VMEM((length, value_width + 256), low),
+            pltpu.VMEM((length, 128), f32),
+            pltpu.VMEM((length, 128), f32),
+            pltpu.VMEM((length, value_width), f32),
+            pltpu.VMEM((length, value_width + 256), low),
+            pltpu.VMEM((length, qkv_width), low),
+            pltpu.VMEM((seq, 2, count // 2, width), low),
+            pltpu.VMEM((seq, wt, qkv_rank, qkv_width), low),
+            pltpu.VMEM((wt, out_rank, width), low),
+            pltpu.VMEM((2, count // 2, width), f32),
+            pltpu.VMEM((8, width), f32),
+            pltpu.VMEM((8, width), f32),
+            pltpu.VMEM(tile, f32),
+            pltpu.VMEM(gate_half, low),
+            pltpu.VMEM(gate_half, low),
+            pltpu.VMEM(down_half, low),
+            pltpu.VMEM(down_half, low),
+            pltpu.VMEM((seq, qkv_rank, qkv_width), f32),
+            pltpu.VMEM((seq,) + tile, f32),
+            pltpu.VMEM(tile, f32),
+            pltpu.VMEM((wt,) + tile, f32),
+        ]
+        + SquareSum.scratch(seq, (count // 2, width))
+        + LineSum.scratch(wt, (seq, qkv_rank, qkv_width))
+        + LineSum.scratch(wt, (out_rank, width))
+        + SquareTerms.scratch(seq, gate_half)
+        + SquareTerms.scratch(seq, down_half)
+        + SquareTerms.scratch(seq, gate_half)
+        + SquareGather.semaphores(seq)
+        + SquareTerms.semaphores(seq)
+        + [
+            pltpu.SemaphoreType.DMA((11,)),
+            pltpu.SemaphoreType.DMA((seq, 2)),
             pltpu.SemaphoreType.DMA((seq, 2)),
             pltpu.SemaphoreType.DMA((wt, 2)),
         ],
-        spread,
-        lined,
-    )
+        *big,
+        *small,
+        *far,
+        in_specs=[ANY] * len(big) + [VMEM] * len(small) + [ANY] * len(far),
+        out_specs=[VMEM] * 7 + [ANY] * 2,
+    )
+    return results[:7]
+
+
+def column_order(heads):
+    head_width = 2 * FEAT + DV
+    column = jnp.arange(heads * head_width)
+    head, place = column // head_width, column % head_width
+    value_width = heads * DV
+    target = jnp.where(
+        place < FEAT,
+        value_width + head * FEAT + place,
+        jnp.where(place < 2 * FEAT, value_width + 128 + head * FEAT + place - FEAT, head * DV + place - 2 * FEAT),
+    )
+    return (target[:, None] == jnp.arange(value_width + 256)[None, :]).astype(jnp.bfloat16)
 
 
 def rows_of_tile(values, row):
@@ -1364,8 +1749,7 @@
     attended = rows_in + square_sum(
         mixed_parts.reshape(seq_parts, 2, tok_count // 2, model_width), "mixed_sum", 1
     ).reshape(tok_count, model_width)
-    normed_value, second_pull = jax.vjp(rms_norm, attended, gain_second)
-    normed_low = normed_value.astype(jnp.bfloat16)
+    normed_low = rms_norm(attended, gain_second).astype(jnp.bfloat16)
     branch_out, normed_all, gate_all, up_all, active_all, down_part = feed_forward(
         normed_low, gate_up_part, w_down
     )
@@ -1377,68 +1761,62 @@
     keep_mask = (positions < sequence_length).astype(jnp.float32)
     residual_error = (outputs - teacher[0].astype(jnp.float32)) * keep_mask[:, None]
     energy = 0.5 * jnp.sum(residual_error * residual_error)
-    branch_grad = residual_error.astype(jnp.bfloat16)
-    normed_grad, error_all, gate_up_grad = feed_back(branch_grad, gate_up_part, down_part, gate_all, up_all)
-    down_term = contract_first(active_all, error_all)
-    gate_up_term = jnp.einsum(
-        "tc,gtf->gcf", normed_all, gate_up_grad, preferred_element_type=jnp.float32
-    )
-    attended_back, gain_two_term = second_pull(normed_grad)
-    attended_grad = residual_error + attended_back
-    mixer_branch = square_gather(attended_grad.astype(jnp.bfloat16), "mix_back_gather", 6)
-    out_term = contract_first(mixer_low, mixer_branch)
-    mixer_grad = contract_last(mixer_branch, out_rows).astype(jnp.bfloat16)
-    head_incoming = (
-        mixer_grad.reshape(length, head_count, DV).transpose(1, 0, 2).astype(jnp.float32)
-    )
-    query_grads, key_grads, value_grads = attend_backward(
-        head_queries,
-        head_keys,
+    (
+        attended_grad,
+        mix_back,
+        gain_two_terms,
+        gate_terms,
+        up_terms,
+        down_terms,
+        gate_from_x,
+        gate_from_y,
+        down_from_x,
+        down_from_y,
+    ) = feed_back(
+        residual_error,
+        attended,
+        gain_second[None],
+        gate_up_part,
+        down_part,
+        gate_all,
+        up_all,
+        active_all,
+        normed_all,
+    )
+    marks = jnp.stack(tap_masks, axis=1) * (
+        jnp.arange(length)[:, None] >= jnp.arange(KCONV)[None, :]
+    ).astype(jnp.float32)
+    inputs_grad, totals, gate_total, up_total, down_total, qkv_total, grad_w_out = mixer_back(
+        mix_back,
+        attended_grad,
+        rows_low,
+        gain_first[None],
+        out_rows,
+        qkv_columns,
+        hidden_low,
+        projected,
+        mixer_low,
         conv_low,
+        head_outputs,
         segments,
-        head_outputs,
-        denominators,
-        head_incoming,
-        block_rows,
-    )
-    mixed_grad = value_grads.transpose(1, 0, 2)
-    conv_terms = [jnp.sum(mixed_grad * raw_values, axis=0)]
-    raw_grad = conv_taps[0] * mixed_grad
-    for tap_index in range(1, KCONV):
-        masked = mixed_grad * tap_masks[tap_index][:, None, None]
-        conv_terms.append(jnp.sum(masked * shift_down(raw_values, tap_index, 0.0), axis=0))
-        raw_grad = raw_grad + conv_taps[tap_index] * shift_up(masked, tap_index)
-    projected_grad = jnp.concatenate(
-        [query_grads.transpose(2, 0, 1), key_grads.transpose(2, 0, 1), raw_grad], axis=2
-    ).astype(jnp.bfloat16)
-    returned = projected_grad.reshape(length, qkv_width)
-    qkv_term = contract_first(hidden_low, returned).astype(jnp.bfloat16)
-    hidden_parts = contract_last(returned, qkv_columns).astype(jnp.bfloat16)
+        marks,
+        conv_taps.reshape(KCONV, head_count * DV),
+        column_order(head_count),
+        gain_two_terms,
+        energy.reshape(1, 1),
+        (gate_terms, gate_from_x, gate_from_y),
+        (up_terms,),
+        (down_terms, down_from_x, down_from_y),
+    )
+    grad_w_qkv = qkv_total.transpose(1, 0, 2).reshape(w_qkv.shape)
     hidden_units = gate_up_part.shape[2]
-    hidden_grad, gate_up_total, down_total, qkv_total, out_total = final_sums(
-        hidden_parts.reshape(seq_parts, 2, tok_count // 2, model_width),
-        gate_up_term.astype(jnp.bfloat16).reshape(2, seq_parts, model_width // seq_parts, hidden_units),
-        down_term.astype(jnp.bfloat16).reshape(2, hidden_units // 2, model_width),
-        qkv_term.reshape(seq_parts, wt_parts, w_qkv.shape[0], qkv_width),
-        out_term.astype(jnp.bfloat16).reshape(wt_parts, w_out.shape[0], model_width),
-    )
-    _, first_pull = jax.vjp(rms_norm, rows_in, gain_first)
-    inputs_back, gain_one_term = first_pull(hidden_grad.reshape(tok_count, model_width))
-    inputs_grad = attended_grad + inputs_back
-    grad_w_qkv = qkv_total.transpose(1, 0, 2).reshape(w_qkv.shape)
-    grad_w_gate_up = gate_up_total
+    grad_w_gate_up = jnp.stack(
+        [total.reshape(model_width // seq_parts, hidden_units) for total in (gate_total, up_total)]
+    )
     grad_w_down = down_total.reshape(w_down.shape)
-    grad_w_out = out_total
-    spread = (
-        rows_of_tile(gain_one_term.reshape(seq_parts, wt_parts, gain_lanes), 0)
-        + rows_of_tile(gain_two_term.reshape(seq_parts, wt_parts, gain_lanes), 1)
-        + rows_of_tile(jnp.broadcast_to(energy, (seq_parts, wt_parts, 1)), 2)
-    )
-    conv_block = jnp.stack(conv_terms).reshape(KCONV, wt_parts, gain_lanes)
-    lined = sum(rows_of_tile(conv_block[tap], 3 + tap) for tap in range(KCONV))
-    totals = small_sums(spread, lined)
-    grad_norm_gain, grad_mlp_gain = totals[0, :gain_lanes], totals[1, :gain_lanes]
-    grad_conv = totals[3 : 3 + KCONV, :gain_lanes]
+    totals = lax.dynamic_slice_in_dim(totals, lax.axis_index("wt") * gain_lanes, gain_lanes, 1)
+    grad_norm_gain, grad_mlp_gain = totals[0], totals[1]
+    grad_conv = totals[3 : 3 + KCONV]
     valid_total = jnp.sum(valid_lengths).astype(jnp.float32)
     mean_loss = 2.0 * totals[2, 0] / (valid_total * model_width)
     return (

time: 539 us -> 462 us (0.86); the launches traced: 529 us -> 461 us
  matrix products: 43.4 us -> 7.89 us
  Pallas kernels: 414 us -> 394 us
  other arithmetic: 24.2 us -> 17.7 us
    dot_general x10 -> x0, matrix products: 33 us -> none  [the longest x3 13.3 us: contract_first(): lax.dot_general(former, latter, (((0,), (0,)), ((), ())), preferred_eleme...]
    pallas_call x7 -> x5, Pallas kernels: 414 us -> 394 us  [remote_call(): pl.pallas_call(kernel, name=name, out_shape=outs, in_specs=[VMEM] * len(o...]
    convert_element_type x1, local copies, waits for them, and re-layouts: 8.63 us -> 1 us  [body(): head_outputs.transpose(1, 0, 2).reshape(length, head_count * DV)]
    another operation x5 -> x7, local copies, waits for them, and re-layouts: 0.41 us -> 6.07 us  [the longest x2 3.71 us: body(): jnp.stack([total.reshape(model_width // seq_parts, hidden_units) for tota...]
    unnamed x100 -> x41, local copies, waits for them, and re-layouts: 12.2 us -> 7.92 us
  transfers between devices with their start and end apart: 1 -> 1, of which waited for: 0 -> 0; matrix products, arithmetic and copies ran while one was open for 4% -> 6% of each run, Pallas kernels for 16% -> 18%
where the time goes in v3:
time: 462 us; the launch traced here: 461 us
  Pallas kernels  394 us (85%)
  local copies, waits for them, and re-layouts  24.2 us (5%)
  other arithmetic  17.7 us (4%)
  between operations  17.5 us (4%)
  matrix products  7.89 us (2%)
    pallas_call x5, Pallas kernels, remote_call(): pl.pallas_call(kernel, name=name, out_shape=outs, in_specs=[VMEM] * len(o...  394 us
  transfers between devices with their start and end apart: 1, of which 0 were waited for; matrix products, arithmetic and copies ran while one was open for 6% of the time, Pallas kernels for 18%

profile of v3, /device:TPU:8, one launch (start us, length us, event | category | flops | bytes accessed | tf_op | source)
XLA Modules:
  0.0 461.0 jit_solution(14922026272819202243)
XLA Ops:
  7.3 2.6 copy.51
  11.3 52.8 %gather_start.1 = (bf16[512,2048]{1,0:T(8,128)(2,1)}, bf16[4,8,64,640]{3,2,1,0:T(8,128)(2,1)}, bf16[8,64,2048]{2,1,0:T(8,128)(2,1)}, f32[4,8,8,128]{3,2,1,0:T(8,128)}) custom-call(bf16[128,2048]{1,0:T(8,128)(2,1)} %bitcast.79, bf16[4,64,640]{2,1,0:T(8,128)(2,1)} %bitcast.92, bf16[64,2048]{1,0:T(8,128)(2,1)} %out_ref.1, f32[8,128]{1,0:T(8,128)} %convert_add_fusion.1.gain_ref), custom_call_target="tpu_custom_call" | custom-call | tf_op jit(solution)/shard_map/gather_start/pallas_call | solution.py:520
  64.1 1.2 slice_reduce_fusion
  65.4 2.2 fusion
  68.2 1.3 copy-done.3
  69.5 1.8 convolution_convert_fusion.1.refs_3_
  75.5 1.4 fusion.3
  76.9 2.1 fusion.12
  80.0 2.6 convolution_convert_fusion
  82.6 32.2 %mixed_sum.1 = f32[2,64,2048]{2,1,0:T(8,128)} custom-call(bf16[4,2,64,2048]{3,2,1,0:T(8,128)(2,1)} %bitcast.86), custom_call_target="tpu_custom_call" | custom-call | tf_op jit(solution)/shard_map/mixed_sum/pallas_call | solution.py:520
  114.8 1.5 fusion.11
  116.4 1.6 copy.52
  122.6 1.2 fusion.8.refs_15_
  123.8 1.3 broadcast_divide_fusion.refs_6_
  125.2 1.3 multiply_convert_fusion
  126.5 82.4 %feed_forward.1 = (f32[128,2048]{1,0:T(8,128)}, bf16[1024,2048]{1,0:T(8,128)(2,1)}, f32[1024,704]{1,0:T(8,128)}, f32[1024,704]{1,0:T(8,128)}, bf16[1024,704]{1,0:T(8,128)(2,1)}, /*index=5*/bf16[704,2048]{1,0:T(8,128)(2,1)}) custom-call(bf16[128,2048]{1,0:T(8,128)(2,1)} %get-tuple-element.167.normed_ref, ...), custom_call_target="tpu_custom_call" | custom-call | tf_op jit(solution)/shard_map/feed_forward/pallas_call | solution.py:520
  208.9 3.6 multiply_reduce_fusion
  213.2 96.0 %feed_back.1 = (f32[128,2048]{1,0:T(8,128)}, bf16[128,2048]{1,0:T(8,128)(2,1)}, f32[8,2048]{1,0:T(8,128)}, bf16[4,2,256,704]{3,2,1,0:T(8,128)(2,1)}, bf16[4,2,25...) custom-call(f32[128,2048]{1,0:T(8,128)} %get-tuple-element.166.refs_, ...), custom_call_target="tpu_custom_call" | custom-call | tf_op jit(solution)/shard_map/feed_back/pallas_call | solution.py:520
  309.2 130.3 %mixer_back.1 = (f32[128,2048]{1,0:T(8,128)}, f32[8,512]{1,0:T(8,128)}, f32[2,256,704]{2,1,0:T(8,128)}, f32[2,256,704]{2,1,0:T(8,128)}, f32[2,352,512]{2,1,0:T(8...) custom-call(bf16[512,2048]{1,0:T(8,128)(2,1)} %bitcast.87, ...), custom_call_target="tpu_custom_call" | custom-call | tf_op jit(solution)/shard_map/mixer_back/pallas_call | solution.py:520
  441.9 2.0 copy.63
  443.9 1.9 copy.57
  445.7 1.9 copy.56
  448.3 1.9 pad_maximum_fusion
  451.9 1.1 copy.71
  (76 shorter events, 15.3 us)
Async XLA Ops:
  7.2 2.7 copy-start.12
  7.2 3.5 copy-start.15
  7.2 3.5 copy-start.16
  7.2 119.3 %all-gather.2.cloned.1.call-start = ((), (), s32[]{:S(2)}) async-start(), calls=%async_computation | async-start | bytes 7864320 | tf_op jit(solution)/shard_map/all_gather | solution.py:1721
  64.1 3.5 copy-start.1
  65.4 4.1 copy-start.5
  68.2 1.3 copy-start.3
  71.3 0.8 copy-start.4
  72.2 0.7 copy-start.17
  72.2 1.9 copy-start.14
  72.2 2.5 copy-start.13
  75.5 1.4 copy-start.6
  76.9 3.1 copy-start.7
  82.6 32.2 %copy-start.2 = (bf16[1,128,2048]{2,1,0:T(8,128)(2,1)S(1)}, bf16[1,128,2048]{2,1,0:T(8,128)(2,1)}, u32[]{:S(2)}) copy-start(bf16[1,128,2048]{2,1,0:T(8,128)(2,1)} %param.11) | copy-start | bytes 1572868
  116.4 8.8 %copy-start = (f32[2,64,2048]{2,1,0:T(8,128)S(1)}, f32[2,64,2048]{2,1,0:T(8,128)}, u32[]{:S(2)}) copy-start(f32[2,64,2048]{2,1,0:T(8,128)} %mixed_sum.1) | copy-start | bytes 3145732
  126.5 82.4 %copy-start.10 = (bf16[1,128,2048]{2,1,0:T(8,128)(2,1)S(1)}, bf16[1,128,2048]{2,1,0:T(8,128)(2,1)}, u32[]{:S(2)}) copy-start(bf16[1,128,2048]{2,1,0:T(8,128)(2,1)} %param.14) | copy-start | bytes 1572868
  448.3 1.9 copy-start.9
  448.3 2.8 copy-start.11
  450.1 1.8 copy-start.8
Sparse Core Ops, SparseCore 0:
  10.0 92.8 all-gather.1

commit v4 on v3

--- a/solution.py
+++ b/solution.py
@@ -12,7 +12,6 @@
 
 
 epsilon = 1e-05
-block_limit = 512
 
 
 def rms_norm(values, gain_vector):
@@ -39,67 +38,6 @@
 
 def gated_unit(gate_in, up_in):
     return jax.nn.silu(gate_in) * up_in
-
-
-def block_kernel(query_block, key_block, query_segments, key_segments, query_start, key_start):
-    row_width = query_segments.shape[0]
-    scaled_dots = (
-        jnp.einsum("hfq,hfk->hqk", query_block, key_block, preferred_element_type=jnp.float32)
-        * 0.25
-    )
-    query_places = query_start + jnp.arange(row_width, dtype=jnp.int32)
-    key_places = key_start + jnp.arange(row_width, dtype=jnp.int32)
-    allowed = (query_segments[:, None] == key_segments[None, :]) & (
-        query_places[:, None] >= key_places[None, :]
-    )
-    kernel = jnp.where(allowed[None], 1.0 + scaled_dots + 0.5 * scaled_dots * scaled_dots, 0.0)
-    return (scaled_dots, allowed, kernel)
-
-
-def attend_forward(queries, key_rows, values, segments, block_rows):
-    head_count, length, value_width = values.shape
-    block_count = length // block_rows
-
-    def query_step(query_index, running):
-        outputs, denominators = running
-        query_start = query_index * block_rows
-        query_block = lax.dynamic_slice_in_dim(queries, query_start, block_rows, 2)
-        query_segments = lax.dynamic_slice_in_dim(segments, query_start, block_rows, 0)
-
-        def key_step(inner_index, inner_running):
-            numerator, denominator = inner_running
-            key_start = inner_index * block_rows
-            key_block = lax.dynamic_slice_in_dim(key_rows, key_start, block_rows, 2)
-            value_block = lax.dynamic_slice_in_dim(values, key_start, block_rows, 1)
-            key_segments = lax.dynamic_slice_in_dim(segments, key_start, block_rows, 0)
-            scaled_dots, allowed, kernel = block_kernel(
-                query_block, key_block, query_segments, key_segments, query_start, key_start
-            )
-            numerator = numerator + jnp.einsum(
-                "hqk,hkd->hqd",
-                kernel.astype(jnp.bfloat16),
-                value_block,
-                preferred_element_type=jnp.float32,
-            )
-            denominator = denominator + jnp.sum(kernel, axis=2)
-            return (numerator, denominator)
-
-        starting = (
-            jnp.zeros((head_count, block_rows, value_width), jnp.float32),
-            jnp.zeros((head_count, block_rows), jnp.float32),
-        )
-        numerator, denominator = lax.fori_loop(0, query_index + 1, key_step, starting)
-        outputs = lax.dynamic_update_slice_in_dim(
-            outputs, numerator / denominator[:, :, None], query_start, 1
-        )
-        denominators = lax.dynamic_update_slice_in_dim(denominators, denominator, query_start, 1)
-        return (outputs, denominators)
-
-    initial = (
-        jnp.zeros((head_count, length, value_width), jnp.float32),
-        jnp.zeros((head_count, length), jnp.float32),
-    )
-    return lax.fori_loop(0, block_count, query_step, initial)
 
 
 MESH = pl.DeviceIdType.MESH
@@ -404,118 +342,6 @@
             self.over(z).wait_send()
 
 
-class LineSum:
-    @staticmethod
-    def scratch(wt, shape):
-        zs = wt // 2
-        return [
-            pltpu.VMEM((zs,) + shape, jnp.bfloat16),
-            pltpu.VMEM((zs,) + shape, jnp.bfloat16),
-            pltpu.VMEM((zs,) + shape, jnp.bfloat16),
-            pltpu.VMEM((zs,) + shape, jnp.bfloat16),
-            pltpu.SemaphoreType.DMA((6, zs)),
-        ]
-
-    def __init__(self, at, part, scratch):
-        self.at, self.part = at, part
-        self.pair, self.held, self.below, self.above, self.sems = scratch
-
-    def over(self, z):
-        return send(
-            self.part(z * 2 + 1 - self.at.c),
-            self.pair.at[z],
-            self.sems.at[0, z],
-            self.sems.at[1, z],
-            self.at.partner(),
-        )
-
-    def up(self, z):
-        return send(
-            self.held.at[z], self.below.at[z], self.sems.at[2, z], self.sems.at[3, z], self.at.level(self.at.z + 1)
-        )
-
-    def down(self, z):
-        return send(
-            self.held.at[z], self.above.at[z], self.sems.at[4, z], self.sems.at[5, z], self.at.level(self.at.z - 1)
-        )
-
-    def start(self):
-        zs = self.at.zs
-        for index in range(zs // 2):
-            self.over(zs - 1 - index).start()
-            self.over(index).start()
-
-    def paired(self, z):
-        self.over(z).wait_recv()
-        return [self.part(z * 2 + self.at.c), self.pair.at[z]]
-
-    def step(self, index):
-        at = self.at
-        high, low = at.zs - 1 - index, index
-
-        @pl.when(at.z < high)
-        def _():
-            terms = self.paired(high)
-
-            @pl.when(at.z == 0)
-            def _():
-                add_into(self.held.at[high], terms)
-
-            @pl.when(at.z > 0)
-            def _():
-                self.up(high).wait_recv()
-                add_into(self.held.at[high], terms + [self.below.at[high]])
-
-            self.up(high).start()
-
-        @pl.when(at.z > low)
-        def _():
-            terms = self.paired(low)
-
-            @pl.when(at.z == at.zs - 1)
-            def _():
-                add_into(self.held.at[low], terms)
-
-            @pl.when(at.z < at.zs - 1)
-            def _():
-                self.down(low).wait_recv()
-                add_into(self.held.at[low], terms + [self.above.at[low]])
-
-            self.down(low).start()
-
-    def finish(self, total):
-        at = self.at
-        terms = self.paired(at.z)
-
-        @pl.when(at.z == 0)
-        def _():
-            self.down(0).wait_recv()
-            add_into(total, terms + [self.above.at[0]])
-
-        @pl.when(at.z == at.zs - 1)
-        def _():
-            self.up(at.zs - 1).wait_recv()
-            add_into(total, terms + [self.below.at[at.zs - 1]])
-
-        @pl.when((at.z > 0) & (at.z < at.zs - 1))
-        def _():
-            self.up(at.z).wait_recv()
-            self.down(at.z).wait_recv()
-            add_into(total, terms + [self.below.at[at.z], self.above.at[at.z]])
-
-        for z in range(at.zs):
-
-            @pl.when(at.z < z)
-            def _():
-                self.up(z).wait_send()
-
-            @pl.when(at.z > z)
-            def _():
-                self.down(z).wait_send()
-
-            self.over(z).wait_send()
-
-
 def remote_call(kernel, name, number, outs, scratch, *operands, in_specs=None, out_specs=None):
     return pl.pallas_call(
         kernel,
@@ -530,16 +356,52 @@
     )(*operands)
 
 
-def gather_start(tokens, qkv_rows, out_rows, gains):
+def mixer_forward(tokens, qkv_rows, out_rows, gains, gate_up, segments, marks, taps, order):
     seq, wt = lax.axis_size("seq"), lax.axis_size("wt")
+    zs = wt // 2
     count, width = tokens.shape
-    parts, rows, columns = qkv_rows.shape
-
-    def kernel(x_ref, qkv_ref, out_ref, gain_ref, xs, qkvs, outs, gains_out, *scratch):
+    length = count * seq
+    _, qkv_rank, qkv_width = qkv_rows.shape
+    out_rank = out_rows.shape[0]
+    heads = H // seq
+    value_width = heads * DV
+    lanes_each = width // (seq * wt)
+    block, units = gate_up.shape[1:]
+    early = early_rows(block)
+    rows_at_once = 256
+    small = [
+        tokens,
+        qkv_rows,
+        out_rows,
+        gains,
+        segments.reshape(1, length),
+        segments.reshape(length, 1),
+        marks,
+        taps,
+        order,
+    ]
+
+    def kernel(*refs):
+        (x_ref, qkv_ref, out_ref, gain_ref, segment_row, segment_column, mark_ref, tap_ref, order_ref), refs = (
+            refs[:9],
+            refs[9:],
+        )
+        gate_up_ref, refs = refs[0], refs[1:]
+        (attended_out, normed_out, gain_rows), refs = refs[:3], refs[3:]
+        (qkv_out, w_out_out, hidden_out, sorted_out, mixer_out, values_out, outputs_out, gates_out), refs = (
+            refs[:8],
+            refs[8:],
+        )
+        (xs, qkvs, outs, gains_all, hidden_v, sorted_v, mixer_v, values_v, outputs_v, parts, total, room), refs = (
+            refs[:12],
+            refs[12:],
+        )
+        sum_scratch, x_sems, gate_sems, refs = refs[:8], refs[8:11], refs[11:14], refs[14:]
+        line_sems, refs = [refs[index : index + 1] for index in range(3)], refs[3:]
+        swap_q, swap_g, local, outgoing = refs
         at = Place(seq, wt)
-        x_sems, scratch = scratch[:3], scratch[3:]
-        line_sems, scratch = [scratch[index : index + 1] for index in range(3)], scratch[3:]
-        swap_q, swap_g, local = scratch
+        room_load = pltpu.make_async_copy(gate_up_ref.at[:, pl.ds(0, early)], room, local.at[4])
+        room_load.start()
         at.meet(True, True)
         half = count // 2
         gather_x = SquareGather(
@@ -549,13 +411,19 @@
             x_sems,
         )
         gather_q = LineGather(at, lambda w: qkvs.at[:, w], line_sems[0])
-        gather_g = LineGather(at, lambda w: gains_out.at[:, w], line_sems[1])
+        gather_g = LineGather(
+            at, lambda w: gains_all.at[:, pl.ds(pl.multiple_of(w * 8, 8), 8)], line_sems[1]
+        )
         gather_o = LineGather(at, lambda w: outs.at[w], line_sems[2])
+        gates = SquareGather(
+            at, lambda s, h: gates_out.at[h, s], lambda h: gate_up_ref.at[h, pl.ds(0, early)], gate_sems
+        )
+        gain_slot = pl.ds(pl.multiple_of(at.w * 8, 8), 8)
         swaps = []
         for step in range(1, seq):
             to = lax.rem(at.s + step, seq)
             swaps.append(
-                send(gain_ref, gains_out.at[at.s, at.w], swap_g.at[step, 0], swap_g.at[at.s, 1], (to, at.w))
+                send(gain_ref, gains_all.at[at.s, gain_slot], swap_g.at[step, 0], swap_g.at[at.s, 1], (to, at.w))
             )
             swaps.append(
                 send(qkv_ref.at[to], qkvs.at[at.s, at.w], swap_q.at[step, 0], swap_q.at[at.s, 1], (to, at.w))
@@ -565,7 +433,7 @@
         gather_x.start()
         own = [
             pltpu.make_async_copy(qkv_ref.at[at.s], qkvs.at[at.s, at.w], local.at[0]),
-            pltpu.make_async_copy(gain_ref, gains_out.at[at.s, at.w], local.at[1]),
+            pltpu.make_async_copy(gain_ref, gains_all.at[at.s, gain_slot], local.at[1]),
             pltpu.make_async_copy(out_ref, outs.at[at.w], local.at[2]),
             pltpu.make_async_copy(x_ref, xs.at[pl.ds(pl.multiple_of(at.s * count, count), count)], local.at[3]),
         ]
@@ -573,71 +441,210 @@
             copy.start()
         for copy in own:
             copy.wait()
+        room_load.wait()
+        room_store = pltpu.make_async_copy(room, gates_out.at[:, at.s], local.at[4])
+        room_store.start()
         for step in range(1, seq):
             s = lax.rem(at.s + step, seq)
-            slot = gains_out.at[s, at.w]
+            slot = gains_all.at[s, gain_slot]
             send(slot, slot, swap_g.at[step, 0], swap_g.at[s, 1], at.across()).wait_recv()
             slot = qkvs.at[s, at.w]
             send(slot, slot, swap_q.at[step, 0], swap_q.at[s, 1], at.across()).wait_recv()
         gather_g.start()
         gather_q.start()
-        gather_o.start()
         gather_x.relay()
-        for index in range(at.zs - 1):
+        gates.start()
+        for index in range(zs - 1):
             gather_g.step(index)
             gather_q.step(index)
+        gather_o.start()
+        gather_g.finish()
+
+        device_rows = gains_all[...].reshape(seq * wt * 8, 128).astype(jnp.bfloat16)
+        gain_rows[...] = jnp.zeros_like(gain_rows)
+
+        def spread_gains(index, carry):
+            begin = pl.multiple_of(index * 256, 256)
+            lane = lax.broadcasted_iota(jnp.int32, (128, 256), 0)
+            column = begin + lax.broadcasted_iota(jnp.int32, (128, 256), 1)
+            copied = jnp.dot(
+                device_rows,
+                (lane == lax.rem(column, lanes_each)).astype(jnp.float32).astype(jnp.bfloat16),
+                preferred_element_type=jnp.float32,
+            )
+            row = lax.broadcasted_iota(jnp.int32, copied.shape, 0)
+            column = begin + lax.broadcasted_iota(jnp.int32, copied.shape, 1)
+            first_row = lax.div(column, lanes_each) * 8
+            for number in range(2):
+                gain_rows[number : number + 1, pl.ds(begin, 256)] = jnp.sum(
+                    jnp.where(row == first_row + number, copied, 0.0), axis=0, keepdims=True
+                )
+            return carry
+
+        lax.fori_loop(0, width // 256, spread_gains, 0)
+        gather_x.finish()
+
+        def norm_rows(index, carry):
+            window = pl.ds(pl.multiple_of(index * 32, 32), 32)
+            hidden_v[window, :] = rms_norm(xs[window, :].astype(jnp.float32), gain_rows[0:1, :]).astype(
+                jnp.bfloat16
+            )
+            return carry
+
+        lax.fori_loop(0, length // 32, norm_rows, 0)
+        gather_q.finish()
+        projected = jnp.dot(
+            hidden_v[...], qkvs[...].reshape(width, qkv_width), preferred_element_type=jnp.float32
+        ).astype(jnp.bfloat16)
+        sorted_v[...] = jnp.dot(projected, order_ref[...], preferred_element_type=jnp.float32).astype(
+            jnp.bfloat16
+        )
+        stores = [
+            pltpu.make_async_copy(source, target, outgoing.at[index])
+            for index, (source, target) in enumerate(
+                (
+                    (qkvs, qkv_out),
+                    (hidden_v, hidden_out),
+                    (sorted_v, sorted_out),
+                    (values_v, values_out),
+                    (outputs_v, outputs_out),
+                    (mixer_v, mixer_out),
+                    (outs, w_out_out),
+                )
+            )
+        ]
+        for copy in stores[:3]:
+            copy.start()
+
+        def convolve(head, carry):
+            columns = pl.ds(pl.multiple_of(head * DV, DV), DV)
+            raw = sorted_v[:, columns].astype(jnp.float32)
+            mixed = tap_ref[0:1, columns] * raw
+            for tap in range(1, KCONV):
+                mixed = mixed + tap_ref[tap : tap + 1, columns] * pltpu.roll(raw, tap, 0) * mark_ref[:, tap : tap + 1]
+            values_v[head] = mixed.astype(jnp.bfloat16)
+            return carry
+
+        lax.fori_loop(0, heads, convolve, 0)
+        stores[3].start()
+        gates.relay()
+        steps = length // rows_at_once
+        lanes = lax.broadcasted_iota(jnp.int32, (1, 128), 1)
+
+        def attend(index, carry):
+            head, start = lax.div(index, steps), lax.rem(index, steps) * rows_at_once
+            rows = pl.ds(pl.multiple_of(start, rows_at_once), rows_at_once)
+            mine = ((lanes >= head * FEAT) & (lanes < head * FEAT + FEAT)).astype(jnp.float32)
+            queries = sorted_v[rows, value_width : value_width + 128] * mine.astype(jnp.bfloat16)
+            scores = contract_last(queries, sorted_v[:, value_width + 128 :]) * 0.25
+            places = start + lax.broadcasted_iota(jnp.int32, scores.shape, 0)
+            allowed = (segment_column[rows, :] == segment_row[...]) & (
+                places >= lax.broadcasted_iota(jnp.int32, scores.shape, 1)
+            )
+            kernel_values = jnp.where(allowed, 1.0 + scores + 0.5 * scores * scores, 0.0)
+            denominator = jnp.sum(kernel_values, axis=1, keepdims=True)
+            mixed = (
+                jnp.dot(kernel_values.astype(jnp.bfloat16), values_v[head], preferred_element_type=jnp.float32)
+                / denominator
+            )
+            outputs_v[head, rows, :] = mixed
+            mixer_v[rows, pl.ds(pl.multiple_of(head * DV, DV), DV)] = mixed.astype(jnp.bfloat16)
+            return carry
+
+        turns = heads * steps
+        for index in range(zs - 1):
+            lax.fori_loop(turns * index // (zs - 1), turns * (index + 1) // (zs - 1), attend, 0)
             gather_o.step(index)
-        gather_x.finish()
-        gather_g.finish()
-        gather_q.finish()
         gather_o.finish()
+        for copy in stores[4:]:
+            copy.start()
+
+        def out_job(index, carry):
+            window = pl.ds(pl.multiple_of(index * 512, 512), 512)
+            term = jnp.dot(
+                mixer_v[...], outs[:, :, window].reshape(value_width, 512), preferred_element_type=jnp.float32
+            ).astype(jnp.bfloat16)
+            for s in range(seq):
+                for h in range(2):
+                    begin = s * count + h * half
+                    parts[s, h, :, window] = term[begin : begin + half]
+            return carry
+
+        lax.fori_loop(0, width // 512, out_job, 0)
+        work = SquareSum(at, lambda s, h: parts.at[s, h], sum_scratch)
+        work.start()
+        work.relay()
+        work.finish(lambda h: total.at[h])
+
+        def finish_rows(index, carry):
+            for h in range(2):
+                window = pl.ds(pl.multiple_of(index * 16, 16), 16)
+                rows = pl.ds(pl.multiple_of(h * half + index * 16, 16), 16)
+                attended = x_ref[rows, :].astype(jnp.float32) + total[h, window, :]
+                attended_out[rows, :] = attended
+                normed_out[rows, :] = rms_norm(attended, gain_rows[1:2, :]).astype(jnp.bfloat16)
+            return carry
+
+        lax.fori_loop(0, half // 16, finish_rows, 0)
+        gates.finish()
+        room_store.wait()
         for copy in swaps:
             copy.wait_send()
-
+        for copy in stores:
+            copy.wait()
+
+    low, f32 = jnp.bfloat16, jnp.float32
+    sorted_width = value_width + 256
     return remote_call(
         kernel,
-        "gather_start",
+        "mixer_forward",
         0,
         [
-            jax.ShapeDtypeStruct((seq * count, width), tokens.dtype),
-            jax.ShapeDtypeStruct((seq, wt, rows, columns), qkv_rows.dtype),
-            jax.ShapeDtypeStruct((wt,) + out_rows.shape, out_rows.dtype),
-            jax.ShapeDtypeStruct((seq, wt) + gains.shape, gains.dtype),
+            jax.ShapeDtypeStruct((count, width), f32),
+            jax.ShapeDtypeStruct((count, width), low),
+            jax.ShapeDtypeStruct((8, width), f32),
+            jax.ShapeDtypeStruct((seq, wt, qkv_rank, qkv_width), low),
+            jax.ShapeDtypeStruct((wt, out_rank, width), low),
+            jax.ShapeDtypeStruct((length, width), low),
+            jax.ShapeDtypeStruct((length, sorted_width), low),
+            jax.ShapeDtypeStruct((length, value_width), low),
+            jax.ShapeDtypeStruct((heads, length, DV), low),
+            jax.ShapeDtypeStruct((heads, length, DV), f32),
+            jax.ShapeDtypeStruct((2, seq, early, units), low),
         ],
-        SquareGather.semaphores(seq)
+        [
+            pltpu.VMEM((length, width), low),
+            pltpu.VMEM((seq, wt, qkv_rank, qkv_width), low),
+            pltpu.VMEM((wt, out_rank, width), low),
+            pltpu.VMEM((seq, wt * 8, 128), f32),
+            pltpu.VMEM((length, width), low),
+            pltpu.VMEM((length, sorted_width), low),
+            pltpu.VMEM((length, value_width), low),
+            pltpu.VMEM((heads, length, DV), low),
+            pltpu.VMEM((heads, length, DV), f32),
+            pltpu.VMEM((seq, 2, count // 2, width), low),
+            pltpu.VMEM((2, count // 2, width), f32),
+            pltpu.VMEM((2, early, units), low),
+        ]
+        + SquareSum.scratch(seq, (count // 2, width))
+        + SquareGather.semaphores(seq)
+        + SquareGather.semaphores(seq)
         + LineGather.semaphores(wt) * 3
         + [
             pltpu.SemaphoreType.DMA((seq, 2)),
             pltpu.SemaphoreType.DMA((seq, 2)),
-            pltpu.SemaphoreType.DMA((4,)),
+            pltpu.SemaphoreType.DMA((5,)),
+            pltpu.SemaphoreType.DMA((7,)),
         ],
-        tokens,
-        qkv_rows,
-        out_rows,
-        gains,
+        *small,
+        gate_up,
+        in_specs=[VMEM] * len(small) + [ANY],
+        out_specs=[VMEM] * 3 + [ANY] * 8,
     )
 
 
-def square_sum(parts, name, number):
-    seq, wt = lax.axis_size("seq"), lax.axis_size("wt")
-    half_shape = parts.shape[2:]
-
-    def kernel(parts_ref, total_ref, *scratch):
-        at = Place(seq, wt)
-        at.meet(True, False)
-        work = SquareSum(at, lambda s, h: parts_ref.at[s, h], scratch)
-        work.start()
-        work.relay()
-        work.finish(lambda h: total_ref.at[h])
-
-    return remote_call(
-        kernel,
-        name,
-        number,
-        jax.ShapeDtypeStruct((2,) + half_shape, jnp.float32),
-        SquareSum.scratch(seq, half_shape),
-        parts,
-    )
+def early_rows(block):
+    return block // 4 * 3
 
 
 class LinePieces:
@@ -650,9 +657,11 @@
         self.at, self.part = at, part
         self.pair, self.below, self.above, self.sems = scratch
         self.pieces = self.sems.shape[2]
-        self.width = self.pair.shape[2] // self.pieces
+        self.width = self.pair.shape[-1] // self.pieces
 
     def cut(self, ref, piece):
+        if len(ref.shape) == 3:
+            return ref.at[piece]
         return ref.at[:, pl.ds(pl.multiple_of(piece * self.width, self.width), self.width)]
 
     def own(self, z, piece):
@@ -702,36 +711,54 @@
             add_into(self.own(z, piece), self.terms(z, piece))
             self.down(z, piece).start()
 
-    def pass_on(self, fill=None):
+    def begin(self):
+        zs = self.at.zs
+
+        def pairs(piece, carry):
+            for index in range(zs // 2):
+                self.over(index, piece).start()
+                self.over(zs - 1 - index, piece).start()
+            return carry
+
+        lax.fori_loop(0, self.pieces, pairs, 0)
+
+        def starts(index, carry):
+            piece = lax.rem(index, self.pieces)
+            far = zs - 1 - lax.div(index, self.pieces)
+            self.ends(jnp.where(self.at.z == 0, far, zs - 1 - far), piece)
+            return carry
+
+        lax.fori_loop(0, (zs - 1) * self.pieces, starts, 0)
+
+    def pass_on(self, index, fill=None):
         at = self.at
         upper = at.z * 2 >= at.zs
-        for index in range(1, at.zs):
-            high, low = index, at.zs - 1 - index
-
-            def lower(piece, when):
-                @pl.when((at.z > low) & (at.z < at.zs - 1) & when)
-                def _():
-                    terms = self.terms(low, piece)
-                    self.down(low, piece).wait_recv()
-                    add_into(self.own(low, piece), terms + [self.cut(self.above.at[low], piece)])
-                    self.down(low, piece).start()
-
-            def step(piece, carry):
-                lower(piece, upper)
-
-                @pl.when((at.z < high) & (at.z > 0))
-                def _():
-                    terms = self.terms(high, piece)
-                    self.up(high, piece).wait_recv()
-                    add_into(self.own(high, piece), terms + [self.cut(self.below.at[high], piece)])
-                    self.up(high, piece).start()
-
-                lower(piece, jnp.logical_not(upper))
-                if fill is not None and index == at.zs - 1:
-                    fill(piece)
-                return carry
-
-            lax.fori_loop(0, self.pieces, step, 0)
+        high, low = index, at.zs - 1 - index
+
+        def lower(piece, when):
+            @pl.when((at.z > low) & (at.z < at.zs - 1) & when)
+            def _():
+                terms = self.terms(low, piece)
+                self.down(low, piece).wait_recv()
+                add_into(self.own(low, piece), terms + [self.cut(self.above.at[low], piece)])
+                self.down(low, piece).start()
+
+        def step(piece, carry):
+            lower(piece, upper)
+
+            @pl.when((at.z < high) & (at.z > 0))
+            def _():
+                terms = self.terms(high, piece)
+                self.up(high, piece).wait_recv()
+                add_into(self.own(high, piece), terms + [self.cut(self.below.at[high], piece)])
+                self.up(high, piece).start()
+
+            lower(piece, jnp.logical_not(upper))
+            if fill is not None:
+                fill(piece)
+            return carry
+
+        lax.fori_loop(0, self.pieces, step, 0)
 
     def finish(self, total, fill=None):
         at = self.at
@@ -784,18 +811,17 @@
         ys = seq // 2
         return [
             pltpu.VMEM((ys,) + half_shape, jnp.bfloat16),
-            pltpu.VMEM((ys,) + half_shape, jnp.bfloat16),
-            pltpu.VMEM(half_shape, jnp.bfloat16),
             pltpu.VMEM(half_shape, jnp.bfloat16),
             pltpu.SemaphoreType.DMA((ys + 1, 2)),
         ]
 
-    def __init__(self, at, terms, from_x, from_y, sems=None, scratch=None):
+    def __init__(self, at, terms, from_x, from_y, sems=None, lasts=None, scratch=None):
         self.at, self.terms, self.from_x, self.from_y = at, terms, from_x, from_y
         if sems is not None:
             self.xs, self.ys = sems
         if scratch is not None:
-            self.sum_y, self.last_y, self.sum_x, self.last_x, self.last = scratch
+            self.last_y, self.last_x = lasts
+            self.sum_y, self.sum_x, self.last = scratch
 
     def first_x(self, y):
         at = self.at
@@ -832,18 +858,16 @@
                 slot = self.from_y.at[y, x]
                 send(slot, slot, self.ys.at[step, x, 0], self.ys.at[y, x, 1], at.across()).wait_recv()
 
-    def second_sends(self):
+    def second_y(self, step):
         at = self.at
-        copies = []
-        for step in range(1, at.ys):
-            y = at.beside(step)
-            copies.append(
-                send(self.sum_y.at[y], self.last_y.at[at.y], self.last.at[step, 0], self.last.at[at.y, 1], at.column(y))
-            )
-        copies.append(
-            send(self.sum_x, self.last_x, self.last.at[at.ys, 0], self.last.at[at.ys, 1], at.across())
-        )
-        return copies
+        y = at.beside(step)
+        return send(
+            self.sum_y.at[y], self.last_y.at[at.y], self.last.at[step, 0], self.last.at[at.y, 1], at.column(y)
+        )
+
+    def second_x(self):
+        at = self.at
+        return send(self.sum_x, self.last_x, self.last.at[at.ys, 0], self.last.at[at.ys, 1], at.across())
 
     def second_start(self, fetch, rooms):
         at = self.at
@@ -858,27 +882,18 @@
             add_into(self.sum_x, [self.sum_x, rooms[0]])
 
     def second_go(self):
-        for copy in self.second_sends():
-            copy.start()
-
-    def finish(self, fetch, rooms, total):
+        for step in range(1, self.at.ys):
+            self.second_y(step).start()
+        self.second_x().start()
+
+    def second_wait(self):
         at = self.at
-        fetch([(self.terms(at.s, 0), rooms[0]), (self.from_x.at[at.y], rooms[1])])
-        terms = [rooms[0], rooms[1]]
         for step in range(1, at.ys):
+            self.second_y(step).wait_send()
             y = at.beside(step)
             slot = self.last_y.at[y]
             send(slot, slot, self.last.at[step, 0], self.last.at[y, 1], at.across()).wait_recv()
-            terms.append(slot)
-        add_into(total(0), terms)
-        fetch([(self.terms(at.s, 1), rooms[0])])
-        self.second_sends()[-1].wait_recv()
-        add_into(total(1), [rooms[0], self.last_x])
-        for step in range(1, at.ys):
-            fetch([(self.from_y.at[at.beside(step), at.x], rooms[0])])
-            add_into(total(1), [total(1), rooms[0]])
-        for copy in self.second_sends():
-            copy.wait_send()
+        self.second_x().wait()
 
 
 def norm_back(rows, load, store, gain, terms):
@@ -953,7 +968,8 @@
         return carry
 
     lax.fori_loop(0, last + 1 + late, turn, 0)
-    sums.pass_on(fill)
+    for index in range(2, at.zs):
+        sums.pass_on(index, fill if index == at.zs - 1 else None)
     sums.finish(total, fill)
     gather.sent()
 
@@ -961,28 +977,51 @@
 PIECES = 4
 
 
-def feed_forward(normed, gate_up, down_shard):
+def feed_forward(normed, attended, teacher, keep, gate_early, gate_up_shard, down_shard):
     seq, wt = lax.axis_size("seq"), lax.axis_size("wt")
     count, width = normed.shape
-    units = gate_up.shape[2]
+    block, units = gate_up_shard.shape[1:]
+    early = early_rows(block)
     columns = down_shard.shape[1]
     tokens = wt * count
     zs = wt // 2
     half = units // 2
 
-    def kernel(normed_ref, gate_up_ref, shard_ref, total_ref, normed_out, gate_out, up_out, active_out, down_out, *scratch):
+    def kernel(*refs):
+        (normed_ref, attended_ref, teacher_ref, keep_ref, early_ref, gate_shard_ref, shard_ref), refs = refs[:7], refs[7:]
+        (final_out, error_out, energy_out), refs = refs[:3], refs[3:]
+        (normed_out, gate_out, up_out, active_out, down_out, gates_out), refs = refs[:6], refs[6:]
+        (everyone, gates, downs, gate_all, up_all, active_all, parts, total), refs = refs[:8], refs[8:]
+        gather_sems, sum_scratch, late_sems, square_sems, (local, outgoing) = (
+            refs[:1],
+            refs[1:5],
+            refs[5:8],
+            refs[8:11],
+            refs[11:],
+        )
         at = Place(seq, wt)
-        everyone, gates, downs, gate_all, up_all, active_all, parts = scratch[:7]
-        gather_sems, sum_scratch, square_sems, local, outgoing = (
-            scratch[7:8],
-            scratch[8:12],
-            scratch[12:15],
-            scratch[15],
-            scratch[16],
-        )
-        load = pltpu.make_async_copy(gate_up_ref, gates, local.at[0])
-        load.start()
+        loads = [
+            pltpu.make_async_copy(
+                early_ref.at[:, s], gates.at[:, pl.ds(s * block, early)], local.at[4 + s]
+            )
+            for s in range(seq)
+        ]
+        loads.append(
+            pltpu.make_async_copy(
+                gate_shard_ref.at[:, pl.ds(early, block - early)],
+                gates.at[:, pl.ds(pl.multiple_of(at.s * block + early, 16), block - early)],
+                local.at[0],
+            )
+        )
+        for load in loads:
+            load.start()
         at.meet(True, True)
+        late = SquareGather(
+            at,
+            lambda s, h: gates.at[h, pl.ds(pl.multiple_of(s * block + early, 16), block - early)],
+            lambda h: gate_shard_ref.at[h, pl.ds(early, block - early)],
+            late_sems,
+        )
         weights = SquareGather(
             at,
             lambda s, h: downs.at[
@@ -995,15 +1034,21 @@
             at, lambda w: parts.at[pl.ds(pl.multiple_of(w * count, count), count)], sum_scratch
         )
         down_store = pltpu.make_async_copy(downs, down_out, local.at[2])
+        gates_store = pltpu.make_async_copy(gates, gates_out, local.at[0])
 
         def ready_first():
-            weights.start()
+            late.start()
             own = pltpu.make_async_copy(
                 shard_ref, downs.at[:, pl.ds(pl.multiple_of(at.s * columns, columns), columns)], local.at[3]
             )
             own.start()
+            late.relay()
+            weights.start()
             own.wait()
-            load.wait()
+            for load in loads:
+                load.wait()
+            late.finish()
+            gates_store.start()
 
         def ready_later():
             weights.relay()
@@ -1046,45 +1091,69 @@
             sums,
             first,
             second,
-            total_ref,
+            total,
             (ready_first, ready_later),
             True,
         )
+        energy_out[...] = jnp.zeros_like(energy_out)
+
+        def finish_rows(index, carry):
+            window = pl.ds(pl.multiple_of(index * 16, 16), 16)
+            final = attended_ref[window, :] + total[window, :]
+            final_out[window, :] = final.astype(jnp.bfloat16)
+            error = (final - teacher_ref[window, :].astype(jnp.float32)) * keep_ref[window, :]
+            error_out[window, :] = error
+            squares = error * error
+            energy_out[...] += 0.5 * (squares[:8] + squares[8:])
+            return carry
+
+        lax.fori_loop(0, count // 16, finish_rows, 0)
         down_store.wait()
+        gates_store.wait()
         for z in range(zs):
             for copy in stores(z):
                 copy.wait()
 
+    low, f32 = jnp.bfloat16, jnp.float32
     return remote_call(
         kernel,
         "feed_forward",
         2,
         [
-            jax.ShapeDtypeStruct((count, width), jnp.float32),
-            jax.ShapeDtypeStruct((tokens, width), jnp.bfloat16),
-            jax.ShapeDtypeStruct((tokens, units), jnp.float32),
-            jax.ShapeDtypeStruct((tokens, units), jnp.float32),
-            jax.ShapeDtypeStruct((tokens, units), jnp.bfloat16),
-            jax.ShapeDtypeStruct((units, width), jnp.bfloat16),
+            jax.ShapeDtypeStruct((count, width), low),
+            jax.ShapeDtypeStruct((count, width), f32),
+            jax.ShapeDtypeStruct((8, width), f32),
+            jax.ShapeDtypeStruct((tokens, width), low),
+            jax.ShapeDtypeStruct((tokens, units), f32),
+            jax.ShapeDtypeStruct((tokens, units), f32),
+            jax.ShapeDtypeStruct((tokens, units), low),
+            jax.ShapeDtypeStruct((units, width), low),
+            jax.ShapeDtypeStruct((2, width, units), low),
         ],
         [
-            pltpu.VMEM((tokens, width), jnp.bfloat16),
-            pltpu.VMEM(gate_up.shape, jnp.bfloat16),
-            pltpu.VMEM((units, width), jnp.bfloat16),
-            pltpu.VMEM((tokens, units), jnp.float32),
-            pltpu.VMEM((tokens, units), jnp.float32),
-            pltpu.VMEM((tokens, units), jnp.bfloat16),
-            pltpu.VMEM((tokens, width), jnp.bfloat16),
+            pltpu.VMEM((tokens, width), low),
+            pltpu.VMEM((2, width, units), low),
+            pltpu.VMEM((units, width), low),
+            pltpu.VMEM((tokens, units), f32),
+            pltpu.VMEM((tokens, units), f32),
+            pltpu.VMEM((tokens, units), low),
+            pltpu.VMEM((tokens, width), low),
+            pltpu.VMEM((count, width), f32),
         ]
         + LineGather.semaphores(wt)
         + LinePieces.scratch(wt, (count, width), PIECES)
         + SquareGather.semaphores(seq)
-        + [pltpu.SemaphoreType.DMA((4,)), pltpu.SemaphoreType.DMA((4, zs))],
+        + SquareGather.semaphores(seq)
+        + [pltpu.SemaphoreType.DMA((4 + seq,)), pltpu.SemaphoreType.DMA((4, zs))],
         normed,
-        gate_up,
+        attended,
+        teacher,
+        keep,
+        gate_early,
+        gate_up_shard,
         down_shard,
-        in_specs=[VMEM, ANY, VMEM],
-        out_specs=[VMEM] + [ANY] * 5,
+        in_specs=[VMEM] * 4 + [ANY] * 2 + [VMEM],
+        out_specs=[VMEM] * 3 + [ANY] * 6,
     )
 
 
@@ -1256,7 +1325,7 @@
             grad_ref[window, :] = value
             mix_ref[window, :] = value.astype(jnp.bfloat16)
 
-        norm_back(count, load_rows, store_rows, gain_ref[...], gain_terms)
+        norm_back(count, load_rows, store_rows, gain_ref[1:2, :], gain_terms)
         for copy in stores:
             copy.wait()
         gate_sum.first_wait()
@@ -1328,7 +1397,7 @@
     out_rows,
     qkv_columns,
     hidden,
-    projected,
+    sorted_columns,
     mixer,
     mixed_values,
     head_outputs,
@@ -1354,7 +1423,7 @@
     rows_at_once = 256
     segment_rows = segments.reshape(1, length)
     segment_columns = segments.reshape(length, 1)
-    big = [out_rows, qkv_columns, hidden, projected, mixer, mixed_values, head_outputs]
+    big = [out_rows, qkv_columns, hidden, sorted_columns, mixer, mixed_values, head_outputs]
     small = [mix_back, attended_grad, tokens, gain, segment_rows, segment_columns, marks, taps, order, gain_terms, energy]
     far = list(gate_parts) + list(down_parts) + list(up_parts)
 
@@ -1362,14 +1431,15 @@
         big_refs, refs = refs[: len(big)], refs[len(big) :]
         small_refs, refs = refs[: len(small)], refs[len(small) :]
         (gate_t, gate_x, gate_y, down_t, down_x, down_y, up_t), refs = refs[: len(far)], refs[len(far) :]
-        (grad_out, sums_out, gate_out, up_out, down_out, qkv_out, w_out_out, up_x, up_y), refs = refs[:9], refs[9:]
-        (w_out_v, w_qkv_v, hidden_v, projected_v, mixer_v, values_v, outputs_v), refs = refs[:7], refs[7:]
-        (mix_all, mixer_grad, sorted_v, query_acc, key_acc, value_acc, back_sorted, back_v), refs = refs[:8], refs[8:]
+        (grad_out, sums_out, qkv_out, w_out_out, up_x, up_y), refs = refs[:6], refs[6:]
+        gate_lasts, up_lasts, down_lasts, refs = refs[:2], refs[2:4], refs[4:6], refs[6:]
+        (w_out_v, w_qkv_v, hidden_v, sorted_v, mixer_v, values_v, outputs_v), refs = refs[:7], refs[7:]
+        (mix_all, mixer_grad, query_acc, key_acc, value_acc, back_sorted, back_v), refs = refs[:7], refs[7:]
         (hidden_parts, qkv_parts, out_parts, hidden_total, gain_acc, spread, taps_acc), refs = refs[:7], refs[7:]
         (room_gate0, room_gate1, room_down0, room_down1, qkv_sum, first, middle, last), refs = refs[:8], refs[8:]
         hidden_scratch, refs = refs[:8], refs[8:]
-        qkv_scratch, out_scratch, refs = refs[:5], refs[5:10], refs[10:]
-        gate_scratch, down_scratch, up_scratch, refs = refs[:5], refs[5:10], refs[10:15], refs[15:]
+        qkv_scratch, out_scratch, refs = refs[:4], refs[4:8], refs[8:]
+        gate_scratch, down_scratch, up_scratch, refs = refs[:3], refs[3:6], refs[6:9], refs[9:]
         gather_sems, up_sems, refs = refs[:3], refs[3:5], refs[5:]
         local, swap, first_sems, last_sems = refs
         (
@@ -1389,7 +1459,7 @@
         loads = [
             pltpu.make_async_copy(source, target, local.at[4 + index])
             for index, (source, target) in enumerate(
-                zip(big_refs, (w_out_v, w_qkv_v, hidden_v, projected_v, mixer_v, values_v, outputs_v))
+                zip(big_refs, (w_out_v, w_qkv_v, hidden_v, sorted_v, mixer_v, values_v, outputs_v))
             )
         ]
         for load in loads:
@@ -1418,18 +1488,15 @@
             for copy in copies:
                 copy.wait()
 
-        gate_sum = SquareTerms(at, lambda s, h: gate_t.at[s, h], gate_x, gate_y, None, gate_scratch)
-        down_sum = SquareTerms(at, lambda s, h: down_t.at[s, h], down_x, down_y, None, down_scratch)
-        up_sum = SquareTerms(at, lambda s, h: up_t.at[s, h], up_x, up_y, up_sems, up_scratch)
+        gate_sum = SquareTerms(at, lambda s, h: gate_t.at[s, h], gate_x, gate_y, None, gate_lasts, gate_scratch)
+        down_sum = SquareTerms(at, lambda s, h: down_t.at[s, h], down_x, down_y, None, down_lasts, down_scratch)
+        up_sum = SquareTerms(at, lambda s, h: up_t.at[s, h], up_x, up_y, up_sems, up_lasts, up_scratch)
         gate_rooms, down_rooms = (room_gate0, room_gate1), (room_down0, room_down1)
         gate_sum.second_start(fetch, gate_rooms)
         down_sum.second_start(fetch, down_rooms)
         own.wait()
         for load in loads:
             load.wait()
-        sorted_v[...] = jnp.dot(
-            projected_v[...], order_ref[...], preferred_element_type=jnp.float32
-        ).astype(jnp.bfloat16)
         query_acc[...] = jnp.zeros_like(query_acc)
         key_acc[...] = jnp.zeros_like(key_acc)
         value_acc[...] = jnp.zeros_like(value_acc)
@@ -1437,9 +1504,8 @@
         gather.finish()
         gate_sum.second_go()
         down_sum.second_go()
-        up_sum.first_start()
         mixer_grad[...] = contract_last(mix_all[...], w_out_v[...]).astype(jnp.bfloat16)
-        out_sum = LineSum(at, lambda w: out_parts.at[w], out_scratch)
+        out_sum = LinePieces(at, lambda w: out_parts.at[w], out_scratch)
         out_rank = out_parts.shape[1]
         out_block = 512 if value_width % 512 == 0 else value_width
 
@@ -1451,7 +1517,7 @@
             return carry
 
         lax.fori_loop(0, width // 512, out_job, 0)
-        out_sum.start()
+        out_sum.begin()
 
         steps = length // rows_at_once
         lanes = lax.broadcasted_iota(jnp.int32, (1, 128), 1)
@@ -1483,7 +1549,12 @@
             value_acc[:, columns] += contract_first(kernel_values.astype(jnp.bfloat16), numerator_back)
             return carry
 
-        lax.fori_loop(0, heads * steps, attend, 0)
+        middle_step = heads * steps // 2
+        lax.fori_loop(0, middle_step, attend, 0)
+        for index in range(zs - 1, 1, -1):
+            if index == zs // 2:
+                lax.fori_loop(middle_step, heads * steps, attend, 0)
+            out_sum.pass_on(index)
         taps_acc[...] = jnp.zeros_like(taps_acc)
 
         def convolve(head, carry):
@@ -1518,7 +1589,7 @@
 
         lax.fori_loop(0, width // 512, hidden_job, 0)
         hidden_sum.start()
-        qkv_sums = LineSum(at, lambda w: qkv_parts.at[:, w], qkv_scratch)
+        qkv_sums = LinePieces(at, lambda w: qkv_parts.at[:, w], qkv_scratch)
         qkv_rank = qkv_parts.shape[2]
 
         def qkv_job(s, carry):
@@ -1530,14 +1601,12 @@
             return carry
 
         lax.fori_loop(0, seq, qkv_job, 0)
-        qkv_sums.start()
+        qkv_sums.begin()
+        qkv_sums.pass_on(zs - 1)
         hidden_sum.relay()
-        for index in range(zs - 1):
-            out_sum.step(index)
-            qkv_sums.step(index)
-        up_sum.first_wait()
-        up_sum.second_start(fetch, gate_rooms)
-        up_sum.second_go()
+        up_sum.first_start()
+        for index in range(zs - 2, 1, -1):
+            qkv_sums.pass_on(index)
         hidden_sum.finish(lambda h: hidden_total.at[h])
         gain_acc[...] = jnp.zeros_like(gain_acc)
         for h in range(2):
@@ -1552,11 +1621,12 @@
             def store_rows(window, value):
                 grad_out[shift(window), :] = value
 
-            norm_back(half, load_rows, store_rows, gain_ref[...], gain_acc)
+            norm_back(half, load_rows, store_rows, gain_ref[0:1, :], gain_acc)
         spread[...] = jnp.zeros_like(spread)
         spread[0:1, :] = jnp.sum(gain_acc[...], axis=0, keepdims=True)
         spread[1:2, :] = jnp.sum(gain_two[...], axis=0, keepdims=True)
-        spread[2:3, :] = jnp.broadcast_to(energy_ref[...], (1, width))
+        energy = jnp.sum(jnp.sum(energy_ref[...], axis=0, keepdims=True), axis=1, keepdims=True)
+        spread[2:3, :] = jnp.broadcast_to(energy, (1, width))
         copies = []
         for step in range(1, seq):
             to = lax.rem(at.s + step, seq)
@@ -1586,8 +1656,11 @@
             copy = send(middle, last.at[at.w], last_sems.at[step, 0], last_sems.at[at.w, 1], (at.s, to))
             copy.start()
             copies.append(copy)
-        gate_sum.finish(fetch, gate_rooms, lambda h: gate_out.at[h])
-        down_sum.finish(fetch, down_rooms, lambda h: down_out.at[h])
+        up_sum.first_wait()
+        up_sum.second_start(fetch, gate_rooms)
+        up_sum.second_go()
+        gate_sum.second_wait()
+        down_sum.second_wait()
         terms = [middle]
         for step in range(1, wt):
             w = lax.rem(at.w + step, wt)
@@ -1599,7 +1672,7 @@
             s = lax.rem(at.s + step, seq)
             slot = qkv_out.at[s]
             send(slot, slot, swap.at[step, 0], swap.at[s, 1], at.across()).wait_recv()
-        up_sum.finish(fetch, gate_rooms, lambda h: up_out.at[h])
+        up_sum.second_wait()
         for copy in copies:
             copy.wait_send()
 
@@ -1613,19 +1686,20 @@
         [
             jax.ShapeDtypeStruct((count, width), f32),
             jax.ShapeDtypeStruct(tile, f32),
-            jax.ShapeDtypeStruct((2,) + gate_half, f32),
-            jax.ShapeDtypeStruct((2,) + gate_half, f32),
-            jax.ShapeDtypeStruct((2,) + down_half, f32),
             jax.ShapeDtypeStruct((seq, qkv_rank, qkv_width), f32),
             jax.ShapeDtypeStruct((out_rank, width), f32),
             jax.ShapeDtypeStruct((ys,) + gate_half, low),
             jax.ShapeDtypeStruct((ys, 2) + gate_half, low),
+        ]
+        + [
+            jax.ShapeDtypeStruct(shape, low)
+            for shape_half in (gate_half, gate_half, down_half)
+            for shape in ((ys,) + shape_half, shape_half)
         ],
         [pltpu.VMEM(array.shape, array.dtype) for array in big]
         + [
             pltpu.VMEM((length, width), low),
             pltpu.VMEM((length, value_width), low),
-            pltpu.VMEM((length, value_width + 256), low),
             pltpu.VMEM((length, 128), f32),
             pltpu.VMEM((length, 128), f32),
             pltpu.VMEM((length, value_width), f32),
@@ -1648,8 +1722,8 @@
             pltpu.VMEM((wt,) + tile, f32),
         ]
         + SquareSum.scratch(seq, (count // 2, width))
-        + LineSum.scratch(wt, (seq, qkv_rank, qkv_width))
-        + LineSum.scratch(wt, (out_rank, width))
+        + LinePieces.scratch(wt, (seq, qkv_rank, qkv_width), seq)
+        + LinePieces.scratch(wt, (out_rank, width), PIECES)
         + SquareTerms.scratch(seq, gate_half)
         + SquareTerms.scratch(seq, down_half)
         + SquareTerms.scratch(seq, gate_half)
@@ -1665,9 +1739,13 @@
         *small,
         *far,
         in_specs=[ANY] * len(big) + [VMEM] * len(small) + [ANY] * len(far),
-        out_specs=[VMEM] * 7 + [ANY] * 2,
+        out_specs=[VMEM] * 4 + [ANY] * 8,
     )
-    return results[:7]
+    grad, totals, qkv_total, out_total, up_x, up_y = results[:6]
+    gate = tuple(gate_parts) + tuple(results[6:8])
+    up = tuple(up_parts) + (up_x, up_y) + tuple(results[8:10])
+    down = tuple(down_parts) + tuple(results[10:12])
+    return grad, totals, gate, up, down, qkv_total, out_total
 
 
 def column_order(heads):
@@ -1683,9 +1761,115 @@
     return (target[:, None] == jnp.arange(value_width + 256)[None, :]).astype(jnp.bfloat16)
 
 
+def last_sums(gate, up, down, qkv_total, out_total, grad, final, qkv_shape):
+    seq = lax.axis_size("seq")
+    ys = seq // 2
+    f32, low = jnp.float32, jnp.bfloat16
+    gate_half, down_half = gate[0].shape[2:], down[0].shape[2:]
+    qkv_width = qkv_total.shape[2]
+    operands = list(gate) + list(up) + list(down)
+    passed = [out_total, grad, final]
+
+    def kernel(*refs):
+        groups, refs = [refs[5 * index : 5 * index + 5] for index in range(3)], refs[15:]
+        qkv_ref, passed_refs, refs = refs[0], refs[1:4], refs[4:]
+        (gate_up_out, down_out, qkv_out), refs = refs[:3], refs[3:]
+        passed_outs, refs = refs[:3], refs[3:]
+        totals, refs = refs[:2], refs[2:]
+        passed_rooms, refs = refs[:3], refs[3:]
+        rooms, (loads, stores, pass_sems) = [refs[5 * index : 5 * index + 5] for index in range(3)], refs[15:]
+        s = lax.axis_index("seq")
+        y, x = lax.div(s, 2), lax.rem(s, 2)
+        copies = []
+        for number, (group, room) in enumerate(zip(groups, rooms)):
+            terms, from_x, from_y, last_y, last_x = group
+            sources = (terms.at[s], from_x.at[y], from_y.at[:, x], last_y, last_x)
+            mine = [
+                pltpu.make_async_copy(source, target, loads.at[number, index])
+                for index, (source, target) in enumerate(zip(sources, room))
+            ]
+            for copy in mine:
+                copy.start()
+            copies.append(mine)
+        ins = [
+            pltpu.make_async_copy(source, room, pass_sems.at[index, 0])
+            for index, (source, room) in enumerate(zip(passed_refs, passed_rooms))
+        ]
+        for copy in ins:
+            copy.start()
+        for index in range(seq):
+            qkv_out[:, index * qkv_width : (index + 1) * qkv_width] = qkv_ref[index]
+        outs = []
+        for index, (room, target) in enumerate(zip(passed_rooms, passed_outs)):
+            ins[index].wait()
+            copy = pltpu.make_async_copy(room, target, pass_sems.at[index, 1])
+            copy.start()
+            outs.append(copy)
+        for number, room in enumerate(rooms):
+            own, near_x, near_y, last_y, last_x = room
+            total = totals[number // 2]
+            base = 2 * (number % 2)
+            for copy in copies[number]:
+                copy.wait()
+            rows = own.shape[1]
+            tile = next(t for t in (64, 32, 16) if rows % t == 0)
+
+            def step(index, carry):
+                window = pl.ds(pl.multiple_of(index * tile, tile), tile)
+                first = own[0, window, :].astype(f32) + near_x[window, :].astype(f32)
+                second = own[1, window, :].astype(f32) + last_x[window, :].astype(f32)
+                for other in range(1, ys):
+                    place = lax.rem(y + other, ys)
+                    first = first + last_y[place, window, :].astype(f32)
+                    second = second + near_y[place, window, :].astype(f32)
+                total[base, window, :] = first
+                total[base + 1, window, :] = second
+                return carry
+
+            lax.fori_loop(0, rows // tile, step, 0)
+            target = gate_up_out.at[pl.ds(base, 2)] if number < 2 else down_out
+            copy = pltpu.make_async_copy(total.at[pl.ds(base, 2)], target, stores.at[number])
+            copy.start()
+            outs.append(copy)
+        for copy in outs:
+            copy.wait()
+
+    def rooms(half):
+        return [
+            pltpu.VMEM((2,) + half, low),
+            pltpu.VMEM(half, low),
+            pltpu.VMEM((ys,) + half, low),
+            pltpu.VMEM((ys,) + half, low),
+            pltpu.VMEM(half, low),
+        ]
+
+    return pl.pallas_call(
+        kernel,
+        name="last_sums",
+        out_shape=[
+            jax.ShapeDtypeStruct((4,) + gate_half, f32),
+            jax.ShapeDtypeStruct((2,) + down_half, f32),
+            jax.ShapeDtypeStruct(qkv_shape, f32),
+        ]
+        + [jax.ShapeDtypeStruct(array.shape, array.dtype) for array in passed],
+        in_specs=[ANY] * 15 + [VMEM] + [ANY] * 3,
+        out_specs=[ANY] * 2 + [VMEM] + [ANY] * 3,
+        scratch_shapes=[pltpu.VMEM((4,) + gate_half, f32), pltpu.VMEM((2,) + down_half, f32)]
+        + [pltpu.VMEM(array.shape, array.dtype) for array in passed]
+        + rooms(gate_half) * 2
+        + rooms(down_half)
+        + [
+            pltpu.SemaphoreType.DMA((3, 5)),
+            pltpu.SemaphoreType.DMA((3,)),
+            pltpu.SemaphoreType.DMA((3, 2)),
+        ],
+        compiler_params=pltpu.CompilerParams(vmem_limit_bytes=VMEM_LIMIT),
+    )(*operands, qkv_total, *passed)
+
+
 def rows_of_tile(values, row):
-    pad = [(0, 0)] * (values.ndim - 1)
-    return jnp.pad(values[..., None, :], pad + [(row, 7 - row), (0, 128 - values.shape[-1])])
+    return jnp.pad(values[None, :], [(row, 7 - row), (0, 128 - values.shape[0])])
+
 
 def body(
     inputs,
@@ -1700,67 +1884,52 @@
     w_down,
     mlp_gain,
 ):
-    seq_parts, wt_parts = lax.axis_size("seq"), lax.axis_size("wt")
+    seq_parts = lax.axis_size("seq")
     tok_count = inputs.shape[1]
     model_width = inputs.shape[2]
     length = tok_count * seq_parts
-    block_rows = min(block_limit, length)
     head_count = H // seq_parts
-    head_width = 2 * FEAT + DV
-    qkv_width = head_count * head_width
+    qkv_width = head_count * (2 * FEAT + DV)
     rows_low = inputs[0]
-    rows_in = rows_low.astype(jnp.float32)
     gain_lanes = norm_gain.shape[0]
     gains = rows_of_tile(norm_gain.astype(jnp.float32), 0) + rows_of_tile(mlp_gain.astype(jnp.float32), 1)
     qkv_rows = w_qkv.reshape(w_qkv.shape[0], seq_parts, qkv_width).transpose(1, 0, 2)
-    tokens_all, qkv_columns, out_rows, gains_all = gather_start(rows_low, qkv_rows, w_out, gains)
-    qkv_columns = qkv_columns.reshape(model_width, qkv_width)
-    out_rows = out_rows.reshape(head_count * DV, model_width)
-    gain_first = gains_all[:, :, 0, :gain_lanes].reshape(model_width)
-    gain_second = gains_all[:, :, 1, :gain_lanes].reshape(model_width)
-    gate_up_part = lax.all_gather(w_gate_up, "seq", axis=1, tiled=True)
-    hidden_low = rms_norm(tokens_all.astype(jnp.float32), gain_first).astype(jnp.bfloat16)
-    projected = jnp.dot(hidden_low, qkv_columns, preferred_element_type=jnp.float32).astype(
-        jnp.bfloat16
-    )
-    grouped = projected.reshape(length, head_count, head_width)
-    head_queries = grouped[:, :, :FEAT].transpose(1, 2, 0)
-    head_keys = grouped[:, :, FEAT : 2 * FEAT].transpose(1, 2, 0)
-    raw_values = grouped[:, :, 2 * FEAT :].astype(jnp.float32)
     segments = segment_ids[0]
-    conv_taps = conv_weight.astype(jnp.float32).reshape(KCONV, head_count, DV)
     tap_masks = [jnp.ones((length,), jnp.float32)]
-    mixed_values = conv_taps[0] * raw_values
     for tap_index in range(1, KCONV):
-        earlier = shift_down(segments, tap_index, -1)
-        tap_masks.append((earlier == segments).astype(jnp.float32))
-        mixed_values = (
-            mixed_values
-            + conv_taps[tap_index]
-            * shift_down(raw_values, tap_index, 0.0)
-            * tap_masks[tap_index][:, None, None]
-        )
-    conv_low = mixed_values.astype(jnp.bfloat16).transpose(1, 0, 2)
-    head_outputs, denominators = attend_forward(
-        head_queries, head_keys, conv_low, segments, block_rows
-    )
-    mixer_low = head_outputs.transpose(1, 0, 2).reshape(length, head_count * DV).astype(jnp.bfloat16)
-    mixed_parts = jnp.dot(mixer_low, out_rows, preferred_element_type=jnp.float32).astype(jnp.bfloat16)
-    attended = rows_in + square_sum(
-        mixed_parts.reshape(seq_parts, 2, tok_count // 2, model_width), "mixed_sum", 1
-    ).reshape(tok_count, model_width)
-    normed_low = rms_norm(attended, gain_second).astype(jnp.bfloat16)
-    branch_out, normed_all, gate_all, up_all, active_all, down_part = feed_forward(
-        normed_low, gate_up_part, w_down
-    )
-    outputs = attended + branch_out
+        tap_masks.append((shift_down(segments, tap_index, -1) == segments).astype(jnp.float32))
+    marks = jnp.stack(tap_masks, axis=1)
+    taps = conv_weight.astype(jnp.float32)
+    order = column_order(head_count)
+    (
+        attended,
+        normed_low,
+        gain_rows,
+        qkv_columns,
+        out_rows,
+        hidden_low,
+        sorted_columns,
+        mixer_low,
+        mixed_values,
+        head_outputs,
+        gate_early,
+    ) = mixer_forward(rows_low, qkv_rows, w_out, gains, w_gate_up, segments, marks, taps, order)
     sequence_length = lax.dynamic_index_in_dim(
         valid_lengths, lax.axis_index("wt"), 0, keepdims=False
     )
     positions = lax.axis_index("seq") * tok_count + jnp.arange(tok_count, dtype=jnp.int32)
-    keep_mask = (positions < sequence_length).astype(jnp.float32)
-    residual_error = (outputs - teacher[0].astype(jnp.float32)) * keep_mask[:, None]
-    energy = 0.5 * jnp.sum(residual_error * residual_error)
+    keep_mask = (positions < sequence_length).astype(jnp.float32)[:, None]
+    (
+        final_low,
+        residual_error,
+        energy,
+        normed_all,
+        gate_all,
+        up_all,
+        active_all,
+        down_part,
+        gate_up_part,
+    ) = feed_forward(normed_low, attended, teacher[0], keep_mask, gate_early, w_gate_up, w_down)
     (
         attended_grad,
         mix_back,
@@ -1775,7 +1944,7 @@
     ) = feed_back(
         residual_error,
         attended,
-        gain_second[None],
+        gain_rows,
         gate_up_part,
         down_part,
         gate_all,
@@ -1783,52 +1952,46 @@
         active_all,
         normed_all,
     )
-    marks = jnp.stack(tap_masks, axis=1) * (
-        jnp.arange(length)[:, None] >= jnp.arange(KCONV)[None, :]
-    ).astype(jnp.float32)
-    inputs_grad, totals, gate_total, up_total, down_total, qkv_total, grad_w_out = mixer_back(
+    inputs_grad, totals, gate, up, down, qkv_total, out_total = mixer_back(
         mix_back,
         attended_grad,
         rows_low,
-        gain_first[None],
-        out_rows,
-        qkv_columns,
+        gain_rows,
+        out_rows.reshape(head_count * DV, model_width),
+        qkv_columns.reshape(model_width, qkv_width),
         hidden_low,
-        projected,
+        sorted_columns,
         mixer_low,
-        conv_low,
+        mixed_values,
         head_outputs,
         segments,
         marks,
-        conv_taps.reshape(KCONV, head_count * DV),
-        column_order(head_count),
+        taps,
+        order,
         gain_two_terms,
-        energy.reshape(1, 1),
+        energy,
         (gate_terms, gate_from_x, gate_from_y),
         (up_terms,),
         (down_terms, down_from_x, down_from_y),
     )
-    grad_w_qkv = qkv_total.transpose(1, 0, 2).reshape(w_qkv.shape)
-    hidden_units = gate_up_part.shape[2]
-    grad_w_gate_up = jnp.stack(
-        [total.reshape(model_width // seq_parts, hidden_units) for total in (gate_total, up_total)]
+    grad_w_gate_up, grad_w_down, grad_w_qkv, grad_w_out, inputs_grad, outputs = last_sums(
+        gate, up, down, qkv_total, out_total, inputs_grad, final_low, w_qkv.shape
     )
-    grad_w_down = down_total.reshape(w_down.shape)
     totals = lax.dynamic_slice_in_dim(totals, lax.axis_index("wt") * gain_lanes, gain_lanes, 1)
     grad_norm_gain, grad_mlp_gain = totals[0], totals[1]
     grad_conv = totals[3 : 3 + KCONV]
     valid_total = jnp.sum(valid_lengths).astype(jnp.float32)
     mean_loss = 2.0 * totals[2, 0] / (valid_total * model_width)
     return (
-        outputs.astype(jnp.bfloat16)[None],
+        outputs[None],
         inputs_grad[None],
         mean_loss,
         grad_w_qkv,
         grad_conv,
         grad_w_out,
         grad_norm_gain,
-        grad_w_gate_up,
-        grad_w_down,
+        grad_w_gate_up.reshape(w_gate_up.shape),
+        grad_w_down.reshape(w_down.shape),
         grad_mlp_gain,
     )
 

time: 462 us -> 411 us (0.89)
  between operations: 17.5 us -> 3.22 us
  other arithmetic: 17.7 us -> 4.53 us
  local copies, waits for them, and re-layouts: 24.2 us -> 11.5 us
  matrix products: 7.89 us -> 0 us
    pallas_call x5 -> x4, Pallas kernels: 394 us -> 382 us  [remote_call(): pl.pallas_call(kernel, name=name, out_shape=outs, in_specs=[VMEM] * len(o...]
    pallas_call x0 -> x1, Pallas kernels: none -> 8.79 us  [last_sums(): pl.pallas_call(kernel, name='last_sums', out_shape=[jax.ShapeDtypeStruct(...]
    dot_general x4 -> x0, matrix products: 7.89 us -> none  [the longest x1 2.59 us: body(): jnp.dot(mixer_low, out_rows, preferred_element_type=jnp.float32)]
    reduce_sum x3 -> x0, other arithmetic: 7.29 us -> none  [the longest x2 3.68 us: rms_norm(): jnp.mean(values * values, axis=-1, keepdims=True) + epsilon]
  transfers between devices with their start and end apart: 1 -> 0, of which waited for: 0 -> 0; matrix products, arithmetic and copies ran while one was open for 6% -> 0% of each run, Pallas kernels for 18% -> 0%
where the time goes in v4:
time: 411 us; the launch traced here: 410 us
  Pallas kernels  391 us (95%)
  local copies, waits for them, and re-layouts  11.5 us (3%)
  other arithmetic  4.53 us (1%)
    pallas_call x4, Pallas kernels, remote_call(): pl.pallas_call(kernel, name=name, out_shape=outs, in_specs=[VMEM] * len(o...  382 us
    pallas_call x1, Pallas kernels, last_sums(): pl.pallas_call(kernel, name='last_sums', out_shape=[jax.ShapeDtypeStruct(...  8.79 us

profile of v4, /device:TPU:8, one launch (start us, length us, event | category | flops | bytes accessed | tf_op | source)
XLA Modules:
  0.0 410.2 jit_solution(17683150590118117348)
XLA Ops:
  0.6 0.0 copy-start.1
  0.7 2.6 copy.44.refs_9_.refs_5_
  3.3 1.2 fusion.refs_8_.refs_15_
  4.5 0.1 compare_convert_fusion
  4.6 0.1 fusion.18
  4.6 0.1 pad_maximum_fusion
  4.7 0.9 copy.43.refs_6_.refs_13_
  5.6 0.9 copy.42.refs_5_.refs_12_
  6.5 0.6 convert_element_type.39.refs_7_.refs_14_
  7.1 0.8 copy.52
  7.8 0.6 convert_add_fusion.refs_3_
  8.4 87.4 %mixer_forward.1 = (f32[128,2048]{1,0:T(8,128)}, bf16[128,2048]{1,0:T(8,128)(2,1)}, f32[8,2048]{1,0:T(8,128)}, bf16[4,8,64,640]{3,2,1,0:T(8,128)(2,1)}, bf16[8,6...) custom-call(bf16[128,2048]{1,0:T(8,128)(2,1)} %bitcast.35, ...), custom_call_target="tpu_custom_call" | custom-call | tf_op jit(solution)/shard_map/mixer_forward/pallas_call | solution.py:346
  95.8 0.6 dynamic_slice.7
  96.4 1.3 fusion.1.refs_3_
  97.7 85.6 %feed_forward.1 = (bf16[128,2048]{1,0:T(8,128)(2,1)}, f32[128,2048]{1,0:T(8,128)}, f32[8,2048]{1,0:T(8,128)}, bf16[1024,2048]{1,0:T(8,128)(2,1)}, f32[1024,704]{...) custom-call(bf16[128,2048]{1,0:T(8,128)(2,1)} %get-tuple-element.58., ...), custom_call_target="tpu_custom_call" | custom-call | tf_op jit(solution)/shard_map/feed_forward/pallas_call | solution.py:346
  183.3 94.2 %feed_back.1 = (f32[128,2048]{1,0:T(8,128)}, bf16[128,2048]{1,0:T(8,128)(2,1)}, f32[8,2048]{1,0:T(8,128)}, bf16[4,2,256,704]{3,2,1,0:T(8,128)(2,1)}, bf16[4,2,25...) custom-call(f32[128,2048]{1,0:T(8,128)} %get-tuple-element.61.refs_0, ...), custom_call_target="tpu_custom_call" | custom-call | tf_op jit(solution)/shard_map/feed_back/pallas_call | solution.py:346
  277.5 115.0 %mixer_back.1 = (f32[128,2048]{1,0:T(8,128)}, f32[8,512]{1,0:T(8,128)}, f32[4,64,640]{2,1,0:T(8,128)}, f32[64,2048]{1,0:T(8,128)}, bf16[2,256,704]{2,1,0:T(8,128...) custom-call(bf16[512,2048]{1,0:T(8,128)(2,1)} %bitcast.34, ...), custom_call_target="tpu_custom_call" | custom-call | tf_op jit(solution)/shard_map/mixer_back/pallas_call | solution.py:346
  392.5 8.8 %last_sums.1 = (f32[4,256,704]{2,1,0:T(8,128)}, f32[2,352,512]{2,1,0:T(8,128)}, f32[64,2560]{1,0:T(8,128)}, f32[64,2048]{1,0:T(8,128)}, f32[128,2048]{1,0:T(8,128)}, /*index=5*/bf16[128,2048]{1,0:T(8,128)(2,1)}) custom-call(bf16[4,2,256,704]{3,2,1,0:T(8,128)(2,1)} %get-tuple-element.69.refs_18_.refs_0_, ...), custom_call_target="tpu_custom_call" | custom-call | tf_op jit(solution)/shard_map/last_sums/pallas_call | solution.py:1846
  401.3 3.4 copy.49
  404.8 0.7 constant_dynamic-slice_fusion
  405.5 0.5 slice.25
  406.7 0.6 reduce_sum.9
  408.0 0.6 slice.26
  408.6 0.5 slice_bitcast_fusion.1
  (14 shorter events, 0.0 us)
Async XLA Ops:
  0.6 3.8 copy-start.1
  0.7 5.8 %copy-start.2 = (bf16[3,512]{1,0:T(4,128)(2,1)S(1)}, bf16[3,512]{1,0:T(4,128)(2,1)}, u32[]{:S(2)}) copy-start(bf16[3,512]{1,0:T(4,128)(2,1)} %param.16) | copy-start | bytes 9220
  0.7 6.4 %copy-start = (bf16[64,2560]{1,0:T(8,128)(2,1)S(1)}, bf16[64,2560]{1,0:T(8,128)(2,1)}, u32[]{:S(2)}) copy-start(bf16[64,2560]{1,0:T(8,128)(2,1)} %param.15) | copy-start | bytes 983044
  0.7 7.1 %copy-start.4 = (bf16[64]{0:T(256)(128)(2,1)S(1)}, bf16[64]{0:T(256)(128)(2,1)}, u32[]{:S(2)}) copy-start(bf16[64]{0:T(256)(128)(2,1)} %param.18) | copy-start | bytes 388
  0.7 7.1 %copy-start.3 = (bf16[64]{0:T(256)(128)(2,1)S(1)}, bf16[64]{0:T(256)(128)(2,1)}, u32[]{:S(2)}) copy-start(bf16[64]{0:T(256)(128)(2,1)} %param.21) | copy-start | bytes 388
  5.6 90.2 %copy-start.5 = (s32[8]{0:T(128)S(1)}, s32[8]{0:T(128)}, u32[]{:S(2)}) copy-start(s32[8]{0:T(128)} %param.13) | copy-start | bytes 100

commit v5 on v4

--- a/solution.py
+++ b/solution.py
@@ -43,6 +43,7 @@
 MESH = pl.DeviceIdType.MESH
 VMEM = pl.BlockSpec(memory_space=pltpu.VMEM)
 ANY = pl.BlockSpec(memory_space=pl.ANY)
+SMEM = pl.BlockSpec(memory_space=pltpu.SMEM)
 VMEM_LIMIT = 63 * 1024 * 1024
 
 
@@ -260,67 +261,83 @@
 
 class LineGather:
     @staticmethod
-    def semaphores(wt):
-        return [pltpu.SemaphoreType.DMA((5, wt // 2))]
+    def semaphores(wt, cuts=1):
+        return [pltpu.SemaphoreType.DMA((5, wt // 2, cuts))]
 
     def __init__(self, at, view, sems):
         self.at, self.view, self.sems = at, view, sems[0]
-
-    def up(self, z, source=None):
+        self.cuts = self.sems.shape[2]
+
+    def cut(self, ref, part):
+        if self.cuts == 1:
+            return ref
+        rows = ref.shape[0] // self.cuts
+        return ref.at[pl.ds(part * rows, rows)]
+
+    def hop(self, z, part, kind, device, source):
         slot = self.view(z * 2 + self.at.c)
         source = slot if source is None else source
-        return send(source, slot, self.sems.at[0, z], self.sems.at[3, z], self.at.level(self.at.z + 1))
-
-    def down(self, z, source=None):
-        slot = self.view(z * 2 + self.at.c)
-        source = slot if source is None else source
-        return send(source, slot, self.sems.at[1, z], self.sems.at[3, z], self.at.level(self.at.z - 1))
-
-    def over(self, z, source=None):
-        slot = self.view(z * 2 + self.at.c)
-        source = slot if source is None else source
-        return send(source, slot, self.sems.at[2, z], self.sems.at[4, z], self.at.partner())
+        arriving = 4 if kind == 2 else 3
+        return send(
+            self.cut(source, part),
+            self.cut(slot, part),
+            self.sems.at[kind, z, part],
+            self.sems.at[arriving, z, part],
+            device,
+        )
+
+    def up(self, z, part, source=None):
+        return self.hop(z, part, 0, self.at.level(self.at.z + 1), source)
+
+    def down(self, z, part, source=None):
+        return self.hop(z, part, 1, self.at.level(self.at.z - 1), source)
+
+    def over(self, z, part, source=None):
+        return self.hop(z, part, 2, self.at.partner(), source)
 
     def start(self, source=None):
         at = self.at
-
-        @pl.when(at.z + 1 < at.zs)
-        def _():
-            self.up(at.z, source).start()
-
-        @pl.when(at.z > 0)
-        def _():
-            self.down(at.z, source).start()
-
-        self.over(at.z, source).start()
+        for part in range(self.cuts):
+
+            @pl.when(at.z + 1 < at.zs)
+            def _():
+                self.up(at.z, part, source).start()
+
+            @pl.when(at.z > 0)
+            def _():
+                self.down(at.z, part, source).start()
+
+            self.over(at.z, part, source).start()
 
     def step(self, index):
         at = self.at
         below, above = at.z - 1 - index, at.z + 1 + index
-
-        @pl.when(below >= 0)
-        def _():
-            self.up(below).wait_recv()
-
-            @pl.when(at.z + 1 < at.zs)
+        for part in range(self.cuts):
+
+            @pl.when(below >= 0)
             def _():
-                self.up(below).start()
-
-            self.over(below).start()
-
-        @pl.when(above < at.zs)
-        def _():
-            self.down(above).wait_recv()
-
-            @pl.when(at.z > 0)
+                self.up(below, part).wait_recv()
+
+                @pl.when(at.z + 1 < at.zs)
+                def _():
+                    self.up(below, part).start()
+
+                self.over(below, part).start()
+
+            @pl.when(above < at.zs)
             def _():
-                self.down(above).start()
-
-            self.over(above).start()
+                self.down(above, part).wait_recv()
+
+                @pl.when(at.z > 0)
+                def _():
+                    self.down(above, part).start()
+
+                self.over(above, part).start()
 
     def wait_over(self, z):
-        slot = self.view(z * 2 + 1 - self.at.c)
-        send(slot, slot, self.sems.at[2, z], self.sems.at[4, z], self.at.partner()).wait_recv()
+        for part in range(self.cuts):
+            slot = self.cut(self.view(z * 2 + 1 - self.at.c), part)
+            send(slot, slot, self.sems.at[2, z, part], self.sems.at[4, z, part], self.at.partner()).wait_recv()
 
     def finish(self):
         for z in range(self.at.zs):
@@ -330,16 +347,17 @@
     def sent(self):
         at = self.at
         for z in range(at.zs):
-
-            @pl.when((at.z >= z) & (at.z + 1 < at.zs))
-            def _():
-                self.up(z).wait_send()
-
-            @pl.when((at.z <= z) & (at.z > 0))
-            def _():
-                self.down(z).wait_send()
-
-            self.over(z).wait_send()
+            for part in range(self.cuts):
+
+                @pl.when((at.z >= z) & (at.z + 1 < at.zs))
+                def _():
+                    self.up(z, part).wait_send()
+
+                @pl.when((at.z <= z) & (at.z > 0))
+                def _():
+                    self.down(z, part).wait_send()
+
+                self.over(z, part).wait_send()
 
 
 def remote_call(kernel, name, number, outs, scratch, *operands, in_specs=None, out_specs=None):
@@ -356,46 +374,42 @@
     )(*operands)
 
 
-def mixer_forward(tokens, qkv_rows, out_rows, gains, gate_up, segments, marks, taps, order):
+def mixer_forward(tokens, qkv_rows, out_rows, gains, gate_up, segments, taps):
     seq, wt = lax.axis_size("seq"), lax.axis_size("wt")
     zs = wt // 2
     count, width = tokens.shape
     length = count * seq
-    _, qkv_rank, qkv_width = qkv_rows.shape
     out_rank = out_rows.shape[0]
     heads = H // seq
     value_width = heads * DV
+    qkv_width = value_width + 2 * FEAT * heads
+    qkv_rank = width // (seq * wt)
     lanes_each = width // (seq * wt)
-    block, units = gate_up.shape[1:]
-    early = early_rows(block)
+    units, block = gate_up.shape[1:]
+    early = early_rows(units)
     rows_at_once = 256
     small = [
         tokens,
         qkv_rows,
         out_rows,
         gains,
-        segments.reshape(1, length),
-        segments.reshape(length, 1),
-        marks,
+        segments,
         taps,
-        order,
     ]
 
     def kernel(*refs):
-        (x_ref, qkv_ref, out_ref, gain_ref, segment_row, segment_column, mark_ref, tap_ref, order_ref), refs = (
+        (x_ref, qkv_ref, out_ref, gain_ref, segment_ref, tap_ref), refs = refs[:6], refs[6:]
+        gate_up_ref, refs = refs[0], refs[1:]
+        (attended_out, normed_out, gain_rows), refs = refs[:3], refs[3:]
+        (qkv_out, w_out_out, hidden_out, sorted_out, mixer_out, values_out, outputs_out, gates_out, order_out), refs = (
             refs[:9],
             refs[9:],
-        )
-        gate_up_ref, refs = refs[0], refs[1:]
-        (attended_out, normed_out, gain_rows), refs = refs[:3], refs[3:]
-        (qkv_out, w_out_out, hidden_out, sorted_out, mixer_out, values_out, outputs_out, gates_out), refs = (
-            refs[:8],
-            refs[8:],
         )
         (xs, qkvs, outs, gains_all, hidden_v, sorted_v, mixer_v, values_v, outputs_v, parts, total, room), refs = (
             refs[:12],
             refs[12:],
         )
+        (order_v, segment_column, tap_v), refs = refs[:3], refs[3:]
         sum_scratch, x_sems, gate_sems, refs = refs[:8], refs[8:11], refs[11:14], refs[14:]
         line_sems, refs = [refs[index : index + 1] for index in range(3)], refs[3:]
         swap_q, swap_g, local, outgoing = refs
@@ -416,9 +430,18 @@
         )
         gather_o = LineGather(at, lambda w: outs.at[w], line_sems[2])
         gates = SquareGather(
-            at, lambda s, h: gates_out.at[h, s], lambda h: gate_up_ref.at[h, pl.ds(0, early)], gate_sems
+            at,
+            lambda s, h: gates_out.at[h, :, pl.ds(pl.multiple_of(s * block, block), block)],
+            lambda h: gate_up_ref.at[h, pl.ds(0, early)],
+            gate_sems,
         )
         gain_slot = pl.ds(pl.multiple_of(at.w * 8, 8), 8)
+
+        def qkv_part(s):
+            if len(qkv_ref.shape) == 3:
+                return qkv_ref.at[s]
+            return qkv_ref.at[:, pl.ds(pl.multiple_of(s * qkv_width, qkv_width), qkv_width)]
+
         swaps = []
         for step in range(1, seq):
             to = lax.rem(at.s + step, seq)
@@ -426,13 +449,13 @@
                 send(gain_ref, gains_all.at[at.s, gain_slot], swap_g.at[step, 0], swap_g.at[at.s, 1], (to, at.w))
             )
             swaps.append(
-                send(qkv_ref.at[to], qkvs.at[at.s, at.w], swap_q.at[step, 0], swap_q.at[at.s, 1], (to, at.w))
+                send(qkv_part(to), qkvs.at[at.s, at.w], swap_q.at[step, 0], swap_q.at[at.s, 1], (to, at.w))
             )
         for copy in swaps:
             copy.start()
         gather_x.start()
         own = [
-            pltpu.make_async_copy(qkv_ref.at[at.s], qkvs.at[at.s, at.w], local.at[0]),
+            pltpu.make_async_copy(qkv_part(at.s), qkvs.at[at.s, at.w], local.at[0]),
             pltpu.make_async_copy(gain_ref, gains_all.at[at.s, gain_slot], local.at[1]),
             pltpu.make_async_copy(out_ref, outs.at[at.w], local.at[2]),
             pltpu.make_async_copy(x_ref, xs.at[pl.ds(pl.multiple_of(at.s * count, count), count)], local.at[3]),
@@ -442,7 +465,9 @@
         for copy in own:
             copy.wait()
         room_load.wait()
-        room_store = pltpu.make_async_copy(room, gates_out.at[:, at.s], local.at[4])
+        room_store = pltpu.make_async_copy(
+            room, gates_out.at[:, :, pl.ds(pl.multiple_of(at.s * block, block), block)], local.at[4]
+        )
         room_store.start()
         for step in range(1, seq):
             s = lax.rem(at.s + step, seq)
@@ -452,12 +477,17 @@
             send(slot, slot, swap_q.at[step, 0], swap_q.at[s, 1], at.across()).wait_recv()
         gather_g.start()
         gather_q.start()
+        tap_v[...] = tap_ref[...].astype(jnp.float32)
+        segment_row = segment_ref[...].astype(jnp.float32)
+        segment_column[...] = jnp.broadcast_to(segment_row, (128, length)).T
+        write_order(order_v, heads)
         gather_x.relay()
         gates.start()
         for index in range(zs - 1):
+            if index == zs - 2:
+                gather_o.start()
             gather_g.step(index)
             gather_q.step(index)
-        gather_o.start()
         gather_g.finish()
 
         device_rows = gains_all[...].reshape(seq * wt * 8, 128).astype(jnp.bfloat16)
@@ -496,7 +526,7 @@
         projected = jnp.dot(
             hidden_v[...], qkvs[...].reshape(width, qkv_width), preferred_element_type=jnp.float32
         ).astype(jnp.bfloat16)
-        sorted_v[...] = jnp.dot(projected, order_ref[...], preferred_element_type=jnp.float32).astype(
+        sorted_v[...] = jnp.dot(projected, order_v[...], preferred_element_type=jnp.float32).astype(
             jnp.bfloat16
         )
         stores = [
@@ -510,18 +540,20 @@
                     (outputs_v, outputs_out),
                     (mixer_v, mixer_out),
                     (outs, w_out_out),
+                    (order_v, order_out),
                 )
             )
         ]
         for copy in stores[:3]:
             copy.start()
+        marks = tap_marks(segment_column)
 
         def convolve(head, carry):
             columns = pl.ds(pl.multiple_of(head * DV, DV), DV)
             raw = sorted_v[:, columns].astype(jnp.float32)
-            mixed = tap_ref[0:1, columns] * raw
+            mixed = tap_v[0:1, columns] * raw
             for tap in range(1, KCONV):
-                mixed = mixed + tap_ref[tap : tap + 1, columns] * pltpu.roll(raw, tap, 0) * mark_ref[:, tap : tap + 1]
+                mixed = mixed + tap_v[tap : tap + 1, columns] * pltpu.roll(raw, tap, 0) * marks[tap]
             values_v[head] = mixed.astype(jnp.bfloat16)
             return carry
 
@@ -538,7 +570,7 @@
             queries = sorted_v[rows, value_width : value_width + 128] * mine.astype(jnp.bfloat16)
             scores = contract_last(queries, sorted_v[:, value_width + 128 :]) * 0.25
             places = start + lax.broadcasted_iota(jnp.int32, scores.shape, 0)
-            allowed = (segment_column[rows, :] == segment_row[...]) & (
+            allowed = (segment_column[rows, :1] == segment_row) & (
                 places >= lax.broadcasted_iota(jnp.int32, scores.shape, 1)
             )
             kernel_values = jnp.where(allowed, 1.0 + scores + 0.5 * scores * scores, 0.0)
@@ -610,7 +642,8 @@
             jax.ShapeDtypeStruct((length, value_width), low),
             jax.ShapeDtypeStruct((heads, length, DV), low),
             jax.ShapeDtypeStruct((heads, length, DV), f32),
-            jax.ShapeDtypeStruct((2, seq, early, units), low),
+            jax.ShapeDtypeStruct((2, early, width), low),
+            jax.ShapeDtypeStruct((qkv_width, sorted_width), low),
         ],
         [
             pltpu.VMEM((length, width), low),
@@ -624,7 +657,10 @@
             pltpu.VMEM((heads, length, DV), f32),
             pltpu.VMEM((seq, 2, count // 2, width), low),
             pltpu.VMEM((2, count // 2, width), f32),
-            pltpu.VMEM((2, early, units), low),
+            pltpu.VMEM((2, early, block), low),
+            pltpu.VMEM((qkv_width, sorted_width), low),
+            pltpu.VMEM((length, 128), f32),
+            pltpu.VMEM((KCONV, value_width), f32),
         ]
         + SquareSum.scratch(seq, (count // 2, width))
         + SquareGather.semaphores(seq)
@@ -634,17 +670,50 @@
             pltpu.SemaphoreType.DMA((seq, 2)),
             pltpu.SemaphoreType.DMA((seq, 2)),
             pltpu.SemaphoreType.DMA((5,)),
-            pltpu.SemaphoreType.DMA((7,)),
+            pltpu.SemaphoreType.DMA((8,)),
         ],
         *small,
         gate_up,
         in_specs=[VMEM] * len(small) + [ANY],
-        out_specs=[VMEM] * 3 + [ANY] * 8,
+        out_specs=[VMEM] * 3 + [ANY] * 9,
     )
 
 
-def early_rows(block):
-    return block // 4 * 3
+def write_order(ref, heads):
+    head_width, value_width = 2 * FEAT + DV, heads * DV
+
+    def step(index, carry):
+        window = pl.ds(pl.multiple_of(index * 32, 32), 32)
+        shape = (32, ref.shape[1])
+        column = index * 32 + lax.broadcasted_iota(jnp.int32, shape, 0)
+        head = lax.div(column, head_width)
+        place = lax.rem(column, head_width)
+        target = jnp.where(
+            place < FEAT,
+            value_width + head * FEAT + place,
+            jnp.where(
+                place < 2 * FEAT, value_width + 128 + head * FEAT + place - FEAT, head * DV + place - 2 * FEAT
+            ),
+        )
+        hit = target == lax.broadcasted_iota(jnp.int32, shape, 1)
+        ref[window, :] = hit.astype(jnp.float32).astype(jnp.bfloat16)
+        return carry
+
+    lax.fori_loop(0, ref.shape[0] // 32, step, 0)
+
+
+def tap_marks(segment_column):
+    segment = segment_column[:, :1]
+    place = lax.broadcasted_iota(jnp.int32, segment_column.shape, 0)[:, :1]
+    marks = [None]
+    for tap in range(1, KCONV):
+        same = (pltpu.roll(segment_column[...], tap, 0)[:, :1] == segment) & (place >= tap)
+        marks.append(same.astype(jnp.float32))
+    return marks
+
+
+def early_rows(units):
+    return units * 3 // 4 // 16 * 16
 
 
 class LinePieces:
@@ -755,17 +824,15 @@
 
             lower(piece, jnp.logical_not(upper))
             if fill is not None:
-                fill(piece)
+                fill(piece, self.pieces)
             return carry
 
         lax.fori_loop(0, self.pieces, step, 0)
 
-    def finish(self, total, fill=None):
+    def finish(self, total):
         at = self.at
 
         def step(piece, carry):
-            if fill is not None:
-                fill(self.pieces + piece)
             terms = self.terms(at.z, piece)
             below, above = self.cut(self.below.at[at.z], piece), self.cut(self.above.at[at.z], piece)
 
@@ -880,6 +947,23 @@
             y = at.beside(step)
             fetch([(self.from_y.at[y, 1 - at.x], rooms[0])])
             add_into(self.sum_x, [self.sum_x, rooms[0]])
+
+    def second_load(self, fetch):
+        at = self.at
+        pairs = [(self.terms(at.y * 2 + 1 - at.x, 1), self.sum_x)]
+        for step in range(1, at.ys):
+            y = at.beside(step)
+            pairs.append((self.terms(y * 2 + at.x, 0), self.sum_y.at[y]))
+        fetch(pairs)
+
+    def second_arrived(self):
+        at = self.at
+        terms = [self.sum_x]
+        for step in range(1, at.ys):
+            y = at.beside(step)
+            add_into(self.sum_y.at[y], [self.sum_y.at[y], self.from_x.at[y]])
+            terms.append(self.from_y.at[y, 1 - at.x])
+        add_into(self.sum_x, terms)
 
     def second_go(self):
         for step in range(1, self.at.ys):
@@ -968,27 +1052,29 @@
         return carry
 
     lax.fori_loop(0, last + 1 + late, turn, 0)
+    if fill is not None:
+        fill(None, PIECES)
     for index in range(2, at.zs):
-        sums.pass_on(index, fill if index == at.zs - 1 else None)
-    sums.finish(total, fill)
+        sums.pass_on(index, fill if index == 2 else None)
+    sums.finish(total)
     gather.sent()
 
 
 PIECES = 4
 
 
-def feed_forward(normed, attended, teacher, keep, gate_early, gate_up_shard, down_shard):
+def feed_forward(normed, attended, teacher, lengths, gate_early, gate_up_shard, down_shard):
     seq, wt = lax.axis_size("seq"), lax.axis_size("wt")
     count, width = normed.shape
-    block, units = gate_up_shard.shape[1:]
-    early = early_rows(block)
+    units, block = gate_up_shard.shape[1:]
+    early = early_rows(units)
     columns = down_shard.shape[1]
     tokens = wt * count
     zs = wt // 2
     half = units // 2
 
     def kernel(*refs):
-        (normed_ref, attended_ref, teacher_ref, keep_ref, early_ref, gate_shard_ref, shard_ref), refs = refs[:7], refs[7:]
+        (normed_ref, attended_ref, teacher_ref, length_ref, early_ref, gate_shard_ref, shard_ref), refs = refs[:7], refs[7:]
         (final_out, error_out, energy_out), refs = refs[:3], refs[3:]
         (normed_out, gate_out, up_out, active_out, down_out, gates_out), refs = refs[:6], refs[6:]
         (everyone, gates, downs, gate_all, up_all, active_all, parts, total), refs = refs[:8], refs[8:]
@@ -1001,25 +1087,22 @@
         )
         at = Place(seq, wt)
         loads = [
+            pltpu.make_async_copy(early_ref, gates.at[:, pl.ds(0, early)], local.at[4]),
             pltpu.make_async_copy(
-                early_ref.at[:, s], gates.at[:, pl.ds(s * block, early)], local.at[4 + s]
-            )
-            for s in range(seq)
+                gate_shard_ref.at[:, pl.ds(early, units - early)],
+                gates.at[:, pl.ds(early, units - early), pl.ds(pl.multiple_of(at.s * block, block), block)],
+                local.at[0],
+            ),
         ]
-        loads.append(
-            pltpu.make_async_copy(
-                gate_shard_ref.at[:, pl.ds(early, block - early)],
-                gates.at[:, pl.ds(pl.multiple_of(at.s * block + early, 16), block - early)],
-                local.at[0],
-            )
-        )
         for load in loads:
             load.start()
         at.meet(True, True)
         late = SquareGather(
             at,
-            lambda s, h: gates.at[h, pl.ds(pl.multiple_of(s * block + early, 16), block - early)],
-            lambda h: gate_shard_ref.at[h, pl.ds(early, block - early)],
+            lambda s, h: gates.at[
+                h, pl.ds(early, units - early), pl.ds(pl.multiple_of(s * block, block), block)
+            ],
+            lambda h: gate_shard_ref.at[h, pl.ds(early, units - early)],
             late_sems,
         )
         weights = SquareGather(
@@ -1068,8 +1151,8 @@
 
         def first(z):
             here = everyone[rows(z), :]
-            gate = jnp.dot(here, gates[0], preferred_element_type=jnp.float32)
-            up = jnp.dot(here, gates[1], preferred_element_type=jnp.float32)
+            gate = contract_last(here, gates[0])
+            up = contract_last(here, gates[1])
             gate_all[rows(z), :] = gate
             up_all[rows(z), :] = up
             active_all[rows(z), :] = gated_unit(gate, up).astype(jnp.bfloat16)
@@ -1096,12 +1179,15 @@
             True,
         )
         energy_out[...] = jnp.zeros_like(energy_out)
+        valid = length_ref[at.w]
 
         def finish_rows(index, carry):
             window = pl.ds(pl.multiple_of(index * 16, 16), 16)
             final = attended_ref[window, :] + total[window, :]
             final_out[window, :] = final.astype(jnp.bfloat16)
-            error = (final - teacher_ref[window, :].astype(jnp.float32)) * keep_ref[window, :]
+            place = at.s * count + index * 16 + lax.broadcasted_iota(jnp.int32, final.shape, 0)
+            keep = (place < valid).astype(jnp.float32)
+            error = (final - teacher_ref[window, :].astype(jnp.float32)) * keep
             error_out[window, :] = error
             squares = error * error
             energy_out[...] += 0.5 * (squares[:8] + squares[8:])
@@ -1128,11 +1214,11 @@
             jax.ShapeDtypeStruct((tokens, units), f32),
             jax.ShapeDtypeStruct((tokens, units), low),
             jax.ShapeDtypeStruct((units, width), low),
-            jax.ShapeDtypeStruct((2, width, units), low),
+            jax.ShapeDtypeStruct((2, units, width), low),
         ],
         [
             pltpu.VMEM((tokens, width), low),
-            pltpu.VMEM((2, width, units), low),
+            pltpu.VMEM((2, units, width), low),
             pltpu.VMEM((units, width), low),
             pltpu.VMEM((tokens, units), f32),
             pltpu.VMEM((tokens, units), f32),
@@ -1140,19 +1226,19 @@
             pltpu.VMEM((tokens, width), low),
             pltpu.VMEM((count, width), f32),
         ]
-        + LineGather.semaphores(wt)
+        + LineGather.semaphores(wt, 2)
         + LinePieces.scratch(wt, (count, width), PIECES)
         + SquareGather.semaphores(seq)
         + SquareGather.semaphores(seq)
-        + [pltpu.SemaphoreType.DMA((4 + seq,)), pltpu.SemaphoreType.DMA((4, zs))],
+        + [pltpu.SemaphoreType.DMA((5,)), pltpu.SemaphoreType.DMA((4, zs))],
         normed,
         attended,
         teacher,
-        keep,
+        lengths,
         gate_early,
         gate_up_shard,
         down_shard,
-        in_specs=[VMEM] * 4 + [ANY] * 2 + [VMEM],
+        in_specs=[VMEM] * 3 + [SMEM] + [ANY] * 2 + [VMEM],
         out_specs=[VMEM] * 3 + [ANY] * 6,
     )
 
@@ -1160,11 +1246,11 @@
 def feed_back(error, attended, gain, gate_up, down, gate, up, active, normed):
     seq, wt = lax.axis_size("seq"), lax.axis_size("wt")
     count, width = error.shape
-    units = gate_up.shape[2]
+    units = gate_up.shape[1]
     tokens = wt * count
-    zs, ys = wt // 2, seq // 2
+    ys = seq // 2
     block = width // seq
-    gate_half, down_half = (block // 2, units), (units // 2, block)
+    half = (units // 2, block)
 
     def kernel(*refs):
         (error_ref, attended_ref, gain_ref, gate_up_ref, down_ref, gate_ref, up_ref, active_ref, normed_ref), refs = (
@@ -1243,9 +1329,9 @@
             column_load(index).wait()
             here = columns.at[lax.rem(index, 2)]
             for number, terms in enumerate((gate_terms, up_terms)):
-                term = contract_first(here[...], back_all[number]).astype(jnp.bfloat16)
-                terms[s, 0] = term[: block // 2]
-                terms[s, 1] = term[block // 2 :]
+                term = contract_first(back_all[number], here[...]).astype(jnp.bfloat16)
+                terms[s, 0] = term[: units // 2]
+                terms[s, 1] = term[units // 2 :]
 
             @pl.when(index + 2 < seq)
             def _():
@@ -1253,21 +1339,16 @@
 
             leave(gate_sum, index)
 
-        def fill(slot):
+        def fill(slot, slots):
+            if slot is None:
+                lax.fori_loop(0, seq, lambda index, carry: (down_job(index), carry)[1], 0)
+                return
+
             def step(index, carry):
-                job = slot * (seq // 4) + index
-
-                @pl.when(job < seq)
-                def _():
-                    down_job(job)
-
-                @pl.when(job >= seq)
-                def _():
-                    gate_job(job - seq)
-
+                gate_job(slot * (seq // slots) + index)
                 return carry
 
-            lax.fori_loop(0, seq // 4, step, 0)
+            lax.fori_loop(0, seq // slots, step, 0)
 
         def ready_first():
             column_load(0).start()
@@ -1290,8 +1371,8 @@
         def second(z, piece):
             window = pl.ds(pl.multiple_of(piece * sums.width, sums.width), sums.width)
             parts[rows(z), window] = (
-                contract_last(back_all[0, rows(z), :], gates[0, window, :])
-                + contract_last(back_all[1, rows(z), :], gates[1, window, :])
+                jnp.dot(back_all[0, rows(z), :], gates[0, :, window], preferred_element_type=jnp.float32)
+                + jnp.dot(back_all[1, rows(z), :], gates[1, :, window], preferred_element_type=jnp.float32)
             ).astype(jnp.bfloat16)
 
         exchange(
@@ -1348,12 +1429,12 @@
             jax.ShapeDtypeStruct((count, width), jnp.float32),
             jax.ShapeDtypeStruct((count, width), jnp.bfloat16),
             jax.ShapeDtypeStruct((8, width), jnp.float32),
-            terms_of(gate_half),
-            terms_of(gate_half),
-            terms_of(down_half),
+            terms_of(half),
+            terms_of(half),
+            terms_of(half),
         ]
-        + first_of(gate_half)
-        + first_of(down_half),
+        + first_of(half)
+        + first_of(half),
         [
             pltpu.VMEM((count, width), jnp.bfloat16),
             pltpu.VMEM((tokens, width), jnp.bfloat16),
@@ -1365,12 +1446,12 @@
             pltpu.VMEM((tokens, width), jnp.bfloat16),
             pltpu.VMEM((tokens, units), jnp.bfloat16),
             pltpu.VMEM((2, tokens, block), jnp.bfloat16),
-            pltpu.VMEM((seq, 2) + gate_half, jnp.bfloat16),
-            pltpu.VMEM((seq, 2) + gate_half, jnp.bfloat16),
-            pltpu.VMEM((seq, 2) + down_half, jnp.bfloat16),
+            pltpu.VMEM((seq, 2) + half, jnp.bfloat16),
+            pltpu.VMEM((seq, 2) + half, jnp.bfloat16),
+            pltpu.VMEM((seq, 2) + half, jnp.bfloat16),
             pltpu.VMEM((count, width), jnp.float32),
         ]
-        + LineGather.semaphores(wt)
+        + LineGather.semaphores(wt, 2)
         + LinePieces.scratch(wt, (count, width), PIECES)
         + SquareTerms.semaphores(seq)
         + SquareTerms.semaphores(seq)
@@ -1402,7 +1483,6 @@
     mixed_values,
     head_outputs,
     segments,
-    marks,
     taps,
     order,
     gain_terms,
@@ -1421,10 +1501,8 @@
     rank = width // (seq * wt)
     gate_half, down_half = gate_parts[0].shape[2:], down_parts[0].shape[2:]
     rows_at_once = 256
-    segment_rows = segments.reshape(1, length)
-    segment_columns = segments.reshape(length, 1)
     big = [out_rows, qkv_columns, hidden, sorted_columns, mixer, mixed_values, head_outputs]
-    small = [mix_back, attended_grad, tokens, gain, segment_rows, segment_columns, marks, taps, order, gain_terms, energy]
+    small = [mix_back, attended_grad, tokens, gain, segments, taps, order, gain_terms, energy]
     far = list(gate_parts) + list(down_parts) + list(up_parts)
 
     def kernel(*refs):
@@ -1436,6 +1514,7 @@
         (w_out_v, w_qkv_v, hidden_v, sorted_v, mixer_v, values_v, outputs_v), refs = refs[:7], refs[7:]
         (mix_all, mixer_grad, query_acc, key_acc, value_acc, back_sorted, back_v), refs = refs[:7], refs[7:]
         (hidden_parts, qkv_parts, out_parts, hidden_total, gain_acc, spread, taps_acc), refs = refs[:7], refs[7:]
+        (segment_column, tap_v), refs = refs[:2], refs[2:]
         (room_gate0, room_gate1, room_down0, room_down1, qkv_sum, first, middle, last), refs = refs[:8], refs[8:]
         hidden_scratch, refs = refs[:8], refs[8:]
         qkv_scratch, out_scratch, refs = refs[:4], refs[4:8], refs[8:]
@@ -1447,9 +1526,7 @@
             grad_ref,
             token_ref,
             gain_ref,
-            segment_row,
-            segment_column,
-            mark_ref,
+            segment_ref,
             tap_ref,
             order_ref,
             gain_two,
@@ -1494,6 +1571,10 @@
         gate_rooms, down_rooms = (room_gate0, room_gate1), (room_down0, room_down1)
         gate_sum.second_start(fetch, gate_rooms)
         down_sum.second_start(fetch, down_rooms)
+        up_sum.second_load(fetch)
+        tap_v[...] = tap_ref[...].astype(jnp.float32)
+        segment_row = segment_ref[...].astype(jnp.float32)
+        segment_column[...] = jnp.broadcast_to(segment_row, (128, length)).T
         own.wait()
         for load in loads:
             load.wait()
@@ -1504,6 +1585,7 @@
         gather.finish()
         gate_sum.second_go()
         down_sum.second_go()
+        up_sum.first_start()
         mixer_grad[...] = contract_last(mix_all[...], w_out_v[...]).astype(jnp.bfloat16)
         out_sum = LinePieces(at, lambda w: out_parts.at[w], out_scratch)
         out_rank = out_parts.shape[1]
@@ -1531,7 +1613,7 @@
             keys = sorted_v[:, value_width + 128 :]
             scores = contract_last(queries, keys) * 0.25
             places = start + lax.broadcasted_iota(jnp.int32, scores.shape, 0)
-            allowed = (segment_column[rows, :] == segment_row[...]) & (
+            allowed = (segment_column[rows, :1] == segment_row) & (
                 places >= lax.broadcasted_iota(jnp.int32, scores.shape, 1)
             )
             kernel_values = jnp.where(allowed, 1.0 + scores + 0.5 * scores * scores, 0.0)
@@ -1556,19 +1638,20 @@
                 lax.fori_loop(middle_step, heads * steps, attend, 0)
             out_sum.pass_on(index)
         taps_acc[...] = jnp.zeros_like(taps_acc)
+        marks = tap_marks(segment_column)
 
         def convolve(head, carry):
             columns = pl.ds(pl.multiple_of(head * DV, DV), DV)
             mixed_back = value_acc[:, columns]
             raw = sorted_v[:, columns].astype(jnp.float32)
-            raw_back = tap_ref[0:1, columns] * mixed_back
+            raw_back = tap_v[0:1, columns] * mixed_back
             taps_acc[3:4, columns] = jnp.sum(mixed_back * raw, axis=0, keepdims=True)
             for tap in range(1, KCONV):
-                masked = mixed_back * mark_ref[:, tap : tap + 1]
+                masked = mixed_back * marks[tap]
                 taps_acc[3 + tap : 4 + tap, columns] = jnp.sum(
                     masked * pltpu.roll(raw, tap, 0), axis=0, keepdims=True
                 )
-                raw_back = raw_back + tap_ref[tap : tap + 1, columns] * pltpu.roll(masked, length - tap, 0)
+                raw_back = raw_back + tap_v[tap : tap + 1, columns] * pltpu.roll(masked, length - tap, 0)
             back_sorted[:, columns] = raw_back.astype(jnp.bfloat16)
             return carry
 
@@ -1604,7 +1687,9 @@
         qkv_sums.begin()
         qkv_sums.pass_on(zs - 1)
         hidden_sum.relay()
-        up_sum.first_start()
+        up_sum.first_wait()
+        up_sum.second_arrived()
+        up_sum.second_go()
         for index in range(zs - 2, 1, -1):
             qkv_sums.pass_on(index)
         hidden_sum.finish(lambda h: hidden_total.at[h])
@@ -1656,9 +1741,6 @@
             copy = send(middle, last.at[at.w], last_sems.at[step, 0], last_sems.at[at.w, 1], (at.s, to))
             copy.start()
             copies.append(copy)
-        up_sum.first_wait()
-        up_sum.second_start(fetch, gate_rooms)
-        up_sum.second_go()
         gate_sum.second_wait()
         down_sum.second_wait()
         terms = [middle]
@@ -1712,6 +1794,8 @@
             pltpu.VMEM((8, width), f32),
             pltpu.VMEM((8, width), f32),
             pltpu.VMEM(tile, f32),
+            pltpu.VMEM((length, 128), f32),
+            pltpu.VMEM((KCONV, value_width), f32),
             pltpu.VMEM(gate_half, low),
             pltpu.VMEM(gate_half, low),
             pltpu.VMEM(down_half, low),
@@ -1739,7 +1823,7 @@
         *small,
         *far,
         in_specs=[ANY] * len(big) + [VMEM] * len(small) + [ANY] * len(far),
-        out_specs=[VMEM] * 4 + [ANY] * 8,
+        out_specs=[VMEM] * 6 + [ANY] * 6,
     )
     grad, totals, qkv_total, out_total, up_x, up_y = results[:6]
     gate = tuple(gate_parts) + tuple(results[6:8])
@@ -1748,32 +1832,22 @@
     return grad, totals, gate, up, down, qkv_total, out_total
 
 
-def column_order(heads):
-    head_width = 2 * FEAT + DV
-    column = jnp.arange(heads * head_width)
-    head, place = column // head_width, column % head_width
-    value_width = heads * DV
-    target = jnp.where(
-        place < FEAT,
-        value_width + head * FEAT + place,
-        jnp.where(place < 2 * FEAT, value_width + 128 + head * FEAT + place - FEAT, head * DV + place - 2 * FEAT),
-    )
-    return (target[:, None] == jnp.arange(value_width + 256)[None, :]).astype(jnp.bfloat16)
-
-
-def last_sums(gate, up, down, qkv_total, out_total, grad, final, qkv_shape):
-    seq = lax.axis_size("seq")
+def last_sums(gate, up, down, qkv_total, totals, lengths, out_total, grad, final, qkv_shape):
+    seq, wt = lax.axis_size("seq"), lax.axis_size("wt")
     ys = seq // 2
     f32, low = jnp.float32, jnp.bfloat16
     gate_half, down_half = gate[0].shape[2:], down[0].shape[2:]
+    total_width = totals.shape[1]
+    lanes_each = total_width // wt
+    width = grad.shape[1]
     qkv_width = qkv_total.shape[2]
     operands = list(gate) + list(up) + list(down)
     passed = [out_total, grad, final]
 
     def kernel(*refs):
         groups, refs = [refs[5 * index : 5 * index + 5] for index in range(3)], refs[15:]
-        qkv_ref, passed_refs, refs = refs[0], refs[1:4], refs[4:]
-        (gate_up_out, down_out, qkv_out), refs = refs[:3], refs[3:]
+        (qkv_ref, totals_ref, length_ref), passed_refs, refs = refs[:3], refs[3:6], refs[6:]
+        (gate_up_out, down_out, qkv_out, first_gain, second_gain, taps_out, loss_out), refs = refs[:7], refs[7:]
         passed_outs, refs = refs[:3], refs[3:]
         totals, refs = refs[:2], refs[2:]
         passed_rooms, refs = refs[:3], refs[3:]
@@ -1797,6 +1871,15 @@
         ]
         for copy in ins:
             copy.start()
+        shift = lax.rem(total_width - lax.axis_index("wt") * lanes_each, total_width)
+        mine = pltpu.roll(totals_ref[...], shift, 1)[:, :lanes_each]
+        first_gain[...] = mine[0:1]
+        second_gain[...] = mine[1:2]
+        taps_out[...] = mine[3 : 3 + KCONV]
+        counted = length_ref[0]
+        for index in range(1, length_ref.shape[0]):
+            counted = counted + length_ref[index]
+        loss_out[...] = 2.0 * totals_ref[2:3, :1] / (jnp.full((1, 1), counted, jnp.int32).astype(f32) * width)
         for index in range(seq):
             qkv_out[:, index * qkv_width : (index + 1) * qkv_width] = qkv_ref[index]
         outs = []
@@ -1850,10 +1933,14 @@
             jax.ShapeDtypeStruct((4,) + gate_half, f32),
             jax.ShapeDtypeStruct((2,) + down_half, f32),
             jax.ShapeDtypeStruct(qkv_shape, f32),
+            jax.ShapeDtypeStruct((1, lanes_each), f32),
+            jax.ShapeDtypeStruct((1, lanes_each), f32),
+            jax.ShapeDtypeStruct((KCONV, lanes_each), f32),
+            jax.ShapeDtypeStruct((1, 1), f32),
         ]
         + [jax.ShapeDtypeStruct(array.shape, array.dtype) for array in passed],
-        in_specs=[ANY] * 15 + [VMEM] + [ANY] * 3,
-        out_specs=[ANY] * 2 + [VMEM] + [ANY] * 3,
+        in_specs=[ANY] * 15 + [VMEM] * 2 + [SMEM] + [ANY] * 3,
+        out_specs=[ANY] * 2 + [VMEM] * 5 + [ANY] * 3,
         scratch_shapes=[pltpu.VMEM((4,) + gate_half, f32), pltpu.VMEM((2,) + down_half, f32)]
         + [pltpu.VMEM(array.shape, array.dtype) for array in passed]
         + rooms(gate_half) * 2
@@ -1864,7 +1951,7 @@
             pltpu.SemaphoreType.DMA((3, 2)),
         ],
         compiler_params=pltpu.CompilerParams(vmem_limit_bytes=VMEM_LIMIT),
-    )(*operands, qkv_total, *passed)
+    )(*operands, qkv_total, totals, lengths, *passed)
 
 
 def rows_of_tile(values, row):
@@ -1893,14 +1980,11 @@
     rows_low = inputs[0]
     gain_lanes = norm_gain.shape[0]
     gains = rows_of_tile(norm_gain.astype(jnp.float32), 0) + rows_of_tile(mlp_gain.astype(jnp.float32), 1)
-    qkv_rows = w_qkv.reshape(w_qkv.shape[0], seq_parts, qkv_width).transpose(1, 0, 2)
-    segments = segment_ids[0]
-    tap_masks = [jnp.ones((length,), jnp.float32)]
-    for tap_index in range(1, KCONV):
-        tap_masks.append((shift_down(segments, tap_index, -1) == segments).astype(jnp.float32))
-    marks = jnp.stack(tap_masks, axis=1)
-    taps = conv_weight.astype(jnp.float32)
-    order = column_order(head_count)
+    qkv_rows = w_qkv
+    if qkv_width % 128:
+        qkv_rows = w_qkv.reshape(w_qkv.shape[0], seq_parts, qkv_width).transpose(1, 0, 2)
+    gate_up_low = w_gate_up.swapaxes(1, 2)
+    segments = segment_ids
     (
         attended,
         normed_low,
@@ -1913,12 +1997,8 @@
         mixed_values,
         head_outputs,
         gate_early,
-    ) = mixer_forward(rows_low, qkv_rows, w_out, gains, w_gate_up, segments, marks, taps, order)
-    sequence_length = lax.dynamic_index_in_dim(
-        valid_lengths, lax.axis_index("wt"), 0, keepdims=False
-    )
-    positions = lax.axis_index("seq") * tok_count + jnp.arange(tok_count, dtype=jnp.int32)
-    keep_mask = (positions < sequence_length).astype(jnp.float32)[:, None]
+        order,
+    ) = mixer_forward(rows_low, qkv_rows, w_out, gains, gate_up_low, segments, conv_weight)
     (
         final_low,
         residual_error,
@@ -1929,7 +2009,7 @@
         active_all,
         down_part,
         gate_up_part,
-    ) = feed_forward(normed_low, attended, teacher[0], keep_mask, gate_early, w_gate_up, w_down)
+    ) = feed_forward(normed_low, attended, teacher[0], valid_lengths, gate_early, gate_up_low, w_down)
     (
         attended_grad,
         mix_back,
@@ -1965,8 +2045,7 @@
         mixed_values,
         head_outputs,
         segments,
-        marks,
-        taps,
+        conv_weight,
         order,
         gain_two_terms,
         energy,
@@ -1974,25 +2053,31 @@
         (up_terms,),
         (down_terms, down_from_x, down_from_y),
     )
-    grad_w_gate_up, grad_w_down, grad_w_qkv, grad_w_out, inputs_grad, outputs = last_sums(
-        gate, up, down, qkv_total, out_total, inputs_grad, final_low, w_qkv.shape
+    (
+        grad_w_gate_up,
+        grad_w_down,
+        grad_w_qkv,
+        grad_norm_gain,
+        grad_mlp_gain,
+        grad_conv,
+        mean_loss,
+        grad_w_out,
+        inputs_grad,
+        outputs,
+    ) = last_sums(
+        gate, up, down, qkv_total, totals, valid_lengths, out_total, inputs_grad, final_low, w_qkv.shape
     )
-    totals = lax.dynamic_slice_in_dim(totals, lax.axis_index("wt") * gain_lanes, gain_lanes, 1)
-    grad_norm_gain, grad_mlp_gain = totals[0], totals[1]
-    grad_conv = totals[3 : 3 + KCONV]
-    valid_total = jnp.sum(valid_lengths).astype(jnp.float32)
-    mean_loss = 2.0 * totals[2, 0] / (valid_total * model_width)
     return (
         outputs[None],
         inputs_grad[None],
-        mean_loss,
+        mean_loss.reshape(()),
         grad_w_qkv,
         grad_conv,
         grad_w_out,
-        grad_norm_gain,
-        grad_w_gate_up.reshape(w_gate_up.shape),
+        grad_norm_gain.reshape(norm_gain.shape),
+        grad_w_gate_up.reshape(gate_up_low.shape).swapaxes(1, 2),
         grad_w_down.reshape(w_down.shape),
-        grad_mlp_gain,
+        grad_mlp_gain.reshape(mlp_gain.shape),
     )
 
 

time: 411 us -> 366 us (0.89)
  Pallas kernels: 391 us -> 361 us
  local copies, waits for them, and re-layouts: 11.5 us -> 0 us
    pallas_call x4, Pallas kernels: 382 us -> 352 us  [remote_call(): pl.pallas_call(kernel, name=name, out_shape=outs, in_specs=[VMEM] * len(o...]
    unnamed x14 -> x0, local copies, waits for them, and re-layouts: 6.07 us -> none
where the time goes in v5:
time: 366 us; the launch traced here: 363 us
  Pallas kernels  361 us (99%)
    pallas_call x4, Pallas kernels, remote_call(): pl.pallas_call(kernel, name=name, out_shape=outs, in_specs=[VMEM] * len(o...  352 us
    pallas_call x1, Pallas kernels, last_sums(): pl.pallas_call(kernel, name='last_sums', out_shape=[jax.ShapeDtypeStruct(...  8.61 us

profile of v5, /device:TPU:8, one launch (start us, length us, event | category | flops | bytes accessed | tf_op | source)
XLA Modules:
  0.0 362.9 jit_solution(11644720283054491475)
XLA Ops:
  0.6 1.3 convert_add_fusion.refs_3_
  1.9 83.8 %mixer_forward.1 = (f32[128,2048]{1,0:T(8,128)}, bf16[128,2048]{1,0:T(8,128)(2,1)}, f32[8,2048]{1,0:T(8,128)}, bf16[4,8,64,640]{3,2,1,0:T(8,128)(2,1)}, bf16[8,6...) custom-call(bf16[128,2048]{1,0:T(8,128)(2,1)} %bitcast.20, ...), custom_call_target="tpu_custom_call" | custom-call | tf_op jit(solution)/shard_map/mixer_forward/pallas_call | solution.py:364
  85.7 86.5 %feed_forward.1 = (bf16[128,2048]{1,0:T(8,128)(2,1)}, f32[128,2048]{1,0:T(8,128)}, f32[8,2048]{1,0:T(8,128)}, bf16[1024,2048]{1,0:T(8,128)(2,1)}, f32[1024,704]{...) custom-call(bf16[128,2048]{1,0:T(8,128)(2,1)} %get-tuple-element.63., ...), custom_call_target="tpu_custom_call" | custom-call | tf_op jit(solution)/shard_map/feed_forward/pallas_call | solution.py:364
  172.3 77.3 %feed_back.1 = (f32[128,2048]{1,0:T(8,128)}, bf16[128,2048]{1,0:T(8,128)(2,1)}, f32[8,2048]{1,0:T(8,128)}, bf16[4,2,352,512]{3,2,1,0:T(8,128)(2,1)}, bf16[4,2,35...) custom-call(f32[128,2048]{1,0:T(8,128)} %get-tuple-element.66.refs_0, ...), custom_call_target="tpu_custom_call" | custom-call | tf_op jit(solution)/shard_map/feed_back/pallas_call | solution.py:364
  249.6 104.5 %mixer_back.1 = (f32[128,2048]{1,0:T(8,128)}, f32[8,512]{1,0:T(8,128)}, f32[4,64,640]{2,1,0:T(8,128)}, f32[64,2048]{1,0:T(8,128)}, bf16[2,352,512]{2,1,0:T(8,128...) custom-call(bf16[512,2048]{1,0:T(8,128)(2,1)} %bitcast.19, ...), custom_call_target="tpu_custom_call" | custom-call | tf_op jit(solution)/shard_map/mixer_back/pallas_call | solution.py:364
  354.1 8.6 %last_sums.1 = (f32[4,352,512]{2,1,0:T(8,128)}, f32[2,352,512]{2,1,0:T(8,128)}, f32[64,2560]{1,0:T(8,128)}, f32[1,64]{1,0:T(1,128)}, f32[1,64]{1,0:T(1,128)}, /*...) custom-call(bf16[4,2,352,512]{3,2,1,0:T(8,128)(2,1)} %get-tuple-elem, ...), custom_call_target="tpu_custom_call" | custom-call | tf_op jit(solution)/shard_map/last_sums/pallas_call | solution.py:1929

commit v6 on v5

--- a/solution.py
+++ b/solution.py
@@ -1,3 +1,5 @@
+from functools import partial
+
 import jax
 import jax.numpy as jnp
 from jax import lax
@@ -130,44 +132,68 @@
         self.over_x, self.over_y, self.got = sems
         self.sent = []
 
-    def go(self, source, s, half, leaving, device):
-        copy = send(source, self.view(s, half), leaving, self.got.at[s, half], device)
-        copy.start()
+    def go(self, copy):
+        copy().start()
         self.sent.append(copy)
+
+    def own_x(self, half):
+        at = self.at
+        target = self.view(at.s, half)
+        return send(self.own(half), target, self.over_x.at[half], self.got.at[at.s, half], at.across())
+
+    def own_y(self, step, half):
+        at = self.at
+        target, device = self.view(at.s, half), at.column(at.beside(step))
+        return send(self.own(half), target, self.over_y.at[step, half], self.got.at[at.s, half], device)
+
+    def pass_y(self, step):
+        at = self.at
+        s = at.y * 2 + 1 - at.x
+        slot, device = self.view(s, 0), at.column(at.beside(step))
+        return send(slot, slot, self.over_y.at[step, 2], self.got.at[s, 0], device)
+
+    def pass_x(self, step):
+        s = self.at.beside(step) * 2 + self.at.x
+        slot = self.view(s, 1)
+        return send(slot, slot, self.over_x.at[1 + step], self.got.at[s, 1], self.at.across())
 
     def wait(self, s, half):
         slot = self.view(s, half)
         send(slot, slot, self.over_x.at[0], self.got.at[s, half], self.at.across()).wait_recv()
 
     def start(self):
-        at = self.at
         for half in range(2):
-            self.go(self.own(half), at.s, half, self.over_x.at[half], at.across())
-            for step in range(1, at.ys):
-                target = at.column(at.beside(step))
-                self.go(self.own(1 - half), at.s, 1 - half, self.over_y.at[step, half], target)
+            self.go(partial(self.own_x, half))
+            for step in range(1, self.at.ys):
+                self.go(partial(self.own_y, step, 1 - half))
 
     def relay(self):
         at = self.at
-        other = at.y * 2 + 1 - at.x
-        self.wait(other, 0)
+        self.wait(at.y * 2 + 1 - at.x, 0)
         for step in range(1, at.ys):
-            self.go(self.view(other, 0), other, 0, self.over_y.at[step, 2], at.column(at.beside(step)))
+            self.go(partial(self.pass_y, step))
         for step in range(1, at.ys):
-            s = at.beside(step) * 2 + at.x
-            self.wait(s, 1)
-            self.go(self.view(s, 1), s, 1, self.over_x.at[1 + step], at.across())
-
-    def finish(self):
+            self.wait(at.beside(step) * 2 + at.x, 1)
+            self.go(partial(self.pass_x, step))
+
+    def direct(self):
         at = self.at
         self.wait(at.y * 2 + 1 - at.x, 1)
         for step in range(1, at.ys):
+            self.wait(at.beside(step) * 2 + at.x, 0)
+
+    def relayed(self):
+        at = self.at
+        for step in range(1, at.ys):
             y = at.beside(step)
-            self.wait(y * 2 + at.x, 0)
             self.wait(y * 2 + 1 - at.x, 0)
             self.wait(y * 2 + 1 - at.x, 1)
         for copy in self.sent:
-            copy.wait_send()
+            copy().wait_send()
+
+    def finish(self):
+        self.direct()
+        self.relayed()
 
 
 class SquareSum:
@@ -722,8 +748,8 @@
         zs = wt // 2
         return [pltpu.VMEM((zs,) + shape, jnp.bfloat16)] * 3 + [pltpu.SemaphoreType.DMA((6, zs, pieces))]
 
-    def __init__(self, at, part, scratch):
-        self.at, self.part = at, part
+    def __init__(self, at, part, scratch, order=None):
+        self.at, self.part, self.order = at, part, order
         self.pair, self.below, self.above, self.sems = scratch
         self.pieces = self.sems.shape[2]
         self.width = self.pair.shape[-1] // self.pieces
@@ -731,7 +757,11 @@
     def cut(self, ref, piece):
         if len(ref.shape) == 3:
             return ref.at[piece]
-        return ref.at[:, pl.ds(pl.multiple_of(piece * self.width, self.width), self.width)]
+        return ref.at[:, self.columns(piece)]
+
+    def columns(self, piece):
+        block = piece if self.order is None else self.order(piece)
+        return pl.ds(pl.multiple_of(block * self.width, self.width), self.width)
 
     def own(self, z, piece):
         return self.cut(self.part(z * 2 + self.at.c), piece)
@@ -799,7 +829,7 @@
 
         lax.fori_loop(0, (zs - 1) * self.pieces, starts, 0)
 
-    def pass_on(self, index, fill=None):
+    def pass_on(self, index, fill=None, begin=0, end=None):
         at = self.at
         upper = at.z * 2 >= at.zs
         high, low = index, at.zs - 1 - index
@@ -827,7 +857,11 @@
                 fill(piece, self.pieces)
             return carry
 
-        lax.fori_loop(0, self.pieces, step, 0)
+        end = self.pieces if end is None else end
+        if end - begin == 1:
+            step(begin, 0)
+        else:
+            lax.fori_loop(begin, end, step, 0)
 
     def finish(self, total):
         at = self.at
@@ -995,72 +1029,138 @@
     lax.fori_loop(0, rows // 16, step, 0)
 
 
-def exchange(
-    at, shard, everyone, gather_sems, local, sums, first, second, total, ready, wait_for_ready, fill=None
-):
-    count = shard.shape[0]
-    gather = LineGather(
-        at, lambda w: everyone.at[pl.ds(pl.multiple_of(w * count, count), count)], gather_sems
-    )
-    gather.start(shard)
-    own = pltpu.make_async_copy(
-        shard, everyone.at[pl.ds(pl.multiple_of(at.w * count, count), count)], local
-    )
-    own.start()
-    own.wait()
-    ready[0]()
-    last = 2 * (at.zs - 1)
-    late = 3 if wait_for_ready else 0
-
-    def turn(index, carry):
-        fresh = index <= last
-        place = jnp.where(fresh, index, jnp.where(index == last + 3, 0, index - last))
-        far, side = lax.div(place + 1, 2), lax.rem(place, 2)
+class Exchange:
+    def __init__(self, at, shard, everyone, gather_sems, local, sums, first, second):
+        self.at, self.sums, self.first, self.second = at, sums, first, second
+        count = shard.shape[0]
+        slot = lambda w: everyone.at[pl.ds(pl.multiple_of(w * count, count), count)]
+        self.gather = LineGather(at, slot, gather_sems)
+        self.gather.start(shard)
+        own = pltpu.make_async_copy(shard, slot(at.w), local)
+        own.start()
+        own.wait()
+        self.last = 2 * (at.zs - 1)
+
+    def level(self, index):
+        at = self.at
+        far, side = lax.div(index + 1, 2), lax.rem(index, 2)
         z = at.z + jnp.where(side == 1, -far, far)
-        valid = (z >= 0) & (z < at.zs)
-
-        @pl.when(fresh & (side == 1))
+        return far, side, z, (z >= 0) & (z < at.zs)
+
+    def arrive(self, index):
+        far, side, z, valid = self.level(index)
+
+        @pl.when(side == 1)
         def _():
-            gather.step(far - 1)
-
-        @pl.when(fresh & valid)
+            self.gather.step(far - 1)
+
+        @pl.when(valid)
         def _():
-            gather.wait_over(z)
-            first(z)
-
-        if wait_for_ready:
-
-            @pl.when(index == late)
+            self.gather.wait_over(z)
+            self.first(z)
+
+        return z, valid
+
+    def put(self, z, begin, end):
+        def step(piece, inner):
+            self.second(z, piece)
+            self.sums.over(z, piece).start()
+
+            @pl.when(piece > begin)
             def _():
-                ready[1]()
-
-        @pl.when(valid & (index >= late))
-        def _():
-            def step(piece, inner):
-                second(z, piece)
-                sums.over(z, piece).start()
-
-                @pl.when(piece > 0)
-                def _():
-                    sums.ends(z, piece - 1)
-
-                return inner
-
-            lax.fori_loop(0, sums.pieces, step, 0)
-            sums.ends(z, sums.pieces - 1)
-
-        return carry
-
-    lax.fori_loop(0, last + 1 + late, turn, 0)
-    if fill is not None:
-        fill(None, PIECES)
-    for index in range(2, at.zs):
-        sums.pass_on(index, fill if index == 2 else None)
-    sums.finish(total)
-    gather.sent()
-
-
-PIECES = 4
+                self.sums.ends(z, piece - 1)
+
+            return inner
+
+        lax.fori_loop(begin, end, step, 0)
+        self.sums.ends(z, end - 1)
+
+    def whole(self, total, fill):
+        at, sums = self.at, self.sums
+
+        def turn(index, carry):
+            z, valid = self.arrive(index)
+
+            @pl.when(valid)
+            def _():
+                self.put(z, 0, sums.pieces)
+
+            return carry
+
+        lax.fori_loop(0, self.last + 1, turn, 0)
+        fill(None, sums.pieces)
+        for index in range(2, at.zs):
+            sums.pass_on(index, fill if index == 2 else None)
+        sums.finish(total)
+        self.gather.sent()
+
+    def by_columns(self, total, direct, relayed, near):
+        at, sums = self.at, self.sums
+        begin = min(3, self.last)
+
+        def turn(index, carry):
+            z, valid = self.arrive(index)
+
+            @pl.when(index == begin)
+            def _():
+                direct()
+
+            @pl.when(valid & (index >= begin))
+            def _():
+                self.put(z, 0, near)
+
+            return carry
+
+        lax.fori_loop(0, self.last + 1, turn, 0)
+
+        def earlier(index, carry):
+            _, _, z, valid = self.level(index)
+
+            @pl.when(valid)
+            def _():
+                self.put(z, 0, near)
+
+            return carry
+
+        lax.fori_loop(1, begin, earlier, 0)
+        if at.zs > 2:
+            sums.pass_on(2, None, 0, near)
+        relayed()
+
+        def over(index, carry):
+            _, _, z, valid = self.level(self.last - index)
+
+            @pl.when(valid)
+            def _():
+                for piece in range(near, sums.pieces):
+                    self.second(z, piece)
+                    sums.over(z, piece).start()
+
+            return carry
+
+        lax.fori_loop(0, self.last, over, 0)
+
+        def start(index, carry):
+            _, _, z, valid = self.level(self.last - index)
+
+            @pl.when(valid)
+            def _():
+                for piece in range(near, sums.pieces):
+                    sums.ends(z, piece)
+
+            return carry
+
+        lax.fori_loop(0, self.last, start, 0)
+        self.put(at.z, 0, sums.pieces)
+        for index in range(3, at.zs):
+            sums.pass_on(index, None, 0, near)
+        for index in range(at.zs - 1, 1, -1):
+            sums.pass_on(index, None, near, sums.pieces)
+        sums.finish(total)
+        self.gather.sent()
+
+
+PIECES = 2
 
 
 def feed_forward(normed, attended, teacher, lengths, gate_early, gate_up_shard, down_shard):
@@ -1113,13 +1213,26 @@
             lambda h: shard_ref.at[pl.ds(h * half, half)],
             square_sems,
         )
+        ys = seq // 2
+
+        def column_block(piece):
+            if isinstance(piece, int):
+                step = 0 if piece < 2 else piece - 1 if piece <= ys else piece - ys
+                return at.beside(step) * 2 + (1 - at.x if piece == 1 or piece > ys else at.x)
+            step = jnp.where(piece < 2, 0, jnp.where(piece <= ys, piece - 1, piece - ys))
+            other = (piece == 1) | (piece > ys)
+            return at.beside(step) * 2 + jnp.where(other, 1 - at.x, at.x)
+
         sums = LinePieces(
-            at, lambda w: parts.at[pl.ds(pl.multiple_of(w * count, count), count)], sum_scratch
+            at,
+            lambda w: parts.at[pl.ds(pl.multiple_of(w * count, count), count)],
+            sum_scratch,
+            column_block,
         )
         down_store = pltpu.make_async_copy(downs, down_out, local.at[2])
         gates_store = pltpu.make_async_copy(gates, gates_out, local.at[0])
 
-        def ready_first():
+        def prepare():
             late.start()
             own = pltpu.make_async_copy(
                 shard_ref, downs.at[:, pl.ds(pl.multiple_of(at.s * columns, columns), columns)], local.at[3]
@@ -1133,9 +1246,12 @@
             late.finish()
             gates_store.start()
 
-        def ready_later():
+        def direct():
             weights.relay()
-            weights.finish()
+            weights.direct()
+
+        def relayed():
+            weights.relayed()
             down_store.start()
 
         def rows(z):
@@ -1160,24 +1276,14 @@
                 copy.start()
 
         def second(z, piece):
-            window = pl.ds(pl.multiple_of(piece * sums.width, sums.width), sums.width)
+            window = sums.columns(piece)
             parts[rows(z), window] = jnp.dot(
                 active_all[rows(z), :], downs[:, window], preferred_element_type=jnp.float32
             ).astype(jnp.bfloat16)
 
-        exchange(
-            at,
-            normed_ref,
-            everyone,
-            gather_sems,
-            local.at[1],
-            sums,
-            first,
-            second,
-            total,
-            (ready_first, ready_later),
-            True,
-        )
+        work = Exchange(at, normed_ref, everyone, gather_sems, local.at[1], sums, first, second)
+        prepare()
+        work.by_columns(total, direct, relayed, ys + 1)
         energy_out[...] = jnp.zeros_like(energy_out)
         valid = length_ref[at.w]
 
@@ -1227,7 +1333,7 @@
             pltpu.VMEM((count, width), f32),
         ]
         + LineGather.semaphores(wt, 2)
-        + LinePieces.scratch(wt, (count, width), PIECES)
+        + LinePieces.scratch(wt, (count, width), seq)
         + SquareGather.semaphores(seq)
         + SquareGather.semaphores(seq)
         + [pltpu.SemaphoreType.DMA((5,)), pltpu.SemaphoreType.DMA((4, zs))],
@@ -1344,13 +1450,20 @@
                 lax.fori_loop(0, seq, lambda index, carry: (down_job(index), carry)[1], 0)
                 return
 
+            each = -(-seq // slots)
+
             def step(index, carry):
-                gate_job(slot * (seq // slots) + index)
+                job = slot * each + index
+
+                @pl.when(job < seq)
+                def _():
+                    gate_job(job)
+
                 return carry
 
-            lax.fori_loop(0, seq // slots, step, 0)
-
-        def ready_first():
+            lax.fori_loop(0, each, step, 0)
+
+        def prepare():
             column_load(0).start()
             column_load(1).start()
             for load in loads:
@@ -1375,20 +1488,9 @@
                 + jnp.dot(back_all[1, rows(z), :], gates[1, :, window], preferred_element_type=jnp.float32)
             ).astype(jnp.bfloat16)
 
-        exchange(
-            at,
-            low,
-            everyone,
-            gather_sems,
-            local.at[5],
-            sums,
-            first,
-            second,
-            total,
-            (ready_first,),
-            False,
-            fill,
-        )
+        work = Exchange(at, low, everyone, gather_sems, local.at[5], sums, first, second)
+        prepare()
+        work.whole(total, fill)
         stores = [
             pltpu.make_async_copy(source, target, outgoing.at[index])
             for index, (source, target) in enumerate(
@@ -1807,7 +1909,7 @@
         ]
         + SquareSum.scratch(seq, (count // 2, width))
         + LinePieces.scratch(wt, (seq, qkv_rank, qkv_width), seq)
-        + LinePieces.scratch(wt, (out_rank, width), PIECES)
+        + LinePieces.scratch(wt, (out_rank, width), 1)
         + SquareTerms.scratch(seq, gate_half)
         + SquareTerms.scratch(seq, down_half)
         + SquareTerms.scratch(seq, gate_half)

time: 366 us -> 356 us (0.973)
  Pallas kernels: 361 us -> 351 us
    pallas_call x4, Pallas kernels: 352 us -> 342 us  [remote_call(): pl.pallas_call(kernel, name=name, out_shape=outs, in_specs=[VMEM] * len(o...]
where the time goes in v6:
time: 356 us; the launch traced here: 353 us
  Pallas kernels  351 us (99%)
    pallas_call x4, Pallas kernels, remote_call(): pl.pallas_call(kernel, name=name, out_shape=outs, in_specs=[VMEM] * len(o...  342 us
    pallas_call x1, Pallas kernels, last_sums(): pl.pallas_call(kernel, name='last_sums', out_shape=[jax.ShapeDtypeStruct(...  8.61 us

profile of v6, /device:TPU:8, one launch (start us, length us, event | category | flops | bytes accessed | tf_op | source)
XLA Modules:
  0.0 353.1 jit_solution(2421808174077921895)
XLA Ops:
  0.6 1.3 convert_add_fusion.refs_3_
  1.9 83.8 %mixer_forward.1 = (f32[128,2048]{1,0:T(8,128)}, bf16[128,2048]{1,0:T(8,128)(2,1)}, f32[8,2048]{1,0:T(8,128)}, bf16[4,8,64,640]{3,2,1,0:T(8,128)(2,1)}, bf16[8,6...) custom-call(bf16[128,2048]{1,0:T(8,128)(2,1)} %bitcast.20, ...), custom_call_target="tpu_custom_call" | custom-call | tf_op jit(solution)/shard_map/mixer_forward/pallas_call | solution.py:390
  85.7 81.3 %feed_forward.1 = (bf16[128,2048]{1,0:T(8,128)(2,1)}, f32[128,2048]{1,0:T(8,128)}, f32[8,2048]{1,0:T(8,128)}, bf16[1024,2048]{1,0:T(8,128)(2,1)}, f32[1024,704]{...) custom-call(bf16[128,2048]{1,0:T(8,128)(2,1)} %get-tuple-element.63., ...), custom_call_target="tpu_custom_call" | custom-call | tf_op jit(solution)/shard_map/feed_forward/pallas_call | solution.py:390
  167.1 76.6 %feed_back.1 = (f32[128,2048]{1,0:T(8,128)}, bf16[128,2048]{1,0:T(8,128)(2,1)}, f32[8,2048]{1,0:T(8,128)}, bf16[4,2,352,512]{3,2,1,0:T(8,128)(2,1)}, bf16[4,2,35...) custom-call(f32[128,2048]{1,0:T(8,128)} %get-tuple-element.66.refs_0, ...), custom_call_target="tpu_custom_call" | custom-call | tf_op jit(solution)/shard_map/feed_back/pallas_call | solution.py:390
  243.7 100.7 %mixer_back.1 = (f32[128,2048]{1,0:T(8,128)}, f32[8,512]{1,0:T(8,128)}, f32[4,64,640]{2,1,0:T(8,128)}, f32[64,2048]{1,0:T(8,128)}, bf16[2,352,512]{2,1,0:T(8,128...) custom-call(bf16[512,2048]{1,0:T(8,128)(2,1)} %bitcast.19, ...), custom_call_target="tpu_custom_call" | custom-call | tf_op jit(solution)/shard_map/mixer_back/pallas_call | solution.py:390
  344.4 8.6 %last_sums.1 = (f32[4,352,512]{2,1,0:T(8,128)}, f32[2,352,512]{2,1,0:T(8,128)}, f32[64,2560]{1,0:T(8,128)}, f32[1,64]{1,0:T(1,128)}, f32[1,64]{1,0:T(1,128)}, /*...) custom-call(bf16[4,2,352,512]{3,2,1,0:T(8,128)(2,1)} %get-tuple-elem, ...), custom_call_target="tpu_custom_call" | custom-call | tf_op jit(solution)/shard_map/last_sums/pallas_call | solution.py:2031

commit v7 on v6

--- a/solution.py
+++ b/solution.py
@@ -810,24 +810,23 @@
             add_into(self.own(z, piece), self.terms(z, piece))
             self.down(z, piece).start()
 
-    def begin(self):
+    def offer(self, piece):
         zs = self.at.zs
-
-        def pairs(piece, carry):
-            for index in range(zs // 2):
-                self.over(index, piece).start()
-                self.over(zs - 1 - index, piece).start()
+        for index in range(zs // 2):
+            self.over(index, piece).start()
+            self.over(zs - 1 - index, piece).start()
+
+    def launch(self, piece, near):
+        self.ends(jnp.where(self.at.z == 0, self.at.zs - 1 - near, near), piece)
+
+    def launch_all(self, near):
+        zs = self.at.zs
+
+        def step(index, carry):
+            self.launch(lax.rem(index, self.pieces), near + lax.div(index, self.pieces))
             return carry
 
-        lax.fori_loop(0, self.pieces, pairs, 0)
-
-        def starts(index, carry):
-            piece = lax.rem(index, self.pieces)
-            far = zs - 1 - lax.div(index, self.pieces)
-            self.ends(jnp.where(self.at.z == 0, far, zs - 1 - far), piece)
-            return carry
-
-        lax.fori_loop(0, (zs - 1) * self.pieces, starts, 0)
+        lax.fori_loop(0, (zs - 1 - near) * self.pieces, step, 0)
 
     def pass_on(self, index, fill=None, begin=0, end=None):
         at = self.at
@@ -863,7 +862,7 @@
         else:
             lax.fori_loop(begin, end, step, 0)
 
-    def finish(self, total):
+    def finish(self, total, done=None):
         at = self.at
 
         def step(piece, carry):
@@ -886,6 +885,8 @@
                 self.down(at.z, piece).wait_recv()
                 add_into(self.cut(total, piece), terms + [below, above])
 
+            if done is not None:
+                done(piece)
             for z in range(at.zs):
 
                 @pl.when(at.z < z)
@@ -1039,7 +1040,11 @@
         own = pltpu.make_async_copy(shard, slot(at.w), local)
         own.start()
         own.wait()
-        self.last = 2 * (at.zs - 1)
+        self.last, self.ahead = 2 * (at.zs - 1), 0
+
+    def step_ahead(self):
+        self.gather.step(0)
+        self.ahead = 1
 
     def level(self, index):
         at = self.at
@@ -1050,7 +1055,7 @@
     def arrive(self, index):
         far, side, z, valid = self.level(index)
 
-        @pl.when(side == 1)
+        @pl.when((side == 1) & (far > self.ahead))
         def _():
             self.gather.step(far - 1)
 
@@ -1240,6 +1245,7 @@
             own.start()
             late.relay()
             weights.start()
+            work.step_ahead()
             own.wait()
             for load in loads:
                 load.wait()
@@ -1672,6 +1678,7 @@
         up_sum = SquareTerms(at, lambda s, h: up_t.at[s, h], up_x, up_y, up_sems, up_lasts, up_scratch)
         gate_rooms, down_rooms = (room_gate0, room_gate1), (room_down0, room_down1)
         gate_sum.second_start(fetch, gate_rooms)
+        gather.relay()
         down_sum.second_start(fetch, down_rooms)
         up_sum.second_load(fetch)
         tap_v[...] = tap_ref[...].astype(jnp.float32)
@@ -1683,7 +1690,6 @@
         query_acc[...] = jnp.zeros_like(query_acc)
         key_acc[...] = jnp.zeros_like(key_acc)
         value_acc[...] = jnp.zeros_like(value_acc)
-        gather.relay()
         gather.finish()
         gate_sum.second_go()
         down_sum.second_go()
@@ -1701,7 +1707,9 @@
             return carry
 
         lax.fori_loop(0, width // 512, out_job, 0)
-        out_sum.begin()
+        for piece in range(out_sum.pieces):
+            out_sum.offer(piece)
+        out_sum.launch_all(0)
 
         steps = length // rows_at_once
         lanes = lax.broadcasted_iota(jnp.int32, (1, 128), 1)
@@ -1761,6 +1769,25 @@
         back_sorted[:, value_width : value_width + 128] = query_acc[...].astype(jnp.bfloat16)
         back_sorted[:, value_width + 128 :] = key_acc[...].astype(jnp.bfloat16)
         back_v[...] = contract_last(back_sorted[...], order_ref[...]).astype(jnp.bfloat16)
+        qkv_sums = LinePieces(at, lambda w: qkv_parts.at[:, w], qkv_scratch)
+        qkv_rank = qkv_parts.shape[2]
+
+        def qkv_job(s, carry):
+            block = wt * qkv_rank
+            window = pl.ds(pl.multiple_of(s * block, block), block)
+            term = contract_first(hidden_v[:, window], back_v[...]).astype(jnp.bfloat16)
+            for w in range(wt):
+                qkv_parts[s, w] = term[w * qkv_rank : (w + 1) * qkv_rank]
+            qkv_sums.offer(s)
+
+            @pl.when(s > 0)
+            def _():
+                qkv_sums.launch(s - 1, 0)
+
+            return carry
+
+        lax.fori_loop(0, seq, qkv_job, 0)
+        qkv_sums.launch(seq - 1, 0)
         hidden_sum = SquareSum(at, lambda s, h: hidden_parts.at[s, h], hidden_scratch)
 
         def hidden_job(index, carry):
@@ -1774,19 +1801,7 @@
 
         lax.fori_loop(0, width // 512, hidden_job, 0)
         hidden_sum.start()
-        qkv_sums = LinePieces(at, lambda w: qkv_parts.at[:, w], qkv_scratch)
-        qkv_rank = qkv_parts.shape[2]
-
-        def qkv_job(s, carry):
-            block = wt * qkv_rank
-            window = pl.ds(pl.multiple_of(s * block, block), block)
-            term = contract_first(hidden_v[:, window], back_v[...]).astype(jnp.bfloat16)
-            for w in range(wt):
-                qkv_parts[s, w] = term[w * qkv_rank : (w + 1) * qkv_rank]
-            return carry
-
-        lax.fori_loop(0, seq, qkv_job, 0)
-        qkv_sums.begin()
+        qkv_sums.launch_all(1)
         qkv_sums.pass_on(zs - 1)
         hidden_sum.relay()
         up_sum.first_wait()
@@ -1823,12 +1838,16 @@
             )
         for copy in copies:
             copy.start()
-        qkv_sums.finish(qkv_sum)
-        for step in range(1, seq):
-            to = lax.rem(at.s + step, seq)
-            copy = send(qkv_sum.at[to], qkv_out.at[at.s], swap.at[step, 0], swap.at[at.s, 1], (to, at.w))
-            copy.start()
-            copies.append(copy)
+
+        def give(s):
+            return send(qkv_sum.at[s], qkv_out.at[at.s], swap.at[s, 0], swap.at[at.s, 1], (s, at.w))
+
+        def done(s):
+            @pl.when(s != at.s)
+            def _():
+                give(s).start()
+
+        qkv_sums.finish(qkv_sum, done)
         add_into(qkv_out.at[at.s], [qkv_sum.at[at.s]])
         out_sum.finish(w_out_out)
         terms = [spread.at[:, pl.ds(pl.multiple_of(at.s * value_width, value_width), value_width)], taps_acc]
@@ -1855,7 +1874,8 @@
         for step in range(1, seq):
             s = lax.rem(at.s + step, seq)
             slot = qkv_out.at[s]
-            send(slot, slot, swap.at[step, 0], swap.at[s, 1], at.across()).wait_recv()
+            send(slot, slot, swap.at[s, 0], swap.at[s, 1], at.across()).wait_recv()
+            give(s).wait_send()
         up_sum.second_wait()
         for copy in copies:
             copy.wait_send()
@@ -1870,7 +1890,7 @@
         [
             jax.ShapeDtypeStruct((count, width), f32),
             jax.ShapeDtypeStruct(tile, f32),
-            jax.ShapeDtypeStruct((seq, qkv_rank, qkv_width), f32),
+            jax.ShapeDtypeStruct((seq, qkv_rank, qkv_width), low),
             jax.ShapeDtypeStruct((out_rank, width), f32),
             jax.ShapeDtypeStruct((ys,) + gate_half, low),
             jax.ShapeDtypeStruct((ys, 2) + gate_half, low),
@@ -1902,7 +1922,7 @@
             pltpu.VMEM(gate_half, low),
             pltpu.VMEM(down_half, low),
             pltpu.VMEM(down_half, low),
-            pltpu.VMEM((seq, qkv_rank, qkv_width), f32),
+            pltpu.VMEM((seq, qkv_rank, qkv_width), low),
             pltpu.VMEM((seq,) + tile, f32),
             pltpu.VMEM(tile, f32),
             pltpu.VMEM((wt,) + tile, f32),
@@ -1959,10 +1979,14 @@
         copies = []
         for number, (group, room) in enumerate(zip(groups, rooms)):
             terms, from_x, from_y, last_y, last_x = group
-            sources = (terms.at[s], from_x.at[y], from_y.at[:, x], last_y, last_x)
+            pairs = [(terms.at[s], room[0]), (from_x.at[y], room[1]), (last_x, room[4])]
+            for other in range(1, ys):
+                place = lax.rem(y + other, ys)
+                pairs.append((from_y.at[place, x], room[2].at[other - 1]))
+                pairs.append((last_y.at[place], room[3].at[other - 1]))
             mine = [
                 pltpu.make_async_copy(source, target, loads.at[number, index])
-                for index, (source, target) in enumerate(zip(sources, room))
+                for index, (source, target) in enumerate(pairs)
             ]
             for copy in mine:
                 copy.start()
@@ -1983,7 +2007,7 @@
             counted = counted + length_ref[index]
         loss_out[...] = 2.0 * totals_ref[2:3, :1] / (jnp.full((1, 1), counted, jnp.int32).astype(f32) * width)
         for index in range(seq):
-            qkv_out[:, index * qkv_width : (index + 1) * qkv_width] = qkv_ref[index]
+            qkv_out[:, index * qkv_width : (index + 1) * qkv_width] = qkv_ref[index].astype(f32)
         outs = []
         for index, (room, target) in enumerate(zip(passed_rooms, passed_outs)):
             ins[index].wait()
@@ -2003,10 +2027,9 @@
                 window = pl.ds(pl.multiple_of(index * tile, tile), tile)
                 first = own[0, window, :].astype(f32) + near_x[window, :].astype(f32)
                 second = own[1, window, :].astype(f32) + last_x[window, :].astype(f32)
-                for other in range(1, ys):
-                    place = lax.rem(y + other, ys)
-                    first = first + last_y[place, window, :].astype(f32)
-                    second = second + near_y[place, window, :].astype(f32)
+                for other in range(ys - 1):
+                    first = first + last_y[other, window, :].astype(f32)
+                    second = second + near_y[other, window, :].astype(f32)
                 total[base, window, :] = first
                 total[base + 1, window, :] = second
                 return carry
@@ -2023,8 +2046,8 @@
         return [
             pltpu.VMEM((2,) + half, low),
             pltpu.VMEM(half, low),
-            pltpu.VMEM((ys,) + half, low),
-            pltpu.VMEM((ys,) + half, low),
+            pltpu.VMEM((ys - 1,) + half, low),
+            pltpu.VMEM((ys - 1,) + half, low),
             pltpu.VMEM(half, low),
         ]
 
@@ -2048,7 +2071,7 @@
         + rooms(gate_half) * 2
         + rooms(down_half)
         + [
-            pltpu.SemaphoreType.DMA((3, 5)),
+            pltpu.SemaphoreType.DMA((3, 1 + seq)),
             pltpu.SemaphoreType.DMA((3,)),
             pltpu.SemaphoreType.DMA((3, 2)),
         ],

time: 356 us -> 349 us (0.980)
  Pallas kernels: 351 us -> 344 us
    pallas_call x4, Pallas kernels: 342 us -> 336 us  [remote_call(): pl.pallas_call(kernel, name=name, out_shape=outs, in_specs=[VMEM] * len(o...]
where the time goes in v7:
time: 349 us; the launch traced here: 346 us
  Pallas kernels  344 us (99%)
    pallas_call x4, Pallas kernels, remote_call(): pl.pallas_call(kernel, name=name, out_shape=outs, in_specs=[VMEM] * len(o...  336 us
    pallas_call x1, Pallas kernels, last_sums(): pl.pallas_call(kernel, name='last_sums', out_shape=[jax.ShapeDtypeStruct(...  7.92 us

profile of v7, /device:TPU:8, one launch (start us, length us, event | category | flops | bytes accessed | tf_op | source)
XLA Modules:
  0.0 346.2 jit_solution(11717358214545698222)
XLA Ops:
  0.6 1.3 convert_add_fusion.refs_3_
  1.9 83.8 %mixer_forward.1 = (f32[128,2048]{1,0:T(8,128)}, bf16[128,2048]{1,0:T(8,128)(2,1)}, f32[8,2048]{1,0:T(8,128)}, bf16[4,8,64,640]{3,2,1,0:T(8,128)(2,1)}, bf16[8,6...) custom-call(bf16[128,2048]{1,0:T(8,128)(2,1)} %bitcast.20, ...), custom_call_target="tpu_custom_call" | custom-call | tf_op jit(solution)/shard_map/mixer_forward/pallas_call | solution.py:390
  85.7 79.9 %feed_forward.1 = (bf16[128,2048]{1,0:T(8,128)(2,1)}, f32[128,2048]{1,0:T(8,128)}, f32[8,2048]{1,0:T(8,128)}, bf16[1024,2048]{1,0:T(8,128)(2,1)}, f32[1024,704]{...) custom-call(bf16[128,2048]{1,0:T(8,128)(2,1)} %get-tuple-element.63., ...), custom_call_target="tpu_custom_call" | custom-call | tf_op jit(solution)/shard_map/feed_forward/pallas_call | solution.py:390
  165.7 75.1 %feed_back.1 = (f32[128,2048]{1,0:T(8,128)}, bf16[128,2048]{1,0:T(8,128)(2,1)}, f32[8,2048]{1,0:T(8,128)}, bf16[4,2,352,512]{3,2,1,0:T(8,128)(2,1)}, bf16[4,2,35...) custom-call(f32[128,2048]{1,0:T(8,128)} %get-tuple-element.66.refs_0, ...), custom_call_target="tpu_custom_call" | custom-call | tf_op jit(solution)/shard_map/feed_back/pallas_call | solution.py:390
  240.8 97.4 %mixer_back.1 = (f32[128,2048]{1,0:T(8,128)}, f32[8,512]{1,0:T(8,128)}, bf16[4,64,640]{2,1,0:T(8,128)(2,1)}, f32[64,2048]{1,0:T(8,128)}, bf16[2,352,512]{2,1,0:T...) custom-call(bf16[512,2048]{1,0:T(8,128)(2,1)} %bitcast.19, ...), custom_call_target="tpu_custom_call" | custom-call | tf_op jit(solution)/shard_map/mixer_back/pallas_call | solution.py:390
  338.1 7.9 %last_sums.1 = (f32[4,352,512]{2,1,0:T(8,128)}, f32[2,352,512]{2,1,0:T(8,128)}, f32[64,2560]{1,0:T(8,128)}, f32[1,64]{1,0:T(1,128)}, f32[1,64]{1,0:T(1,128)}, /*...) custom-call(bf16[4,2,352,512]{3,2,1,0:T(8,128)(2,1)} %get-tuple-elem, ...), custom_call_target="tpu_custom_call" | custom-call | tf_op jit(solution)/shard_map/last_sums/pallas_call | solution.py:2054

commit v8 on v7

--- a/solution.py
+++ b/solution.py
@@ -46,7 +46,7 @@
 VMEM = pl.BlockSpec(memory_space=pltpu.VMEM)
 ANY = pl.BlockSpec(memory_space=pl.ANY)
 SMEM = pl.BlockSpec(memory_space=pltpu.SMEM)
-VMEM_LIMIT = 63 * 1024 * 1024
+VMEM_LIMIT = 67043328
 
 
 class Place:
@@ -400,7 +400,592 @@
     )(*operands)
 
 
-def mixer_forward(tokens, qkv_rows, out_rows, gains, gate_up, segments, taps):
+def write_order(ref, heads):
+    head_width, value_width = 2 * FEAT + DV, heads * DV
+
+    def step(index, carry):
+        window = pl.ds(pl.multiple_of(index * 32, 32), 32)
+        shape = (32, ref.shape[1])
+        column = index * 32 + lax.broadcasted_iota(jnp.int32, shape, 0)
+        head = lax.div(column, head_width)
+        place = lax.rem(column, head_width)
+        target = jnp.where(
+            place < FEAT,
+            value_width + head * FEAT + place,
+            jnp.where(
+                place < 2 * FEAT, value_width + 128 + head * FEAT + place - FEAT, head * DV + place - 2 * FEAT
+            ),
+        )
+        hit = target == lax.broadcasted_iota(jnp.int32, shape, 1)
+        ref[window, :] = hit.astype(jnp.float32).astype(jnp.bfloat16)
+        return carry
+
+    lax.fori_loop(0, ref.shape[0] // 32, step, 0)
+
+
+def tap_marks(segment_column):
+    segment = segment_column[:, :1]
+    place = lax.broadcasted_iota(jnp.int32, segment_column.shape, 0)[:, :1]
+    marks = [None]
+    for tap in range(1, KCONV):
+        same = (pltpu.roll(segment_column[...], tap, 0)[:, :1] == segment) & (place >= tap)
+        marks.append(same.astype(jnp.float32))
+    return marks
+
+
+def early_rows(units):
+    return units * 3 // 4 // 16 * 16
+
+
+class LinePieces:
+    @staticmethod
+    def scratch(wt, shape, pieces):
+        zs = wt // 2
+        return [pltpu.VMEM((zs,) + shape, jnp.bfloat16)] * 3 + [pltpu.SemaphoreType.DMA((6, zs, pieces))]
+
+    def __init__(self, at, part, scratch, order=None):
+        self.at, self.part, self.order = at, part, order
+        self.pair, self.below, self.above, self.sems = scratch
+        self.pieces = self.sems.shape[2]
+        self.width = self.pair.shape[-1] // self.pieces
+
+    def cut(self, ref, piece):
+        if len(ref.shape) == 3:
+            return ref.at[piece]
+        return ref.at[:, self.columns(piece)]
+
+    def columns(self, piece):
+        block = piece if self.order is None else self.order(piece)
+        return pl.ds(pl.multiple_of(block * self.width, self.width), self.width)
+
+    def own(self, z, piece):
+        return self.cut(self.part(z * 2 + self.at.c), piece)
+
+    def over(self, z, piece):
+        return send(
+            self.cut(self.part(z * 2 + 1 - self.at.c), piece),
+            self.cut(self.pair.at[z], piece),
+            self.sems.at[0, z, piece],
+            self.sems.at[1, z, piece],
+            self.at.partner(),
+        )
+
+    def up(self, z, piece):
+        return send(
+            self.own(z, piece),
+            self.cut(self.below.at[z], piece),
+            self.sems.at[2, z, piece],
+            self.sems.at[3, z, piece],
+            self.at.level(self.at.z + 1),
+        )
+
+    def down(self, z, piece):
+        return send(
+            self.own(z, piece),
+            self.cut(self.above.at[z], piece),
+            self.sems.at[4, z, piece],
+            self.sems.at[5, z, piece],
+            self.at.level(self.at.z - 1),
+        )
+
+    def terms(self, z, piece):
+        self.over(z, piece).wait_recv()
+        return [self.own(z, piece), self.cut(self.pair.at[z], piece)]
+
+    def ends(self, z, piece):
+        at = self.at
+
+        @pl.when((at.z == 0) & (z > 0))
+        def _():
+            add_into(self.own(z, piece), self.terms(z, piece))
+            self.up(z, piece).start()
+
+        @pl.when((at.z == at.zs - 1) & (z < at.zs - 1))
+        def _():
+            add_into(self.own(z, piece), self.terms(z, piece))
+            self.down(z, piece).start()
+
+    def offer(self, piece):
+        zs = self.at.zs
+        for index in range(zs // 2):
+            self.over(index, piece).start()
+            self.over(zs - 1 - index, piece).start()
+
+    def launch(self, piece, near):
+        self.ends(jnp.where(self.at.z == 0, self.at.zs - 1 - near, near), piece)
+
+    def launch_all(self, near):
+        zs = self.at.zs
+
+        def step(index, carry):
+            self.launch(lax.rem(index, self.pieces), near + lax.div(index, self.pieces))
+            return carry
+
+        lax.fori_loop(0, (zs - 1 - near) * self.pieces, step, 0)
+
+    def pass_on(self, index, fill=None, begin=0, end=None):
+        at = self.at
+        upper = at.z * 2 >= at.zs
+        high, low = index, at.zs - 1 - index
+
+        def lower(piece, when):
+            @pl.when((at.z > low) & (at.z < at.zs - 1) & when)
+            def _():
+                terms = self.terms(low, piece)
+                self.down(low, piece).wait_recv()
+                add_into(self.own(low, piece), terms + [self.cut(self.above.at[low], piece)])
+                self.down(low, piece).start()
+
+        def step(piece, carry):
+            lower(piece, upper)
+
+            @pl.when((at.z < high) & (at.z > 0))
+            def _():
+                terms = self.terms(high, piece)
+                self.up(high, piece).wait_recv()
+                add_into(self.own(high, piece), terms + [self.cut(self.below.at[high], piece)])
+                self.up(high, piece).start()
+
+            lower(piece, jnp.logical_not(upper))
+            if fill is not None:
+                fill(piece, self.pieces)
+            return carry
+
+        end = self.pieces if end is None else end
+        if end - begin == 1:
+            step(begin, 0)
+        else:
+            lax.fori_loop(begin, end, step, 0)
+
+    def finish(self, total, done=None):
+        at = self.at
+
+        def step(piece, carry):
+            terms = self.terms(at.z, piece)
+            below, above = self.cut(self.below.at[at.z], piece), self.cut(self.above.at[at.z], piece)
+
+            @pl.when(at.z == 0)
+            def _():
+                self.down(at.z, piece).wait_recv()
+                add_into(self.cut(total, piece), terms + [above])
+
+            @pl.when(at.z == at.zs - 1)
+            def _():
+                self.up(at.z, piece).wait_recv()
+                add_into(self.cut(total, piece), terms + [below])
+
+            @pl.when((at.z > 0) & (at.z < at.zs - 1))
+            def _():
+                self.up(at.z, piece).wait_recv()
+                self.down(at.z, piece).wait_recv()
+                add_into(self.cut(total, piece), terms + [below, above])
+
+            if done is not None:
+                done(piece)
+            for z in range(at.zs):
+
+                @pl.when(at.z < z)
+                def _():
+                    self.up(z, piece).wait_send()
+
+                @pl.when(at.z > z)
+                def _():
+                    self.down(z, piece).wait_send()
+
+                self.over(z, piece).wait_send()
+            return carry
+
+        lax.fori_loop(0, self.pieces, step, 0)
+
+
+class SquareTerms:
+    @staticmethod
+    def semaphores(seq):
+        return [pltpu.SemaphoreType.DMA((seq // 2, 2)), pltpu.SemaphoreType.DMA((seq // 2, 2, 2))]
+
+    @staticmethod
+    def scratch(seq, half_shape):
+        ys = seq // 2
+        return [
+            pltpu.VMEM((ys,) + half_shape, jnp.bfloat16),
+            pltpu.VMEM(half_shape, jnp.bfloat16),
+            pltpu.SemaphoreType.DMA((ys + 1, 2)),
+        ]
+
+    def __init__(self, at, terms, from_x, from_y, sems=None, lasts=None, scratch=None):
+        self.at, self.terms, self.from_x, self.from_y = at, terms, from_x, from_y
+        if sems is not None:
+            self.xs, self.ys = sems
+        if scratch is not None:
+            self.last_y, self.last_x = lasts
+            self.sum_y, self.sum_x, self.last = scratch
+
+    def first_x(self, y):
+        at = self.at
+        return send(
+            self.terms(y * 2 + 1 - at.x, 0), self.from_x.at[y], self.xs.at[y, 0], self.xs.at[y, 1], at.across()
+        )
+
+    def first_y(self, step, x):
+        at = self.at
+        y = at.beside(step)
+        return send(
+            self.terms(y * 2 + x, 1),
+            self.from_y.at[at.y, x],
+            self.ys.at[step, x, 0],
+            self.ys.at[at.y, x, 1],
+            at.column(y),
+        )
+
+    def first_start(self):
+        for y in range(self.at.ys):
+            self.first_x(y).start()
+        for step in range(1, self.at.ys):
+            for x in range(2):
+                self.first_y(step, x).start()
+
+    def first_wait(self):
+        at = self.at
+        for y in range(at.ys):
+            self.first_x(y).wait()
+        for step in range(1, at.ys):
+            y = at.beside(step)
+            for x in range(2):
+                self.first_y(step, x).wait_send()
+                slot = self.from_y.at[y, x]
+                send(slot, slot, self.ys.at[step, x, 0], self.ys.at[y, x, 1], at.across()).wait_recv()
+
+    def second_y(self, step):
+        at = self.at
+        y = at.beside(step)
+        return send(
+            self.sum_y.at[y], self.last_y.at[at.y], self.last.at[step, 0], self.last.at[at.y, 1], at.column(y)
+        )
+
+    def second_x(self):
+        at = self.at
+        return send(self.sum_x, self.last_x, self.last.at[at.ys, 0], self.last.at[at.ys, 1], at.across())
+
+    def second_start(self, fetch, rooms):
+        at = self.at
+        for step in range(1, at.ys):
+            y = at.beside(step)
+            fetch([(self.terms(y * 2 + at.x, 0), rooms[0]), (self.from_x.at[y], rooms[1])])
+            add_into(self.sum_y.at[y], [rooms[0], rooms[1]])
+        fetch([(self.terms(at.y * 2 + 1 - at.x, 1), self.sum_x)])
+        for step in range(1, at.ys):
+            y = at.beside(step)
+            fetch([(self.from_y.at[y, 1 - at.x], rooms[0])])
+            add_into(self.sum_x, [self.sum_x, rooms[0]])
+
+    def second_load(self, fetch):
+        at = self.at
+        pairs = [(self.terms(at.y * 2 + 1 - at.x, 1), self.sum_x)]
+        for step in range(1, at.ys):
+            y = at.beside(step)
+            pairs.append((self.terms(y * 2 + at.x, 0), self.sum_y.at[y]))
+        fetch(pairs)
+
+    def second_arrived(self):
+        at = self.at
+        terms = [self.sum_x]
+        for step in range(1, at.ys):
+            y = at.beside(step)
+            add_into(self.sum_y.at[y], [self.sum_y.at[y], self.from_x.at[y]])
+            terms.append(self.from_y.at[y, 1 - at.x])
+        add_into(self.sum_x, terms)
+
+    def second_go(self):
+        for step in range(1, self.at.ys):
+            self.second_y(step).start()
+        self.second_x().start()
+
+    def second_wait(self):
+        at = self.at
+        for step in range(1, at.ys):
+            self.second_y(step).wait_send()
+            y = at.beside(step)
+            slot = self.last_y.at[y]
+            send(slot, slot, self.last.at[step, 0], self.last.at[y, 1], at.across()).wait_recv()
+        self.second_x().wait()
+
+
+def norm_back(rows, load, store, gain, terms):
+    def step(index, carry):
+        window = pl.ds(pl.multiple_of(index * 16, 16), 16)
+        values, incoming, base = load(window)
+        root = lax.rsqrt(jnp.mean(values * values, axis=-1, keepdims=True) + epsilon)
+        scaled = incoming * gain
+        share = jnp.mean(values * scaled, axis=-1, keepdims=True)
+        store(window, base + root * scaled - values * (root * root * root * share))
+        term = incoming * values * root
+        terms[...] += term[:8] + term[8:]
+        return carry
+
+    lax.fori_loop(0, rows // 16, step, 0)
+
+
+class Exchange:
+    def __init__(self, at, shard, everyone, gather_sems, local, sums, first, second):
+        self.at, self.sums, self.first, self.second = at, sums, first, second
+        count = shard.shape[0]
+        slot = lambda w: everyone.at[pl.ds(pl.multiple_of(w * count, count), count)]
+        self.gather = LineGather(at, slot, gather_sems)
+        self.gather.start(shard)
+        own = pltpu.make_async_copy(shard, slot(at.w), local)
+        own.start()
+        own.wait()
+        self.last, self.ahead = 2 * (at.zs - 1), 0
+
+    def step_ahead(self):
+        self.gather.step(0)
+        self.ahead = 1
+
+    def level(self, index):
+        at = self.at
+        far, side = lax.div(index + 1, 2), lax.rem(index, 2)
+        z = at.z + jnp.where(side == 1, -far, far)
+        return far, side, z, (z >= 0) & (z < at.zs)
+
+    def arrive(self, index):
+        far, side, z, valid = self.level(index)
+
+        @pl.when((side == 1) & (far > self.ahead))
+        def _():
+            self.gather.step(far - 1)
+
+        @pl.when(valid)
+        def _():
+            self.gather.wait_over(z)
+            self.first(z)
+
+        return z, valid
+
+    def put(self, z, begin, end):
+        def step(piece, inner):
+            self.second(z, piece)
+            self.sums.over(z, piece).start()
+
+            @pl.when(piece > begin)
+            def _():
+                self.sums.ends(z, piece - 1)
+
+            return inner
+
+        lax.fori_loop(begin, end, step, 0)
+        self.sums.ends(z, end - 1)
+
+    def whole(self, total, fill):
+        at, sums = self.at, self.sums
+
+        def turn(index, carry):
+            z, valid = self.arrive(index)
+
+            @pl.when(valid)
+            def _():
+                self.put(z, 0, sums.pieces)
+
+            return carry
+
+        lax.fori_loop(0, self.last + 1, turn, 0)
+        fill(None, sums.pieces)
+        for index in range(2, at.zs):
+            sums.pass_on(index, fill if index == 2 else None)
+        sums.finish(total)
+        self.gather.sent()
+
+    def by_columns(self, total, direct, relayed, near):
+        at, sums = self.at, self.sums
+        begin = min(3, self.last)
+
+        def turn(index, carry):
+            z, valid = self.arrive(index)
+
+            @pl.when(index == begin)
+            def _():
+                direct()
+
+            @pl.when(valid & (index >= begin))
+            def _():
+                self.put(z, 0, near)
+
+            return carry
+
+        lax.fori_loop(0, self.last + 1, turn, 0)
+
+        def earlier(index, carry):
+            _, _, z, valid = self.level(index)
+
+            @pl.when(valid)
+            def _():
+                self.put(z, 0, near)
+
+            return carry
+
+        lax.fori_loop(1, begin, earlier, 0)
+        if at.zs > 2:
+            sums.pass_on(2, None, 0, near)
+        relayed()
+
+        def over(index, carry):
+            _, _, z, valid = self.level(self.last - index)
+
+            @pl.when(valid)
+            def _():
+                for piece in range(near, sums.pieces):
+                    self.second(z, piece)
+                    sums.over(z, piece).start()
+
+            return carry
+
+        lax.fori_loop(0, self.last, over, 0)
+
+        def start(index, carry):
+            _, _, z, valid = self.level(self.last - index)
+
+            @pl.when(valid)
+            def _():
+                for piece in range(near, sums.pieces):
+                    sums.ends(z, piece)
+
+            return carry
+
+        lax.fori_loop(0, self.last, start, 0)
+        self.put(at.z, 0, sums.pieces)
+        for index in range(3, at.zs):
+            sums.pass_on(index, None, 0, near)
+        for index in range(at.zs - 1, 1, -1):
+            sums.pass_on(index, None, near, sums.pieces)
+        sums.finish(total)
+        self.gather.sent()
+
+
+PIECES = 2
+
+
+def feed_forward(at, sizes, inputs, outputs, scratch):
+    count, width, units, block, columns = sizes
+    early, half, zs, seq = early_rows(units), units // 2, at.zs, at.seq
+    normed_ref, attended_ref, teacher_ref, length_ref, gate_shard_ref, shard_ref = inputs
+    (final_out, error_out, energy_out), outputs = outputs[:3], outputs[3:]
+    normed_out, gate_out, up_out, active_out, down_out, gates_out = outputs
+    everyone, gates, downs, gate_all, up_all, active_all, parts, total = scratch[:8]
+    gather_sems, sum_scratch, late_sems, square_sems, (local, outgoing) = (
+        scratch[8:9],
+        scratch[9:13],
+        scratch[13:16],
+        scratch[16:19],
+        scratch[19:],
+    )
+    late = SquareGather(
+        at,
+        lambda s, h: gates.at[
+            h, pl.ds(early, units - early), pl.ds(pl.multiple_of(s * block, block), block)
+        ],
+        lambda h: gate_shard_ref.at[h, pl.ds(early, units - early)],
+        late_sems,
+    )
+    weights = SquareGather(
+        at,
+        lambda s, h: downs.at[
+            pl.ds(h * half, half), pl.ds(pl.multiple_of(s * columns, columns), columns)
+        ],
+        lambda h: shard_ref.at[pl.ds(h * half, half)],
+        square_sems,
+    )
+    ys = seq // 2
+
+    def column_block(piece):
+        if isinstance(piece, int):
+            step = 0 if piece < 2 else piece - 1 if piece <= ys else piece - ys
+            return at.beside(step) * 2 + (1 - at.x if piece == 1 or piece > ys else at.x)
+        step = jnp.where(piece < 2, 0, jnp.where(piece <= ys, piece - 1, piece - ys))
+        other = (piece == 1) | (piece > ys)
+        return at.beside(step) * 2 + jnp.where(other, 1 - at.x, at.x)
+
+    sums = LinePieces(
+        at,
+        lambda w: parts.at[pl.ds(pl.multiple_of(w * count, count), count)],
+        sum_scratch,
+        column_block,
+    )
+    down_store = pltpu.make_async_copy(downs, down_out, local.at[2])
+    gates_store = pltpu.make_async_copy(gates, gates_out, local.at[0])
+
+    def direct():
+        weights.relay()
+        weights.direct()
+
+    def relayed():
+        weights.relayed()
+        down_store.start()
+
+    def rows(z):
+        return pl.ds(pl.multiple_of(z * 2 * count, 2 * count), 2 * count)
+
+    def stores(z):
+        return [
+            pltpu.make_async_copy(source.at[rows(z)], target.at[rows(z)], outgoing.at[index, z])
+            for index, (source, target) in enumerate(
+                ((everyone, normed_out), (gate_all, gate_out), (up_all, up_out), (active_all, active_out))
+            )
+        ]
+
+    def first(z):
+        here = everyone[rows(z), :]
+        gate = contract_last(here, gates[0])
+        up = contract_last(here, gates[1])
+        gate_all[rows(z), :] = gate
+        up_all[rows(z), :] = up
+        active_all[rows(z), :] = gated_unit(gate, up).astype(jnp.bfloat16)
+        for copy in stores(z):
+            copy.start()
+
+    def second(z, piece):
+        window = sums.columns(piece)
+        parts[rows(z), window] = jnp.dot(
+            active_all[rows(z), :], downs[:, window], preferred_element_type=jnp.float32
+        ).astype(jnp.bfloat16)
+
+    def run():
+        work = Exchange(at, normed_ref, everyone, gather_sems, local.at[1], sums, first, second)
+        late.relay()
+        weights.start()
+        own = pltpu.make_async_copy(
+            shard_ref, downs.at[:, pl.ds(pl.multiple_of(at.s * columns, columns), columns)], local.at[3]
+        )
+        own.start()
+        work.step_ahead()
+        own.wait()
+        late.finish()
+        gates_store.start()
+        work.by_columns(total, direct, relayed, ys + 1)
+        energy_out[...] = jnp.zeros_like(energy_out)
+        valid = length_ref[at.w]
+
+        def finish_rows(index, carry):
+            window = pl.ds(pl.multiple_of(index * 16, 16), 16)
+            final = attended_ref[window, :] + total[window, :]
+            final_out[window, :] = final.astype(jnp.bfloat16)
+            place = at.s * count + index * 16 + lax.broadcasted_iota(jnp.int32, final.shape, 0)
+            keep = (place < valid).astype(jnp.float32)
+            error = (final - teacher_ref[window, :].astype(jnp.float32)) * keep
+            error_out[window, :] = error
+            squares = error * error
+            energy_out[...] += 0.5 * (squares[:8] + squares[8:])
+            return carry
+
+        lax.fori_loop(0, count // 16, finish_rows, 0)
+        down_store.wait()
+        gates_store.wait()
+        for z in range(zs):
+            for copy in stores(z):
+                copy.wait()
+
+    return late.start, run
+
+
+def forward_pass(tokens, qkv_rows, out_rows, gains, segments, taps, teacher, down, lengths, gate_up):
     seq, wt = lax.axis_size("seq"), lax.axis_size("wt")
     zs = wt // 2
     count, width = tokens.shape
@@ -421,27 +1006,40 @@
         gains,
         segments,
         taps,
+        teacher,
+        down,
     ]
+    token_count = wt * count
 
     def kernel(*refs):
-        (x_ref, qkv_ref, out_ref, gain_ref, segment_ref, tap_ref), refs = refs[:6], refs[6:]
-        gate_up_ref, refs = refs[0], refs[1:]
+        (x_ref, qkv_ref, out_ref, gain_ref, segment_ref, tap_ref, teacher_ref, down_ref), refs = refs[:8], refs[8:]
+        (length_ref, gate_up_ref), refs = refs[:2], refs[2:]
         (attended_out, normed_out, gain_rows), refs = refs[:3], refs[3:]
-        (qkv_out, w_out_out, hidden_out, sorted_out, mixer_out, values_out, outputs_out, gates_out, order_out), refs = (
-            refs[:9],
-            refs[9:],
+        (qkv_out, w_out_out, hidden_out, sorted_out, mixer_out, values_out, outputs_out, order_out), refs = (
+            refs[:8],
+            refs[8:],
         )
-        (xs, qkvs, outs, gains_all, hidden_v, sorted_v, mixer_v, values_v, outputs_v, parts, total, room), refs = (
-            refs[:12],
-            refs[12:],
-        )
+        feed_outputs, refs = refs[:9], refs[9:]
+        (xs, qkvs, outs, gains_all, sorted_v, values_v, outputs_v), refs = refs[:7], refs[7:]
         (order_v, segment_column, tap_v), refs = refs[:3], refs[3:]
         sum_scratch, x_sems, gate_sems, refs = refs[:8], refs[8:11], refs[11:14], refs[14:]
         line_sems, refs = [refs[index : index + 1] for index in range(3)], refs[3:]
-        swap_q, swap_g, local, outgoing = refs
+        (swap_q, swap_g, local, outgoing), feed_scratch = refs[:4], refs[4:]
         at = Place(seq, wt)
-        room_load = pltpu.make_async_copy(gate_up_ref.at[:, pl.ds(0, early)], room, local.at[4])
-        room_load.start()
+        gates_ref, parts, total = feed_scratch[1], feed_scratch[6], feed_scratch[7]
+        hidden_v = parts.at[pl.ds(length, length)]
+        mixer_v = feed_scratch[5].at[pl.ds(0, length), pl.ds(0, value_width)]
+        gates_own = pltpu.make_async_copy(
+            gate_up_ref, gates_ref.at[:, :, pl.ds(pl.multiple_of(at.s * block, block), block)], local.at[4]
+        )
+        gates_own.start()
+        late_start, feed = feed_forward(
+            at,
+            (count, width, units, block, down.shape[1]),
+            (normed_out, attended_out, teacher_ref, length_ref, gate_up_ref, down_ref),
+            feed_outputs,
+            feed_scratch,
+        )
         at.meet(True, True)
         half = count // 2
         gather_x = SquareGather(
@@ -457,7 +1055,7 @@
         gather_o = LineGather(at, lambda w: outs.at[w], line_sems[2])
         gates = SquareGather(
             at,
-            lambda s, h: gates_out.at[h, :, pl.ds(pl.multiple_of(s * block, block), block)],
+            lambda s, h: gates_ref.at[h, pl.ds(0, early), pl.ds(pl.multiple_of(s * block, block), block)],
             lambda h: gate_up_ref.at[h, pl.ds(0, early)],
             gate_sems,
         )
@@ -490,11 +1088,6 @@
             copy.start()
         for copy in own:
             copy.wait()
-        room_load.wait()
-        room_store = pltpu.make_async_copy(
-            room, gates_out.at[:, :, pl.ds(pl.multiple_of(at.s * block, block), block)], local.at[4]
-        )
-        room_store.start()
         for step in range(1, seq):
             s = lax.rem(at.s + step, seq)
             slot = gains_all.at[s, gain_slot]
@@ -625,37 +1218,43 @@
             for s in range(seq):
                 for h in range(2):
                     begin = s * count + h * half
-                    parts[s, h, :, window] = term[begin : begin + half]
+                    parts[begin : begin + half, window] = term[begin : begin + half]
             return carry
 
         lax.fori_loop(0, width // 512, out_job, 0)
-        work = SquareSum(at, lambda s, h: parts.at[s, h], sum_scratch)
+        work = SquareSum(
+            at, lambda s, h: parts.at[pl.ds(pl.multiple_of(s * count + h * half, half), half)], sum_scratch
+        )
         work.start()
         work.relay()
-        work.finish(lambda h: total.at[h])
+        late_start()
+        work.finish(lambda h: total.at[pl.ds(h * half, half)])
 
         def finish_rows(index, carry):
             for h in range(2):
-                window = pl.ds(pl.multiple_of(index * 16, 16), 16)
                 rows = pl.ds(pl.multiple_of(h * half + index * 16, 16), 16)
-                attended = x_ref[rows, :].astype(jnp.float32) + total[h, window, :]
+                attended = x_ref[rows, :].astype(jnp.float32) + total[rows, :]
                 attended_out[rows, :] = attended
                 normed_out[rows, :] = rms_norm(attended, gain_rows[1:2, :]).astype(jnp.bfloat16)
             return carry
 
         lax.fori_loop(0, half // 16, finish_rows, 0)
         gates.finish()
-        room_store.wait()
+        gates_own.wait()
+        stores[1].wait()
+        stores[5].wait()
+        feed()
         for copy in swaps:
             copy.wait_send()
-        for copy in stores:
-            copy.wait()
+        for index, copy in enumerate(stores):
+            if index not in (1, 5):
+                copy.wait()
 
     low, f32 = jnp.bfloat16, jnp.float32
     sorted_width = value_width + 256
     return remote_call(
         kernel,
-        "mixer_forward",
+        "forward_pass",
         0,
         [
             jax.ShapeDtypeStruct((count, width), f32),
@@ -668,22 +1267,25 @@
             jax.ShapeDtypeStruct((length, value_width), low),
             jax.ShapeDtypeStruct((heads, length, DV), low),
             jax.ShapeDtypeStruct((heads, length, DV), f32),
-            jax.ShapeDtypeStruct((2, early, width), low),
             jax.ShapeDtypeStruct((qkv_width, sorted_width), low),
+            jax.ShapeDtypeStruct((count, width), low),
+            jax.ShapeDtypeStruct((count, width), f32),
+            jax.ShapeDtypeStruct((8, width), f32),
+            jax.ShapeDtypeStruct((token_count, width), low),
+            jax.ShapeDtypeStruct((token_count, units), f32),
+            jax.ShapeDtypeStruct((token_count, units), f32),
+            jax.ShapeDtypeStruct((token_count, units), low),
+            jax.ShapeDtypeStruct((units, width), low),
+            jax.ShapeDtypeStruct((2, units, width), low),
         ],
         [
             pltpu.VMEM((length, width), low),
             pltpu.VMEM((seq, wt, qkv_rank, qkv_width), low),
             pltpu.VMEM((wt, out_rank, width), low),
             pltpu.VMEM((seq, wt * 8, 128), f32),
-            pltpu.VMEM((length, width), low),
             pltpu.VMEM((length, sorted_width), low),
-            pltpu.VMEM((length, value_width), low),
             pltpu.VMEM((heads, length, DV), low),
             pltpu.VMEM((heads, length, DV), f32),
-            pltpu.VMEM((seq, 2, count // 2, width), low),
-            pltpu.VMEM((2, count // 2, width), f32),
-            pltpu.VMEM((2, early, block), low),
             pltpu.VMEM((qkv_width, sorted_width), low),
             pltpu.VMEM((length, 128), f32),
             pltpu.VMEM((KCONV, value_width), f32),
@@ -697,645 +1299,13 @@
             pltpu.SemaphoreType.DMA((seq, 2)),
             pltpu.SemaphoreType.DMA((5,)),
             pltpu.SemaphoreType.DMA((8,)),
-        ],
-        *small,
-        gate_up,
-        in_specs=[VMEM] * len(small) + [ANY],
-        out_specs=[VMEM] * 3 + [ANY] * 9,
-    )
-
-
-def write_order(ref, heads):
-    head_width, value_width = 2 * FEAT + DV, heads * DV
-
-    def step(index, carry):
-        window = pl.ds(pl.multiple_of(index * 32, 32), 32)
-        shape = (32, ref.shape[1])
-        column = index * 32 + lax.broadcasted_iota(jnp.int32, shape, 0)
-        head = lax.div(column, head_width)
-        place = lax.rem(column, head_width)
-        target = jnp.where(
-            place < FEAT,
-            value_width + head * FEAT + place,
-            jnp.where(
-                place < 2 * FEAT, value_width + 128 + head * FEAT + place - FEAT, head * DV + place - 2 * FEAT
-            ),
-        )
-        hit = target == lax.broadcasted_iota(jnp.int32, shape, 1)
-        ref[window, :] = hit.astype(jnp.float32).astype(jnp.bfloat16)
-        return carry
-
-    lax.fori_loop(0, ref.shape[0] // 32, step, 0)
-
-
-def tap_marks(segment_column):
-    segment = segment_column[:, :1]
-    place = lax.broadcasted_iota(jnp.int32, segment_column.shape, 0)[:, :1]
-    marks = [None]
-    for tap in range(1, KCONV):
-        same = (pltpu.roll(segment_column[...], tap, 0)[:, :1] == segment) & (place >= tap)
-        marks.append(same.astype(jnp.float32))
-    return marks
-
-
-def early_rows(units):
-    return units * 3 // 4 // 16 * 16
-
-
-class LinePieces:
-    @staticmethod
-    def scratch(wt, shape, pieces):
-        zs = wt // 2
-        return [pltpu.VMEM((zs,) + shape, jnp.bfloat16)] * 3 + [pltpu.SemaphoreType.DMA((6, zs, pieces))]
-
-    def __init__(self, at, part, scratch, order=None):
-        self.at, self.part, self.order = at, part, order
-        self.pair, self.below, self.above, self.sems = scratch
-        self.pieces = self.sems.shape[2]
-        self.width = self.pair.shape[-1] // self.pieces
-
-    def cut(self, ref, piece):
-        if len(ref.shape) == 3:
-            return ref.at[piece]
-        return ref.at[:, self.columns(piece)]
-
-    def columns(self, piece):
-        block = piece if self.order is None else self.order(piece)
-        return pl.ds(pl.multiple_of(block * self.width, self.width), self.width)
-
-    def own(self, z, piece):
-        return self.cut(self.part(z * 2 + self.at.c), piece)
-
-    def over(self, z, piece):
-        return send(
-            self.cut(self.part(z * 2 + 1 - self.at.c), piece),
-            self.cut(self.pair.at[z], piece),
-            self.sems.at[0, z, piece],
-            self.sems.at[1, z, piece],
-            self.at.partner(),
-        )
-
-    def up(self, z, piece):
-        return send(
-            self.own(z, piece),
-            self.cut(self.below.at[z], piece),
-            self.sems.at[2, z, piece],
-            self.sems.at[3, z, piece],
-            self.at.level(self.at.z + 1),
-        )
-
-    def down(self, z, piece):
-        return send(
-            self.own(z, piece),
-            self.cut(self.above.at[z], piece),
-            self.sems.at[4, z, piece],
-            self.sems.at[5, z, piece],
-            self.at.level(self.at.z - 1),
-        )
-
-    def terms(self, z, piece):
-        self.over(z, piece).wait_recv()
-        return [self.own(z, piece), self.cut(self.pair.at[z], piece)]
-
-    def ends(self, z, piece):
-        at = self.at
-
-        @pl.when((at.z == 0) & (z > 0))
-        def _():
-            add_into(self.own(z, piece), self.terms(z, piece))
-            self.up(z, piece).start()
-
-        @pl.when((at.z == at.zs - 1) & (z < at.zs - 1))
-        def _():
-            add_into(self.own(z, piece), self.terms(z, piece))
-            self.down(z, piece).start()
-
-    def offer(self, piece):
-        zs = self.at.zs
-        for index in range(zs // 2):
-            self.over(index, piece).start()
-            self.over(zs - 1 - index, piece).start()
-
-    def launch(self, piece, near):
-        self.ends(jnp.where(self.at.z == 0, self.at.zs - 1 - near, near), piece)
-
-    def launch_all(self, near):
-        zs = self.at.zs
-
-        def step(index, carry):
-            self.launch(lax.rem(index, self.pieces), near + lax.div(index, self.pieces))
-            return carry
-
-        lax.fori_loop(0, (zs - 1 - near) * self.pieces, step, 0)
-
-    def pass_on(self, index, fill=None, begin=0, end=None):
-        at = self.at
-        upper = at.z * 2 >= at.zs
-        high, low = index, at.zs - 1 - index
-
-        def lower(piece, when):
-            @pl.when((at.z > low) & (at.z < at.zs - 1) & when)
-            def _():
-                terms = self.terms(low, piece)
-                self.down(low, piece).wait_recv()
-                add_into(self.own(low, piece), terms + [self.cut(self.above.at[low], piece)])
-                self.down(low, piece).start()
-
-        def step(piece, carry):
-            lower(piece, upper)
-
-            @pl.when((at.z < high) & (at.z > 0))
-            def _():
-                terms = self.terms(high, piece)
-                self.up(high, piece).wait_recv()
-                add_into(self.own(high, piece), terms + [self.cut(self.below.at[high], piece)])
-                self.up(high, piece).start()
-
-            lower(piece, jnp.logical_not(upper))
-            if fill is not None:
-                fill(piece, self.pieces)
-            return carry
-
-        end = self.pieces if end is None else end
-        if end - begin == 1:
-            step(begin, 0)
-        else:
-            lax.fori_loop(begin, end, step, 0)
-
-    def finish(self, total, done=None):
-        at = self.at
-
-        def step(piece, carry):
-            terms = self.terms(at.z, piece)
-            below, above = self.cut(self.below.at[at.z], piece), self.cut(self.above.at[at.z], piece)
-
-            @pl.when(at.z == 0)
-            def _():
-                self.down(at.z, piece).wait_recv()
-                add_into(self.cut(total, piece), terms + [above])
-
-            @pl.when(at.z == at.zs - 1)
-            def _():
-                self.up(at.z, piece).wait_recv()
-                add_into(self.cut(total, piece), terms + [below])
-
-            @pl.when((at.z > 0) & (at.z < at.zs - 1))
-            def _():
-                self.up(at.z, piece).wait_recv()
-                self.down(at.z, piece).wait_recv()
-                add_into(self.cut(total, piece), terms + [below, above])
-
-            if done is not None:
-                done(piece)
-            for z in range(at.zs):
-
-                @pl.when(at.z < z)
-                def _():
-                    self.up(z, piece).wait_send()
-
-                @pl.when(at.z > z)
-                def _():
-                    self.down(z, piece).wait_send()
-
-                self.over(z, piece).wait_send()
-            return carry
-
-        lax.fori_loop(0, self.pieces, step, 0)
-
-
-class SquareTerms:
-    @staticmethod
-    def semaphores(seq):
-        return [pltpu.SemaphoreType.DMA((seq // 2, 2)), pltpu.SemaphoreType.DMA((seq // 2, 2, 2))]
-
-    @staticmethod
-    def scratch(seq, half_shape):
-        ys = seq // 2
-        return [
-            pltpu.VMEM((ys,) + half_shape, jnp.bfloat16),
-            pltpu.VMEM(half_shape, jnp.bfloat16),
-            pltpu.SemaphoreType.DMA((ys + 1, 2)),
-        ]
-
-    def __init__(self, at, terms, from_x, from_y, sems=None, lasts=None, scratch=None):
-        self.at, self.terms, self.from_x, self.from_y = at, terms, from_x, from_y
-        if sems is not None:
-            self.xs, self.ys = sems
-        if scratch is not None:
-            self.last_y, self.last_x = lasts
-            self.sum_y, self.sum_x, self.last = scratch
-
-    def first_x(self, y):
-        at = self.at
-        return send(
-            self.terms(y * 2 + 1 - at.x, 0), self.from_x.at[y], self.xs.at[y, 0], self.xs.at[y, 1], at.across()
-        )
-
-    def first_y(self, step, x):
-        at = self.at
-        y = at.beside(step)
-        return send(
-            self.terms(y * 2 + x, 1),
-            self.from_y.at[at.y, x],
-            self.ys.at[step, x, 0],
-            self.ys.at[at.y, x, 1],
-            at.column(y),
-        )
-
-    def first_start(self):
-        for y in range(self.at.ys):
-            self.first_x(y).start()
-        for step in range(1, self.at.ys):
-            for x in range(2):
-                self.first_y(step, x).start()
-
-    def first_wait(self):
-        at = self.at
-        for y in range(at.ys):
-            self.first_x(y).wait()
-        for step in range(1, at.ys):
-            y = at.beside(step)
-            for x in range(2):
-                self.first_y(step, x).wait_send()
-                slot = self.from_y.at[y, x]
-                send(slot, slot, self.ys.at[step, x, 0], self.ys.at[y, x, 1], at.across()).wait_recv()
-
-    def second_y(self, step):
-        at = self.at
-        y = at.beside(step)
-        return send(
-            self.sum_y.at[y], self.last_y.at[at.y], self.last.at[step, 0], self.last.at[at.y, 1], at.column(y)
-        )
-
-    def second_x(self):
-        at = self.at
-        return send(self.sum_x, self.last_x, self.last.at[at.ys, 0], self.last.at[at.ys, 1], at.across())
-
-    def second_start(self, fetch, rooms):
-        at = self.at
-        for step in range(1, at.ys):
-            y = at.beside(step)
-            fetch([(self.terms(y * 2 + at.x, 0), rooms[0]), (self.from_x.at[y], rooms[1])])
-            add_into(self.sum_y.at[y], [rooms[0], rooms[1]])
-        fetch([(self.terms(at.y * 2 + 1 - at.x, 1), self.sum_x)])
-        for step in range(1, at.ys):
-            y = at.beside(step)
-            fetch([(self.from_y.at[y, 1 - at.x], rooms[0])])
-            add_into(self.sum_x, [self.sum_x, rooms[0]])
-
-    def second_load(self, fetch):
-        at = self.at
-        pairs = [(self.terms(at.y * 2 + 1 - at.x, 1), self.sum_x)]
-        for step in range(1, at.ys):
-            y = at.beside(step)
-            pairs.append((self.terms(y * 2 + at.x, 0), self.sum_y.at[y]))
-        fetch(pairs)
-
-    def second_arrived(self):
-        at = self.at
-        terms = [self.sum_x]
-        for step in range(1, at.ys):
-            y = at.beside(step)
-            add_into(self.sum_y.at[y], [self.sum_y.at[y], self.from_x.at[y]])
-            terms.append(self.from_y.at[y, 1 - at.x])
-        add_into(self.sum_x, terms)
-
-    def second_go(self):
-        for step in range(1, self.at.ys):
-            self.second_y(step).start()
-        self.second_x().start()
-
-    def second_wait(self):
-        at = self.at
-        for step in range(1, at.ys):
-            self.second_y(step).wait_send()
-            y = at.beside(step)
-            slot = self.last_y.at[y]
-            send(slot, slot, self.last.at[step, 0], self.last.at[y, 1], at.across()).wait_recv()
-        self.second_x().wait()
-
-
-def norm_back(rows, load, store, gain, terms):
-    def step(index, carry):
-        window = pl.ds(pl.multiple_of(index * 16, 16), 16)
-        values, incoming, base = load(window)
-        root = lax.rsqrt(jnp.mean(values * values, axis=-1, keepdims=True) + epsilon)
-        scaled = incoming * gain
-        share = jnp.mean(values * scaled, axis=-1, keepdims=True)
-        store(window, base + root * scaled - values * (root * root * root * share))
-        term = incoming * values * root
-        terms[...] += term[:8] + term[8:]
-        return carry
-
-    lax.fori_loop(0, rows // 16, step, 0)
-
-
-class Exchange:
-    def __init__(self, at, shard, everyone, gather_sems, local, sums, first, second):
-        self.at, self.sums, self.first, self.second = at, sums, first, second
-        count = shard.shape[0]
-        slot = lambda w: everyone.at[pl.ds(pl.multiple_of(w * count, count), count)]
-        self.gather = LineGather(at, slot, gather_sems)
-        self.gather.start(shard)
-        own = pltpu.make_async_copy(shard, slot(at.w), local)
-        own.start()
-        own.wait()
-        self.last, self.ahead = 2 * (at.zs - 1), 0
-
-    def step_ahead(self):
-        self.gather.step(0)
-        self.ahead = 1
-
-    def level(self, index):
-        at = self.at
-        far, side = lax.div(index + 1, 2), lax.rem(index, 2)
-        z = at.z + jnp.where(side == 1, -far, far)
-        return far, side, z, (z >= 0) & (z < at.zs)
-
-    def arrive(self, index):
-        far, side, z, valid = self.level(index)
-
-        @pl.when((side == 1) & (far > self.ahead))
-        def _():
-            self.gather.step(far - 1)
-
-        @pl.when(valid)
-        def _():
-            self.gather.wait_over(z)
-            self.first(z)
-
-        return z, valid
-
-    def put(self, z, begin, end):
-        def step(piece, inner):
-            self.second(z, piece)
-            self.sums.over(z, piece).start()
-
-            @pl.when(piece > begin)
-            def _():
-                self.sums.ends(z, piece - 1)
-
-            return inner
-
-        lax.fori_loop(begin, end, step, 0)
-        self.sums.ends(z, end - 1)
-
-    def whole(self, total, fill):
-        at, sums = self.at, self.sums
-
-        def turn(index, carry):
-            z, valid = self.arrive(index)
-
-            @pl.when(valid)
-            def _():
-                self.put(z, 0, sums.pieces)
-
-            return carry
-
-        lax.fori_loop(0, self.last + 1, turn, 0)
-        fill(None, sums.pieces)
-        for index in range(2, at.zs):
-            sums.pass_on(index, fill if index == 2 else None)
-        sums.finish(total)
-        self.gather.sent()
-
-    def by_columns(self, total, direct, relayed, near):
-        at, sums = self.at, self.sums
-        begin = min(3, self.last)
-
-        def turn(index, carry):
-            z, valid = self.arrive(index)
-
-            @pl.when(index == begin)
-            def _():
-                direct()
-
-            @pl.when(valid & (index >= begin))
-            def _():
-                self.put(z, 0, near)
-
-            return carry
-
-        lax.fori_loop(0, self.last + 1, turn, 0)
-
-        def earlier(index, carry):
-            _, _, z, valid = self.level(index)
-
-            @pl.when(valid)
-            def _():
-                self.put(z, 0, near)
-
-            return carry
-
-        lax.fori_loop(1, begin, earlier, 0)
-        if at.zs > 2:
-            sums.pass_on(2, None, 0, near)
-        relayed()
-
-        def over(index, carry):
-            _, _, z, valid = self.level(self.last - index)
-
-            @pl.when(valid)
-            def _():
-                for piece in range(near, sums.pieces):
-                    self.second(z, piece)
-                    sums.over(z, piece).start()
-
-            return carry
-
-        lax.fori_loop(0, self.last, over, 0)
-
-        def start(index, carry):
-            _, _, z, valid = self.level(self.last - index)
-
-            @pl.when(valid)
-            def _():
-                for piece in range(near, sums.pieces):
-                    sums.ends(z, piece)
-
-            return carry
-
-        lax.fori_loop(0, self.last, start, 0)
-        self.put(at.z, 0, sums.pieces)
-        for index in range(3, at.zs):
-            sums.pass_on(index, None, 0, near)
-        for index in range(at.zs - 1, 1, -1):
-            sums.pass_on(index, None, near, sums.pieces)
-        sums.finish(total)
-        self.gather.sent()
-
-
-PIECES = 2
-
-
-def feed_forward(normed, attended, teacher, lengths, gate_early, gate_up_shard, down_shard):
-    seq, wt = lax.axis_size("seq"), lax.axis_size("wt")
-    count, width = normed.shape
-    units, block = gate_up_shard.shape[1:]
-    early = early_rows(units)
-    columns = down_shard.shape[1]
-    tokens = wt * count
-    zs = wt // 2
-    half = units // 2
-
-    def kernel(*refs):
-        (normed_ref, attended_ref, teacher_ref, length_ref, early_ref, gate_shard_ref, shard_ref), refs = refs[:7], refs[7:]
-        (final_out, error_out, energy_out), refs = refs[:3], refs[3:]
-        (normed_out, gate_out, up_out, active_out, down_out, gates_out), refs = refs[:6], refs[6:]
-        (everyone, gates, downs, gate_all, up_all, active_all, parts, total), refs = refs[:8], refs[8:]
-        gather_sems, sum_scratch, late_sems, square_sems, (local, outgoing) = (
-            refs[:1],
-            refs[1:5],
-            refs[5:8],
-            refs[8:11],
-            refs[11:],
-        )
-        at = Place(seq, wt)
-        loads = [
-            pltpu.make_async_copy(early_ref, gates.at[:, pl.ds(0, early)], local.at[4]),
-            pltpu.make_async_copy(
-                gate_shard_ref.at[:, pl.ds(early, units - early)],
-                gates.at[:, pl.ds(early, units - early), pl.ds(pl.multiple_of(at.s * block, block), block)],
-                local.at[0],
-            ),
-        ]
-        for load in loads:
-            load.start()
-        at.meet(True, True)
-        late = SquareGather(
-            at,
-            lambda s, h: gates.at[
-                h, pl.ds(early, units - early), pl.ds(pl.multiple_of(s * block, block), block)
-            ],
-            lambda h: gate_shard_ref.at[h, pl.ds(early, units - early)],
-            late_sems,
-        )
-        weights = SquareGather(
-            at,
-            lambda s, h: downs.at[
-                pl.ds(h * half, half), pl.ds(pl.multiple_of(s * columns, columns), columns)
-            ],
-            lambda h: shard_ref.at[pl.ds(h * half, half)],
-            square_sems,
-        )
-        ys = seq // 2
-
-        def column_block(piece):
-            if isinstance(piece, int):
-                step = 0 if piece < 2 else piece - 1 if piece <= ys else piece - ys
-                return at.beside(step) * 2 + (1 - at.x if piece == 1 or piece > ys else at.x)
-            step = jnp.where(piece < 2, 0, jnp.where(piece <= ys, piece - 1, piece - ys))
-            other = (piece == 1) | (piece > ys)
-            return at.beside(step) * 2 + jnp.where(other, 1 - at.x, at.x)
-
-        sums = LinePieces(
-            at,
-            lambda w: parts.at[pl.ds(pl.multiple_of(w * count, count), count)],
-            sum_scratch,
-            column_block,
-        )
-        down_store = pltpu.make_async_copy(downs, down_out, local.at[2])
-        gates_store = pltpu.make_async_copy(gates, gates_out, local.at[0])
-
-        def prepare():
-            late.start()
-            own = pltpu.make_async_copy(
-                shard_ref, downs.at[:, pl.ds(pl.multiple_of(at.s * columns, columns), columns)], local.at[3]
-            )
-            own.start()
-            late.relay()
-            weights.start()
-            work.step_ahead()
-            own.wait()
-            for load in loads:
-                load.wait()
-            late.finish()
-            gates_store.start()
-
-        def direct():
-            weights.relay()
-            weights.direct()
-
-        def relayed():
-            weights.relayed()
-            down_store.start()
-
-        def rows(z):
-            return pl.ds(pl.multiple_of(z * 2 * count, 2 * count), 2 * count)
-
-        def stores(z):
-            return [
-                pltpu.make_async_copy(source.at[rows(z)], target.at[rows(z)], outgoing.at[index, z])
-                for index, (source, target) in enumerate(
-                    ((everyone, normed_out), (gate_all, gate_out), (up_all, up_out), (active_all, active_out))
-                )
-            ]
-
-        def first(z):
-            here = everyone[rows(z), :]
-            gate = contract_last(here, gates[0])
-            up = contract_last(here, gates[1])
-            gate_all[rows(z), :] = gate
-            up_all[rows(z), :] = up
-            active_all[rows(z), :] = gated_unit(gate, up).astype(jnp.bfloat16)
-            for copy in stores(z):
-                copy.start()
-
-        def second(z, piece):
-            window = sums.columns(piece)
-            parts[rows(z), window] = jnp.dot(
-                active_all[rows(z), :], downs[:, window], preferred_element_type=jnp.float32
-            ).astype(jnp.bfloat16)
-
-        work = Exchange(at, normed_ref, everyone, gather_sems, local.at[1], sums, first, second)
-        prepare()
-        work.by_columns(total, direct, relayed, ys + 1)
-        energy_out[...] = jnp.zeros_like(energy_out)
-        valid = length_ref[at.w]
-
-        def finish_rows(index, carry):
-            window = pl.ds(pl.multiple_of(index * 16, 16), 16)
-            final = attended_ref[window, :] + total[window, :]
-            final_out[window, :] = final.astype(jnp.bfloat16)
-            place = at.s * count + index * 16 + lax.broadcasted_iota(jnp.int32, final.shape, 0)
-            keep = (place < valid).astype(jnp.float32)
-            error = (final - teacher_ref[window, :].astype(jnp.float32)) * keep
-            error_out[window, :] = error
-            squares = error * error
-            energy_out[...] += 0.5 * (squares[:8] + squares[8:])
-            return carry
-
-        lax.fori_loop(0, count // 16, finish_rows, 0)
-        down_store.wait()
-        gates_store.wait()
-        for z in range(zs):
-            for copy in stores(z):
-                copy.wait()
-
-    low, f32 = jnp.bfloat16, jnp.float32
-    return remote_call(
-        kernel,
-        "feed_forward",
-        2,
-        [
-            jax.ShapeDtypeStruct((count, width), low),
-            jax.ShapeDtypeStruct((count, width), f32),
-            jax.ShapeDtypeStruct((8, width), f32),
-            jax.ShapeDtypeStruct((tokens, width), low),
-            jax.ShapeDtypeStruct((tokens, units), f32),
-            jax.ShapeDtypeStruct((tokens, units), f32),
-            jax.ShapeDtypeStruct((tokens, units), low),
-            jax.ShapeDtypeStruct((units, width), low),
-            jax.ShapeDtypeStruct((2, units, width), low),
-        ],
-        [
-            pltpu.VMEM((tokens, width), low),
+            pltpu.VMEM((token_count, width), low),
             pltpu.VMEM((2, units, width), low),
             pltpu.VMEM((units, width), low),
-            pltpu.VMEM((tokens, units), f32),
-            pltpu.VMEM((tokens, units), f32),
-            pltpu.VMEM((tokens, units), low),
-            pltpu.VMEM((tokens, width), low),
+            pltpu.VMEM((token_count, units), f32),
+            pltpu.VMEM((token_count, units), f32),
+            pltpu.VMEM((token_count, units), low),
+            pltpu.VMEM((token_count, width), low),
             pltpu.VMEM((count, width), f32),
         ]
         + LineGather.semaphores(wt, 2)
@@ -1343,15 +1313,11 @@
         + SquareGather.semaphores(seq)
         + SquareGather.semaphores(seq)
         + [pltpu.SemaphoreType.DMA((5,)), pltpu.SemaphoreType.DMA((4, zs))],
-        normed,
-        attended,
-        teacher,
+        *small,
         lengths,
-        gate_early,
-        gate_up_shard,
-        down_shard,
-        in_specs=[VMEM] * 3 + [SMEM] + [ANY] * 2 + [VMEM],
-        out_specs=[VMEM] * 3 + [ANY] * 6,
+        gate_up,
+        in_specs=[VMEM] * len(small) + [SMEM, ANY],
+        out_specs=[VMEM] * 3 + [ANY] * 8 + [VMEM] * 3 + [ANY] * 6,
     )
 
 
@@ -2112,7 +2078,7 @@
     segments = segment_ids
     (
         attended,
-        normed_low,
+        _,
         gain_rows,
         qkv_columns,
         out_rows,
@@ -2121,10 +2087,7 @@
         mixer_low,
         mixed_values,
         head_outputs,
-        gate_early,
         order,
-    ) = mixer_forward(rows_low, qkv_rows, w_out, gains, gate_up_low, segments, conv_weight)
-    (
         final_low,
         residual_error,
         energy,
@@ -2134,7 +2097,18 @@
         active_all,
         down_part,
         gate_up_part,
-    ) = feed_forward(normed_low, attended, teacher[0], valid_lengths, gate_early, gate_up_low, w_down)
+    ) = forward_pass(
+        rows_low,
+        qkv_rows,
+        w_out,
+        gains,
+        segments,
+        conv_weight,
+        teacher[0],
+        w_down,
+        valid_lengths,
+        gate_up_low,
+    )
     (
         attended_grad,
         mix_back,

time: 349 us -> 343 us (0.983)
  Pallas kernels: 344 us -> 338 us
    pallas_call x4 -> x3, Pallas kernels: 336 us -> 330 us  [remote_call(): pl.pallas_call(kernel, name=name, out_shape=outs, in_specs=[VMEM] * len(o...]
where the time goes in v8:
time: 343 us; the launch traced here: 340 us
  Pallas kernels  338 us (99%)
    pallas_call x3, Pallas kernels, remote_call(): pl.pallas_call(kernel, name=name, out_shape=outs, in_specs=[VMEM] * len(o...  330 us
    pallas_call x1, Pallas kernels, last_sums(): pl.pallas_call(kernel, name='last_sums', out_shape=[jax.ShapeDtypeStruct(...  7.89 us

profile of v8, /device:TPU:8, one launch (start us, length us, event | category | flops | bytes accessed | tf_op | source)
XLA Modules:
  0.0 340.5 jit_solution(10912936645723519013)
XLA Ops:
  0.6 1.3 convert_add_fusion.refs_3_
  1.9 158.7 %forward_pass.1 = (f32[128,2048]{1,0:T(8,128)}, bf16[128,2048]{1,0:T(8,128)(2,1)}, f32[8,2048]{1,0:T(8,128)}, bf16[4,8,64,640]{3,2,1,0:T(8,128)(2,1)}, bf16[8,64...) custom-call(bf16[128,2048]{1,0:T(8,128)(2,1)} %bitcast.18, ...), custom_call_target="tpu_custom_call" | custom-call | tf_op jit(solution)/shard_map/forward_pass/pallas_call | solution.py:390
  160.6 75.4 %feed_back.1 = (f32[128,2048]{1,0:T(8,128)}, bf16[128,2048]{1,0:T(8,128)(2,1)}, f32[8,2048]{1,0:T(8,128)}, bf16[4,2,352,512]{3,2,1,0:T(8,128)(2,1)}, bf16[4,2,35...) custom-call(f32[128,2048]{1,0:T(8,128)} %get-tuple-element.61.refs_0, ...), custom_call_target="tpu_custom_call" | custom-call | tf_op jit(solution)/shard_map/feed_back/pallas_call | solution.py:390
  236.1 96.4 %mixer_back.1 = (f32[128,2048]{1,0:T(8,128)}, f32[8,512]{1,0:T(8,128)}, bf16[4,64,640]{2,1,0:T(8,128)(2,1)}, f32[64,2048]{1,0:T(8,128)}, bf16[2,352,512]{2,1,0:T...) custom-call(bf16[512,2048]{1,0:T(8,128)(2,1)} %bitcast.17, ...), custom_call_target="tpu_custom_call" | custom-call | tf_op jit(solution)/shard_map/mixer_back/pallas_call | solution.py:390
  332.4 7.9 %last_sums.1 = (f32[4,352,512]{2,1,0:T(8,128)}, f32[2,352,512]{2,1,0:T(8,128)}, f32[64,2560]{1,0:T(8,128)}, f32[1,64]{1,0:T(1,128)}, f32[1,64]{1,0:T(1,128)}, /*...) custom-call(bf16[4,2,352,512]{3,2,1,0:T(8,128)(2,1)} %get-tuple-elem, ...), custom_call_target="tpu_custom_call" | custom-call | tf_op jit(solution)/shard_map/last_sums/pallas_call | solution.py:2020

commit v9 on v8

--- a/solution.py
+++ b/solution.py
@@ -31,11 +31,6 @@
     return lax.dot_general(
         former, latter, (((0,), (0,)), ((), ())), preferred_element_type=jnp.float32
     )
-
-
-def shift_down(values, amount, filler):
-    padding = jnp.full((amount,) + values.shape[1:], filler, values.dtype)
-    return jnp.concatenate([padding, values[:-amount]], axis=0)
 
 
 def gated_unit(gate_in, up_in):
@@ -666,33 +661,25 @@
         at = self.at
         return send(self.sum_x, self.last_x, self.last.at[at.ys, 0], self.last.at[at.ys, 1], at.across())
 
-    def second_start(self, fetch, rooms):
-        at = self.at
-        for step in range(1, at.ys):
-            y = at.beside(step)
-            fetch([(self.terms(y * 2 + at.x, 0), rooms[0]), (self.from_x.at[y], rooms[1])])
-            add_into(self.sum_y.at[y], [rooms[0], rooms[1]])
-        fetch([(self.terms(at.y * 2 + 1 - at.x, 1), self.sum_x)])
-        for step in range(1, at.ys):
-            y = at.beside(step)
-            fetch([(self.from_y.at[y, 1 - at.x], rooms[0])])
-            add_into(self.sum_x, [self.sum_x, rooms[0]])
-
-    def second_load(self, fetch):
+    def second_pairs(self, rooms=None):
         at = self.at
         pairs = [(self.terms(at.y * 2 + 1 - at.x, 1), self.sum_x)]
         for step in range(1, at.ys):
             y = at.beside(step)
             pairs.append((self.terms(y * 2 + at.x, 0), self.sum_y.at[y]))
-        fetch(pairs)
-
-    def second_arrived(self):
+            if rooms is not None:
+                pairs.append((self.from_x.at[y], rooms[0].at[step - 1]))
+                pairs.append((self.from_y.at[y, 1 - at.x], rooms[1].at[step - 1]))
+        return pairs
+
+    def second_add(self, rooms=None):
         at = self.at
         terms = [self.sum_x]
         for step in range(1, at.ys):
             y = at.beside(step)
-            add_into(self.sum_y.at[y], [self.sum_y.at[y], self.from_x.at[y]])
-            terms.append(self.from_y.at[y, 1 - at.x])
+            near = self.from_x.at[y] if rooms is None else rooms[0].at[step - 1]
+            add_into(self.sum_y.at[y], [self.sum_y.at[y], near])
+            terms.append(self.from_y.at[y, 1 - at.x] if rooms is None else rooms[1].at[step - 1])
         add_into(self.sum_x, terms)
 
     def second_go(self):
@@ -985,7 +972,7 @@
     return late.start, run
 
 
-def forward_pass(tokens, qkv_rows, out_rows, gains, segments, taps, teacher, down, lengths, gate_up):
+def forward_pass(tokens, qkv_rows, out_rows, norm_gain, mlp_gain, segments, taps, teacher, down, lengths, gate_up):
     seq, wt = lax.axis_size("seq"), lax.axis_size("wt")
     zs = wt // 2
     count, width = tokens.shape
@@ -1003,7 +990,8 @@
         tokens,
         qkv_rows,
         out_rows,
-        gains,
+        norm_gain[None],
+        mlp_gain[None],
         segments,
         taps,
         teacher,
@@ -1012,7 +1000,8 @@
     token_count = wt * count
 
     def kernel(*refs):
-        (x_ref, qkv_ref, out_ref, gain_ref, segment_ref, tap_ref, teacher_ref, down_ref), refs = refs[:8], refs[8:]
+        (x_ref, qkv_ref, out_ref, first_gain, second_gain, segment_ref, tap_ref), refs = refs[:7], refs[7:]
+        (teacher_ref, down_ref), refs = refs[:2], refs[2:]
         (length_ref, gate_up_ref), refs = refs[:2], refs[2:]
         (attended_out, normed_out, gain_rows), refs = refs[:3], refs[3:]
         (qkv_out, w_out_out, hidden_out, sorted_out, mixer_out, values_out, outputs_out, order_out), refs = (
@@ -1021,7 +1010,7 @@
         )
         feed_outputs, refs = refs[:9], refs[9:]
         (xs, qkvs, outs, gains_all, sorted_v, values_v, outputs_v), refs = refs[:7], refs[7:]
-        (order_v, segment_column, tap_v), refs = refs[:3], refs[3:]
+        (order_v, segment_column, tap_v, gain_ref), refs = refs[:4], refs[4:]
         sum_scratch, x_sems, gate_sems, refs = refs[:8], refs[8:11], refs[11:14], refs[14:]
         line_sems, refs = [refs[index : index + 1] for index in range(3)], refs[3:]
         (swap_q, swap_g, local, outgoing), feed_scratch = refs[:4], refs[4:]
@@ -1033,6 +1022,9 @@
             gate_up_ref, gates_ref.at[:, :, pl.ds(pl.multiple_of(at.s * block, block), block)], local.at[4]
         )
         gates_own.start()
+        gain_ref[...] = jnp.zeros_like(gain_ref)
+        gain_ref[0:1, :lanes_each] = first_gain[...].astype(jnp.float32)
+        gain_ref[1:2, :lanes_each] = second_gain[...].astype(jnp.float32)
         late_start, feed = feed_forward(
             at,
             (count, width, units, block, down.shape[1]),
@@ -1088,6 +1080,7 @@
             copy.start()
         for copy in own:
             copy.wait()
+        gather_o.start()
         for step in range(1, seq):
             s = lax.rem(at.s + step, seq)
             slot = gains_all.at[s, gain_slot]
@@ -1103,10 +1096,9 @@
         gather_x.relay()
         gates.start()
         for index in range(zs - 1):
-            if index == zs - 2:
-                gather_o.start()
             gather_g.step(index)
             gather_q.step(index)
+        gather_o.step(0)
         gather_g.finish()
 
         device_rows = gains_all[...].reshape(seq * wt * 8, 128).astype(jnp.bfloat16)
@@ -1205,7 +1197,8 @@
         turns = heads * steps
         for index in range(zs - 1):
             lax.fori_loop(turns * index // (zs - 1), turns * (index + 1) // (zs - 1), attend, 0)
-            gather_o.step(index)
+            if index > 0:
+                gather_o.step(index)
         gather_o.finish()
         for copy in stores[4:]:
             copy.start()
@@ -1289,11 +1282,14 @@
             pltpu.VMEM((qkv_width, sorted_width), low),
             pltpu.VMEM((length, 128), f32),
             pltpu.VMEM((KCONV, value_width), f32),
+            pltpu.VMEM((8, 128), f32),
         ]
         + SquareSum.scratch(seq, (count // 2, width))
         + SquareGather.semaphores(seq)
         + SquareGather.semaphores(seq)
-        + LineGather.semaphores(wt) * 3
+        + LineGather.semaphores(wt, 2)
+        + LineGather.semaphores(wt)
+        + LineGather.semaphores(wt, 2)
         + [
             pltpu.SemaphoreType.DMA((seq, 2)),
             pltpu.SemaphoreType.DMA((seq, 2)),
@@ -1575,6 +1571,7 @@
     rank = width // (seq * wt)
     gate_half, down_half = gate_parts[0].shape[2:], down_parts[0].shape[2:]
     rows_at_once = 256
+    turns = heads * length // rows_at_once
     big = [out_rows, qkv_columns, hidden, sorted_columns, mixer, mixed_values, head_outputs]
     small = [mix_back, attended_grad, tokens, gain, segments, taps, order, gain_terms, energy]
     far = list(gate_parts) + list(down_parts) + list(up_parts)
@@ -1588,13 +1585,13 @@
         (w_out_v, w_qkv_v, hidden_v, sorted_v, mixer_v, values_v, outputs_v), refs = refs[:7], refs[7:]
         (mix_all, mixer_grad, query_acc, key_acc, value_acc, back_sorted, back_v), refs = refs[:7], refs[7:]
         (hidden_parts, qkv_parts, out_parts, hidden_total, gain_acc, spread, taps_acc), refs = refs[:7], refs[7:]
-        (segment_column, tap_v), refs = refs[:2], refs[2:]
+        (segment_column, tap_v, slopes_v, weights_v, denominators_v), refs = refs[:5], refs[5:]
         (room_gate0, room_gate1, room_down0, room_down1, qkv_sum, first, middle, last), refs = refs[:8], refs[8:]
         hidden_scratch, refs = refs[:8], refs[8:]
         qkv_scratch, out_scratch, refs = refs[:4], refs[4:8], refs[8:]
         gate_scratch, down_scratch, up_scratch, refs = refs[:3], refs[3:6], refs[6:9], refs[9:]
         gather_sems, up_sems, refs = refs[:3], refs[3:5], refs[5:]
-        local, swap, first_sems, last_sems = refs
+        local, swap, first_sems, last_sems, fetch_sems = refs
         (
             mix_ref,
             grad_ref,
@@ -1615,6 +1612,19 @@
         ]
         for load in loads:
             load.start()
+        gate_sum = SquareTerms(at, lambda s, h: gate_t.at[s, h], gate_x, gate_y, None, gate_lasts, gate_scratch)
+        down_sum = SquareTerms(at, lambda s, h: down_t.at[s, h], down_x, down_y, None, down_lasts, down_scratch)
+        up_sum = SquareTerms(at, lambda s, h: up_t.at[s, h], up_x, up_y, up_sems, up_lasts, up_scratch)
+        gate_rooms, down_rooms = (room_gate0, room_gate1), (room_down0, room_down1)
+        fetches = [
+            pltpu.make_async_copy(source, target, fetch_sems.at[number, index])
+            for number, pairs in enumerate(
+                (gate_sum.second_pairs(gate_rooms), down_sum.second_pairs(down_rooms), up_sum.second_pairs())
+            )
+            for index, (source, target) in enumerate(pairs)
+        ]
+        for copy in fetches:
+            copy.start()
         at.meet(True, True)
         half = count // 2
         gather = SquareGather(
@@ -1629,37 +1639,52 @@
         )
         own.start()
 
-        def fetch(pairs):
-            copies = [
-                pltpu.make_async_copy(source, target, local.at[index])
-                for index, (source, target) in enumerate(pairs)
-            ]
-            for copy in copies:
-                copy.start()
-            for copy in copies:
-                copy.wait()
-
-        gate_sum = SquareTerms(at, lambda s, h: gate_t.at[s, h], gate_x, gate_y, None, gate_lasts, gate_scratch)
-        down_sum = SquareTerms(at, lambda s, h: down_t.at[s, h], down_x, down_y, None, down_lasts, down_scratch)
-        up_sum = SquareTerms(at, lambda s, h: up_t.at[s, h], up_x, up_y, up_sems, up_lasts, up_scratch)
-        gate_rooms, down_rooms = (room_gate0, room_gate1), (room_down0, room_down1)
-        gate_sum.second_start(fetch, gate_rooms)
-        gather.relay()
-        down_sum.second_start(fetch, down_rooms)
-        up_sum.second_load(fetch)
         tap_v[...] = tap_ref[...].astype(jnp.float32)
         segment_row = segment_ref[...].astype(jnp.float32)
         segment_column[...] = jnp.broadcast_to(segment_row, (128, length)).T
-        own.wait()
         for load in loads:
             load.wait()
         query_acc[...] = jnp.zeros_like(query_acc)
         key_acc[...] = jnp.zeros_like(key_acc)
         value_acc[...] = jnp.zeros_like(value_acc)
+        steps = length // rows_at_once
+        lanes = lax.broadcasted_iota(jnp.int32, (1, 128), 1)
+
+        def turn_of(index):
+            head, start = lax.div(index, steps), lax.rem(index, steps) * rows_at_once
+            rows = pl.ds(pl.multiple_of(start, rows_at_once), rows_at_once)
+            mine = ((lanes >= head * FEAT) & (lanes < head * FEAT + FEAT)).astype(jnp.float32)
+            queries = sorted_v[rows, value_width : value_width + 128] * mine.astype(jnp.bfloat16)
+            return head, start, rows, mine, queries
+
+        def prepare(index, carry):
+            head, start, rows, mine, queries = turn_of(index)
+            scores = contract_last(queries, sorted_v[:, value_width + 128 :]) * 0.25
+            places = start + lax.broadcasted_iota(jnp.int32, scores.shape, 0)
+            allowed = (segment_column[rows, :1] == segment_row) & (
+                places >= lax.broadcasted_iota(jnp.int32, scores.shape, 1)
+            )
+            kernel_values = jnp.where(allowed, 1.0 + scores + 0.5 * scores * scores, 0.0)
+            slopes_v[index] = jnp.where(allowed, 0.25 * (1.0 + scores), 0.0)
+            weights_v[index] = kernel_values.astype(jnp.bfloat16)
+            denominators_v[index] = jnp.broadcast_to(
+                jnp.sum(kernel_values, axis=1, keepdims=True), (rows_at_once, 128)
+            )
+            return carry
+
+        middle_step = heads * steps // 2
+        lax.fori_loop(0, middle_step, prepare, 0)
+        gather.relay()
+        lax.fori_loop(middle_step, heads * steps, prepare, 0)
+        for copy in fetches:
+            copy.wait()
+        gate_sum.second_add(gate_rooms)
+        down_sum.second_add(down_rooms)
+        own.wait()
         gather.finish()
+        up_sum.first_start()
         gate_sum.second_go()
         down_sum.second_go()
-        up_sum.first_start()
         mixer_grad[...] = contract_last(mix_all[...], w_out_v[...]).astype(jnp.bfloat16)
         out_sum = LinePieces(at, lambda w: out_parts.at[w], out_scratch)
         out_rank = out_parts.shape[1]
@@ -1675,44 +1700,28 @@
         lax.fori_loop(0, width // 512, out_job, 0)
         for piece in range(out_sum.pieces):
             out_sum.offer(piece)
-        out_sum.launch_all(0)
-
-        steps = length // rows_at_once
-        lanes = lax.broadcasted_iota(jnp.int32, (1, 128), 1)
+        for piece in range(out_sum.pieces):
+            out_sum.launch(piece, 0)
 
         def attend(index, carry):
-            head, start = lax.div(index, steps), lax.rem(index, steps) * rows_at_once
-            rows = pl.ds(pl.multiple_of(start, rows_at_once), rows_at_once)
+            head, start, rows, mine, queries = turn_of(index)
             columns = pl.ds(pl.multiple_of(head * DV, DV), DV)
-            mine = ((lanes >= head * FEAT) & (lanes < head * FEAT + FEAT)).astype(jnp.float32)
-            queries = sorted_v[rows, value_width : value_width + 128] * mine.astype(jnp.bfloat16)
-            keys = sorted_v[:, value_width + 128 :]
-            scores = contract_last(queries, keys) * 0.25
-            places = start + lax.broadcasted_iota(jnp.int32, scores.shape, 0)
-            allowed = (segment_column[rows, :1] == segment_row) & (
-                places >= lax.broadcasted_iota(jnp.int32, scores.shape, 1)
-            )
-            kernel_values = jnp.where(allowed, 1.0 + scores + 0.5 * scores * scores, 0.0)
-            denominator = jnp.sum(kernel_values, axis=1, keepdims=True)
+            denominator = denominators_v[index][:, :1]
             incoming = mixer_grad[rows, columns].astype(jnp.float32)
             numerator_back = (incoming / denominator).astype(jnp.bfloat16)
             denominator_back = (
                 -jnp.sum(incoming * outputs_v[head, rows, :], axis=1, keepdims=True) / denominator
             )
             weight_back = contract_last(numerator_back, values_v[head])
-            kernel_back = jnp.where(allowed, weight_back + denominator_back, 0.0)
-            dots_back = (0.25 * kernel_back * (1.0 + scores)).astype(jnp.bfloat16)
-            query_acc[rows, :] += jnp.dot(dots_back, keys, preferred_element_type=jnp.float32) * mine
+            dots_back = ((weight_back + denominator_back) * slopes_v[index]).astype(jnp.bfloat16)
+            query_acc[rows, :] += (
+                jnp.dot(dots_back, sorted_v[:, value_width + 128 :], preferred_element_type=jnp.float32) * mine
+            )
             key_acc[...] += contract_first(dots_back, queries)
-            value_acc[:, columns] += contract_first(kernel_values.astype(jnp.bfloat16), numerator_back)
+            value_acc[:, columns] += contract_first(weights_v[index], numerator_back)
             return carry
 
-        middle_step = heads * steps // 2
-        lax.fori_loop(0, middle_step, attend, 0)
-        for index in range(zs - 1, 1, -1):
-            if index == zs // 2:
-                lax.fori_loop(middle_step, heads * steps, attend, 0)
-            out_sum.pass_on(index)
+        lax.fori_loop(0, heads * steps, attend, 0)
         taps_acc[...] = jnp.zeros_like(taps_acc)
         marks = tap_marks(segment_column)
 
@@ -1735,6 +1744,7 @@
         back_sorted[:, value_width : value_width + 128] = query_acc[...].astype(jnp.bfloat16)
         back_sorted[:, value_width + 128 :] = key_acc[...].astype(jnp.bfloat16)
         back_v[...] = contract_last(back_sorted[...], order_ref[...]).astype(jnp.bfloat16)
+        out_sum.launch_all(1)
         qkv_sums = LinePieces(at, lambda w: qkv_parts.at[:, w], qkv_scratch)
         qkv_rank = qkv_parts.shape[2]
 
@@ -1767,11 +1777,13 @@
 
         lax.fori_loop(0, width // 512, hidden_job, 0)
         hidden_sum.start()
+        for index in range(zs - 1, 1, -1):
+            out_sum.pass_on(index)
         qkv_sums.launch_all(1)
         qkv_sums.pass_on(zs - 1)
         hidden_sum.relay()
         up_sum.first_wait()
-        up_sum.second_arrived()
+        up_sum.second_add()
         up_sum.second_go()
         for index in range(zs - 2, 1, -1):
             qkv_sums.pass_on(index)
@@ -1884,10 +1896,13 @@
             pltpu.VMEM(tile, f32),
             pltpu.VMEM((length, 128), f32),
             pltpu.VMEM((KCONV, value_width), f32),
-            pltpu.VMEM(gate_half, low),
-            pltpu.VMEM(gate_half, low),
-            pltpu.VMEM(down_half, low),
-            pltpu.VMEM(down_half, low),
+            pltpu.VMEM((turns, rows_at_once, length), f32),
+            pltpu.VMEM((turns, rows_at_once, length), low),
+            pltpu.VMEM((turns, rows_at_once, 128), f32),
+            pltpu.VMEM((ys - 1,) + gate_half, low),
+            pltpu.VMEM((ys - 1,) + gate_half, low),
+            pltpu.VMEM((ys - 1,) + down_half, low),
+            pltpu.VMEM((ys - 1,) + down_half, low),
             pltpu.VMEM((seq, qkv_rank, qkv_width), low),
             pltpu.VMEM((seq,) + tile, f32),
             pltpu.VMEM(tile, f32),
@@ -1906,6 +1921,7 @@
             pltpu.SemaphoreType.DMA((seq, 2)),
             pltpu.SemaphoreType.DMA((seq, 2)),
             pltpu.SemaphoreType.DMA((wt, 2)),
+            pltpu.SemaphoreType.DMA((3, 3 * (ys - 1) + 1)),
         ],
         *big,
         *small,
@@ -2045,10 +2061,6 @@
     )(*operands, qkv_total, totals, lengths, *passed)
 
 
-def rows_of_tile(values, row):
-    return jnp.pad(values[None, :], [(row, 7 - row), (0, 128 - values.shape[0])])
-
-
 def body(
     inputs,
     segment_ids,
@@ -2070,7 +2082,6 @@
     qkv_width = head_count * (2 * FEAT + DV)
     rows_low = inputs[0]
     gain_lanes = norm_gain.shape[0]
-    gains = rows_of_tile(norm_gain.astype(jnp.float32), 0) + rows_of_tile(mlp_gain.astype(jnp.float32), 1)
     qkv_rows = w_qkv
     if qkv_width % 128:
         qkv_rows = w_qkv.reshape(w_qkv.shape[0], seq_parts, qkv_width).transpose(1, 0, 2)
@@ -2101,7 +2112,8 @@
         rows_low,
         qkv_rows,
         w_out,
-        gains,
+        norm_gain,
+        mlp_gain,
         segments,
         conv_weight,
         teacher[0],

time: 343 us -> 342 us (level)
  no operation moved by 1% of the time
where the time goes in v9:
time: 342 us; the launch traced here: 339 us
  Pallas kernels  338 us (99%)
    pallas_call x3, Pallas kernels, remote_call(): pl.pallas_call(kernel, name=name, out_shape=outs, in_specs=[VMEM] * len(o...  331 us
    pallas_call x1, Pallas kernels, last_sums(): pl.pallas_call(kernel, name='last_sums', out_shape=[jax.ShapeDtypeStruct(...  7.89 us

profile of v9, /device:TPU:8, one launch (start us, length us, event | category | flops | bytes accessed | tf_op | source)
XLA Modules:
  0.0 339.3 jit_solution(12051804227090507597)
XLA Ops:
  0.6 159.1 %forward_pass.1 = (f32[128,2048]{1,0:T(8,128)}, bf16[128,2048]{1,0:T(8,128)(2,1)}, f32[8,2048]{1,0:T(8,128)}, bf16[4,8,64,640]{3,2,1,0:T(8,128)(2,1)}, bf16[8,64...) custom-call(bf16[128,2048]{1,0:T(8,128)(2,1)} %bitcast.18, ...), custom_call_target="tpu_custom_call" | custom-call | tf_op jit(solution)/shard_map/forward_pass/pallas_call | solution.py:385
  159.8 75.5 %feed_back.1 = (f32[128,2048]{1,0:T(8,128)}, bf16[128,2048]{1,0:T(8,128)(2,1)}, f32[8,2048]{1,0:T(8,128)}, bf16[4,2,352,512]{3,2,1,0:T(8,128)(2,1)}, bf16[4,2,35...) custom-call(f32[128,2048]{1,0:T(8,128)} %get-tuple-element.61.refs_0, ...), custom_call_target="tpu_custom_call" | custom-call | tf_op jit(solution)/shard_map/feed_back/pallas_call | solution.py:385
  235.3 96.0 %mixer_back.1 = (f32[128,2048]{1,0:T(8,128)}, f32[8,512]{1,0:T(8,128)}, bf16[4,64,640]{2,1,0:T(8,128)(2,1)}, f32[64,2048]{1,0:T(8,128)}, bf16[2,352,512]{2,1,0:T...) custom-call(bf16[512,2048]{1,0:T(8,128)(2,1)} %bitcast.17, ...), custom_call_target="tpu_custom_call" | custom-call | tf_op jit(solution)/shard_map/mixer_back/pallas_call | solution.py:385
  331.3 7.9 %last_sums.1 = (f32[4,352,512]{2,1,0:T(8,128)}, f32[2,352,512]{2,1,0:T(8,128)}, f32[64,2560]{1,0:T(8,128)}, f32[1,64]{1,0:T(1,128)}, f32[1,64]{1,0:T(1,128)}, /*...) custom-call(bf16[4,2,352,512]{3,2,1,0:T(8,128)(2,1)} %get-tuple-elem, ...), custom_call_target="tpu_custom_call" | custom-call | tf_op jit(solution)/shard_map/last_sums/pallas_call | solution.py:2036

commit v10 on v9

--- a/solution.py
+++ b/solution.py
@@ -995,14 +995,12 @@
         segments,
         taps,
         teacher,
-        down,
     ]
     token_count = wt * count
 
     def kernel(*refs):
         (x_ref, qkv_ref, out_ref, first_gain, second_gain, segment_ref, tap_ref), refs = refs[:7], refs[7:]
-        (teacher_ref, down_ref), refs = refs[:2], refs[2:]
-        (length_ref, gate_up_ref), refs = refs[:2], refs[2:]
+        (teacher_ref, length_ref, gate_up_ref, down_ref), refs = refs[:4], refs[4:]
         (attended_out, normed_out, gain_rows), refs = refs[:3], refs[3:]
         (qkv_out, w_out_out, hidden_out, sorted_out, mixer_out, values_out, outputs_out, order_out), refs = (
             refs[:8],
@@ -1312,7 +1310,8 @@
         *small,
         lengths,
         gate_up,
-        in_specs=[VMEM] * len(small) + [SMEM, ANY],
+        down,
+        in_specs=[VMEM] * len(small) + [SMEM, ANY, ANY],
         out_specs=[VMEM] * 3 + [ANY] * 8 + [VMEM] * 3 + [ANY] * 6,
     )
 
@@ -1572,8 +1571,9 @@
     gate_half, down_half = gate_parts[0].shape[2:], down_parts[0].shape[2:]
     rows_at_once = 256
     turns = heads * length // rows_at_once
-    big = [out_rows, qkv_columns, hidden, sorted_columns, mixer, mixed_values, head_outputs]
-    small = [mix_back, attended_grad, tokens, gain, segments, taps, order, gain_terms, energy]
+    soon = [out_rows, qkv_columns, hidden, sorted_columns, mixer, mixed_values, head_outputs]
+    big = soon + [attended_grad, tokens, order, gain_terms, energy]
+    small = [mix_back, gain, segments, taps]
     far = list(gate_parts) + list(down_parts) + list(up_parts)
 
     def kernel(*refs):
@@ -1582,7 +1582,9 @@
         (gate_t, gate_x, gate_y, down_t, down_x, down_y, up_t), refs = refs[: len(far)], refs[len(far) :]
         (grad_out, sums_out, qkv_out, w_out_out, up_x, up_y), refs = refs[:6], refs[6:]
         gate_lasts, up_lasts, down_lasts, refs = refs[:2], refs[2:4], refs[4:6], refs[6:]
-        (w_out_v, w_qkv_v, hidden_v, sorted_v, mixer_v, values_v, outputs_v), refs = refs[:7], refs[7:]
+        big_rooms, refs = refs[: len(big)], refs[len(big) :]
+        w_out_v, w_qkv_v, hidden_v, sorted_v, mixer_v, values_v, outputs_v = big_rooms[: len(soon)]
+        grad_ref, token_ref, order_ref, gain_two, energy_ref = big_rooms[len(soon) :]
         (mix_all, mixer_grad, query_acc, key_acc, value_acc, back_sorted, back_v), refs = refs[:7], refs[7:]
         (hidden_parts, qkv_parts, out_parts, hidden_total, gain_acc, spread, taps_acc), refs = refs[:7], refs[7:]
         (segment_column, tap_v, slopes_v, weights_v, denominators_v), refs = refs[:5], refs[5:]
@@ -1592,23 +1594,11 @@
         gate_scratch, down_scratch, up_scratch, refs = refs[:3], refs[3:6], refs[6:9], refs[9:]
         gather_sems, up_sems, refs = refs[:3], refs[3:5], refs[5:]
         local, swap, first_sems, last_sems, fetch_sems = refs
-        (
-            mix_ref,
-            grad_ref,
-            token_ref,
-            gain_ref,
-            segment_ref,
-            tap_ref,
-            order_ref,
-            gain_two,
-            energy_ref,
-        ) = small_refs
+        mix_ref, gain_ref, segment_ref, tap_ref = small_refs
         at = Place(seq, wt)
         loads = [
             pltpu.make_async_copy(source, target, local.at[4 + index])
-            for index, (source, target) in enumerate(
-                zip(big_refs, (w_out_v, w_qkv_v, hidden_v, sorted_v, mixer_v, values_v, outputs_v))
-            )
+            for index, (source, target) in enumerate(zip(big_refs, big_rooms))
         ]
         for load in loads:
             load.start()
@@ -1642,7 +1632,7 @@
         tap_v[...] = tap_ref[...].astype(jnp.float32)
         segment_row = segment_ref[...].astype(jnp.float32)
         segment_column[...] = jnp.broadcast_to(segment_row, (128, length)).T
-        for load in loads:
+        for load in loads[: len(soon)]:
             load.wait()
         query_acc[...] = jnp.zeros_like(query_acc)
         key_acc[...] = jnp.zeros_like(key_acc)
@@ -1681,6 +1671,8 @@
         gate_sum.second_add(gate_rooms)
         down_sum.second_add(down_rooms)
         own.wait()
+        for load in loads[len(soon) :]:
+            load.wait()
         gather.finish()
         up_sum.first_start()
         gate_sum.second_go()
@@ -1917,7 +1909,7 @@
         + SquareGather.semaphores(seq)
         + SquareTerms.semaphores(seq)
         + [
-            pltpu.SemaphoreType.DMA((11,)),
+            pltpu.SemaphoreType.DMA((4 + len(big),)),
             pltpu.SemaphoreType.DMA((seq, 2)),
             pltpu.SemaphoreType.DMA((seq, 2)),
             pltpu.SemaphoreType.DMA((wt, 2)),
@@ -2003,7 +1995,7 @@
             for copy in copies[number]:
                 copy.wait()
             rows = own.shape[1]
-            tile = next(t for t in (64, 32, 16) if rows % t == 0)
+            tile = next(t for t in (176, 64, 32, 16) if rows % t == 0)
 
             def step(index, carry):
                 window = pl.ds(pl.multiple_of(index * tile, tile), tile)

time: 342 us -> 341 us (level)
  no operation moved by 1% of the time
where the time goes in v10:
time: 341 us; the launch traced here: 338 us
  Pallas kernels  337 us (99%)
    pallas_call x3, Pallas kernels, remote_call(): pl.pallas_call(kernel, name=name, out_shape=outs, in_specs=[VMEM] * len(o...  330 us
    pallas_call x1, Pallas kernels, last_sums(): pl.pallas_call(kernel, name='last_sums', out_shape=[jax.ShapeDtypeStruct(...  7.89 us

profile of v10, /device:TPU:8, one launch (start us, length us, event | category | flops | bytes accessed | tf_op | source)
XLA Modules:
  0.0 338.3 jit_solution(3422565147790363341)
XLA Ops:
  0.6 158.9 %forward_pass.1 = (f32[128,2048]{1,0:T(8,128)}, bf16[128,2048]{1,0:T(8,128)(2,1)}, f32[8,2048]{1,0:T(8,128)}, bf16[4,8,64,640]{3,2,1,0:T(8,128)(2,1)}, bf16[8,64...) custom-call(bf16[128,2048]{1,0:T(8,128)(2,1)} %bitcast.18, ...), custom_call_target="tpu_custom_call" | custom-call | tf_op jit(solution)/shard_map/forward_pass/pallas_call | solution.py:385
  159.6 75.4 %feed_back.1 = (f32[128,2048]{1,0:T(8,128)}, bf16[128,2048]{1,0:T(8,128)(2,1)}, f32[8,2048]{1,0:T(8,128)}, bf16[4,2,352,512]{3,2,1,0:T(8,128)(2,1)}, bf16[4,2,35...) custom-call(f32[128,2048]{1,0:T(8,128)} %get-tuple-element.61.refs_0, ...), custom_call_target="tpu_custom_call" | custom-call | tf_op jit(solution)/shard_map/feed_back/pallas_call | solution.py:385
  235.0 95.3 %mixer_back.1 = (f32[128,2048]{1,0:T(8,128)}, f32[8,512]{1,0:T(8,128)}, bf16[4,64,640]{2,1,0:T(8,128)(2,1)}, f32[64,2048]{1,0:T(8,128)}, bf16[2,352,512]{2,1,0:T...) custom-call(bf16[512,2048]{1,0:T(8,128)(2,1)} %bitcast.17, ...), custom_call_target="tpu_custom_call" | custom-call | tf_op jit(solution)/shard_map/mixer_back/pallas_call | solution.py:385
  330.3 7.9 %last_sums.1 = (f32[4,352,512]{2,1,0:T(8,128)}, f32[2,352,512]{2,1,0:T(8,128)}, f32[64,2560]{1,0:T(8,128)}, f32[1,64]{1,0:T(1,128)}, f32[1,64]{1,0:T(1,128)}, /*...) custom-call(bf16[4,2,352,512]{3,2,1,0:T(8,128)(2,1)} %get-tuple-elem, ...), custom_call_target="tpu_custom_call" | custom-call | tf_op jit(solution)/shard_map/last_sums/pallas_call | solution.py:2028
